TPU v7x, 32 devices: a whole 2x2x4 slice. The times are simulated.
32 devices in a mesh: grp: 2 (over y), rows: 4 (over z), wt: 4 (over x, core).
Axes of the slice: x: 2, y: 2, z: 4, core: 2. Of those that a mesh axis runs over, the one named last changes fastest.
Arguments:
- latents: float32 [8, 640, 8, 128], P(('grp', 'wt'), None, 'rows'), parts along dimension 0, may hold values from -48 to 48
- teacher: float32 [8, 640, 8, 128], P(('grp', 'wt'), None, 'rows'), parts along dimension 0, may hold values from -6 to 6
- norm_gain: float32 [640], replicated, may hold values from 0.25 to 1.75
- norm_shift: float32 [640], replicated, may hold values from -3 to 3
- conv_weight: bfloat16 [640, 9, 640], P('wt'), may hold values from -0.078125 to 0.078125
- conv_bias: float32 [640], replicated, may hold values from -3 to 3
Outputs:
- mean_loss: float32 [2], P('grp'), parts along dimension 0
- grad_latents: float32 [8, 640, 8, 128], P(('grp', 'wt'), None, 'rows'), parts along dimension 0
- grad_weight: float32 [1280, 9, 640], P(('grp', 'wt')), parts along dimension 0
- param_grads: float32 [6, 640], P('grp'), parts along dimension 0
There are 2 independent parts, one for each index of `grp`. A program takes and returns all parts, laid end to end along the dimension named above; an argument that names none is the same for every part. Nothing has to cross between parts.
All inputs are finite; a program needn't handle non-finite values.
Results may differ from a plain program's by a relative error of at most 0.0013.
Values may be sent and summed in bfloat16 or wider, within the bound.
No kernel may reach another device: no remote copies, remote signals or barrier semaphores. Data moves between devices by JAX's collectives and lax.ppermute only.
A program may use at most 64 MiB of HBM per device.

v0:
```python
import jax
import jax.numpy as jnp
from jax import lax
from jax.sharding import PartitionSpec as P

GROUPS = 32


epsilon = 1e-05


def with_halo(shard, sides, width):
    for axis, dim in sides:
        devices, length = (lax.axis_size(axis), shard.shape[dim])
        up = [(i, (i + 1) % devices) for i in range(devices - 1)]
        down = [(j, i) for i, j in up]
        last = lax.slice_in_dim(shard, length - width, length, axis=dim)
        leading = lax.slice_in_dim(shard, 0, width, axis=dim)
        before = lax.ppermute(last, axis, up)
        after = lax.ppermute(leading, axis, down)
        shard = jnp.concatenate([before, shard, after], axis=dim)
    return shard


def conv_taps(weights, padded, strip_rows, column_count):
    running = None
    for tap_index in range(9):
        tap_row, tap_col = (tap_index // 3, tap_index % 3)
        window = padded[:, :, tap_row : tap_row + strip_rows, tap_col : tap_col + column_count]
        window = window.reshape(padded.shape[0], padded.shape[1], strip_rows * column_count)
        product = jnp.einsum(
            "oi,nip->nop", weights[:, tap_index, :], window, preferred_element_type=jnp.float32
        )
        running = product if running is None else running + product
    return running


def transpose_taps(weights, padded, strip_rows, column_count):
    running = None
    for tap_index in range(9):
        tap_row, tap_col = (tap_index // 3, tap_index % 3)
        window = padded[
            :, :, 2 - tap_row : 2 - tap_row + strip_rows, 2 - tap_col : 2 - tap_col + column_count
        ]
        window = window.reshape(padded.shape[0], padded.shape[1], strip_rows * column_count)
        product = jnp.einsum(
            "oi,nop->nip", weights[:, tap_index, :], window, preferred_element_type=jnp.float32
        )
        running = product if running is None else running + product
    return running


def weight_terms(residual, padded, strip_rows, column_count):
    columns = []
    for tap_index in range(9):
        tap_row, tap_col = (tap_index // 3, tap_index % 3)
        window = padded[:, :, tap_row : tap_row + strip_rows, tap_col : tap_col + column_count]
        window = window.reshape(padded.shape[0], padded.shape[1], strip_rows * column_count)
        columns.append(
            jnp.einsum("nop,nip->oi", residual, window, preferred_element_type=jnp.float32)
        )
    return jnp.stack(columns, axis=1)


def on_device(latents, teacher, norm_gain, norm_shift, conv_weight, conv_bias):
    row_devices = lax.axis_size("rows")
    panel_devices = lax.axis_size("wt")
    images, channels, strip_rows, column_count = latents.shape
    cell_count = strip_rows * column_count
    total_cells = panel_devices * row_devices * cell_count
    group_cells = channels // GROUPS * cell_count * row_devices
    grouped = latents.reshape(images, GROUPS, channels // GROUPS, cell_count)
    group_sum, square_sum = lax.psum(
        (
            jnp.sum(grouped, axis=(2, 3), keepdims=True),
            jnp.sum(jnp.square(grouped), axis=(2, 3), keepdims=True),
        ),
        "rows",
    )
    group_mean = group_sum / group_cells
    centered = grouped - group_mean
    group_var = square_sum / group_cells - jnp.square(group_mean)
    inverse = lax.rsqrt(group_var + epsilon)
    normed = (centered * inverse).reshape(images, channels, cell_count)
    gain_column = norm_gain[None, :, None]
    pre_norm = normed * gain_column + norm_shift[None, :, None]
    sigmoid_pre = jax.nn.sigmoid(pre_norm)
    hidden = (pre_norm * sigmoid_pre).astype(jnp.bfloat16)
    column_pad = ((0, 0), (0, 0), (0, 0), (1, 1))
    framed_hidden = with_halo(
        hidden.reshape(images, channels, strip_rows, column_count), (("rows", 2),), 1
    )
    padded = jnp.pad(framed_hidden, column_pad)
    all_images = lax.all_gather(framed_hidden, "wt", axis=0, tiled=True)
    all_padded = jnp.pad(all_images, column_pad)
    conv_out = conv_taps(
        lax.all_gather(conv_weight, "wt", axis=0, tiled=True), padded, strip_rows, column_count
    )
    residual = (
        latents.reshape(images, channels, cell_count)
        + conv_out
        + conv_bias[None, :, None]
        - teacher.reshape(images, channels, cell_count)
    )
    low_residual = residual.astype(jnp.bfloat16)
    framed_residual = with_halo(
        low_residual.reshape(images, channels, strip_rows, column_count), (("rows", 2),), 1
    )
    padded_residual = jnp.pad(framed_residual, column_pad)
    panel_residual = lax.all_to_all(framed_residual, "wt", split_axis=1, concat_axis=0, tiled=True)
    panel_rows = channels // panel_devices
    panel_inner = panel_residual[:, :, 1 : strip_rows + 1, :].reshape(
        panel_residual.shape[0], panel_rows, cell_count
    )
    window = padded_residual
    grad_hidden = transpose_taps(
        lax.all_gather(conv_weight, "wt", axis=0, tiled=True), window, strip_rows, column_count
    )
    window = panel_inner
    weight_share = lax.psum_scatter(
        weight_terms(window, all_padded, strip_rows, column_count),
        "rows",
        scatter_dimension=0,
        tiled=True,
    )
    grad_weight = lax.all_gather(weight_share, "rows", axis=0, tiled=True) / total_cells
    grad_pre = grad_hidden * sigmoid_pre * (1.0 + pre_norm * (1.0 - sigmoid_pre))
    grad_norm = (grad_pre * gain_column).reshape(grouped.shape)
    normed_groups = normed.reshape(grouped.shape)
    first_sum, second_sum = lax.psum(
        (
            jnp.sum(grad_norm, axis=(2, 3), keepdims=True),
            jnp.sum(grad_norm * normed_groups, axis=(2, 3), keepdims=True),
        ),
        "rows",
    )
    first_mean = first_sum / group_cells
    second_mean = second_sum / group_cells
    grad_latents = residual.reshape(latents.shape) + (
        inverse * (grad_norm - first_mean - normed_groups * second_mean)
    ).reshape(latents.shape)
    totals = lax.psum(
        (
            jnp.sum(jnp.square(residual)),
            jnp.sum(residual, axis=(0, 2)),
            jnp.sum(grad_pre * normed, axis=(0, 2)),
            jnp.sum(grad_pre, axis=(0, 2)),
        ),
        ("rows", "wt"),
    )
    mean_loss = (totals[0] / (total_cells * channels)).reshape(1)
    param_grads = jnp.stack([totals[1], totals[2], totals[3]]) / total_cells
    return (mean_loss, grad_latents, grad_weight, param_grads)


def solution(mesh):
    placed = (
        P(("grp", "wt"), None, "rows", None),
        P(("grp", "wt"), None, "rows", None),
        P(),
        P(),
        P("wt", None, None),
        P(),
    )
    return jax.shard_map(
        on_device,
        mesh=mesh,
        in_specs=placed,
        out_specs=(
            P("grp"),
            P(("grp", "wt"), None, "rows", None),
            P(("grp", "wt"), None, None),
            P("grp", None),
        ),
        check_vma=False,
    )
```

profile of v0, /device:TPU:0, one launch (start us, length us, event | category | flops | bytes accessed | tf_op | source)
XLA Modules:
  0.0 272.6 jit_solution(3519481623313573264)
XLA Ops:
  9.4 3.7 %fusion.73 = (f32[640]{0:T(1024)S(1)}, f32[640]{0:T(1024)S(1)}) fusion(f32[1,640,2,128]{3,2,1,0:T(2,128)} %param.6), kind=kLoop, calls=%fused_computation.123 | loop fusion | flops 490240 | bytes 660480 | tf_op jit(solution)/shard_map/reduce_sum | solution.py:75
  13.6 13.5 %all-reduce.5 = (f32[1,32,1,1]{1,3,2,0:T(1,128)S(1)}, f32[1,32,1,1]{1,3,2,0:T(1,128)S(1)}) all-reduce(f32[1,32,1,1]{1,3,2,0:T(1,128)S(1)} %bitcast.223, f32[1,32,1,1]{1,3,2,0:T(1,128)S(1)} %bitcast.221), channel_id=1, replica_groups=mesh['grp'=2,'rows'=4,'wt'=4] {'rows'}, use_global_device_ids=true, to_apply=%region_5.6 | all-reduce | flops 64 | bytes 512 | tf_op jit(solution)/shard_map/psum | solution.py:73
  31.8 4.4 %collective-permute-done.1 = bf16[1,640,1,128]{1,3,2,0:T(8,128)(2,1)S(1)} collective-permute-done((bf16[1,640,1,128]{1,3,2,0:T(8,128)(2,1)S(1)}, bf16[1,640,1,128]{1,3,2,0:T(8,128)(2,1)S(1)}, u32[]{:S(2)}, u32[]{:S(2)}) %collective-permute-start.1) | collective-permute-done | bytes 163872 | tf_op jit(solution)/shard_map/ppermute | solution.py:20
  41.0 23.8 %all-gather.4.cloned.1.call-done = bf16[640,9,640]{2,0,1:T(8,128)(2,1)} async-done(((bf16[160,9,640]{2,0,1:T(8,128)(2,1)}), bf16[640,9,640]{2,0,1:T(8,128)(2,1)}) %all-gather.4.cloned.1.call-update) | async-done | bytes 7372816 | tf_op jit(solution)/shard_map/all_gather | solution.py:97
  64.8 1.8 fusion.52
  66.7 2.5 fusion.54
  69.2 1.6 convolution_add_fusion.13
  74.4 2.0 fusion.72
  76.4 3.4 %collective-permute-start.2 = (bf16[1,640,1,128]{1,3,2,0:T(8,128)(2,1)S(1)}, bf16[1,640,1,128]{1,3,2,0:T(8,128)(2,1)S(1)}, u32[]{:S(2)}, u32[]{:S(2)}) collective-permute-start(bf16[1,640,1,128]{1,3,2,0:T(8,128)(2,1)S(1)} %get-tuple-element.52), channel_id=1, source_target_pairs={{0,4},{4,8},{8,12},{1,5},{5,9},{9,13},{2,6},{6,10},{10,14},{3,7},{... | collective-permute-start | bytes 491528 | tf_op jit(solution)/shard_map/ppermute | solution.py:19
  81.1 2.6 collective-permute-done.2
  83.6 4.1 %collective-permute-done.3 = bf16[1,640,1,128]{1,3,2,0:T(8,128)(2,1)S(1)} collective-permute-done((bf16[1,640,1,128]{1,3,2,0:T(8,128)(2,1)S(1)}, bf16[1,640,1,128]{1,3,2,0:T(8,128)(2,1)S(1)}, u32[]{:S(2)}, u32[]{:S(2)}) %collective-permute-start.3) | collective-permute-done | bytes 163872 | tf_op jit(solution)/shard_map/ppermute | solution.py:20
  89.4 12.7 %all_to_all.12 = bf16[1,640,4,128]{3,2,0,1:T(4,128)(2,1)S(1)} all-to-all(bf16[1,640,4,128]{3,2,0,1:T(4,128)(2,1)S(1)} %copy.57), channel_id=1, replica_groups=mesh['grp'=2,'rows'=4,'wt'=4] {'wt'}, dimensions={1} | all-to-all | bytes 1310720 | tf_op jit(solution)/shard_map/all_to_all | solution.py:110
  102.5 2.9 %fusion.32 = f32[160,9,640]{2,0,1:T(8,128)} fusion(bf16[4,640,4,128]{3,1,2,0:T(8,128)(2,1)} %all-gather.6.cloned.1.call-done, bf16[4,160,2,128]{3,2,1,0:T(2,128)(2,1)S(1)} %slice.193), kind=kOutput, calls=%fused_computation.53 | convolution fusion | flops 209715200 | bytes 3358720 | tf_op jit(solution)/shard_map/nop,nip->oi/dot_general | solution.py:60
  105.3 2.6 fusion.36
  117.8 68.0 %reduce-scatter.2.cloned.1.call-done = f32[40,9,640]{2,0,1:T(8,128)} async-done(((f32[160,9,640]{2,0,1:T(8,128)}), f32[40,9,640]{2,0,1:T(8,128)}) %reduce-scatter.2.cloned.1.call-update) | async-done | bytes 921616 | tf_op jit(solution)/shard_map/reduce_scatter | solution.py:120
  188.4 2.1 pad_slice_fusion.37
  190.5 1.6 fusion.51
  192.1 1.6 fusion.53
  196.5 1.6 multiply_reduce_fusion
  198.2 35.5 %all-reduce.3 = (f32[]{:T(128)}, f32[1,640]{1,0:T(1,128)S(1)}, f32[1,640]{1,0:T(1,128)S(1)}, f32[1,640]{1,0:T(1,128)S(1)}) all-reduce(f32[]{:T(128)} %get-tuple-element.24, f32[1,640]{1,0:T(1,128)S(1)} %stack.54, f32[1,640]{1,0:T(1,128)S(1)} %stack.53, f32[1,640]{1,0:T(1,128)S(1)} %stack.52), channel_id=1, replica_groups=mesh['grp'=2,'rows'=4,'wt'=4] {'rows','wt'}, use_global_device_ids=true, to_apply=%region_7.8 | all-reduce | flops 1921 | bytes 15368 | tf_op jit(solution)/shard_map/psum | solution.py:142
  234.1 9.1 %all-reduce.4 = (f32[1,32,1,1]{1,3,2,0:T(1,128)S(1)}, f32[1,32,1,1]{1,3,2,0:T(1,128)S(1)}) all-reduce(f32[1,32,1,1]{1,3,2,0:T(1,128)S(1)} %bitcast.222, f32[1,32,1,1]{1,3,2,0:T(1,128)S(1)} %bitcast.220), channel_id=1, replica_groups=mesh['grp'=2,'rows'=4,'wt'=4] {'rows'}, use_global_device_ids=true, to_apply=%region_13.14 | all-reduce | flops 64 | bytes 512 | tf_op jit(solution)/shard_map/psum | solution.py:130
  243.5 1.6 multiply_add_fusion
  247.6 13.2 %all-gather.8.cloned.1.call-done = f32[160,9,640]{2,0,1:T(8,128)} async-done(((f32[40,9,640]{2,0,1:T(8,128)}), f32[160,9,640]{2,0,1:T(8,128)}) %all-gather.8.cloned.1.call-update) | async-done | bytes 3686416 | tf_op jit(solution)/shard_map/all_gather | solution.py:126
  260.8 4.1 %broadcast_multiply_fusion = f32[160,9,640]{2,0,1:T(8,128)} fusion(f32[160,9,640]{2,0,1:T(8,128)} %all-gather.8.cloned.1.call-done), kind=kLoop, calls=%fused_computation.6 | loop fusion | flops 921600 | bytes 7372800 | tf_op jit(solution)/shard_map/div | solution.py:126
  (103 shorter events, 36.6 us)
Async XLA Ops:
  7.2 20.2 %copy-start.14 = (f32[640]{0:T(1024)S(1)}, f32[640]{0:T(1024)}, u32[]{:S(2)}) copy-start(f32[640]{0:T(1024)} %param.8) | copy-start | bytes 7684
  7.2 20.2 %copy-start.13 = (f32[640]{0:T(1024)S(1)}, f32[640]{0:T(1024)}, u32[]{:S(2)}) copy-start(f32[640]{0:T(1024)} %param.9) | copy-start | bytes 7684
  7.2 57.6 %all-gather.4.cloned.1.call-start = ((), (), s32[]{:S(2)}) async-start(), calls=%async_computation.2 | async-start | bytes 9216000 | tf_op jit(solution)/shard_map/all_gather | solution.py:97
  7.9 94.5 %all-gather.6.cloned.1.call-start = ((), (), s32[]{:S(2)}) async-start(), calls=%async_computation.3 | async-start | bytes 3276800 | tf_op jit(solution)/shard_map/all_gather | solution.py:94
  9.4 64.9 %copy-start.2 = (f32[1,640,2,128]{1,3,2,0:T(8,128)}, f32[1,640,2,128]{1,3,2,0:T(8,128)S(1)}, u32[]{:S(2)}) copy-start(f32[1,640,2,128]{1,3,2,0:T(8,128)S(1)} %copy.54) | copy-start | bytes 1966084
  27.7 4.1 %collective-permute-start = (bf16[1,640,1,128]{1,3,2,0:T(8,128)(2,1)S(1)}, bf16[1,640,1,128]{1,3,2,0:T(8,128)(2,1)S(1)}, u32[]{:S(2)}, u32[]{:S(2)}) collective-permute-start(bf16[1,640,1,128]{1,3,2,0:T(8,128)(2,1)S(1)} %get-tuple-element.56), channel_id=1, source_target_pairs={{0,4},{4,8},{8,12},{1,5},{5,9},{9,13},{2,6},{6,10},{10,14},{3,7},{... | collective-permute-start | bytes 491528 | tf_op jit(solution)/shard_map/ppermute | solution.py:19
  29.0 7.2 %collective-permute-start.1 = (bf16[1,640,1,128]{1,3,2,0:T(8,128)(2,1)S(1)}, bf16[1,640,1,128]{1,3,2,0:T(8,128)(2,1)S(1)}, u32[]{:S(2)}, u32[]{:S(2)}) collective-permute-start(bf16[1,640,1,128]{1,3,2,0:T(8,128)(2,1)S(1)} %get-tuple-element.57), channel_id=1, source_target_pairs={{4,0},{8,4},{12,8},{5,1},{9,5},{13,9},{6,2},{10,6},{14,10},{7,3},{... | collective-permute-start | bytes 491528 | tf_op jit(solution)/shard_map/ppermute | solution.py:20
  37.4 148.4 %reduce-scatter.2.cloned.1.call-start = ((), (), s32[]{:S(2)}) async-start(), calls=%async_computation.4 | async-start | bytes 4608000 | tf_op jit(solution)/shard_map/reduce_scatter | solution.py:120
  64.8 4.4 %copy-start.7 = (bf16[1,640,2,128]{1,3,2,0:T(8,128)(2,1)S(1)}, bf16[1,640,2,128]{1,3,2,0:T(8,128)(2,1)}, u32[]{:S(2)}) copy-start(bf16[1,640,2,128]{1,3,2,0:T(8,128)(2,1)} %get-tuple-element.55) | copy-start | bytes 983044
  64.8 6.0 %copy-start.9 = (bf16[1,640,2,128]{1,3,2,0:T(8,128)(2,1)S(1)}, bf16[1,640,2,128]{1,3,2,0:T(8,128)(2,1)}, u32[]{:S(2)}) copy-start(bf16[1,640,2,128]{1,3,2,0:T(8,128)(2,1)} %get-tuple-element.45) | copy-start | bytes 983044
  64.8 7.6 %copy-start.1 = (bf16[640,9,640]{2,0,1:T(8,128)(2,1)S(1)}, bf16[640,9,640]{2,0,1:T(8,128)(2,1)}, u32[]{:S(2)}) copy-start(bf16[640,9,640]{2,0,1:T(8,128)(2,1)} %all-gather.4.cloned.1.call-done) | copy-start | bytes 22118404
  66.7 5.7 %copy-start.8 = (bf16[1,640,2,128]{1,3,2,0:T(8,128)(2,1)S(1)}, bf16[1,640,2,128]{1,3,2,0:T(8,128)(2,1)}, u32[]{:S(2)}) copy-start(bf16[1,640,2,128]{1,3,2,0:T(8,128)(2,1)} %get-tuple-element.46) | copy-start | bytes 983044
  72.9 1.4 copy-start.12
  76.3 11.4 %copy-start.4 = (bf16[1,640,256]{1,2,0:T(8,128)(2,1)}, bf16[1,640,256]{1,2,0:T(8,128)(2,1)S(1)}, u32[]{:S(2)}) copy-start(bf16[1,640,256]{1,2,0:T(8,128)(2,1)S(1)} %get-tuple-element.43) | copy-start | bytes 983044
  76.4 7.3 %collective-permute-start.2 = (bf16[1,640,1,128]{1,3,2,0:T(8,128)(2,1)S(1)}, bf16[1,640,1,128]{1,3,2,0:T(8,128)(2,1)S(1)}, u32[]{:S(2)}, u32[]{:S(2)}) collective-permute-start(bf16[1,640,1,128]{1,3,2,0:T(8,128)(2,1)S(1)} %get-tuple-element.52), channel_id=1, source_target_pairs={{0,4},{4,8},{8,12},{1,5},{5,9},{9,13},{2,6},{6,10},{10,14},{3,7},{... | collective-permute-start | bytes 491528 | tf_op jit(solution)/shard_map/ppermute | solution.py:19
  79.8 8.0 %collective-permute-start.3 = (bf16[1,640,1,128]{1,3,2,0:T(8,128)(2,1)S(1)}, bf16[1,640,1,128]{1,3,2,0:T(8,128)(2,1)S(1)}, u32[]{:S(2)}, u32[]{:S(2)}) collective-permute-start(bf16[1,640,1,128]{1,3,2,0:T(8,128)(2,1)S(1)} %get-tuple-element.53), channel_id=1, source_target_pairs={{4,0},{8,4},{12,8},{5,1},{9,5},{13,9},{6,2},{10,6},{14,10},{7,3},{... | collective-permute-start | bytes 491528 | tf_op jit(solution)/shard_map/ppermute | solution.py:20
  83.6 4.1 %copy-start.10 = (bf16[1,640,1,128]{1,3,2,0:T(8,128)(2,1)}, bf16[1,640,1,128]{1,3,2,0:T(8,128)(2,1)S(1)}, u32[]{:S(2)}) copy-start(bf16[1,640,1,128]{1,3,2,0:T(8,128)(2,1)S(1)} %collective-permute-done.2) | copy-start | bytes 491524
  88.5 19.5 %copy-start.6 = (bf16[1,640,4,128]{1,3,2,0:T(8,128)(2,1)}, bf16[1,640,4,128]{1,3,2,0:T(8,128)(2,1)S(1)}, u32[]{:S(2)}) copy-start(bf16[1,640,4,128]{1,3,2,0:T(8,128)(2,1)S(1)} %pad_maximum_fusion.1) | copy-start | bytes 1966084
  102.4 5.5 %copy-start = (bf16[4,640,4,128]{3,1,2,0:T(8,128)(2,1)S(1)}, bf16[4,640,4,128]{3,1,2,0:T(8,128)(2,1)}, u32[]{:S(2)}) copy-start(bf16[4,640,4,128]{3,1,2,0:T(8,128)(2,1)} %all-gather.6.cloned.1.call-done) | copy-start | bytes 7864324
  116.3 77.4 %slice-start = ((s8[7372800]{0:T(1024)(128)(4,1)}), s8[3178496]{0:T(1024)(128)(4,1)S(1)}, s32[]{:S(2)}) async-start(s8[7372800]{0:T(1024)(128)(4,1)} %bitcast.193), calls=%async_computation.6 | async-start | bytes 6356992
  117.7 69.4 %copy-start.5 = (bf16[1,640,256]{1,2,0:T(8,128)(2,1)S(1)}, bf16[1,640,256]{1,2,0:T(8,128)(2,1)}, u32[]{:S(2)}) copy-start(bf16[1,640,256]{1,2,0:T(8,128)(2,1)} %copy-done.4) | copy-start | bytes 983044
  117.8 143.1 %all-gather.8.cloned.1.call-start = ((), (), s32[]{:S(2)}) async-start(), calls=%async_computation.5 | async-start | bytes 4608000 | tf_op jit(solution)/shard_map/all_gather | solution.py:126
  185.8 7.9 %slice-start.1 = ((s8[7372800]{0:T(1024)(128)(4,1)}), s8[4194304]{0:T(1024)(128)(4,1)S(1)}, s32[]{:S(2)}) async-start(s8[7372800]{0:T(1024)(128)(4,1)} %bitcast.193), calls=%async_computation.7 | async-start | bytes 8388608
  195.1 1.4 copy-start.3
  (1 other events, 0.7 us)
Sparse Core Ops, SparseCore 0:
  9.6 55.2 all-gather.3
  67.0 25.5 all-gather.5
  117.9 67.8 reduce-scatter.1
  187.2 73.5 all-gather.7
where the time goes:
time: 273 us
  waiting for transfers between devices  118 us (43%)
  blocking collectives  70.6 us (26%)
  matrix products  34.3 us (13%)
  between operations  16 us (6%)
  other arithmetic  14.3 us (5%)
  local copies, waits for them, and re-layouts  11.6 us (4%)
  starting transfers between devices  7.44 us (3%)
    reduce_scatter x1, waiting for transfers between devices, on_device(): lax.psum_scatter(weight_terms(window, all_padded, strip_rows, column_coun...  68 us
    psum x1, blocking collectives, on_device(): lax.psum((jnp.sum(jnp.square(residual)), jnp.sum(residual, axis=(0, 2)),...  35.5 us
    all_gather x1, waiting for transfers between devices, on_device(): lax.all_gather(conv_weight, 'wt', axis=0, tiled=True)  23.8 us
    dot_general x9, matrix products, weight_terms(): jnp.einsum('nop,nip->oi', residual, window, preferred_element_type=jnp.fl...  15.3 us
    psum x1, blocking collectives, on_device(): lax.psum((jnp.sum(grouped, axis=(2, 3), keepdims=True), jnp.sum(jnp.squar...  13.5 us
    all_gather x1, waiting for transfers between devices, on_device(): lax.all_gather(weight_share, 'rows', axis=0, tiled=True) / total_cells  13.2 us
    all_to_all x1, blocking collectives, on_device(): lax.all_to_all(framed_residual, 'wt', split_axis=1, concat_axis=0, tiled=...  12.7 us
    dot_general x9, matrix products, conv_taps(): jnp.einsum('oi,nip->nop', weights[:, tap_index, :], window, preferred_ele...  11.4 us
  transfers between devices with their start and end apart: 8, of which 7 were waited for; matrix products, arithmetic and copies ran while one was open for 15% of the time, Pallas kernels for 0%

commit v1 on v0

--- a/solution.py
+++ b/solution.py
@@ -1,12 +1,17 @@
+import functools
+
 import jax
 import jax.numpy as jnp
 from jax import lax
+from jax.experimental import pallas as pl
+from jax.experimental.pallas import tpu as pltpu
 from jax.sharding import PartitionSpec as P
 
 GROUPS = 32
-
-
+LANES = 128
 epsilon = 1e-05
+F32 = jnp.float32
+BF16 = jnp.bfloat16
 
 
 def with_halo(shard, sides, width):
@@ -62,7 +67,7 @@
     return jnp.stack(columns, axis=1)
 
 
-def on_device(latents, teacher, norm_gain, norm_shift, conv_weight, conv_bias):
+def generic(latents, teacher, norm_gain, norm_shift, conv_weight, conv_bias):
     row_devices = lax.axis_size("rows")
     panel_devices = lax.axis_size("wt")
     images, channels, strip_rows, column_count = latents.shape
@@ -153,6 +158,359 @@
     return (mean_loss, grad_latents, grad_weight, param_grads)
 
 
+def plane(ref, row, channels):
+    return ref[pl.ds(row, channels, stride=2), :]
+
+
+def split3(x):
+    a = x.astype(BF16)
+    rest = x - a.astype(F32)
+    b = rest.astype(BF16)
+    c = (rest - b.astype(F32)).astype(BF16)
+    return a, b, c
+
+
+def membership(channels):
+    size = channels // GROUPS
+    channel = lax.broadcasted_iota(jnp.int32, (channels, LANES), 0)
+    first = lax.broadcasted_iota(jnp.int32, (channels, LANES), 1) * size
+    inside = (channel >= first) & (channel < first + size)
+    return jnp.where(inside, 1.0, 0.0).astype(BF16)
+
+
+def dot_nn(a, b):
+    return lax.dot_general(a, b, (((1,), (0,)), ((), ())), preferred_element_type=F32)
+
+
+def dot_nt(a, b):
+    return lax.dot_general(a, b, (((1,), (1,)), ((), ())), preferred_element_type=F32)
+
+
+def group_sums(rows, member):
+    a, b, c = split3(rows)
+    return dot_nn(a, member) + (dot_nn(b, member) + dot_nn(c, member))
+
+
+def to_channels(rows, member):
+    a, b, c = split3(rows)
+    return dot_nt(a, member) + (dot_nt(b, member) + dot_nt(c, member))
+
+
+def as_rows(columns, channels):
+    lane = lax.broadcasted_iota(jnp.int32, (channels, LANES), 1)
+    table = jnp.zeros((channels, LANES), F32)
+    for i, column in enumerate(columns):
+        table = jnp.where(lane == i, column, table)
+    return jnp.transpose(table)[:8, :]
+
+
+def as_columns(rows, channels):
+    pad = jnp.zeros((LANES - len(rows), channels), F32)
+    return jnp.transpose(jnp.concatenate(rows + [pad], axis=0))
+
+
+def row_sum(a, b):
+    return jnp.sum(a + b, axis=1, keepdims=True)
+
+
+def stats_kernel(lat, out):
+    channels = out.shape[1]
+    a, b = plane(lat, 0, channels), plane(lat, 1, channels)
+    out[...] = as_rows([row_sum(a, b), row_sum(a * a, b * b)], channels)
+
+
+def hidden_kernel(cells, lat, s0, s1, s2, s3, gain, shift, hidden, table):
+    channels = s0.shape[1]
+    member = membership(channels)
+    sums = group_sums((s0[...] + s1[...]) + (s2[...] + s3[...]), member)
+    mean = sums[0:1] / cells
+    var = sums[1:2] / cells - mean * mean
+    inverse = lax.rsqrt(var + epsilon)
+    pad = jnp.zeros((6, LANES), F32)
+    rows = to_channels(jnp.concatenate([mean, inverse, pad], axis=0), member)
+    columns = as_columns([rows[0:1], rows[1:2], gain[...], shift[...]], channels)
+    table[...] = columns
+    for row in range(2):
+        normed = (plane(lat, row, channels) - columns[:, 0:1]) * columns[:, 1:2]
+        pre = normed * columns[:, 2:3] + columns[:, 3:4]
+        hidden[row] = (pre * jax.nn.sigmoid(pre)).astype(BF16)
+
+
+def shifts(x):
+    wide = x.astype(F32)
+    lane = lax.broadcasted_iota(jnp.int32, x.shape, 1)
+    left = jnp.where(lane == 0, 0.0, pltpu.roll(wide, 1, 1)).astype(BF16)
+    right = jnp.where(lane == LANES - 1, 0.0, pltpu.roll(wide, LANES - 1, 1)).astype(BF16)
+    return left, x, right
+
+
+def conv_kernel(
+    place, near, far0, far1, far2, side, diag0, diag1, diag2, before, mine, after, lat, tea, bias,
+    res, low, full, framed, total,
+):
+    me, part = place[0], place[1]
+    panel = near.shape[1]
+    channels = near.shape[2]
+
+    def rows(k):
+        return pl.ds(pl.multiple_of((me ^ k) * panel, panel), panel)
+
+    for row, source in enumerate((before[0], mine[0], mine[1], after[0])):
+        for kx, moved in enumerate(shifts(source)):
+            framed[kx, row] = moved
+    other = 1 - part
+
+    def gather(i, carry):
+        for first in (0, 3, 6):
+            full[first + i, rows(0), :] = near[first + i]
+            full[first + i, rows(1), :] = side[first + i]
+        for k, first, second, third in ((2, far0, far1, far2), (3, diag0, diag1, diag2)):
+            full[part * 3 + i, rows(k), :] = first[i]
+            full[other * 3 + i, rows(k), :] = second[i]
+            full[6 + i, rows(k), :] = third[i]
+        return carry
+
+    lax.fori_loop(0, 3, gather, 0)
+
+    total[...] = jnp.zeros_like(total)
+
+    def tap_step(tap, carry):
+        ky = tap // 3
+        kx = tap - 3 * ky
+        window = jnp.concatenate([framed[kx, ky], framed[kx, ky + 1]], axis=1)
+        total[...] += dot_nn(full[tap], window)
+        return carry
+
+    lax.fori_loop(0, 9, tap_step, 0)
+    for row in range(2):
+        value = (
+            plane(lat, row, channels)
+            + total[:, row * LANES : (row + 1) * LANES]
+            + bias[:, 0:1]
+            - plane(tea, row, channels)
+        )
+        res[row] = value
+        low[row] = value.astype(BF16)
+
+
+def back_kernel(full, before, low, after, res, lat, table, grad, sums, framed, total):
+    channels = low.shape[1]
+    for row, source in enumerate((before[0], low[0], low[1], after[0])):
+        for kx, moved in enumerate(shifts(source)):
+            framed[kx, row] = jnp.transpose(moved)
+    total[...] = jnp.zeros_like(total)
+
+    def tap_step(tap, carry):
+        ky = tap // 3
+        kx = tap - 3 * ky
+        window = jnp.concatenate([framed[2 - kx, 2 - ky], framed[2 - kx, 3 - ky]], axis=0)
+        total[...] += dot_nn(window, full[tap])
+        return carry
+
+    lax.fori_loop(0, 9, tap_step, 0)
+    columns = table[...]
+    first = second = bottom = loss = None
+    for row in range(2):
+        normed = (plane(lat, row, channels) - columns[:, 0:1]) * columns[:, 1:2]
+        pre = normed * columns[:, 2:3] + columns[:, 3:4]
+        s = jax.nn.sigmoid(pre)
+        value = jnp.transpose(total[row * LANES : (row + 1) * LANES, :]) * s * (1.0 + pre * (1.0 - s))
+        grad[row] = value
+        r = res[row]
+        terms = (value, value * normed, r, r * r)
+        if row == 0:
+            first, second, bottom, loss = terms
+        else:
+            first, second, bottom, loss = (
+                first + terms[0], second + terms[1], bottom + terms[2], loss + terms[3],
+            )
+    add = functools.partial(jnp.sum, axis=1, keepdims=True)
+    sums[...] = as_rows([add(first), add(second), add(bottom), add(loss)], channels)
+
+
+def latents_kernel(cells, s0, s1, s2, s3, res, grad, lat, table, gain, out, both):
+    channels = s0.shape[1]
+    member = membership(channels)
+    sums = (s0[...] + s1[...]) + (s2[...] + s3[...])
+    both[...] = sums
+    rows = sums * gain[...]
+    means = group_sums(rows, member) / cells
+    rows = to_channels(means, member)
+    columns = as_columns([rows[0:1], rows[1:2]], channels)
+    constants = table[...]
+    inverse = constants[:, 1:2]
+    for row in range(2):
+        normed = (plane(lat, row, channels) - constants[:, 0:1]) * inverse
+        change = grad[row] * constants[:, 2:3] - columns[:, 0:1] - normed * columns[:, 1:2]
+        out[pl.ds(row, channels, stride=2), :] = res[row] + inverse * change
+
+
+def weight_kernel(cells, place, *refs):
+    panels, hiddens, out, spread, lefts = refs[:4], refs[4:20], refs[20], refs[21], refs[22]
+    strip = place[0]
+    panel = panels[0].shape[2]
+    channels = hiddens[0].shape[1]
+    for k in range(4):
+        spread[k, 0] = jnp.zeros((channels, LANES), BF16)
+        spread[k, 9] = jnp.zeros((channels, LANES), BF16)
+        for m in range(4):
+            for row in range(2):
+                spread[k, 1 + 2 * (strip ^ m) + row] = hiddens[4 * m + k][row]
+    for m in range(4):
+        for k in range(4):
+            for row in range(2):
+                lane = pl.ds((2 * k + row) * LANES, LANES)
+                moved = shifts(panels[m][k, row])
+                for kx in range(3):
+                    lefts[strip ^ m, kx * panel : (kx + 1) * panel, lane] = moved[2 - kx]
+    out[...] = jnp.zeros_like(out)
+
+    def step(i, carry):
+        s = i // 3
+        ky = i - 3 * s
+        right = jnp.concatenate(
+            [spread[k, 2 * s + ky + row] for k in range(4) for row in range(2)], axis=1
+        )
+        product = dot_nt(lefts[s], right).reshape(3, panel, channels)
+        scale = jnp.where(s == 3, 1.0 / cells, 1.0)
+        out[pl.ds(3 * ky, 3)] = (out[pl.ds(3 * ky, 3)] + product) * scale
+        return carry
+
+    lax.fori_loop(0, 12, step, 0)
+
+
+VM = pl.BlockSpec(memory_space=pltpu.VMEM)
+SM = pl.BlockSpec(memory_space=pltpu.SMEM)
+
+
+def call(kernel, outs, specs, args, scratch=(), mib=8, us=3):
+    return pl.pallas_call(
+        kernel,
+        out_shape=outs,
+        in_specs=specs,
+        out_specs=jax.tree.map(lambda _: VM, outs),
+        scratch_shapes=scratch,
+        compiler_params=pltpu.CompilerParams(vmem_limit_bytes=mib << 20),
+        cost_estimate=pl.CostEstimate(
+            flops=int(us * 1e9), bytes_accessed=int(us * 3e6), transcendentals=0
+        ),
+    )(*args)
+
+
+def shape(dims, dtype):
+    return jax.ShapeDtypeStruct(dims, dtype)
+
+
+def swap(x, axis, mask):
+    size = lax.axis_size(axis)
+    return lax.ppermute(x, axis, [(i, i ^ mask) for i in range(size)])
+
+
+def strips_of_four(latents, teacher, norm_gain, norm_shift, conv_weight, conv_bias):
+    row_devices = lax.axis_size("rows")
+    panel_devices = lax.axis_size("wt")
+    _, channels, strip_rows, width = latents.shape
+    panel = conv_weight.shape[0]
+    strip_cells = strip_rows * width
+    total_cells = panel_devices * row_devices * strip_cells
+    group_cells = channels // GROUPS * strip_cells * row_devices
+    up = [(i, i + 1) for i in range(row_devices - 1)]
+    down = [(i + 1, i) for i in range(row_devices - 1)]
+    lat = latents.reshape(channels * strip_rows, width)
+    tea = teacher.reshape(channels * strip_rows, width)
+    gain, shift = norm_gain.reshape(1, channels), norm_shift.reshape(1, channels)
+    part = lax.axis_index("grp").astype(jnp.int32)
+    here = lax.axis_index("wt").astype(jnp.int32)
+    strip = lax.axis_index("rows").astype(jnp.int32)
+
+    near = jnp.transpose(conv_weight, (1, 0, 2))
+    far0 = swap(lax.dynamic_slice_in_dim(near, part * 3, 3, axis=0), "wt", 2)
+    far2 = swap(near[6:9], "wt", 2)
+    side = swap(near, "wt", 1)
+
+    stats = call(stats_kernel, shape((8, channels), F32), [VM], (lat,))
+    hidden, table = call(
+        functools.partial(hidden_kernel, group_cells),
+        (shape((strip_rows, channels, width), BF16), shape((channels, LANES), F32)),
+        [VM] * 7,
+        (lat, stats, *(swap(stats, "rows", m) for m in (1, 2, 3)), gain, shift),
+    )
+    before = lax.ppermute(hidden[1:2], "rows", up)
+    after = lax.ppermute(hidden[0:1], "rows", down)
+    far0, far2, hidden = lax.optimization_barrier((far0, far2, hidden))
+    far1 = swap(far0, "grp", 1)
+    own = [hidden] + [swap(hidden, "rows", m) for m in (1, 2, 3)]
+    across = [swap(hidden, "wt", 2)]
+    diag0, diag1, diag2 = swap(far0, "wt", 1), swap(far1, "wt", 1), swap(far2, "wt", 1)
+
+    res, low, full = call(
+        conv_kernel,
+        (
+            shape((strip_rows, channels, width), F32),
+            shape((strip_rows, channels, width), BF16),
+            shape((9, channels, channels), BF16),
+        ),
+        [SM] + [VM] * 14,
+        (
+            jnp.stack([here, part]), near, far0, far1, far2, side, diag0, diag1, diag2,
+            before, hidden, after, lat, tea, conv_bias.reshape(channels, 1),
+        ),
+        [pltpu.VMEM((3, 4, channels, LANES), BF16), pltpu.VMEM((channels, 2 * LANES), F32)],
+        mib=30, us=8,
+    )
+
+    low_before = lax.ppermute(low[1:2], "rows", up)
+    low_after = lax.ppermute(low[0:1], "rows", down)
+
+    def block(k):
+        return lax.dynamic_slice_in_dim(low, (here ^ k) * panel, panel, axis=1)
+
+    stacked = jnp.stack([block(0)] + [swap(block(k), "wt", k) for k in (1, 2, 3)])
+    panels = [stacked] + [swap(stacked, "rows", m) for m in (1, 2, 3)]
+
+    across += [swap(x, "wt", 2) for x in own[1:]]
+    hiddens = []
+    for x, y in zip(own, across):
+        hiddens += [x, swap(x, "wt", 1), y, swap(y, "wt", 1)]
+
+    grad, sums = call(
+        back_kernel,
+        (shape((strip_rows, channels, width), F32), shape((8, channels), F32)),
+        [VM] * 7,
+        (full, low_before, low, low_after, res, lat, table),
+        [pltpu.VMEM((3, 4, LANES, channels), BF16), pltpu.VMEM((2 * LANES, channels), F32)],
+        mib=22, us=8,
+    )
+    grad_latents, sums = call(
+        functools.partial(latents_kernel, group_cells),
+        (shape((channels * strip_rows, width), F32), shape((8, channels), F32)),
+        [VM] * 9,
+        (sums, *(swap(sums, "rows", m) for m in (1, 2, 3)), res, grad, lat, table, gain),
+    )
+    one, two, three = (swap(sums, "wt", m) for m in (1, 2, 3))
+    sums = (sums + one) + (two + three)
+    mean_loss = (jnp.sum(sums[3]) / (total_cells * channels)).reshape(1)
+    param_grads = jnp.stack([sums[2], sums[1], sums[0]]) / total_cells
+
+    grad_weight = call(
+        functools.partial(weight_kernel, total_cells),
+        shape((9, panel, channels), F32),
+        [SM] + [VM] * 20,
+        [strip.reshape(1)] + panels + hiddens,
+        [
+            pltpu.VMEM((4, 10, channels, LANES), BF16),
+            pltpu.VMEM((4, 3 * panel, 8 * LANES), BF16),
+        ],
+        mib=34, us=15,
+    )
+    return (
+        mean_loss,
+        grad_latents.reshape(latents.shape),
+        jnp.transpose(grad_weight, (1, 0, 2)),
+        param_grads,
+    )
+
+
 def solution(mesh):
     placed = (
         P(("grp", "wt"), None, "rows", None),
@@ -162,8 +520,9 @@
         P("wt", None, None),
         P(),
     )
+    small = mesh.shape["rows"] == 4 and mesh.shape["wt"] == 4 and mesh.shape["grp"] == 2
     return jax.shard_map(
-        on_device,
+        strips_of_four if small else generic,
         mesh=mesh,
         in_specs=placed,
         out_specs=(

time: 273 us -> 186 us (0.68)
  the two profiles are of different devices: /device:TPU:0 before, /device:TPU:12 now
where the time goes in v1:
time: 186 us; the launch traced here: 185 us
  waiting for transfers between devices  80.1 us (43%)
  starting transfers between devices  41.6 us (22%)
  Pallas kernels  34.4 us (18%)
  local copies, waits for them, and re-layouts  23.1 us (12%)
  other arithmetic  3 us (2%)
  between operations  2.7 us (1%)
    ppermute x37, waiting for transfers between devices, swap(): return lax.ppermute(x, axis, [(i, i ^ mask) for i in range(size)])  69.5 us
    pallas_call x6, Pallas kernels, call(): pl.pallas_call(kernel, out_shape=outs, in_specs=specs, out_specs=jax.tree...  34.4 us
    ppermute x37, starting transfers between devices, swap(): return lax.ppermute(x, axis, [(i, i ^ mask) for i in range(size)])  30.3 us
    unnamed x54, local copies, waits for them, and re-layouts  20.5 us
    ppermute x1, waiting for transfers between devices, strips_of_four(): after = lax.ppermute(hidden[0:1], 'rows', down)  5.56 us
    ppermute x1, waiting for transfers between devices, strips_of_four(): before = lax.ppermute(hidden[1:2], 'rows', up)  5.01 us
  transfers between devices with their start and end apart: 41, of which 16 were waited for; matrix products, arithmetic and copies ran while one was open for 2% of the time, Pallas kernels for 9%

profile of v1, /device:TPU:12, one launch (start us, length us, event | category | flops | bytes accessed | tf_op | source)
XLA Modules:
  0.0 184.8 jit_solution(13563058571249474252)
XLA Ops:
  7.1 2.6 %collective-permute-start.3 = (f32[8,640]{1,0:T(8,128)S(1)}, f32[8,640]{1,0:T(8,128)S(1)}, u32[]{:S(2)}, u32[]{:S(2)}) collective-permute-start(f32[8,640]{1,0:T(8,128)S(1)} %shard_map.93.s0), channel_id=1, source_target_pairs={{0,8},{4,12},{8,0},{12,4},{1,9},{5,13},{9,1},{13,5},{2,10},{6,14},... | collective-permute-start | bytes 61448 | tf_op jit(solution)/shard_map/ppermute | solution.py:406
  12.1 2.2 %collective-permute-done.4.s3 = f32[8,640]{1,0:T(8,128)S(1)} collective-permute-done((f32[8,640]{1,0:T(8,128)S(1)}, f32[8,640]{1,0:T(8,128)S(1)}, u32[]{:S(2)}, u32[]{:S(2)}) %collective-permute-start.4) | collective-permute-done | bytes 20512 | tf_op jit(solution)/shard_map/ppermute | solution.py:406
  16.1 2.7 %collective-permute-done.far0 = bf16[3,160,640]{2,1,0:T(8,128)(2,1)} collective-permute-done((bf16[3,160,640]{2,1,0:T(8,128)(2,1)S(1)}, bf16[3,160,640]{2,1,0:T(8,128)(2,1)}, u32[]{:S(2)}, u32[]{:S(2)}) %collective-permute-start) | collective-permute-done | bytes 614432 | tf_op jit(solution)/shard_map/ppermute | solution.py:406
  18.8 12.0 %collective-permute-done.1.far2 = bf16[3,160,640]{2,1,0:T(8,128)(2,1)} collective-permute-done((bf16[3,160,640]{2,1,0:T(8,128)(2,1)S(1)}, bf16[3,160,640]{2,1,0:T(8,128)(2,1)}, u32[]{:S(2)}, u32[]{:S(2)}) %collective-permute-start.1) | collective-permute-done | bytes 614432 | tf_op jit(solution)/shard_map/ppermute | solution.py:406
  31.9 14.0 %collective-permute-done.5.far1 = bf16[3,160,640]{2,1,0:T(8,128)(2,1)} collective-permute-done((bf16[3,160,640]{2,1,0:T(8,128)(2,1)}, bf16[3,160,640]{2,1,0:T(8,128)(2,1)}, u32[]{:S(2)}, u32[]{:S(2)}) %collective-permute-start.5) | collective-permute-done | bytes 614432 | tf_op jit(solution)/shard_map/ppermute | solution.py:406
  45.9 3.5 %collective-permute-start.10 = (bf16[1,640,128]{2,1,0:T(8,128)(2,1)S(1)}, bf16[1,640,128]{2,1,0:T(8,128)(2,1)S(1)}, u32[]{:S(2)}, u32[]{:S(2)}) collective-permute-start(bf16[1,640,128]{2,1,0:T(8,128)(2,1)S(1)} %get-tuple-element.35), channel_id=1, source_target_pairs={{0,4},{4,8},{8,12},{1,5},{5,9},{9,13},{2,6},{6,10},{10,14},{3,7},{... | collective-permute-start | bytes 491528 | tf_op jit(solution)/shard_map/ppermute | solution.py:438
  49.4 5.0 %collective-permute-done.10.before = bf16[1,640,128]{2,1,0:T(8,128)(2,1)S(1)} collective-permute-done((bf16[1,640,128]{2,1,0:T(8,128)(2,1)S(1)}, bf16[1,640,128]{2,1,0:T(8,128)(2,1)S(1)}, u32[]{:S(2)}, u32[]{:S(2)}) %collective-permute-start.10) | collective-permute-done | bytes 163872 | tf_op jit(solution)/shard_map/ppermute | solution.py:438
  55.1 1.9 %collective-permute-start.11 = (bf16[1,640,128]{2,1,0:T(8,128)(2,1)S(1)}, bf16[1,640,128]{2,1,0:T(8,128)(2,1)S(1)}, u32[]{:S(2)}, u32[]{:S(2)}) collective-permute-start(bf16[1,640,128]{2,1,0:T(8,128)(2,1)S(1)} %get-tuple-element.34), channel_id=1, source_target_pairs={{4,0},{8,4},{12,8},{5,1},{9,5},{13,9},{6,2},{10,6},{14,10},{7,3},{... | collective-permute-start | bytes 491528 | tf_op jit(solution)/shard_map/ppermute | solution.py:439
  57.2 5.6 %collective-permute-done.11.after = bf16[1,640,128]{2,1,0:T(8,128)(2,1)S(1)} collective-permute-done((bf16[1,640,128]{2,1,0:T(8,128)(2,1)S(1)}, bf16[1,640,128]{2,1,0:T(8,128)(2,1)S(1)}, u32[]{:S(2)}, u32[]{:S(2)}) %collective-permute-start.11) | collective-permute-done | bytes 163872 | tf_op jit(solution)/shard_map/ppermute | solution.py:439
  63.8 2.7 %collective-permute-start.33 = (bf16[2,640,128]{2,1,0:T(8,128)(2,1)S(1)}, bf16[2,640,128]{2,1,0:T(8,128)(2,1)}, u32[]{:S(2)}, u32[]{:S(2)}) collective-permute-start(bf16[2,640,128]{2,1,0:T(8,128)(2,1)S(1)} %get-tuple-element.19.mine.refs_4_), channel_id=1, source_target_pairs={{0,8},{4,12},{8,0},{12,4},{1,9},{5,13},{9,1},{13,5},{2,10},{6,14},... | collective-permute-start | bytes 983048 | tf_op jit(solution)/shard_map/ppermute | solution.py:406
  69.9 7.9 %shard_map.95 = (f32[2,640,128]{2,1,0:T(8,128)S(1)}, bf16[2,640,128]{2,1,0:T(8,128)(2,1)S(1)}, bf16[9,640,640]{2,1,0:T(8,128)(2,1)S(1)}) custom-call(s32[2]{0:T(128)S(1)} %pad_add_fusion.place, bf16[9,160,640]{2,1,0:T(8,128)(2,1)S(1)} %bitcast.18, bf16[3,160,640]{2,1,0:T(8,128)(2,1)} %collective-permute-done.far0, ...), custom_call_target="tpu_custom_call" | custom-call | flops 8000000000 | bytes 24000000 | tf_op jit(solution)/shard_map/pallas_call | solution.py:387
  77.8 2.9 %copy-done.16 = bf16[9,640,640]{2,1,0:T(8,128)(2,1)} copy-done((bf16[9,640,640]{2,1,0:T(8,128)(2,1)}, bf16[9,640,640]{2,1,0:T(8,128)(2,1)S(1)}, u32[]{:S(2)}) %copy-start.16) | copy-done | bytes 7372824
  80.7 3.5 %collective-permute-start.12 = (bf16[1,640,128]{2,1,0:T(8,128)(2,1)S(1)}, bf16[1,640,128]{2,1,0:T(8,128)(2,1)S(1)}, u32[]{:S(2)}, u32[]{:S(2)}) collective-permute-start(bf16[1,640,128]{2,1,0:T(8,128)(2,1)S(1)} %get-tuple-element.33), channel_id=1, source_target_pairs={{0,4},{4,8},{8,12},{1,5},{5,9},{9,13},{2,6},{6,10},{10,14},{3,7},{... | collective-permute-start | bytes 491528 | tf_op jit(solution)/shard_map/ppermute | solution.py:462
  84.2 2.4 %collective-permute-start.13 = (bf16[1,640,128]{2,1,0:T(8,128)(2,1)S(1)}, bf16[1,640,128]{2,1,0:T(8,128)(2,1)S(1)}, u32[]{:S(2)}, u32[]{:S(2)}) collective-permute-start(bf16[1,640,128]{2,1,0:T(8,128)(2,1)S(1)} %get-tuple-element.32), channel_id=1, source_target_pairs={{4,0},{8,4},{12,8},{5,1},{9,5},{13,9},{6,2},{10,6},{14,10},{7,3},{... | collective-permute-start | bytes 491528 | tf_op jit(solution)/shard_map/ppermute | solution.py:463
  88.7 7.4 %collective-permute-done.37.refs_16_ = bf16[2,640,128]{2,1,0:T(8,128)(2,1)} collective-permute-done((bf16[2,640,128]{2,1,0:T(8,128)(2,1)S(1)}, bf16[2,640,128]{2,1,0:T(8,128)(2,1)}, u32[]{:S(2)}, u32[]{:S(2)}) %collective-permute-start.37) | collective-permute-done | bytes 327712 | tf_op jit(solution)/shard_map/ppermute | solution.py:406
  100.7 3.1 %copy-done.17 = bf16[9,640,640]{2,1,0:T(8,128)(2,1)S(1)} copy-done((bf16[9,640,640]{2,1,0:T(8,128)(2,1)S(1)}, bf16[9,640,640]{2,1,0:T(8,128)(2,1)}, u32[]{:S(2)}) %copy-start.17) | copy-done | bytes 7372824
  105.9 6.2 %shard_map.96 = (f32[2,640,128]{2,1,0:T(8,128)S(1)}, f32[8,640]{1,0:T(8,128)S(1)}) custom-call(bf16[9,640,640]{2,1,0:T(8,128)(2,1)S(1)} %copy-done.17, bf16[1,640,128]{2,1,0:T(8,128)(2,1)S(1)} %collective-permute-done.12.before, bf16[2,640,128]{2,1,0:T(8,128)(2,1)S(1)} %get-tuple-element.21.low, bf16[1,640,128]{2,1,0:T(8,128)(2,1)S(1)} %collective-permute-done.13.after, ...), custom_call_target="tpu_custom_call" | custom-call | flops 8000000000 | bytes 24000000 | tf_op jit(solution)/shard_map/pallas_call | solution.py:387
  112.2 3.2 %collective-permute-start.15 = (f32[8,640]{1,0:T(8,128)S(1)}, f32[8,640]{1,0:T(8,128)S(1)}, u32[]{:S(2)}, u32[]{:S(2)}) collective-permute-start(f32[8,640]{1,0:T(8,128)S(1)} %get-tuple-element.24.s0), channel_id=1, source_target_pairs={{0,8},{4,12},{8,0},{12,4},{1,9},{5,13},{9,1},{13,5},{2,10},{6,14},... | collective-permute-start | bytes 61448 | tf_op jit(solution)/shard_map/ppermute | solution.py:406
  119.1 1.8 shard_map.97
  130.3 1.9 %collective-permute-start.23 = (bf16[4,2,160,128]{3,2,1,0:T(8,128)(2,1)S(1)}, bf16[4,2,160,128]{3,2,1,0:T(8,128)(2,1)}, u32[]{:S(2)}, u32[]{:S(2)}) collective-permute-start(bf16[4,2,160,128]{3,2,1,0:T(8,128)(2,1)S(1)} %pad_maximum_fusion.refs_0_), channel_id=1, source_target_pairs={{0,4},{4,0},{8,12},{12,8},{1,5},{5,1},{9,13},{13,9},{2,6},{6,2},{1... | collective-permute-start | bytes 983048 | tf_op jit(solution)/shard_map/ppermute | solution.py:406
  137.1 7.7 %collective-permute-done.23.refs_1_ = bf16[4,2,160,128]{3,2,1,0:T(8,128)(2,1)} collective-permute-done((bf16[4,2,160,128]{3,2,1,0:T(8,128)(2,1)S(1)}, bf16[4,2,160,128]{3,2,1,0:T(8,128)(2,1)}, u32[]{:S(2)}, u32[]{:S(2)}) %collective-permute-start.23) | collective-permute-done | bytes 327712 | tf_op jit(solution)/shard_map/ppermute | solution.py:406
  144.9 10.6 %collective-permute-done.24.refs_2_ = bf16[4,2,160,128]{3,2,1,0:T(8,128)(2,1)} collective-permute-done((bf16[4,2,160,128]{3,2,1,0:T(8,128)(2,1)S(1)}, bf16[4,2,160,128]{3,2,1,0:T(8,128)(2,1)}, u32[]{:S(2)}, u32[]{:S(2)}) %collective-permute-start.24) | collective-permute-done | bytes 327712 | tf_op jit(solution)/shard_map/ppermute | solution.py:406
  155.5 8.2 %collective-permute-done.25.refs_3_ = bf16[4,2,160,128]{3,2,1,0:T(8,128)(2,1)} collective-permute-done((bf16[4,2,160,128]{3,2,1,0:T(8,128)(2,1)S(1)}, bf16[4,2,160,128]{3,2,1,0:T(8,128)(2,1)}, u32[]{:S(2)}, u32[]{:S(2)}) %collective-permute-start.25) | collective-permute-done | bytes 327712 | tf_op jit(solution)/shard_map/ppermute | solution.py:406
  166.5 17.2 %shard_map.98 = f32[9,160,640]{2,1,0:T(8,128)} custom-call(s32[1]{0:T(128)} %bitcast.8.place, bf16[4,2,160,128]{3,2,1,0:T(8,128)(2,1)S(1)} %pad_maximum_fusion.refs_0_, bf16[4,2,160,128]{3,2,1,0:T(8,128)(2,1)} %collective-permute-done.23.refs_1_, bf16[4,2,160,128]{3,2,1,0:T(8,128)(2,1)} %collective-permute-done.24.refs_2_, ...), custom_call_target="tpu_custom_call" | custom-call | flops 15000000512 | bytes 45000000 | tf_op jit(solution)/shard_map/pallas_call | solution.py:387
  (131 shorter events, 46.2 us)
Async XLA Ops:
  1.9 16.9 %collective-permute-start = (bf16[3,160,640]{2,1,0:T(8,128)(2,1)S(1)}, bf16[3,160,640]{2,1,0:T(8,128)(2,1)}, u32[]{:S(2)}, u32[]{:S(2)}) collective-permute-start(bf16[3,160,640]{2,1,0:T(8,128)(2,1)S(1)} %dynamic-slice_bitcast_fusion), channel_id=1, source_target_pairs={{0,2},{1,3},{2,0},{3,1},{4,6},{5,7},{6,4},{7,5},{8,10},{9,11},{10,... | collective-permute-start | bytes 1843208 | tf_op jit(solution)/shard_map/ppermute | solution.py:406
  4.6 26.2 %collective-permute-start.1 = (bf16[3,160,640]{2,1,0:T(8,128)(2,1)S(1)}, bf16[3,160,640]{2,1,0:T(8,128)(2,1)}, u32[]{:S(2)}, u32[]{:S(2)}) collective-permute-start(bf16[3,160,640]{2,1,0:T(8,128)(2,1)S(1)} %slice.36), channel_id=1, source_target_pairs={{0,2},{1,3},{2,0},{3,1},{4,6},{5,7},{6,4},{7,5},{8,10},{9,11},{10,... | collective-permute-start | bytes 1843208 | tf_op jit(solution)/shard_map/ppermute | solution.py:406
  5.2 61.8 %collective-permute-start.6 = (bf16[9,160,640]{2,1,0:T(8,128)(2,1)S(1)}, bf16[9,160,640]{2,1,0:T(8,128)(2,1)}, u32[]{:S(2)}, u32[]{:S(2)}) collective-permute-start(bf16[9,160,640]{2,1,0:T(8,128)(2,1)S(1)} %bitcast.17), channel_id=1, source_target_pairs={{0,1},{1,0},{2,3},{3,2},{4,5},{5,4},{6,7},{7,6},{8,9},{9,8},{10,11... | collective-permute-start | bytes 5529608 | tf_op jit(solution)/shard_map/ppermute | solution.py:406
  30.8 15.0 %collective-permute-start.5 = (bf16[3,160,640]{2,1,0:T(8,128)(2,1)}, bf16[3,160,640]{2,1,0:T(8,128)(2,1)}, u32[]{:S(2)}, u32[]{:S(2)}) collective-permute-start(bf16[3,160,640]{2,1,0:T(8,128)(2,1)} %collective-permute-done.far0), channel_id=1, source_target_pairs={{0,16},{16,0},{1,17},{17,1},{2,18},{18,2},{3,19},{19,3},{4,20},{20... | collective-permute-start | bytes 1843208 | tf_op jit(solution)/shard_map/ppermute | solution.py:406
  31.4 32.4 %collective-permute-start.7 = (bf16[3,160,640]{2,1,0:T(8,128)(2,1)}, bf16[3,160,640]{2,1,0:T(8,128)(2,1)}, u32[]{:S(2)}, u32[]{:S(2)}) collective-permute-start(bf16[3,160,640]{2,1,0:T(8,128)(2,1)} %collective-permute-done.far0), channel_id=1, source_target_pairs={{0,1},{1,0},{2,3},{3,2},{4,5},{5,4},{6,7},{7,6},{8,9},{9,8},{10,11... | collective-permute-start | bytes 1843208 | tf_op jit(solution)/shard_map/ppermute | solution.py:406
  31.4 35.2 %collective-permute-start.9 = (bf16[3,160,640]{2,1,0:T(8,128)(2,1)}, bf16[3,160,640]{2,1,0:T(8,128)(2,1)}, u32[]{:S(2)}, u32[]{:S(2)}) collective-permute-start(bf16[3,160,640]{2,1,0:T(8,128)(2,1)} %collective-permute-done.1.far2), channel_id=1, source_target_pairs={{0,1},{1,0},{2,3},{3,2},{4,5},{5,4},{6,7},{7,6},{8,9},{9,8},{10,11... | collective-permute-start | bytes 1843208 | tf_op jit(solution)/shard_map/ppermute | solution.py:406
  45.9 21.1 %collective-permute-start.8 = (bf16[3,160,640]{2,1,0:T(8,128)(2,1)}, bf16[3,160,640]{2,1,0:T(8,128)(2,1)}, u32[]{:S(2)}, u32[]{:S(2)}) collective-permute-start(bf16[3,160,640]{2,1,0:T(8,128)(2,1)} %collective-permute-done.5.far1), channel_id=1, source_target_pairs={{0,1},{1,0},{2,3},{3,2},{4,5},{5,4},{6,7},{7,6},{8,9},{9,8},{10,11... | collective-permute-start | bytes 1843208 | tf_op jit(solution)/shard_map/ppermute | solution.py:406
  45.9 8.5 %collective-permute-start.10 = (bf16[1,640,128]{2,1,0:T(8,128)(2,1)S(1)}, bf16[1,640,128]{2,1,0:T(8,128)(2,1)S(1)}, u32[]{:S(2)}, u32[]{:S(2)}) collective-permute-start(bf16[1,640,128]{2,1,0:T(8,128)(2,1)S(1)} %get-tuple-element.35), channel_id=1, source_target_pairs={{0,4},{4,8},{8,12},{1,5},{5,9},{9,13},{2,6},{6,10},{10,14},{3,7},{... | collective-permute-start | bytes 491528 | tf_op jit(solution)/shard_map/ppermute | solution.py:438
  55.1 7.7 %collective-permute-start.11 = (bf16[1,640,128]{2,1,0:T(8,128)(2,1)S(1)}, bf16[1,640,128]{2,1,0:T(8,128)(2,1)S(1)}, u32[]{:S(2)}, u32[]{:S(2)}) collective-permute-start(bf16[1,640,128]{2,1,0:T(8,128)(2,1)S(1)} %get-tuple-element.34), channel_id=1, source_target_pairs={{4,0},{8,4},{12,8},{5,1},{9,5},{13,9},{6,2},{10,6},{14,10},{7,3},{... | collective-permute-start | bytes 491528 | tf_op jit(solution)/shard_map/ppermute | solution.py:439
  63.5 23.1 %collective-permute-start.29 = (bf16[2,640,128]{2,1,0:T(8,128)(2,1)S(1)}, bf16[2,640,128]{2,1,0:T(8,128)(2,1)S(1)}, u32[]{:S(2)}, u32[]{:S(2)}) collective-permute-start(bf16[2,640,128]{2,1,0:T(8,128)(2,1)S(1)} %get-tuple-element.19.mine.refs_4_), channel_id=1, source_target_pairs={{0,4},{4,0},{8,12},{12,8},{1,5},{5,1},{9,13},{13,9},{2,6},{6,2},{1... | collective-permute-start | bytes 983048 | tf_op jit(solution)/shard_map/ppermute | solution.py:406
  63.8 25.0 %collective-permute-start.33 = (bf16[2,640,128]{2,1,0:T(8,128)(2,1)S(1)}, bf16[2,640,128]{2,1,0:T(8,128)(2,1)}, u32[]{:S(2)}, u32[]{:S(2)}) collective-permute-start(bf16[2,640,128]{2,1,0:T(8,128)(2,1)S(1)} %get-tuple-element.19.mine.refs_4_), channel_id=1, source_target_pairs={{0,8},{4,12},{8,0},{12,4},{1,9},{5,13},{9,1},{13,5},{2,10},{6,14},... | collective-permute-start | bytes 983048 | tf_op jit(solution)/shard_map/ppermute | solution.py:406
  66.5 29.6 %collective-permute-start.37 = (bf16[2,640,128]{2,1,0:T(8,128)(2,1)S(1)}, bf16[2,640,128]{2,1,0:T(8,128)(2,1)}, u32[]{:S(2)}, u32[]{:S(2)}) collective-permute-start(bf16[2,640,128]{2,1,0:T(8,128)(2,1)S(1)} %get-tuple-element.19.mine.refs_4_), channel_id=1, source_target_pairs={{0,12},{4,8},{8,4},{12,0},{1,13},{5,9},{9,5},{13,1},{2,14},{6,10},... | collective-permute-start | bytes 983048 | tf_op jit(solution)/shard_map/ppermute | solution.py:406
  80.7 16.9 %collective-permute-start.12 = (bf16[1,640,128]{2,1,0:T(8,128)(2,1)S(1)}, bf16[1,640,128]{2,1,0:T(8,128)(2,1)S(1)}, u32[]{:S(2)}, u32[]{:S(2)}) collective-permute-start(bf16[1,640,128]{2,1,0:T(8,128)(2,1)S(1)} %get-tuple-element.33), channel_id=1, source_target_pairs={{0,4},{4,8},{8,12},{1,5},{5,9},{9,13},{2,6},{6,10},{10,14},{3,7},{... | collective-permute-start | bytes 491528 | tf_op jit(solution)/shard_map/ppermute | solution.py:462
  84.2 14.1 %collective-permute-start.13 = (bf16[1,640,128]{2,1,0:T(8,128)(2,1)S(1)}, bf16[1,640,128]{2,1,0:T(8,128)(2,1)S(1)}, u32[]{:S(2)}, u32[]{:S(2)}) collective-permute-start(bf16[1,640,128]{2,1,0:T(8,128)(2,1)S(1)} %get-tuple-element.32), channel_id=1, source_target_pairs={{4,0},{8,4},{12,8},{5,1},{9,5},{13,9},{6,2},{10,6},{14,10},{7,3},{... | collective-permute-start | bytes 491528 | tf_op jit(solution)/shard_map/ppermute | solution.py:463
  86.6 25.5 %collective-permute-start.27 = (bf16[2,640,128]{2,1,0:T(8,128)(2,1)S(1)}, bf16[2,640,128]{2,1,0:T(8,128)(2,1)S(1)}, u32[]{:S(2)}, u32[]{:S(2)}) collective-permute-start(bf16[2,640,128]{2,1,0:T(8,128)(2,1)S(1)} %get-tuple-element.19.mine.refs_4_), channel_id=1, source_target_pairs={{0,2},{1,3},{2,0},{3,1},{4,6},{5,7},{6,4},{7,5},{8,10},{9,11},{10,... | collective-permute-start | bytes 983048 | tf_op jit(solution)/shard_map/ppermute | solution.py:406
  88.7 23.4 %collective-permute-start.26 = (bf16[2,640,128]{2,1,0:T(8,128)(2,1)S(1)}, bf16[2,640,128]{2,1,0:T(8,128)(2,1)S(1)}, u32[]{:S(2)}, u32[]{:S(2)}) collective-permute-start(bf16[2,640,128]{2,1,0:T(8,128)(2,1)S(1)} %get-tuple-element.19.mine.refs_4_), channel_id=1, source_target_pairs={{0,1},{1,0},{2,3},{3,2},{4,5},{5,4},{6,7},{7,6},{8,9},{9,8},{10,11... | collective-permute-start | bytes 983048 | tf_op jit(solution)/shard_map/ppermute | solution.py:406
  96.1 19.2 %collective-permute-start.31 = (bf16[2,640,128]{2,1,0:T(8,128)(2,1)S(1)}, bf16[2,640,128]{2,1,0:T(8,128)(2,1)S(1)}, u32[]{:S(2)}, u32[]{:S(2)}) collective-permute-start(bf16[2,640,128]{2,1,0:T(8,128)(2,1)S(1)} %collective-permute-done.29.refs_8_), channel_id=1, source_target_pairs={{0,2},{1,3},{2,0},{3,1},{4,6},{5,7},{6,4},{7,5},{8,10},{9,11},{10,... | collective-permute-start | bytes 983048 | tf_op jit(solution)/shard_map/ppermute | solution.py:406
  97.6 23.3 %collective-permute-start.35 = (bf16[2,640,128]{2,1,0:T(8,128)(2,1)}, bf16[2,640,128]{2,1,0:T(8,128)(2,1)S(1)}, u32[]{:S(2)}, u32[]{:S(2)}) collective-permute-start(bf16[2,640,128]{2,1,0:T(8,128)(2,1)} %collective-permute-done.33.refs_12_), channel_id=1, source_target_pairs={{0,2},{1,3},{2,0},{3,1},{4,6},{5,7},{6,4},{7,5},{8,10},{9,11},{10,... | collective-permute-start | bytes 983048 | tf_op jit(solution)/shard_map/ppermute | solution.py:406
  98.3 24.2 %collective-permute-start.39 = (bf16[2,640,128]{2,1,0:T(8,128)(2,1)}, bf16[2,640,128]{2,1,0:T(8,128)(2,1)S(1)}, u32[]{:S(2)}, u32[]{:S(2)}) collective-permute-start(bf16[2,640,128]{2,1,0:T(8,128)(2,1)} %collective-permute-done.37.refs_16_), channel_id=1, source_target_pairs={{0,2},{1,3},{2,0},{3,1},{4,6},{5,7},{6,4},{7,5},{8,10},{9,11},{10,... | collective-permute-start | bytes 983048 | tf_op jit(solution)/shard_map/ppermute | solution.py:406
  128.9 8.2 %collective-permute-start.36 = (bf16[2,640,128]{2,1,0:T(8,128)(2,1)S(1)}, bf16[2,640,128]{2,1,0:T(8,128)(2,1)}, u32[]{:S(2)}, u32[]{:S(2)}) collective-permute-start(bf16[2,640,128]{2,1,0:T(8,128)(2,1)S(1)} %collective-permute-done.35.refs_14_), channel_id=1, source_target_pairs={{0,1},{1,0},{2,3},{3,2},{4,5},{5,4},{6,7},{7,6},{8,9},{9,8},{10,11... | collective-permute-start | bytes 983048 | tf_op jit(solution)/shard_map/ppermute | solution.py:406
  129.5 7.7 %collective-permute-start.40 = (bf16[2,640,128]{2,1,0:T(8,128)(2,1)S(1)}, bf16[2,640,128]{2,1,0:T(8,128)(2,1)}, u32[]{:S(2)}, u32[]{:S(2)}) collective-permute-start(bf16[2,640,128]{2,1,0:T(8,128)(2,1)S(1)} %collective-permute-done.39.refs_18_), channel_id=1, source_target_pairs={{0,1},{1,0},{2,3},{3,2},{4,5},{5,4},{6,7},{7,6},{8,9},{9,8},{10,11... | collective-permute-start | bytes 983048 | tf_op jit(solution)/shard_map/ppermute | solution.py:406
  130.3 14.6 %collective-permute-start.23 = (bf16[4,2,160,128]{3,2,1,0:T(8,128)(2,1)S(1)}, bf16[4,2,160,128]{3,2,1,0:T(8,128)(2,1)}, u32[]{:S(2)}, u32[]{:S(2)}) collective-permute-start(bf16[4,2,160,128]{3,2,1,0:T(8,128)(2,1)S(1)} %pad_maximum_fusion.refs_0_), channel_id=1, source_target_pairs={{0,4},{4,0},{8,12},{12,8},{1,5},{5,1},{9,13},{13,9},{2,6},{6,2},{1... | collective-permute-start | bytes 983048 | tf_op jit(solution)/shard_map/ppermute | solution.py:406
  132.9 22.5 %collective-permute-start.24 = (bf16[4,2,160,128]{3,2,1,0:T(8,128)(2,1)S(1)}, bf16[4,2,160,128]{3,2,1,0:T(8,128)(2,1)}, u32[]{:S(2)}, u32[]{:S(2)}) collective-permute-start(bf16[4,2,160,128]{3,2,1,0:T(8,128)(2,1)S(1)} %pad_maximum_fusion.refs_0_), channel_id=1, source_target_pairs={{0,8},{4,12},{8,0},{12,4},{1,9},{5,13},{9,1},{13,5},{2,10},{6,14},... | collective-permute-start | bytes 983048 | tf_op jit(solution)/shard_map/ppermute | solution.py:406
  134.0 29.6 %collective-permute-start.25 = (bf16[4,2,160,128]{3,2,1,0:T(8,128)(2,1)S(1)}, bf16[4,2,160,128]{3,2,1,0:T(8,128)(2,1)}, u32[]{:S(2)}, u32[]{:S(2)}) collective-permute-start(bf16[4,2,160,128]{3,2,1,0:T(8,128)(2,1)S(1)} %pad_maximum_fusion.refs_0_), channel_id=1, source_target_pairs={{0,12},{4,8},{8,4},{12,0},{1,13},{5,9},{9,5},{13,1},{2,14},{6,10},... | collective-permute-start | bytes 983048 | tf_op jit(solution)/shard_map/ppermute | solution.py:406
  (44 other events, 233.8 us)

commit v2 on v1

--- a/solution.py
+++ b/solution.py
@@ -219,7 +219,7 @@
     out[...] = as_rows([row_sum(a, b), row_sum(a * a, b * b)], channels)
 
 
-def hidden_kernel(cells, lat, s0, s1, s2, s3, gain, shift, hidden, table):
+def hidden_kernel(cells, lat, s0, s1, s2, s3, given, hidden, table):
     channels = s0.shape[1]
     member = membership(channels)
     sums = group_sums((s0[...] + s1[...]) + (s2[...] + s3[...]), member)
@@ -228,7 +228,7 @@
     inverse = lax.rsqrt(var + epsilon)
     pad = jnp.zeros((6, LANES), F32)
     rows = to_channels(jnp.concatenate([mean, inverse, pad], axis=0), member)
-    columns = as_columns([rows[0:1], rows[1:2], gain[...], shift[...]], channels)
+    columns = as_columns([rows[0:1], rows[1:2], given[0:1], given[1:2], given[2:3]], channels)
     table[...] = columns
     for row in range(2):
         normed = (plane(lat, row, channels) - columns[:, 0:1]) * columns[:, 1:2]
@@ -244,57 +244,99 @@
     return left, x, right
 
 
-def conv_kernel(
-    place, near, far0, far1, far2, side, diag0, diag1, diag2, before, mine, after, lat, tea, bias,
-    res, low, full, framed, total,
-):
-    me, part = place[0], place[1]
-    panel = near.shape[1]
-    channels = near.shape[2]
-
-    def rows(k):
-        return pl.ds(pl.multiple_of((me ^ k) * panel, panel), panel)
-
-    for row, source in enumerate((before[0], mine[0], mine[1], after[0])):
+def frame_kernel(place, mine, above, below, lat, tea, table, framed, packed, base):
+    strip = place[0]
+    edge = jnp.zeros_like(mine[0])
+    before = jnp.where(strip > 0, below[1], edge)
+    after = jnp.where(strip < 3, above[0], edge)
+    for row, source in enumerate((before, mine[0], mine[1], after)):
         for kx, moved in enumerate(shifts(source)):
             framed[kx, row] = moved
-    other = 1 - part
+    packed[0] = mine[...]
+    packed[1] = above[...]
+    packed[2] = below[...]
+    channels = mine.shape[1]
+    for row in range(2):
+        base[row] = plane(lat, row, channels) + table[:, 4:5] - plane(tea, row, channels)
+
+
+def panel_rows(me, k, panel):
+    return pl.ds(pl.multiple_of((me ^ k) * panel, panel), panel)
+
+
+def conv_step(total, framed, ky, kx, first, second):
+    window = jnp.concatenate([framed[kx, ky], framed[kx, ky + 1]], axis=1)
+    total[...] += dot_nn(jnp.concatenate([first, second], axis=0), window)
+
+
+def near_conv_kernel(place, near, side, framed, base, part, block0, block1, total):
+    me = place[1]
+    panel = near.shape[1]
+    total[...] = jnp.zeros_like(total)
+
+    def step(tap, carry):
+        ky = tap // 3
+        conv_step(total, framed, ky, tap - 3 * ky, near[tap], side[tap])
+        return carry
+
+    lax.fori_loop(0, 9, step, 0)
+    for k, block in enumerate((block0, block1)):
+        for row in range(2):
+            value = base[row, panel_rows(me, k, panel), :] + (
+                total[k * panel : (k + 1) * panel, row * LANES : (row + 1) * LANES]
+            )
+            part[k, row] = value
+            block[row] = value.astype(BF16)
+
+
+def far_conv_kernel(
+    place, far0, far1, far2, diag0, diag1, diag2, framed, base, part, res, low, block23, total
+):
+    me, half = place[1], place[2]
+    panel = far0.shape[1]
+    total[...] = jnp.zeros_like(total)
+
+    def step(i, carry):
+        conv_step(total, framed, half, i, far0[i], diag0[i])
+        conv_step(total, framed, 1 - half, i, far1[i], diag1[i])
+        conv_step(total, framed, 2, i, far2[i], diag2[i])
+        return carry
+
+    lax.fori_loop(0, 3, step, 0)
+    for k in range(4):
+        rows = panel_rows(me, k, panel)
+        for row in range(2):
+            if k < 2:
+                value = part[k, row]
+            else:
+                value = base[row, rows, :] + (
+                    total[(k - 2) * panel : (k - 1) * panel, row * LANES : (row + 1) * LANES]
+                )
+                block23[k - 2, row] = value.astype(BF16)
+            res[row, rows, :] = value
+            low[row, rows, :] = value.astype(BF16)
+
+
+def back_kernel(
+    place, near, side, far0, far1, far2, diag0, diag1, diag2, before, low, after, res, lat, table,
+    grad, sums, framed, total, full,
+):
+    me, half = place[1], place[2]
+    panel, channels = near.shape[1:]
+    other = 1 - half
 
     def gather(i, carry):
         for first in (0, 3, 6):
-            full[first + i, rows(0), :] = near[first + i]
-            full[first + i, rows(1), :] = side[first + i]
+            full[first + i, panel_rows(me, 0, panel), :] = near[first + i]
+            full[first + i, panel_rows(me, 1, panel), :] = side[first + i]
         for k, first, second, third in ((2, far0, far1, far2), (3, diag0, diag1, diag2)):
-            full[part * 3 + i, rows(k), :] = first[i]
-            full[other * 3 + i, rows(k), :] = second[i]
-            full[6 + i, rows(k), :] = third[i]
+            rows = panel_rows(me, k, panel)
+            full[half * 3 + i, rows, :] = first[i]
+            full[other * 3 + i, rows, :] = second[i]
+            full[6 + i, rows, :] = third[i]
         return carry
 
     lax.fori_loop(0, 3, gather, 0)
-
-    total[...] = jnp.zeros_like(total)
-
-    def tap_step(tap, carry):
-        ky = tap // 3
-        kx = tap - 3 * ky
-        window = jnp.concatenate([framed[kx, ky], framed[kx, ky + 1]], axis=1)
-        total[...] += dot_nn(full[tap], window)
-        return carry
-
-    lax.fori_loop(0, 9, tap_step, 0)
-    for row in range(2):
-        value = (
-            plane(lat, row, channels)
-            + total[:, row * LANES : (row + 1) * LANES]
-            + bias[:, 0:1]
-            - plane(tea, row, channels)
-        )
-        res[row] = value
-        low[row] = value.astype(BF16)
-
-
-def back_kernel(full, before, low, after, res, lat, table, grad, sums, framed, total):
-    channels = low.shape[1]
     for row, source in enumerate((before[0], low[0], low[1], after[0])):
         for kx, moved in enumerate(shifts(source)):
             framed[kx, row] = jnp.transpose(moved)
@@ -328,12 +370,10 @@
     sums[...] = as_rows([add(first), add(second), add(bottom), add(loss)], channels)
 
 
-def latents_kernel(cells, s0, s1, s2, s3, res, grad, lat, table, gain, out, both):
-    channels = s0.shape[1]
+def latents_kernel(cells, total, given, res, grad, lat, table, out):
+    channels = total.shape[1]
     member = membership(channels)
-    sums = (s0[...] + s1[...]) + (s2[...] + s3[...])
-    both[...] = sums
-    rows = sums * gain[...]
+    rows = total[...] * given[0:1]
     means = group_sums(rows, member) / cells
     rows = to_channels(means, member)
     columns = as_columns([rows[0:1], rows[1:2]], channels)
@@ -345,38 +385,54 @@
         out[pl.ds(row, channels, stride=2), :] = res[row] + inverse * change
 
 
-def weight_kernel(cells, place, *refs):
-    panels, hiddens, out, spread, lefts = refs[:4], refs[4:20], refs[20], refs[21], refs[22]
-    strip = place[0]
-    panel = panels[0].shape[2]
-    channels = hiddens[0].shape[1]
-    for k in range(4):
-        spread[k, 0] = jnp.zeros((channels, LANES), BF16)
-        spread[k, 9] = jnp.zeros((channels, LANES), BF16)
-        for m in range(4):
-            for row in range(2):
-                spread[k, 1 + 2 * (strip ^ m) + row] = hiddens[4 * m + k][row]
-    for m in range(4):
+def weight_pair(place, pair, panels, spread, lefts, emit):
+    panel, channels = panels[0].shape[2], spread.shape[2]
+    for m in range(2):
         for k in range(4):
             for row in range(2):
                 lane = pl.ds((2 * k + row) * LANES, LANES)
                 moved = shifts(panels[m][k, row])
                 for kx in range(3):
-                    lefts[strip ^ m, kx * panel : (kx + 1) * panel, lane] = moved[2 - kx]
-    out[...] = jnp.zeros_like(out)
-
-    def step(i, carry):
-        s = i // 3
-        ky = i - 3 * s
-        right = jnp.concatenate(
-            [spread[k, 2 * s + ky + row] for k in range(4) for row in range(2)], axis=1
-        )
-        product = dot_nt(lefts[s], right).reshape(3, panel, channels)
-        scale = jnp.where(s == 3, 1.0 / cells, 1.0)
-        out[pl.ds(3 * ky, 3)] = (out[pl.ds(3 * ky, 3)] + product) * scale
+                    lefts[(place & 1) ^ m, kx * panel : (kx + 1) * panel, lane] = moved[2 - kx]
+
+    def step(ky, carry):
+        product = None
+        for m in range(2):
+            right = jnp.concatenate(
+                [spread[k, 4 * pair + 2 * m + ky + row] for k in range(4) for row in range(2)], axis=1
+            )
+            part = dot_nt(lefts[m], right)
+            product = part if product is None else product + part
+        emit(pl.ds(3 * ky, 3), product.reshape(3, panel, channels))
         return carry
 
-    lax.fori_loop(0, 12, step, 0)
+    lax.fori_loop(0, 3, step, 0)
+
+
+def near_weight_kernel(place, *refs):
+    panels, threes, ones, out, spread, lefts = refs[:2], refs[2:6], refs[6:10], refs[10], refs[11], refs[12]
+    strip = place[0]
+    channels = spread.shape[2]
+    for k in range(4):
+        spread[k, 0] = jnp.zeros((channels, LANES), BF16)
+        spread[k, 9] = jnp.zeros((channels, LANES), BF16)
+        for m, source in ((0, threes[k].at[0]), (1, threes[k].at[1]), (3, threes[k].at[2]), (2, ones[k])):
+            for row in range(2):
+                spread[k, 1 + 2 * ((strip + m) & 3) + row] = source[row]
+
+    def emit(taps, product):
+        out[taps] = product
+
+    weight_pair(strip, strip // 2, panels, spread, lefts, emit)
+
+
+def far_weight_kernel(cells, place, panel2, panel3, spread, near, out, lefts):
+    strip = place[0]
+
+    def emit(taps, product):
+        out[taps] = (near[taps] + product) / cells
+
+    weight_pair(strip, 1 - strip // 2, (panel2, panel3), spread, lefts, emit)
 
 
 VM = pl.BlockSpec(memory_space=pltpu.VMEM)
@@ -404,6 +460,15 @@
 def swap(x, axis, mask):
     size = lax.axis_size(axis)
     return lax.ppermute(x, axis, [(i, i ^ mask) for i in range(size)])
+
+
+def ring(x, axis, step):
+    size = lax.axis_size(axis)
+    return lax.ppermute(x, axis, [((i + step) % size, i) for i in range(size)])
+
+
+def after_all(x, *others):
+    return lax.optimization_barrier((x, *others))[0]
 
 
 def strips_of_four(latents, teacher, norm_gain, norm_shift, conv_weight, conv_bias):
@@ -418,74 +483,110 @@
     down = [(i + 1, i) for i in range(row_devices - 1)]
     lat = latents.reshape(channels * strip_rows, width)
     tea = teacher.reshape(channels * strip_rows, width)
-    gain, shift = norm_gain.reshape(1, channels), norm_shift.reshape(1, channels)
+    given = jnp.stack([norm_gain, norm_shift, conv_bias])
     part = lax.axis_index("grp").astype(jnp.int32)
     here = lax.axis_index("wt").astype(jnp.int32)
     strip = lax.axis_index("rows").astype(jnp.int32)
+    place = jnp.stack([strip, here, part])
 
     near = jnp.transpose(conv_weight, (1, 0, 2))
     far0 = swap(lax.dynamic_slice_in_dim(near, part * 3, 3, axis=0), "wt", 2)
-    far2 = swap(near[6:9], "wt", 2)
     side = swap(near, "wt", 1)
 
     stats = call(stats_kernel, shape((8, channels), F32), [VM], (lat,))
     hidden, table = call(
         functools.partial(hidden_kernel, group_cells),
         (shape((strip_rows, channels, width), BF16), shape((channels, LANES), F32)),
-        [VM] * 7,
-        (lat, stats, *(swap(stats, "rows", m) for m in (1, 2, 3)), gain, shift),
-    )
-    before = lax.ppermute(hidden[1:2], "rows", up)
-    after = lax.ppermute(hidden[0:1], "rows", down)
-    far0, far2, hidden = lax.optimization_barrier((far0, far2, hidden))
-    far1 = swap(far0, "grp", 1)
-    own = [hidden] + [swap(hidden, "rows", m) for m in (1, 2, 3)]
-    across = [swap(hidden, "wt", 2)]
+        [VM] * 6,
+        (lat, after_all(stats, far0, side), *(swap(stats, "rows", m) for m in (1, 2, 3)), given),
+    )
+    above, below = ring(hidden, "rows", 1), ring(hidden, "rows", 3)
+    far1 = swap(after_all(far0, hidden), "grp", 1)
+    far2 = swap(after_all(near, hidden)[6:9], "wt", 2)
+    framed, packed, base = call(
+        frame_kernel,
+        (
+            shape((3, 4, channels, width), BF16),
+            shape((3, strip_rows, channels, width), BF16),
+            shape((strip_rows, channels, width), F32),
+        ),
+        [SM] + [VM] * 6,
+        (place, after_all(hidden, far1, far2), above, below, lat, tea, table),
+        us=10,
+    )
+    beyond = ring(hidden, "rows", 2)
+    threes = [packed, None, swap(packed, "wt", 2), None]
+    part0, block0, block1 = call(
+        near_conv_kernel,
+        (
+            shape((2, strip_rows, panel, width), F32),
+            shape((strip_rows, panel, width), BF16),
+            shape((strip_rows, panel, width), BF16),
+        ),
+        [SM] + [VM] * 4,
+        (place, near, side, framed, base),
+        [pltpu.VMEM((2 * panel, 2 * LANES), F32)],
+        us=20,
+    )
+    far0, far1, far2, _ = lax.optimization_barrier((far0, far1, far2, framed))
     diag0, diag1, diag2 = swap(far0, "wt", 1), swap(far1, "wt", 1), swap(far2, "wt", 1)
-
-    res, low, full = call(
-        conv_kernel,
+    weights = (near, side, far0, far1, far2, diag0, diag1, diag2)
+    res, low, block23 = call(
+        far_conv_kernel,
         (
             shape((strip_rows, channels, width), F32),
             shape((strip_rows, channels, width), BF16),
-            shape((9, channels, channels), BF16),
-        ),
-        [SM] + [VM] * 14,
-        (
-            jnp.stack([here, part]), near, far0, far1, far2, side, diag0, diag1, diag2,
-            before, hidden, after, lat, tea, conv_bias.reshape(channels, 1),
-        ),
-        [pltpu.VMEM((3, 4, channels, LANES), BF16), pltpu.VMEM((channels, 2 * LANES), F32)],
-        mib=30, us=8,
+            shape((2, strip_rows, panel, width), BF16),
+        ),
+        [SM] + [VM] * 9,
+        (place, *weights[2:], framed, base, part0),
+        [pltpu.VMEM((2 * panel, 2 * LANES), F32)],
+        us=0.05,
     )
 
     low_before = lax.ppermute(low[1:2], "rows", up)
     low_after = lax.ppermute(low[0:1], "rows", down)
-
-    def block(k):
-        return lax.dynamic_slice_in_dim(low, (here ^ k) * panel, panel, axis=1)
-
-    stacked = jnp.stack([block(0)] + [swap(block(k), "wt", k) for k in (1, 2, 3)])
-    panels = [stacked] + [swap(stacked, "rows", m) for m in (1, 2, 3)]
-
-    across += [swap(x, "wt", 2) for x in own[1:]]
-    hiddens = []
-    for x, y in zip(own, across):
-        hiddens += [x, swap(x, "wt", 1), y, swap(y, "wt", 1)]
+    block1 = swap(block1, "wt", 1)
+    block23 = swap(block23, "wt", 2)
+    stacked = after_all(jnp.stack([block0, block1, block23[0], swap(block23[1], "wt", 1)]), beyond)
+    panels = [stacked] + [swap(stacked, "rows", m) for m in (1, 3, 2)]
+    panels[2:] = panels[:1:-1]
+
+    ones = [beyond, None, swap(beyond, "wt", 2), None]
+    for k in (0, 2):
+        threes[k + 1], ones[k + 1] = swap(threes[k], "wt", 1), swap(ones[k], "wt", 1)
 
     grad, sums = call(
         back_kernel,
         (shape((strip_rows, channels, width), F32), shape((8, channels), F32)),
-        [VM] * 7,
-        (full, low_before, low, low_after, res, lat, table),
-        [pltpu.VMEM((3, 4, LANES, channels), BF16), pltpu.VMEM((2 * LANES, channels), F32)],
-        mib=22, us=8,
-    )
-    grad_latents, sums = call(
+        [SM] + [VM] * 14,
+        (
+            place, *weights, low_before, after_all(low, panels[1], threes[2]), low_after, res, lat, table,
+        ),
+        [
+            pltpu.VMEM((3, 4, LANES, channels), BF16),
+            pltpu.VMEM((2 * LANES, channels), F32),
+            pltpu.VMEM((9, channels, channels), BF16),
+        ],
+        mib=20, us=30,
+    )
+    sums = after_all(sums, panels[3])
+    one, two, three = (swap(sums, "rows", m) for m in (1, 2, 3))
+    sums = (sums + one) + (two + three)
+    near_weight, spread = call(
+        near_weight_kernel,
+        (shape((9, panel, channels), F32), shape((4, 10, channels, width), BF16)),
+        [SM] + [VM] * 10,
+        [after_all(place, sums)] + panels[:2] + threes + ones,
+        [pltpu.VMEM((2, 3 * panel, 8 * LANES), BF16)],
+        mib=12, us=30,
+    )
+    grad_latents = call(
         functools.partial(latents_kernel, group_cells),
-        (shape((channels * strip_rows, width), F32), shape((8, channels), F32)),
-        [VM] * 9,
-        (sums, *(swap(sums, "rows", m) for m in (1, 2, 3)), res, grad, lat, table, gain),
+        shape((channels * strip_rows, width), F32),
+        [VM] * 6,
+        (after_all(sums, near_weight, panels[2]), given, res, grad, lat, table),
+        us=0.05,
     )
     one, two, three = (swap(sums, "wt", m) for m in (1, 2, 3))
     sums = (sums + one) + (two + three)
@@ -493,15 +594,12 @@
     param_grads = jnp.stack([sums[2], sums[1], sums[0]]) / total_cells
 
     grad_weight = call(
-        functools.partial(weight_kernel, total_cells),
+        functools.partial(far_weight_kernel, total_cells),
         shape((9, panel, channels), F32),
-        [SM] + [VM] * 20,
-        [strip.reshape(1)] + panels + hiddens,
-        [
-            pltpu.VMEM((4, 10, channels, LANES), BF16),
-            pltpu.VMEM((4, 3 * panel, 8 * LANES), BF16),
-        ],
-        mib=34, us=15,
+        [SM] + [VM] * 4,
+        [place] + panels[2:] + [spread, near_weight],
+        [pltpu.VMEM((2, 3 * panel, 8 * LANES), BF16)],
+        mib=14, us=0.05,
     )
     return (
         mean_loss,

time: 186 us -> 144 us (0.77)
  the two profiles are of different devices: /device:TPU:12 before, /device:TPU:0 now
where the time goes in v2:
time: 144 us; the launch traced here: 143 us
  waiting for transfers between devices  52.1 us (36%)
  starting transfers between devices  39.8 us (28%)
  Pallas kernels  39.5 us (27%)
  local copies, waits for them, and re-layouts  6.88 us (5%)
  between operations  2.66 us (2%)
  other arithmetic  2.11 us (1%)
    pallas_call x9, Pallas kernels, call(): pl.pallas_call(kernel, out_shape=outs, in_specs=specs, out_specs=jax.tree...  39.5 us
    ppermute x28, waiting for transfers between devices, swap(): return lax.ppermute(x, axis, [(i, i ^ mask) for i in range(size)])  37.3 us
    ppermute x28, starting transfers between devices, swap(): return lax.ppermute(x, axis, [(i, i ^ mask) for i in range(size)])  30 us
    ppermute x3, waiting for transfers between devices, ring(): return lax.ppermute(x, axis, [((i + step) % size, i) for i in range(size)])  14.8 us
    unnamed x30, local copies, waits for them, and re-layouts  4.83 us
    ppermute x3, starting transfers between devices, ring(): return lax.ppermute(x, axis, [((i + step) % size, i) for i in range(size)])  4.34 us
    ppermute x1, starting transfers between devices, strips_of_four(): low_before = lax.ppermute(low[1:2], 'rows', up)  3.94 us
  transfers between devices with their start and end apart: 33, of which 13 were waited for; matrix products, arithmetic and copies ran while one was open for 3% of the time, Pallas kernels for 15%

profile of v2, /device:TPU:0, one launch (start us, length us, event | category | flops | bytes accessed | tf_op | source)
XLA Modules:
  0.0 143.1 jit_solution(11860054079356652105)
XLA Ops:
  2.3 2.6 %collective-permute-start.1 = (bf16[3,160,640]{2,1,0:T(8,128)(2,1)S(1)}, bf16[3,160,640]{2,1,0:T(8,128)(2,1)S(1)}, u32[]{:S(2)}, u32[]{:S(2)}) collective-permute-start(bf16[3,160,640]{2,1,0:T(8,128)(2,1)S(1)} %dynamic-slice_bitcast_fusion), channel_id=1, source_target_pairs={{0,2},{1,3},{2,0},{3,1},{4,6},{5,7},{6,4},{7,5},{8,10},{9,11},{10,... | collective-permute-start | bytes 1843208 | tf_op jit(solution)/shard_map/ppermute | solution.py:462
  7.9 2.6 %collective-permute-start.3 = (f32[8,640]{1,0:T(8,128)S(1)}, f32[8,640]{1,0:T(8,128)S(1)}, u32[]{:S(2)}, u32[]{:S(2)}) collective-permute-start(f32[8,640]{1,0:T(8,128)S(1)} %shard_map.93.s0), channel_id=1, source_target_pairs={{0,8},{4,12},{8,0},{12,4},{1,9},{5,13},{9,1},{13,5},{2,10},{6,14},... | collective-permute-start | bytes 61448 | tf_op jit(solution)/shard_map/ppermute | solution.py:462
  10.8 8.6 %collective-permute-done.1.far0 = bf16[3,160,640]{2,1,0:T(8,128)(2,1)S(1)} collective-permute-done((bf16[3,160,640]{2,1,0:T(8,128)(2,1)S(1)}, bf16[3,160,640]{2,1,0:T(8,128)(2,1)S(1)}, u32[]{:S(2)}, u32[]{:S(2)}) %collective-permute-start.1) | collective-permute-done | bytes 614432 | tf_op jit(solution)/shard_map/ppermute | solution.py:462
  19.4 1.8 %shard_map.94 = (bf16[2,640,128]{2,1,0:T(8,128)(2,1)}, f32[640,128]{1,0:T(8,128)S(1)}) custom-call(f32[1280,128]{1,0:T(8,128)S(1)} %bitcast.21, f32[8,640]{1,0:T(8,128)S(1)} %shard_map.93.s0, f32[8,640]{1,0:T(8,128)S(1)} %collective-permute-done.2.s1, f32[8,640]{1,0:T(8,128)S(1)} %collective-permute-done.3.s2, f32[8,640]{1,0:T(8,128)S(1)} %collective-permute-done.4.s3, ...), custom_call_target="tpu_custom_call" | custom-call | flops 3000000000 | bytes 9000000 | tf_op jit(solution)/shard_map/pallas_call | solution.py:443
  25.4 3.6 %collective-permute-start.7 = (bf16[2,640,128]{2,1,0:T(8,128)(2,1)}, bf16[2,640,128]{2,1,0:T(8,128)(2,1)}, u32[]{:S(2)}, u32[]{:S(2)}) collective-permute-start(bf16[2,640,128]{2,1,0:T(8,128)(2,1)} %get-tuple-element.35.mine), channel_id=1, source_target_pairs={{4,0},{8,4},{12,8},{0,12},{5,1},{9,5},{13,9},{1,13},{6,2},{10,6},{... | collective-permute-start | bytes 983048 | tf_op jit(solution)/shard_map/ppermute | solution.py:467
  29.1 8.0 %collective-permute-done.5.far1 = bf16[3,160,640]{2,1,0:T(8,128)(2,1)} collective-permute-done((bf16[3,160,640]{2,1,0:T(8,128)(2,1)S(1)}, bf16[3,160,640]{2,1,0:T(8,128)(2,1)}, u32[]{:S(2)}, u32[]{:S(2)}) %collective-permute-start.5) | collective-permute-done | bytes 614432 | tf_op jit(solution)/shard_map/ppermute | solution.py:462
  37.0 2.4 %collective-permute-done.6.far2 = bf16[3,160,640]{2,1,0:T(8,128)(2,1)} collective-permute-done((bf16[3,160,640]{2,1,0:T(8,128)(2,1)}, bf16[3,160,640]{2,1,0:T(8,128)(2,1)}, u32[]{:S(2)}, u32[]{:S(2)}) %collective-permute-start.6) | collective-permute-done | bytes 614432 | tf_op jit(solution)/shard_map/ppermute | solution.py:462
  39.4 4.1 %collective-permute-done.8.below = bf16[2,640,128]{2,1,0:T(8,128)(2,1)} collective-permute-done((bf16[2,640,128]{2,1,0:T(8,128)(2,1)}, bf16[2,640,128]{2,1,0:T(8,128)(2,1)}, u32[]{:S(2)}, u32[]{:S(2)}) %collective-permute-start.8) | collective-permute-done | bytes 327712 | tf_op jit(solution)/shard_map/ppermute | solution.py:467
  44.6 2.8 %shard_map.95 = (bf16[3,4,640,128]{3,2,1,0:T(8,128)(2,1)S(1)}, bf16[3,2,640,128]{3,2,1,0:T(8,128)(2,1)}, f32[2,640,128]{2,1,0:T(8,128)S(1)}) custom-call(s32[3]{0:T(128)S(1)} %pad_add_fusion.place, bf16[2,640,128]{2,1,0:T(8,128)(2,1)} %get-tuple-element.35.mine, bf16[2,640,128]{2,1,0:T(8,128)(2,1)} %collective-permute-done.7.above, ...), custom_call_target="tpu_custom_call" | custom-call | flops 10000000000 | bytes 30000000 | tf_op jit(solution)/shard_map/pallas_call | solution.py:443
  47.9 4.4 %shard_map.96 = (f32[2,2,160,128]{3,2,1,0:T(8,128)S(1)}, bf16[2,160,128]{2,1,0:T(8,128)(2,1)S(1)}, bf16[2,160,128]{2,1,0:T(8,128)(2,1)S(1)}) custom-call(s32[3]{0:T(128)S(1)} %pad_add_fusion.place, bf16[9,160,640]{2,1,0:T(8,128)(2,1)S(1)} %bitcast.18, bf16[9,160,640]{2,1,0:T(8,128)(2,1)} %collective-permute-done.side, ...), custom_call_target="tpu_custom_call" | custom-call | flops 20000000000 | bytes 60000000 | tf_op jit(solution)/shard_map/pallas_call | solution.py:443
  52.3 3.0 %shard_map.97 = (f32[2,640,128]{2,1,0:T(8,128)S(1)}, bf16[2,640,128]{2,1,0:T(8,128)(2,1)S(1)}, bf16[2,2,160,128]{3,2,1,0:T(8,128)(2,1)S(1)}) custom-call(s32[3]{0:T(128)S(1)} %pad_add_fusion.place, bf16[3,160,640]{2,1,0:T(8,128)(2,1)S(1)} %copy-done.6, bf16[3,160,640]{2,1,0:T(8,128)(2,1)} %collective-permute-done.5.far1, ...), custom_call_target="tpu_custom_call" | custom-call | flops 50000000 | bytes 150000 | tf_op jit(solution)/shard_map/pallas_call | solution.py:443
  58.2 4.2 %collective-permute-done.14 = bf16[2,2,160,128]{3,2,1,0:T(8,128)(2,1)S(1)} collective-permute-done((bf16[2,2,160,128]{3,2,1,0:T(8,128)(2,1)S(1)}, bf16[2,2,160,128]{3,2,1,0:T(8,128)(2,1)S(1)}, u32[]{:S(2)}, u32[]{:S(2)}) %collective-permute-start.14) | collective-permute-done | bytes 163872 | tf_op jit(solution)/shard_map/ppermute | solution.py:462
  64.6 10.7 %collective-permute-done.16.refs_6_ = bf16[2,640,128]{2,1,0:T(8,128)(2,1)} collective-permute-done((bf16[2,640,128]{2,1,0:T(8,128)(2,1)}, bf16[2,640,128]{2,1,0:T(8,128)(2,1)}, u32[]{:S(2)}, u32[]{:S(2)}) %collective-permute-start.16) | collective-permute-done | bytes 327712 | tf_op jit(solution)/shard_map/ppermute | solution.py:467
  75.3 3.9 %collective-permute-start.12 = (bf16[1,640,128]{2,1,0:T(8,128)(2,1)S(1)}, bf16[1,640,128]{2,1,0:T(8,128)(2,1)S(1)}, u32[]{:S(2)}, u32[]{:S(2)}) collective-permute-start(bf16[1,640,128]{2,1,0:T(8,128)(2,1)S(1)} %get-tuple-element.59), channel_id=1, source_target_pairs={{0,4},{4,8},{8,12},{1,5},{5,9},{9,13},{2,6},{6,10},{10,14},{3,7},{... | collective-permute-start | bytes 491528 | tf_op jit(solution)/shard_map/ppermute | solution.py:547
  81.3 2.3 %collective-permute-done.18.refs_4_ = bf16[3,2,640,128]{3,2,1,0:T(8,128)(2,1)} collective-permute-done((bf16[3,2,640,128]{3,2,1,0:T(8,128)(2,1)}, bf16[3,2,640,128]{3,2,1,0:T(8,128)(2,1)}, u32[]{:S(2)}, u32[]{:S(2)}) %collective-permute-start.18) | collective-permute-done | bytes 983072 | tf_op jit(solution)/shard_map/ppermute | solution.py:462
  83.6 2.3 %collective-permute-done.17.refs_1_ = bf16[4,2,160,128]{3,2,1,0:T(8,128)(2,1)S(1)} collective-permute-done((bf16[4,2,160,128]{3,2,1,0:T(8,128)(2,1)}, bf16[4,2,160,128]{3,2,1,0:T(8,128)(2,1)S(1)}, u32[]{:S(2)}, u32[]{:S(2)}) %collective-permute-start.17) | collective-permute-done | bytes 327712 | tf_op jit(solution)/shard_map/ppermute | solution.py:462
  87.7 8.6 %shard_map.98 = (f32[2,640,128]{2,1,0:T(8,128)S(1)}, f32[8,640]{1,0:T(8,128)S(1)}) custom-call(s32[3]{0:T(128)S(1)} %pad_add_fusion.place, bf16[9,160,640]{2,1,0:T(8,128)(2,1)S(1)} %bitcast.19, bf16[9,160,640]{2,1,0:T(8,128)(2,1)} %collective-permute-done.side, bf16[3,160,640]{2,1,0:T(8,128)(2,1)S(1)} %copy-done.6, ...), custom_call_target="tpu_custom_call" | custom-call | flops 30000001024 | bytes 90000000 | tf_op jit(solution)/shard_map/pallas_call | solution.py:443
  97.9 4.9 %collective-permute-start.22 = (f32[8,640]{1,0:T(8,128)S(1)}, f32[8,640]{1,0:T(8,128)S(1)}, u32[]{:S(2)}, u32[]{:S(2)}) collective-permute-start(f32[8,640]{1,0:T(8,128)S(1)} %get-tuple-element.52), channel_id=1, source_target_pairs={{0,8},{4,12},{8,0},{12,4},{1,9},{5,13},{9,1},{13,5},{2,10},{6,14},... | collective-permute-start | bytes 61448 | tf_op jit(solution)/shard_map/ppermute | solution.py:462
  102.8 2.6 %collective-permute-start.23 = (f32[8,640]{1,0:T(8,128)S(1)}, f32[8,640]{1,0:T(8,128)S(1)}, u32[]{:S(2)}, u32[]{:S(2)}) collective-permute-start(f32[8,640]{1,0:T(8,128)S(1)} %get-tuple-element.52), channel_id=1, source_target_pairs={{0,12},{4,8},{8,4},{12,0},{1,13},{5,9},{9,5},{13,1},{2,14},{6,10},... | collective-permute-start | bytes 61448 | tf_op jit(solution)/shard_map/ppermute | solution.py:462
  105.5 2.4 %collective-permute-start.21 = (f32[8,640]{1,0:T(8,128)S(1)}, f32[8,640]{1,0:T(8,128)S(1)}, u32[]{:S(2)}, u32[]{:S(2)}) collective-permute-start(f32[8,640]{1,0:T(8,128)S(1)} %get-tuple-element.52), channel_id=1, source_target_pairs={{0,4},{4,0},{8,12},{12,8},{1,5},{5,1},{9,13},{13,9},{2,6},{6,2},{1... | collective-permute-start | bytes 61448 | tf_op jit(solution)/shard_map/ppermute | solution.py:462
  118.6 8.6 %shard_map.99 = (f32[9,160,640]{2,1,0:T(8,128)S(1)}, bf16[4,10,640,128]{3,2,1,0:T(8,128)(2,1)S(1)}) custom-call(s32[3]{0:T(128)S(1)} %pad_add_fusion.place, bf16[4,2,160,128]{3,2,1,0:T(8,128)(2,1)} %pad_maximum_fusion.refs_0_, bf16[4,2,160,128]{3,2,1,0:T(8,128)(2,1)S(1)} %copy-done.11, bf16[3,2,640,128]{3,2,1,0:T(8,128)(2,1)} %get-tuple-element.48.refs_2_, ...), custom_call_target="tpu_custom_call" | custom-call | flops 30000001024 | bytes 90000000 | tf_op jit(solution)/shard_map/pallas_call | solution.py:443
  127.2 4.7 %collective-permute-done.32.panel2 = bf16[4,2,160,128]{3,2,1,0:T(8,128)(2,1)S(1)} collective-permute-done((bf16[4,2,160,128]{3,2,1,0:T(8,128)(2,1)}, bf16[4,2,160,128]{3,2,1,0:T(8,128)(2,1)S(1)}, u32[]{:S(2)}, u32[]{:S(2)}) %collective-permute-start.32) | collective-permute-done | bytes 327712 | tf_op jit(solution)/shard_map/ppermute | solution.py:462
  132.0 1.8 %shard_map.100 = f32[1280,128]{1,0:T(8,128)} custom-call(f32[8,640]{1,0:T(8,128)S(1)} %add_add_fusion.1.total, f32[3,640]{1,0:T(4,128)S(1)} %pad_maximum_fusion.1.given, f32[2,640,128]{2,1,0:T(8,128)S(1)} %get-tuple-element.50.res, f32[2,640,128]{2,1,0:T(8,128)S(1)} %copy-done.4, f32[1280,128]{1,0:T(8,128)S(1)} %bitcast.24, ...), custom_call_target="tpu_custom_call" | custom-call | flops 50000000 | bytes 150000 | tf_op jit(solution)/shard_map/pallas_call | solution.py:443
  133.8 8.2 %shard_map.101 = f32[9,160,640]{2,1,0:T(8,128)} custom-call(s32[3]{0:T(128)S(1)} %pad_add_fusion.place, bf16[4,2,160,128]{3,2,1,0:T(8,128)(2,1)S(1)} %collective-permute-done.32.panel2, bf16[4,2,160,128]{3,2,1,0:T(8,128)(2,1)S(1)} %copy-done.8, bf16[4,10,640,128]{3,2,1,0:T(8,128)(2,1)S(1)} %get-tuple-element.57.spread, f32[9,160,640]{2,1,0:T(8,128)S(1)} %get-tuple-element.54.near), custom_call_target="tpu_custom_call" | custom-call | flops 50000000 | bytes 150000 | tf_op jit(solution)/shard_map/pallas_call | solution.py:443
  (95 shorter events, 31.2 us)
Async XLA Ops:
  0.6 18.7 %collective-permute-start = (bf16[9,160,640]{2,1,0:T(8,128)(2,1)}, bf16[9,160,640]{2,1,0:T(8,128)(2,1)}, u32[]{:S(2)}, u32[]{:S(2)}) collective-permute-start(bf16[9,160,640]{2,1,0:T(8,128)(2,1)} %bitcast.16), channel_id=1, source_target_pairs={{0,1},{1,0},{2,3},{3,2},{4,5},{5,4},{6,7},{7,6},{8,9},{9,8},{10,11... | collective-permute-start | bytes 5529608 | tf_op jit(solution)/shard_map/ppermute | solution.py:462
  2.3 17.1 %collective-permute-start.1 = (bf16[3,160,640]{2,1,0:T(8,128)(2,1)S(1)}, bf16[3,160,640]{2,1,0:T(8,128)(2,1)S(1)}, u32[]{:S(2)}, u32[]{:S(2)}) collective-permute-start(bf16[3,160,640]{2,1,0:T(8,128)(2,1)S(1)} %dynamic-slice_bitcast_fusion), channel_id=1, source_target_pairs={{0,2},{1,3},{2,0},{3,1},{4,6},{5,7},{6,4},{7,5},{8,10},{9,11},{10,... | collective-permute-start | bytes 1843208 | tf_op jit(solution)/shard_map/ppermute | solution.py:462
  6.3 13.1 %collective-permute-start.2 = (f32[8,640]{1,0:T(8,128)S(1)}, f32[8,640]{1,0:T(8,128)S(1)}, u32[]{:S(2)}, u32[]{:S(2)}) collective-permute-start(f32[8,640]{1,0:T(8,128)S(1)} %shard_map.93.s0), channel_id=1, source_target_pairs={{0,4},{4,0},{8,12},{12,8},{1,5},{5,1},{9,13},{13,9},{2,6},{6,2},{1... | collective-permute-start | bytes 61448 | tf_op jit(solution)/shard_map/ppermute | solution.py:462
  7.9 11.5 %collective-permute-start.3 = (f32[8,640]{1,0:T(8,128)S(1)}, f32[8,640]{1,0:T(8,128)S(1)}, u32[]{:S(2)}, u32[]{:S(2)}) collective-permute-start(f32[8,640]{1,0:T(8,128)S(1)} %shard_map.93.s0), channel_id=1, source_target_pairs={{0,8},{4,12},{8,0},{12,4},{1,9},{5,13},{9,1},{13,5},{2,10},{6,14},... | collective-permute-start | bytes 61448 | tf_op jit(solution)/shard_map/ppermute | solution.py:462
  10.5 8.9 %collective-permute-start.4 = (f32[8,640]{1,0:T(8,128)S(1)}, f32[8,640]{1,0:T(8,128)S(1)}, u32[]{:S(2)}, u32[]{:S(2)}) collective-permute-start(f32[8,640]{1,0:T(8,128)S(1)} %shard_map.93.s0), channel_id=1, source_target_pairs={{0,12},{4,8},{8,4},{12,0},{1,13},{5,9},{9,5},{13,1},{2,14},{6,10},... | collective-permute-start | bytes 61448 | tf_op jit(solution)/shard_map/ppermute | solution.py:462
  21.3 15.8 %collective-permute-start.5 = (bf16[3,160,640]{2,1,0:T(8,128)(2,1)S(1)}, bf16[3,160,640]{2,1,0:T(8,128)(2,1)}, u32[]{:S(2)}, u32[]{:S(2)}) collective-permute-start(bf16[3,160,640]{2,1,0:T(8,128)(2,1)S(1)} %collective-permute-done.1.far0), channel_id=1, source_target_pairs={{0,16},{16,0},{1,17},{17,1},{2,18},{18,2},{3,19},{19,3},{4,20},{20... | collective-permute-start | bytes 1843208 | tf_op jit(solution)/shard_map/ppermute | solution.py:462
  23.9 15.5 %collective-permute-start.6 = (bf16[3,160,640]{2,1,0:T(8,128)(2,1)}, bf16[3,160,640]{2,1,0:T(8,128)(2,1)}, u32[]{:S(2)}, u32[]{:S(2)}) collective-permute-start(bf16[3,160,640]{2,1,0:T(8,128)(2,1)} %slice.27), channel_id=1, source_target_pairs={{0,2},{1,3},{2,0},{3,1},{4,6},{5,7},{6,4},{7,5},{8,10},{9,11},{10,... | collective-permute-start | bytes 1843208 | tf_op jit(solution)/shard_map/ppermute | solution.py:462
  25.4 14.0 %collective-permute-start.7 = (bf16[2,640,128]{2,1,0:T(8,128)(2,1)}, bf16[2,640,128]{2,1,0:T(8,128)(2,1)}, u32[]{:S(2)}, u32[]{:S(2)}) collective-permute-start(bf16[2,640,128]{2,1,0:T(8,128)(2,1)} %get-tuple-element.35.mine), channel_id=1, source_target_pairs={{4,0},{8,4},{12,8},{0,12},{5,1},{9,5},{13,9},{1,13},{6,2},{10,6},{... | collective-permute-start | bytes 983048 | tf_op jit(solution)/shard_map/ppermute | solution.py:467
  29.0 14.5 %collective-permute-start.8 = (bf16[2,640,128]{2,1,0:T(8,128)(2,1)}, bf16[2,640,128]{2,1,0:T(8,128)(2,1)}, u32[]{:S(2)}, u32[]{:S(2)}) collective-permute-start(bf16[2,640,128]{2,1,0:T(8,128)(2,1)} %get-tuple-element.35.mine), channel_id=1, source_target_pairs={{12,0},{0,4},{4,8},{8,12},{13,1},{1,5},{5,9},{9,13},{14,2},{2,6},{... | collective-permute-start | bytes 983048 | tf_op jit(solution)/shard_map/ppermute | solution.py:467
  47.4 4.9 %collective-permute-start.9 = (bf16[3,160,640]{2,1,0:T(8,128)(2,1)S(1)}, bf16[3,160,640]{2,1,0:T(8,128)(2,1)S(1)}, u32[]{:S(2)}, u32[]{:S(2)}) collective-permute-start(bf16[3,160,640]{2,1,0:T(8,128)(2,1)S(1)} %collective-permute-done.1.far0), channel_id=1, source_target_pairs={{0,1},{1,0},{2,3},{3,2},{4,5},{5,4},{6,7},{7,6},{8,9},{9,8},{10,11... | collective-permute-start | bytes 1843208 | tf_op jit(solution)/shard_map/ppermute | solution.py:462
  47.4 4.9 %collective-permute-start.10 = (bf16[3,160,640]{2,1,0:T(8,128)(2,1)}, bf16[3,160,640]{2,1,0:T(8,128)(2,1)S(1)}, u32[]{:S(2)}, u32[]{:S(2)}) collective-permute-start(bf16[3,160,640]{2,1,0:T(8,128)(2,1)} %collective-permute-done.5.far1), channel_id=1, source_target_pairs={{0,1},{1,0},{2,3},{3,2},{4,5},{5,4},{6,7},{7,6},{8,9},{9,8},{10,11... | collective-permute-start | bytes 1843208 | tf_op jit(solution)/shard_map/ppermute | solution.py:462
  55.4 7.1 %collective-permute-start.14 = (bf16[2,2,160,128]{3,2,1,0:T(8,128)(2,1)S(1)}, bf16[2,2,160,128]{3,2,1,0:T(8,128)(2,1)S(1)}, u32[]{:S(2)}, u32[]{:S(2)}) collective-permute-start(bf16[2,2,160,128]{3,2,1,0:T(8,128)(2,1)S(1)} %get-tuple-element.46), channel_id=1, source_target_pairs={{0,2},{1,3},{2,0},{3,1},{4,6},{5,7},{6,4},{7,5},{8,10},{9,11},{10,... | collective-permute-start | bytes 491528 | tf_op jit(solution)/shard_map/ppermute | solution.py:462
  56.0 27.6 %collective-permute-start.18 = (bf16[3,2,640,128]{3,2,1,0:T(8,128)(2,1)}, bf16[3,2,640,128]{3,2,1,0:T(8,128)(2,1)}, u32[]{:S(2)}, u32[]{:S(2)}) collective-permute-start(bf16[3,2,640,128]{3,2,1,0:T(8,128)(2,1)} %get-tuple-element.48.refs_2_), channel_id=1, source_target_pairs={{0,2},{1,3},{2,0},{3,1},{4,6},{5,7},{6,4},{7,5},{8,10},{9,11},{10,... | collective-permute-start | bytes 2949128 | tf_op jit(solution)/shard_map/ppermute | solution.py:462
  57.5 17.8 %collective-permute-start.16 = (bf16[2,640,128]{2,1,0:T(8,128)(2,1)}, bf16[2,640,128]{2,1,0:T(8,128)(2,1)}, u32[]{:S(2)}, u32[]{:S(2)}) collective-permute-start(bf16[2,640,128]{2,1,0:T(8,128)(2,1)} %get-tuple-element.35.mine), channel_id=1, source_target_pairs={{8,0},{12,4},{0,8},{4,12},{9,1},{13,5},{1,9},{5,13},{10,2},{14,6},... | collective-permute-start | bytes 983048 | tf_op jit(solution)/shard_map/ppermute | solution.py:467
  75.3 10.7 %collective-permute-start.17 = (bf16[4,2,160,128]{3,2,1,0:T(8,128)(2,1)}, bf16[4,2,160,128]{3,2,1,0:T(8,128)(2,1)S(1)}, u32[]{:S(2)}, u32[]{:S(2)}) collective-permute-start(bf16[4,2,160,128]{3,2,1,0:T(8,128)(2,1)} %pad_maximum_fusion.refs_0_), channel_id=1, source_target_pairs={{0,4},{4,0},{8,12},{12,8},{1,5},{5,1},{9,13},{13,9},{2,6},{6,2},{1... | collective-permute-start | bytes 983048 | tf_op jit(solution)/shard_map/ppermute | solution.py:462
  75.3 12.4 %collective-permute-start.12 = (bf16[1,640,128]{2,1,0:T(8,128)(2,1)S(1)}, bf16[1,640,128]{2,1,0:T(8,128)(2,1)S(1)}, u32[]{:S(2)}, u32[]{:S(2)}) collective-permute-start(bf16[1,640,128]{2,1,0:T(8,128)(2,1)S(1)} %get-tuple-element.59), channel_id=1, source_target_pairs={{0,4},{4,8},{8,12},{1,5},{5,9},{9,13},{2,6},{6,10},{10,14},{3,7},{... | collective-permute-start | bytes 491528 | tf_op jit(solution)/shard_map/ppermute | solution.py:547
  79.2 8.5 %collective-permute-start.19 = (bf16[1,640,128]{2,1,0:T(8,128)(2,1)S(1)}, bf16[1,640,128]{2,1,0:T(8,128)(2,1)S(1)}, u32[]{:S(2)}, u32[]{:S(2)}) collective-permute-start(bf16[1,640,128]{2,1,0:T(8,128)(2,1)S(1)} %get-tuple-element.58), channel_id=1, source_target_pairs={{4,0},{8,4},{12,8},{5,1},{9,5},{13,9},{6,2},{10,6},{14,10},{7,3},{... | collective-permute-start | bytes 491528 | tf_op jit(solution)/shard_map/ppermute | solution.py:548
  80.7 29.5 %collective-permute-start.30 = (bf16[2,640,128]{2,1,0:T(8,128)(2,1)}, bf16[2,640,128]{2,1,0:T(8,128)(2,1)}, u32[]{:S(2)}, u32[]{:S(2)}) collective-permute-start(bf16[2,640,128]{2,1,0:T(8,128)(2,1)} %collective-permute-done.16.refs_6_), channel_id=1, source_target_pairs={{0,2},{1,3},{2,0},{3,1},{4,6},{5,7},{6,4},{7,5},{8,10},{9,11},{10,... | collective-permute-start | bytes 983048 | tf_op jit(solution)/shard_map/ppermute | solution.py:462
  83.6 34.0 %collective-permute-start.27 = (bf16[3,2,640,128]{3,2,1,0:T(8,128)(2,1)}, bf16[3,2,640,128]{3,2,1,0:T(8,128)(2,1)}, u32[]{:S(2)}, u32[]{:S(2)}) collective-permute-start(bf16[3,2,640,128]{3,2,1,0:T(8,128)(2,1)} %get-tuple-element.48.refs_2_), channel_id=1, source_target_pairs={{0,1},{1,0},{2,3},{3,2},{4,5},{5,4},{6,7},{7,6},{8,9},{9,8},{10,11... | collective-permute-start | bytes 2949128 | tf_op jit(solution)/shard_map/ppermute | solution.py:462
  86.0 11.2 %collective-permute-start.20 = (bf16[4,2,160,128]{3,2,1,0:T(8,128)(2,1)}, bf16[4,2,160,128]{3,2,1,0:T(8,128)(2,1)S(1)}, u32[]{:S(2)}, u32[]{:S(2)}) collective-permute-start(bf16[4,2,160,128]{3,2,1,0:T(8,128)(2,1)} %pad_maximum_fusion.refs_0_), channel_id=1, source_target_pairs={{0,12},{4,8},{8,4},{12,0},{1,13},{5,9},{9,5},{13,1},{2,14},{6,10},... | collective-permute-start | bytes 983048 | tf_op jit(solution)/shard_map/ppermute | solution.py:462
  87.7 29.9 %collective-permute-start.28 = (bf16[3,2,640,128]{3,2,1,0:T(8,128)(2,1)}, bf16[3,2,640,128]{3,2,1,0:T(8,128)(2,1)}, u32[]{:S(2)}, u32[]{:S(2)}) collective-permute-start(bf16[3,2,640,128]{3,2,1,0:T(8,128)(2,1)} %collective-permute-done.18.refs_4_), channel_id=1, source_target_pairs={{0,1},{1,0},{2,3},{3,2},{4,5},{5,4},{6,7},{7,6},{8,9},{9,8},{10,11... | collective-permute-start | bytes 2949128 | tf_op jit(solution)/shard_map/ppermute | solution.py:462
  97.9 7.6 %collective-permute-start.22 = (f32[8,640]{1,0:T(8,128)S(1)}, f32[8,640]{1,0:T(8,128)S(1)}, u32[]{:S(2)}, u32[]{:S(2)}) collective-permute-start(f32[8,640]{1,0:T(8,128)S(1)} %get-tuple-element.52), channel_id=1, source_target_pairs={{0,8},{4,12},{8,0},{12,4},{1,9},{5,13},{9,1},{13,5},{2,10},{6,14},... | collective-permute-start | bytes 61448 | tf_op jit(solution)/shard_map/ppermute | solution.py:462
  102.8 5.6 %collective-permute-start.23 = (f32[8,640]{1,0:T(8,128)S(1)}, f32[8,640]{1,0:T(8,128)S(1)}, u32[]{:S(2)}, u32[]{:S(2)}) collective-permute-start(f32[8,640]{1,0:T(8,128)S(1)} %get-tuple-element.52), channel_id=1, source_target_pairs={{0,12},{4,8},{8,4},{12,0},{1,13},{5,9},{9,5},{13,1},{2,14},{6,10},... | collective-permute-start | bytes 61448 | tf_op jit(solution)/shard_map/ppermute | solution.py:462
  114.1 17.8 %collective-permute-start.32 = (bf16[4,2,160,128]{3,2,1,0:T(8,128)(2,1)}, bf16[4,2,160,128]{3,2,1,0:T(8,128)(2,1)S(1)}, u32[]{:S(2)}, u32[]{:S(2)}) collective-permute-start(bf16[4,2,160,128]{3,2,1,0:T(8,128)(2,1)} %pad_maximum_fusion.refs_0_), channel_id=1, source_target_pairs={{0,8},{4,12},{8,0},{12,4},{1,9},{5,13},{9,1},{13,5},{2,10},{6,14},... | collective-permute-start | bytes 983048 | tf_op jit(solution)/shard_map/ppermute | solution.py:462
  (24 other events, 142.1 us)

commit v3 on v2

--- a/solution.py
+++ b/solution.py
@@ -244,7 +244,13 @@
     return left, x, right
 
 
-def frame_kernel(place, mine, above, below, lat, tea, table, framed, packed, base):
+def base_kernel(lat, tea, table, base):
+    channels = table.shape[0]
+    for row in range(2):
+        base[row] = plane(lat, row, channels) + table[:, 4:5] - plane(tea, row, channels)
+
+
+def frame_kernel(place, mine, above, below, framed, packed):
     strip = place[0]
     edge = jnp.zeros_like(mine[0])
     before = jnp.where(strip > 0, below[1], edge)
@@ -255,9 +261,6 @@
     packed[0] = mine[...]
     packed[1] = above[...]
     packed[2] = below[...]
-    channels = mine.shape[1]
-    for row in range(2):
-        base[row] = plane(lat, row, channels) + table[:, 4:5] - plane(tea, row, channels)
 
 
 def panel_rows(me, k, panel):
@@ -296,13 +299,18 @@
     panel = far0.shape[1]
     total[...] = jnp.zeros_like(total)
 
-    def step(i, carry):
-        conv_step(total, framed, half, i, far0[i], diag0[i])
-        conv_step(total, framed, 1 - half, i, far1[i], diag1[i])
-        conv_step(total, framed, 2, i, far2[i], diag2[i])
-        return carry
-
-    lax.fori_loop(0, 3, step, 0)
+    def run(first, far, diag):
+        def step(i, carry):
+            tap = first + i
+            ky = tap // 3
+            conv_step(total, framed, ky, tap - 3 * ky, far[i], diag[i])
+            return carry
+
+        lax.fori_loop(0, far.shape[0], step, 0)
+
+    run(2 * half, far0, diag0)
+    run(2 - 2 * half, far1, diag1)
+    run(4, far2, diag2)
     for k in range(4):
         rows = panel_rows(me, k, panel)
         for row in range(2):
@@ -317,26 +325,29 @@
             low[row, rows, :] = value.astype(BF16)
 
 
-def back_kernel(
-    place, near, side, far0, far1, far2, diag0, diag1, diag2, before, low, after, res, lat, table,
-    grad, sums, framed, total, full,
-):
+def assemble_kernel(place, near, side, far0, far1, far2, diag0, diag1, diag2, full):
     me, half = place[1], place[2]
-    panel, channels = near.shape[1:]
-    other = 1 - half
-
-    def gather(i, carry):
-        for first in (0, 3, 6):
-            full[first + i, panel_rows(me, 0, panel), :] = near[first + i]
-            full[first + i, panel_rows(me, 1, panel), :] = side[first + i]
-        for k, first, second, third in ((2, far0, far1, far2), (3, diag0, diag1, diag2)):
-            rows = panel_rows(me, k, panel)
-            full[half * 3 + i, rows, :] = first[i]
-            full[other * 3 + i, rows, :] = second[i]
-            full[6 + i, rows, :] = third[i]
+    panel = near.shape[1]
+    near_taps, side_taps = panel_rows(me, 0, panel), panel_rows(me, 1, panel)
+    far_taps, diag_taps = panel_rows(me, 2, panel), panel_rows(me, 3, panel)
+
+    def local(tap, carry):
+        full[tap, near_taps, :] = near[tap]
+        full[tap, side_taps, :] = side[tap]
         return carry
 
-    lax.fori_loop(0, 3, gather, 0)
+    lax.fori_loop(0, 9, local, 0)
+    for first, far, diag in ((2 * half, far0, diag0), (2 - 2 * half, far1, diag1), (4, far2, diag2)):
+        def remote(i, carry, first=first, far=far, diag=diag):
+            full[first + i, far_taps, :] = far[i]
+            full[first + i, diag_taps, :] = diag[i]
+            return carry
+
+        lax.fori_loop(0, far.shape[0], remote, 0)
+
+
+def back_kernel(full, before, low, after, res, lat, table, grad, sums, framed, total):
+    channels = low.shape[1]
     for row, source in enumerate((before[0], low[0], low[1], after[0])):
         for kx, moved in enumerate(shifts(source)):
             framed[kx, row] = jnp.transpose(moved)
@@ -385,15 +396,16 @@
         out[pl.ds(row, channels, stride=2), :] = res[row] + inverse * change
 
 
-def weight_pair(place, pair, panels, spread, lefts, emit):
-    panel, channels = panels[0].shape[2], spread.shape[2]
+def weight_pair(strip, pair, aligned, one, two, first, spread, lefts, emit):
+    panel, channels = aligned.shape[2], spread.shape[2]
     for m in range(2):
         for k in range(4):
             for row in range(2):
                 lane = pl.ds((2 * k + row) * LANES, LANES)
-                moved = shifts(panels[m][k, row])
+                source = aligned[k, row] if m == 0 else jnp.where(first, one[k, row], two[k, row])
+                moved = shifts(source)
                 for kx in range(3):
-                    lefts[(place & 1) ^ m, kx * panel : (kx + 1) * panel, lane] = moved[2 - kx]
+                    lefts[(strip & 1) ^ m, kx * panel : (kx + 1) * panel, lane] = moved[2 - kx]
 
     def step(ky, carry):
         product = None
@@ -409,8 +421,8 @@
     lax.fori_loop(0, 3, step, 0)
 
 
-def near_weight_kernel(place, *refs):
-    panels, threes, ones, out, spread, lefts = refs[:2], refs[2:6], refs[6:10], refs[10], refs[11], refs[12]
+def spread_kernel(place, *refs):
+    threes, ones, spread = refs[:4], refs[4:8], refs[8]
     strip = place[0]
     channels = spread.shape[2]
     for k in range(4):
@@ -420,19 +432,23 @@
             for row in range(2):
                 spread[k, 1 + 2 * ((strip + m) & 3) + row] = source[row]
 
+
+def near_weight_kernel(place, own, plus, minus, spread, out, lefts):
+    strip = place[0]
+
     def emit(taps, product):
         out[taps] = product
 
-    weight_pair(strip, strip // 2, panels, spread, lefts, emit)
-
-
-def far_weight_kernel(cells, place, panel2, panel3, spread, near, out, lefts):
+    weight_pair(strip, strip // 2, own, plus, minus, (strip & 1) == 0, spread, lefts, emit)
+
+
+def far_weight_kernel(cells, place, plus, minus, far, spread, near, out, lefts):
     strip = place[0]
 
     def emit(taps, product):
         out[taps] = (near[taps] + product) / cells
 
-    weight_pair(strip, 1 - strip // 2, (panel2, panel3), spread, lefts, emit)
+    weight_pair(strip, 1 - strip // 2, far, minus, plus, (strip & 1) == 0, spread, lefts, emit)
 
 
 VM = pl.BlockSpec(memory_space=pltpu.VMEM)
@@ -490,31 +506,30 @@
     place = jnp.stack([strip, here, part])
 
     near = jnp.transpose(conv_weight, (1, 0, 2))
-    far0 = swap(lax.dynamic_slice_in_dim(near, part * 3, 3, axis=0), "wt", 2)
-    side = swap(near, "wt", 1)
+    far0 = swap(lax.dynamic_slice_in_dim(near, part * 2, 2, axis=0), "wt", 2)
 
     stats = call(stats_kernel, shape((8, channels), F32), [VM], (lat,))
     hidden, table = call(
         functools.partial(hidden_kernel, group_cells),
         (shape((strip_rows, channels, width), BF16), shape((channels, LANES), F32)),
         [VM] * 6,
-        (lat, after_all(stats, far0, side), *(swap(stats, "rows", m) for m in (1, 2, 3)), given),
+        (lat, after_all(stats, far0), *(swap(stats, "rows", m) for m in (1, 2, 3)), given),
     )
     above, below = ring(hidden, "rows", 1), ring(hidden, "rows", 3)
+    side = swap(after_all(near, hidden), "wt", 1)
+    far2 = swap(after_all(near, hidden)[4:9], "wt", 2)
     far1 = swap(after_all(far0, hidden), "grp", 1)
-    far2 = swap(after_all(near, hidden)[6:9], "wt", 2)
-    framed, packed, base = call(
+    base = call(
+        base_kernel, shape((strip_rows, channels, width), F32), [VM] * 3, (lat, tea, table), us=5
+    )
+    framed, packed = call(
         frame_kernel,
-        (
-            shape((3, 4, channels, width), BF16),
-            shape((3, strip_rows, channels, width), BF16),
-            shape((strip_rows, channels, width), F32),
-        ),
-        [SM] + [VM] * 6,
-        (place, after_all(hidden, far1, far2), above, below, lat, tea, table),
-        us=10,
-    )
-    beyond = ring(hidden, "rows", 2)
+        (shape((3, 4, channels, width), BF16), shape((3, strip_rows, channels, width), BF16)),
+        [SM] + [VM] * 3,
+        (place, after_all(hidden, base), above, below),
+        us=5,
+    )
+    beyond = ring(above, "rows", 1)
     threes = [packed, None, swap(packed, "wt", 2), None]
     part0, block0, block1 = call(
         near_conv_kernel,
@@ -548,9 +563,16 @@
     low_after = lax.ppermute(low[0:1], "rows", down)
     block1 = swap(block1, "wt", 1)
     block23 = swap(block23, "wt", 2)
-    stacked = after_all(jnp.stack([block0, block1, block23[0], swap(block23[1], "wt", 1)]), beyond)
-    panels = [stacked] + [swap(stacked, "rows", m) for m in (1, 3, 2)]
-    panels[2:] = panels[:1:-1]
+    full = call(
+        assemble_kernel,
+        shape((9, channels, channels), BF16),
+        [SM] + [VM] * 8,
+        (after_all(place, low), *weights),
+        us=5,
+    )
+    stacked = jnp.stack([block0, block1, block23[0], swap(block23[1], "wt", 1)])
+    plus, minus = ring(stacked, "rows", 1), ring(stacked, "rows", 3)
+    far = ring(plus, "rows", 1)
 
     ones = [beyond, None, swap(beyond, "wt", 2), None]
     for k in (0, 2):
@@ -559,34 +581,38 @@
     grad, sums = call(
         back_kernel,
         (shape((strip_rows, channels, width), F32), shape((8, channels), F32)),
-        [SM] + [VM] * 14,
-        (
-            place, *weights, low_before, after_all(low, panels[1], threes[2]), low_after, res, lat, table,
-        ),
+        [VM] * 7,
+        (full, low_before, low, low_after, res, lat, table),
         [
             pltpu.VMEM((3, 4, LANES, channels), BF16),
             pltpu.VMEM((2 * LANES, channels), F32),
-            pltpu.VMEM((9, channels, channels), BF16),
         ],
-        mib=20, us=30,
-    )
-    sums = after_all(sums, panels[3])
+        mib=12, us=30,
+    )
+    sums = after_all(sums, plus, minus)
     one, two, three = (swap(sums, "rows", m) for m in (1, 2, 3))
     sums = (sums + one) + (two + three)
-    near_weight, spread = call(
-        near_weight_kernel,
-        (shape((9, panel, channels), F32), shape((4, 10, channels, width), BF16)),
-        [SM] + [VM] * 10,
-        [after_all(place, sums)] + panels[:2] + threes + ones,
-        [pltpu.VMEM((2, 3 * panel, 8 * LANES), BF16)],
-        mib=12, us=30,
-    )
     grad_latents = call(
         functools.partial(latents_kernel, group_cells),
         shape((channels * strip_rows, width), F32),
         [VM] * 6,
-        (after_all(sums, near_weight, panels[2]), given, res, grad, lat, table),
+        (sums, given, res, grad, lat, table),
         us=0.05,
+    )
+    spread = call(
+        spread_kernel,
+        shape((4, 10, channels, width), BF16),
+        [SM] + [VM] * 8,
+        (place, *threes, *ones),
+        us=5,
+    )
+    near_weight = call(
+        near_weight_kernel,
+        shape((9, panel, channels), F32),
+        [SM] + [VM] * 4,
+        (after_all(place, grad_latents), stacked, plus, minus, spread),
+        [pltpu.VMEM((2, 3 * panel, 8 * LANES), BF16)],
+        mib=12, us=30,
     )
     one, two, three = (swap(sums, "wt", m) for m in (1, 2, 3))
     sums = (sums + one) + (two + three)
@@ -596,8 +622,8 @@
     grad_weight = call(
         functools.partial(far_weight_kernel, total_cells),
         shape((9, panel, channels), F32),
-        [SM] + [VM] * 4,
-        [place] + panels[2:] + [spread, near_weight],
+        [SM] + [VM] * 5,
+        (place, plus, minus, far, spread, near_weight),
         [pltpu.VMEM((2, 3 * panel, 8 * LANES), BF16)],
         mib=14, us=0.05,
     )

time: 144 us -> 134 us (0.931)
  waiting for transfers between devices: 52.1 us -> 45.5 us
  local copies, waits for them, and re-layouts: 6.88 us -> 10.8 us
  starting transfers between devices: 39.8 us -> 36.1 us
  Pallas kernels: 39.5 us -> 36.8 us
    ppermute x28 -> x25, starting transfers between devices: 30 us -> 19.5 us  [swap(): return lax.ppermute(x, axis, [(i, i ^ mask) for i in range(size)])]
    ppermute x3 -> x6, starting transfers between devices: 4.34 us -> 13.3 us  [ring(): return lax.ppermute(x, axis, [((i + step) % size, i) for i in range(size)])]
    ppermute x28 -> x25, waiting for transfers between devices: 37.3 us -> 31.1 us  [swap(): return lax.ppermute(x, axis, [(i, i ^ mask) for i in range(size)])]
    unnamed x30 -> x26, local copies, waits for them, and re-layouts: 4.83 us -> 9.66 us
    pallas_call x9 -> x12, Pallas kernels: 39.5 us -> 36.8 us  [call(): pl.pallas_call(kernel, out_shape=outs, in_specs=specs, out_specs=jax.tree...]
    ppermute x1, starting transfers between devices: 3.94 us -> 2.03 us  [strips_of_four(): low_before = lax.ppermute(low[1:2], 'rows', up)]
    ppermute x3 -> x6, waiting for transfers between devices: 14.8 us -> 14.3 us  [ring(): return lax.ppermute(x, axis, [((i + step) % size, i) for i in range(size)])]
  transfers between devices with their start and end apart: 33 -> 33, of which waited for: 13 -> 8; matrix products, arithmetic and copies ran while one was open for 3% -> 1% of each run, Pallas kernels for 15% -> 20%
where the time goes in v3:
time: 134 us; the launch traced here: 133 us
  waiting for transfers between devices  45.5 us (34%)
  Pallas kernels  36.8 us (27%)
  starting transfers between devices  36.1 us (27%)
  local copies, waits for them, and re-layouts  10.8 us (8%)
  between operations  2.71 us (2%)
  other arithmetic  1.37 us (1%)
    pallas_call x12, Pallas kernels, call(): pl.pallas_call(kernel, out_shape=outs, in_specs=specs, out_specs=jax.tree...  36.8 us
    ppermute x25, waiting for transfers between devices, swap(): return lax.ppermute(x, axis, [(i, i ^ mask) for i in range(size)])  31.1 us
    ppermute x25, starting transfers between devices, swap(): return lax.ppermute(x, axis, [(i, i ^ mask) for i in range(size)])  19.5 us
    ppermute x6, waiting for transfers between devices, ring(): return lax.ppermute(x, axis, [((i + step) % size, i) for i in range(size)])  14.3 us
    ppermute x6, starting transfers between devices, ring(): return lax.ppermute(x, axis, [((i + step) % size, i) for i in range(size)])  13.3 us
    unnamed x26, local copies, waits for them, and re-layouts  9.66 us
  transfers between devices with their start and end apart: 33, of which 8 were waited for; matrix products, arithmetic and copies ran while one was open for 1% of the time, Pallas kernels for 20%

profile of v3, /device:TPU:0, one launch (start us, length us, event | category | flops | bytes accessed | tf_op | source)
XLA Modules:
  0.0 133.4 jit_solution(4275846132655572396)
XLA Ops:
  1.7 3.0 %collective-permute-start = (bf16[2,160,640]{2,1,0:T(8,128)(2,1)S(1)}, bf16[2,160,640]{2,1,0:T(8,128)(2,1)S(1)}, u32[]{:S(2)}, u32[]{:S(2)}) collective-permute-start(bf16[2,160,640]{2,1,0:T(8,128)(2,1)S(1)} %dynamic-slice_bitcast_fusion), channel_id=1, source_target_pairs={{0,2},{1,3},{2,0},{3,1},{4,6},{5,7},{6,4},{7,5},{8,10},{9,11},{10,... | collective-permute-start | bytes 1228808 | tf_op jit(solution)/shard_map/ppermute | solution.py:478
  7.7 2.6 %collective-permute-start.2 = (f32[8,640]{1,0:T(8,128)S(1)}, f32[8,640]{1,0:T(8,128)S(1)}, u32[]{:S(2)}, u32[]{:S(2)}) collective-permute-start(f32[8,640]{1,0:T(8,128)S(1)} %shard_map.93.s0), channel_id=1, source_target_pairs={{0,8},{4,12},{8,0},{12,4},{1,9},{5,13},{9,1},{13,5},{2,10},{6,14},... | collective-permute-start | bytes 61448 | tf_op jit(solution)/shard_map/ppermute | solution.py:478
  10.6 3.6 %collective-permute-done.far0 = bf16[2,160,640]{2,1,0:T(8,128)(2,1)S(1)} collective-permute-done((bf16[2,160,640]{2,1,0:T(8,128)(2,1)S(1)}, bf16[2,160,640]{2,1,0:T(8,128)(2,1)S(1)}, u32[]{:S(2)}, u32[]{:S(2)}) %collective-permute-start) | collective-permute-done | bytes 409632 | tf_op jit(solution)/shard_map/ppermute | solution.py:478
  18.5 3.1 %collective-permute-start.6 = (bf16[2,640,128]{2,1,0:T(8,128)(2,1)}, bf16[2,640,128]{2,1,0:T(8,128)(2,1)S(1)}, u32[]{:S(2)}, u32[]{:S(2)}) collective-permute-start(bf16[2,640,128]{2,1,0:T(8,128)(2,1)} %copy-done.8), channel_id=1, source_target_pairs={{4,0},{8,4},{12,8},{0,12},{5,1},{9,5},{13,9},{1,13},{6,2},{10,6},{... | collective-permute-start | bytes 983048 | tf_op jit(solution)/shard_map/ppermute | solution.py:483
  24.5 5.6 %collective-permute-done.6.above = bf16[2,640,128]{2,1,0:T(8,128)(2,1)S(1)} collective-permute-done((bf16[2,640,128]{2,1,0:T(8,128)(2,1)}, bf16[2,640,128]{2,1,0:T(8,128)(2,1)S(1)}, u32[]{:S(2)}, u32[]{:S(2)}) %collective-permute-start.6) | collective-permute-done | bytes 327712 | tf_op jit(solution)/shard_map/ppermute | solution.py:483
  30.0 4.2 %collective-permute-start.29 = (bf16[2,640,128]{2,1,0:T(8,128)(2,1)S(1)}, bf16[2,640,128]{2,1,0:T(8,128)(2,1)S(1)}, u32[]{:S(2)}, u32[]{:S(2)}) collective-permute-start(bf16[2,640,128]{2,1,0:T(8,128)(2,1)S(1)} %collective-permute-done.6.above), channel_id=1, source_target_pairs={{4,0},{8,4},{12,8},{0,12},{5,1},{9,5},{13,9},{1,13},{6,2},{10,6},{... | collective-permute-start | bytes 983048 | tf_op jit(solution)/shard_map/ppermute | solution.py:483
  34.2 3.6 %collective-permute-done.7.below = bf16[2,640,128]{2,1,0:T(8,128)(2,1)S(1)} collective-permute-done((bf16[2,640,128]{2,1,0:T(8,128)(2,1)}, bf16[2,640,128]{2,1,0:T(8,128)(2,1)S(1)}, u32[]{:S(2)}, u32[]{:S(2)}) %collective-permute-start.7) | collective-permute-done | bytes 327712 | tf_op jit(solution)/shard_map/ppermute | solution.py:483
  38.9 4.1 %collective-permute-done.5.far2 = bf16[5,160,640]{2,1,0:T(8,128)(2,1)S(1)} collective-permute-done((bf16[5,160,640]{2,1,0:T(8,128)(2,1)S(1)}, bf16[5,160,640]{2,1,0:T(8,128)(2,1)S(1)}, u32[]{:S(2)}, u32[]{:S(2)}) %collective-permute-start.5) | collective-permute-done | bytes 1024032 | tf_op jit(solution)/shard_map/ppermute | solution.py:478
  43.5 4.3 %shard_map.97 = (f32[2,2,160,128]{3,2,1,0:T(8,128)S(1)}, bf16[2,160,128]{2,1,0:T(8,128)(2,1)S(1)}, bf16[2,160,128]{2,1,0:T(8,128)(2,1)S(1)}) custom-call(s32[3]{0:T(128)S(1)} %pad_add_fusion.place, bf16[9,160,640]{2,1,0:T(8,128)(2,1)S(1)} %bitcast.18, bf16[9,160,640]{2,1,0:T(8,128)(2,1)} %collective-permute-done.11.side, ...), custom_call_target="tpu_custom_call" | custom-call | flops 20000000000 | bytes 60000000 | tf_op jit(solution)/shard_map/pallas_call | solution.py:459
  47.9 3.4 %shard_map.98 = (f32[2,640,128]{2,1,0:T(8,128)S(1)}, bf16[2,640,128]{2,1,0:T(8,128)(2,1)S(1)}, bf16[2,2,160,128]{3,2,1,0:T(8,128)(2,1)S(1)}) custom-call(s32[3]{0:T(128)S(1)} %pad_add_fusion.place, bf16[2,160,640]{2,1,0:T(8,128)(2,1)S(1)} %collective-permute-done.far0, bf16[2,160,640]{2,1,0:T(8,128)(2,1)S(1)} %collective-permute-done.4.far1, ...), custom_call_target="tpu_custom_call" | custom-call | flops 50000000 | bytes 150000 | tf_op jit(solution)/shard_map/pallas_call | solution.py:459
  53.9 4.4 %collective-permute-done.15 = bf16[2,2,160,128]{3,2,1,0:T(8,128)(2,1)S(1)} collective-permute-done((bf16[2,2,160,128]{3,2,1,0:T(8,128)(2,1)S(1)}, bf16[2,2,160,128]{3,2,1,0:T(8,128)(2,1)S(1)}, u32[]{:S(2)}, u32[]{:S(2)}) %collective-permute-start.15) | collective-permute-done | bytes 163872 | tf_op jit(solution)/shard_map/ppermute | solution.py:478
  58.5 2.0 %collective-permute-start.12 = (bf16[1,640,128]{2,1,0:T(8,128)(2,1)S(1)}, bf16[1,640,128]{2,1,0:T(8,128)(2,1)S(1)}, u32[]{:S(2)}, u32[]{:S(2)}) collective-permute-start(bf16[1,640,128]{2,1,0:T(8,128)(2,1)S(1)} %get-tuple-element.49), channel_id=1, source_target_pairs={{0,4},{4,8},{8,12},{1,5},{5,9},{9,13},{2,6},{6,10},{10,14},{3,7},{... | collective-permute-start | bytes 491528 | tf_op jit(solution)/shard_map/ppermute | solution.py:562
  61.9 4.7 %collective-permute-start.17 = (bf16[4,2,160,128]{3,2,1,0:T(8,128)(2,1)S(1)}, bf16[4,2,160,128]{3,2,1,0:T(8,128)(2,1)}, u32[]{:S(2)}, u32[]{:S(2)}) collective-permute-start(bf16[4,2,160,128]{3,2,1,0:T(8,128)(2,1)S(1)} %pad_maximum_fusion.own), channel_id=1, source_target_pairs={{4,0},{8,4},{12,8},{0,12},{5,1},{9,5},{13,9},{1,13},{6,2},{10,6},{... | collective-permute-start | bytes 983048 | tf_op jit(solution)/shard_map/ppermute | solution.py:483
  66.6 2.1 %shard_map.99.full = bf16[9,640,640]{2,1,0:T(8,128)(2,1)S(1)} custom-call(s32[3]{0:T(128)S(1)} %pad_add_fusion.place, bf16[9,160,640]{2,1,0:T(8,128)(2,1)S(1)} %bitcast.19, bf16[9,160,640]{2,1,0:T(8,128)(2,1)} %collective-permute-done.11.side, bf16[2,160,640]{2,1,0:T(8,128)(2,1)S(1)} %collective-permute-done.far0, ...), custom_call_target="tpu_custom_call" | custom-call | flops 5000000000 | bytes 15000000 | tf_op jit(solution)/shard_map/pallas_call | solution.py:459
  68.7 17.3 %collective-permute-done.31.refs_6_ = bf16[2,640,128]{2,1,0:T(8,128)(2,1)S(1)} collective-permute-done((bf16[2,640,128]{2,1,0:T(8,128)(2,1)S(1)}, bf16[2,640,128]{2,1,0:T(8,128)(2,1)S(1)}, u32[]{:S(2)}, u32[]{:S(2)}) %collective-permute-start.31) | collective-permute-done | bytes 327712 | tf_op jit(solution)/shard_map/ppermute | solution.py:478
  87.2 6.2 %shard_map.100 = (f32[2,640,128]{2,1,0:T(8,128)S(1)}, f32[8,640]{1,0:T(8,128)S(1)}) custom-call(bf16[9,640,640]{2,1,0:T(8,128)(2,1)S(1)} %shard_map.99.full, bf16[1,640,128]{2,1,0:T(8,128)(2,1)S(1)} %collective-permute-done.12.before, bf16[2,640,128]{2,1,0:T(8,128)(2,1)S(1)} %get-tuple-element.37.low, ...), custom_call_target="tpu_custom_call" | custom-call | flops 30000001024 | bytes 90000000 | tf_op jit(solution)/shard_map/pallas_call | solution.py:459
  93.4 5.1 %collective-permute-done.18.minus = bf16[4,2,160,128]{3,2,1,0:T(8,128)(2,1)S(1)} collective-permute-done((bf16[4,2,160,128]{3,2,1,0:T(8,128)(2,1)S(1)}, bf16[4,2,160,128]{3,2,1,0:T(8,128)(2,1)S(1)}, u32[]{:S(2)}, u32[]{:S(2)}) %collective-permute-start.18) | collective-permute-done | bytes 327712 | tf_op jit(solution)/shard_map/ppermute | solution.py:483
  99.4 2.6 %collective-permute-start.19 = (f32[8,640]{1,0:T(8,128)S(1)}, f32[8,640]{1,0:T(8,128)S(1)}, u32[]{:S(2)}, u32[]{:S(2)}) collective-permute-start(f32[8,640]{1,0:T(8,128)S(1)} %get-tuple-element.44), channel_id=1, source_target_pairs={{0,4},{4,0},{8,12},{12,8},{1,5},{5,1},{9,13},{13,9},{2,6},{6,2},{1... | collective-permute-start | bytes 61448 | tf_op jit(solution)/shard_map/ppermute | solution.py:478
  106.6 1.8 %shard_map.101 = f32[1280,128]{1,0:T(8,128)} custom-call(f32[8,640]{1,0:T(8,128)S(1)} %add_add_fusion.1.total, f32[3,640]{1,0:T(4,128)S(1)} %pad_maximum_fusion.1.given, f32[2,640,128]{2,1,0:T(8,128)S(1)} %get-tuple-element.39.res, f32[2,640,128]{2,1,0:T(8,128)S(1)} %get-tuple-element.45.grad, f32[1280,128]{1,0:T(8,128)S(1)} %bitcast.24, ...), custom_call_target="tpu_custom_call" | custom-call | flops 50000000 | bytes 150000 | tf_op jit(solution)/shard_map/pallas_call | solution.py:459
  108.3 6.7 %shard_map.103.near = f32[9,160,640]{2,1,0:T(8,128)S(1)} custom-call(s32[3]{0:T(128)S(1)} %pad_add_fusion.place, bf16[4,2,160,128]{3,2,1,0:T(8,128)(2,1)S(1)} %pad_maximum_fusion.own, bf16[4,2,160,128]{3,2,1,0:T(8,128)(2,1)} %collective-permute-done.17.plus, bf16[4,2,160,128]{3,2,1,0:T(8,128)(2,1)S(1)} %collective-permute-done.18.minus, ...), custom_call_target="tpu_custom_call" | custom-call | flops 30000001024 | bytes 90000000 | tf_op jit(solution)/shard_map/pallas_call | solution.py:459
  115.0 1.8 %copy-done.2 = f32[9,160,640]{2,1,0:T(8,128)} copy-done((f32[9,160,640]{2,1,0:T(8,128)}, f32[9,160,640]{2,1,0:T(8,128)S(1)}, u32[]{:S(2)}) %copy-start.2) | copy-done | bytes 3686424
  118.8 2.9 %copy-done.1 = bf16[4,10,640,128]{3,2,1,0:T(8,128)(2,1)S(1)} copy-done((bf16[4,10,640,128]{3,2,1,0:T(8,128)(2,1)S(1)}, bf16[4,10,640,128]{3,2,1,0:T(8,128)(2,1)}, u32[]{:S(2)}) %copy-start.1) | copy-done | bytes 6553624
  121.6 2.0 %copy-done.3 = f32[9,160,640]{2,1,0:T(8,128)S(1)} copy-done((f32[9,160,640]{2,1,0:T(8,128)S(1)}, f32[9,160,640]{2,1,0:T(8,128)}, u32[]{:S(2)}) %copy-start.3) | copy-done | bytes 3686424
  123.7 8.5 %shard_map.104 = f32[9,160,640]{2,1,0:T(8,128)} custom-call(s32[3]{0:T(128)S(1)} %pad_add_fusion.place, bf16[4,2,160,128]{3,2,1,0:T(8,128)(2,1)} %collective-permute-done.17.plus, bf16[4,2,160,128]{3,2,1,0:T(8,128)(2,1)S(1)} %collective-permute-done.18.minus, bf16[4,2,160,128]{3,2,1,0:T(8,128)(2,1)S(1)} %collective-permute-done.25.far, ...), custom_call_target="tpu_custom_call" | custom-call | flops 50000000 | bytes 150000 | tf_op jit(solution)/shard_map/pallas_call | solution.py:459
  (94 shorter events, 24.8 us)
Async XLA Ops:
  1.7 12.5 %collective-permute-start = (bf16[2,160,640]{2,1,0:T(8,128)(2,1)S(1)}, bf16[2,160,640]{2,1,0:T(8,128)(2,1)S(1)}, u32[]{:S(2)}, u32[]{:S(2)}) collective-permute-start(bf16[2,160,640]{2,1,0:T(8,128)(2,1)S(1)} %dynamic-slice_bitcast_fusion), channel_id=1, source_target_pairs={{0,2},{1,3},{2,0},{3,1},{4,6},{5,7},{6,4},{7,5},{8,10},{9,11},{10,... | collective-permute-start | bytes 1228808 | tf_op jit(solution)/shard_map/ppermute | solution.py:478
  6.1 8.1 %collective-permute-start.1 = (f32[8,640]{1,0:T(8,128)S(1)}, f32[8,640]{1,0:T(8,128)S(1)}, u32[]{:S(2)}, u32[]{:S(2)}) collective-permute-start(f32[8,640]{1,0:T(8,128)S(1)} %shard_map.93.s0), channel_id=1, source_target_pairs={{0,4},{4,0},{8,12},{12,8},{1,5},{5,1},{9,13},{13,9},{2,6},{6,2},{1... | collective-permute-start | bytes 61448 | tf_op jit(solution)/shard_map/ppermute | solution.py:478
  17.7 25.7 %collective-permute-start.11 = (bf16[9,160,640]{2,1,0:T(8,128)(2,1)S(1)}, bf16[9,160,640]{2,1,0:T(8,128)(2,1)}, u32[]{:S(2)}, u32[]{:S(2)}) collective-permute-start(bf16[9,160,640]{2,1,0:T(8,128)(2,1)S(1)} %bitcast.16), channel_id=1, source_target_pairs={{0,1},{1,0},{2,3},{3,2},{4,5},{5,4},{6,7},{7,6},{8,9},{9,8},{10,11... | collective-permute-start | bytes 5529608 | tf_op jit(solution)/shard_map/ppermute | solution.py:478
  17.8 25.1 %collective-permute-start.5 = (bf16[5,160,640]{2,1,0:T(8,128)(2,1)S(1)}, bf16[5,160,640]{2,1,0:T(8,128)(2,1)S(1)}, u32[]{:S(2)}, u32[]{:S(2)}) collective-permute-start(bf16[5,160,640]{2,1,0:T(8,128)(2,1)S(1)} %slice.27), channel_id=1, source_target_pairs={{0,2},{1,3},{2,0},{3,1},{4,6},{5,7},{6,4},{7,5},{8,10},{9,11},{10,... | collective-permute-start | bytes 3072008 | tf_op jit(solution)/shard_map/ppermute | solution.py:478
  18.5 11.5 %collective-permute-start.6 = (bf16[2,640,128]{2,1,0:T(8,128)(2,1)}, bf16[2,640,128]{2,1,0:T(8,128)(2,1)S(1)}, u32[]{:S(2)}, u32[]{:S(2)}) collective-permute-start(bf16[2,640,128]{2,1,0:T(8,128)(2,1)} %copy-done.8), channel_id=1, source_target_pairs={{4,0},{8,4},{12,8},{0,12},{5,1},{9,5},{13,9},{1,13},{6,2},{10,6},{... | collective-permute-start | bytes 983048 | tf_op jit(solution)/shard_map/ppermute | solution.py:483
  21.6 16.2 %collective-permute-start.7 = (bf16[2,640,128]{2,1,0:T(8,128)(2,1)}, bf16[2,640,128]{2,1,0:T(8,128)(2,1)S(1)}, u32[]{:S(2)}, u32[]{:S(2)}) collective-permute-start(bf16[2,640,128]{2,1,0:T(8,128)(2,1)} %copy-done.8), channel_id=1, source_target_pairs={{12,0},{0,4},{4,8},{8,12},{13,1},{1,5},{5,9},{9,13},{14,2},{2,6},{... | collective-permute-start | bytes 983048 | tf_op jit(solution)/shard_map/ppermute | solution.py:483
  21.6 17.2 %collective-permute-start.4 = (bf16[2,160,640]{2,1,0:T(8,128)(2,1)S(1)}, bf16[2,160,640]{2,1,0:T(8,128)(2,1)S(1)}, u32[]{:S(2)}, u32[]{:S(2)}) collective-permute-start(bf16[2,160,640]{2,1,0:T(8,128)(2,1)S(1)} %collective-permute-done.far0), channel_id=1, source_target_pairs={{0,16},{16,0},{1,17},{17,1},{2,18},{18,2},{3,19},{19,3},{4,20},{20... | collective-permute-start | bytes 1228808 | tf_op jit(solution)/shard_map/ppermute | solution.py:478
  30.0 23.3 %collective-permute-start.29 = (bf16[2,640,128]{2,1,0:T(8,128)(2,1)S(1)}, bf16[2,640,128]{2,1,0:T(8,128)(2,1)S(1)}, u32[]{:S(2)}, u32[]{:S(2)}) collective-permute-start(bf16[2,640,128]{2,1,0:T(8,128)(2,1)S(1)} %collective-permute-done.6.above), channel_id=1, source_target_pairs={{4,0},{8,4},{12,8},{0,12},{5,1},{9,5},{13,9},{1,13},{6,2},{10,6},{... | collective-permute-start | bytes 983048 | tf_op jit(solution)/shard_map/ppermute | solution.py:483
  51.3 7.1 %collective-permute-start.15 = (bf16[2,2,160,128]{3,2,1,0:T(8,128)(2,1)S(1)}, bf16[2,2,160,128]{3,2,1,0:T(8,128)(2,1)S(1)}, u32[]{:S(2)}, u32[]{:S(2)}) collective-permute-start(bf16[2,2,160,128]{3,2,1,0:T(8,128)(2,1)S(1)} %get-tuple-element.43), channel_id=1, source_target_pairs={{0,2},{1,3},{2,0},{3,1},{4,6},{5,7},{6,4},{7,5},{8,10},{9,11},{10,... | collective-permute-start | bytes 491528 | tf_op jit(solution)/shard_map/ppermute | solution.py:478
  51.9 34.2 %collective-permute-start.27 = (bf16[3,2,640,128]{3,2,1,0:T(8,128)(2,1)S(1)}, bf16[3,2,640,128]{3,2,1,0:T(8,128)(2,1)S(1)}, u32[]{:S(2)}, u32[]{:S(2)}) collective-permute-start(bf16[3,2,640,128]{3,2,1,0:T(8,128)(2,1)S(1)} %get-tuple-element.46.refs_0_), channel_id=1, source_target_pairs={{0,2},{1,3},{2,0},{3,1},{4,6},{5,7},{6,4},{7,5},{8,10},{9,11},{10,... | collective-permute-start | bytes 2949128 | tf_op jit(solution)/shard_map/ppermute | solution.py:478
  53.4 32.7 %collective-permute-start.31 = (bf16[2,640,128]{2,1,0:T(8,128)(2,1)S(1)}, bf16[2,640,128]{2,1,0:T(8,128)(2,1)S(1)}, u32[]{:S(2)}, u32[]{:S(2)}) collective-permute-start(bf16[2,640,128]{2,1,0:T(8,128)(2,1)S(1)} %collective-permute-done.29.refs_4_), channel_id=1, source_target_pairs={{0,2},{1,3},{2,0},{3,1},{4,6},{5,7},{6,4},{7,5},{8,10},{9,11},{10,... | collective-permute-start | bytes 983048 | tf_op jit(solution)/shard_map/ppermute | solution.py:478
  53.9 6.6 %collective-permute-start.14 = (bf16[2,160,128]{2,1,0:T(8,128)(2,1)S(1)}, bf16[2,160,128]{2,1,0:T(8,128)(2,1)S(1)}, u32[]{:S(2)}, u32[]{:S(2)}) collective-permute-start(bf16[2,160,128]{2,1,0:T(8,128)(2,1)S(1)} %get-tuple-element.42), channel_id=1, source_target_pairs={{0,1},{1,0},{2,3},{3,2},{4,5},{5,4},{6,7},{7,6},{8,9},{9,8},{10,11... | collective-permute-start | bytes 245768 | tf_op jit(solution)/shard_map/ppermute | solution.py:478
  58.5 28.1 %collective-permute-start.12 = (bf16[1,640,128]{2,1,0:T(8,128)(2,1)S(1)}, bf16[1,640,128]{2,1,0:T(8,128)(2,1)S(1)}, u32[]{:S(2)}, u32[]{:S(2)}) collective-permute-start(bf16[1,640,128]{2,1,0:T(8,128)(2,1)S(1)} %get-tuple-element.49), channel_id=1, source_target_pairs={{0,4},{4,8},{8,12},{1,5},{5,9},{9,13},{2,6},{6,10},{10,14},{3,7},{... | collective-permute-start | bytes 491528 | tf_op jit(solution)/shard_map/ppermute | solution.py:562
  60.5 26.1 %collective-permute-start.13 = (bf16[1,640,128]{2,1,0:T(8,128)(2,1)S(1)}, bf16[1,640,128]{2,1,0:T(8,128)(2,1)S(1)}, u32[]{:S(2)}, u32[]{:S(2)}) collective-permute-start(bf16[1,640,128]{2,1,0:T(8,128)(2,1)S(1)} %get-tuple-element.48), channel_id=1, source_target_pairs={{4,0},{8,4},{12,8},{5,1},{9,5},{13,9},{6,2},{10,6},{14,10},{7,3},{... | collective-permute-start | bytes 491528 | tf_op jit(solution)/shard_map/ppermute | solution.py:563
  61.9 25.2 %collective-permute-start.17 = (bf16[4,2,160,128]{3,2,1,0:T(8,128)(2,1)S(1)}, bf16[4,2,160,128]{3,2,1,0:T(8,128)(2,1)}, u32[]{:S(2)}, u32[]{:S(2)}) collective-permute-start(bf16[4,2,160,128]{3,2,1,0:T(8,128)(2,1)S(1)} %pad_maximum_fusion.own), channel_id=1, source_target_pairs={{4,0},{8,4},{12,8},{0,12},{5,1},{9,5},{13,9},{1,13},{6,2},{10,6},{... | collective-permute-start | bytes 983048 | tf_op jit(solution)/shard_map/ppermute | solution.py:483
  86.0 13.4 %collective-permute-start.26 = (bf16[3,2,640,128]{3,2,1,0:T(8,128)(2,1)S(1)}, bf16[3,2,640,128]{3,2,1,0:T(8,128)(2,1)S(1)}, u32[]{:S(2)}, u32[]{:S(2)}) collective-permute-start(bf16[3,2,640,128]{3,2,1,0:T(8,128)(2,1)S(1)} %get-tuple-element.46.refs_0_), channel_id=1, source_target_pairs={{0,1},{1,0},{2,3},{3,2},{4,5},{5,4},{6,7},{7,6},{8,9},{9,8},{10,11... | collective-permute-start | bytes 2949128 | tf_op jit(solution)/shard_map/ppermute | solution.py:478
  86.0 12.5 %collective-permute-start.30 = (bf16[2,640,128]{2,1,0:T(8,128)(2,1)S(1)}, bf16[2,640,128]{2,1,0:T(8,128)(2,1)S(1)}, u32[]{:S(2)}, u32[]{:S(2)}) collective-permute-start(bf16[2,640,128]{2,1,0:T(8,128)(2,1)S(1)} %collective-permute-done.29.refs_4_), channel_id=1, source_target_pairs={{0,1},{1,0},{2,3},{3,2},{4,5},{5,4},{6,7},{7,6},{8,9},{9,8},{10,11... | collective-permute-start | bytes 983048 | tf_op jit(solution)/shard_map/ppermute | solution.py:478
  86.6 15.5 %collective-permute-start.32 = (bf16[2,640,128]{2,1,0:T(8,128)(2,1)S(1)}, bf16[2,640,128]{2,1,0:T(8,128)(2,1)S(1)}, u32[]{:S(2)}, u32[]{:S(2)}) collective-permute-start(bf16[2,640,128]{2,1,0:T(8,128)(2,1)S(1)} %collective-permute-done.31.refs_6_), channel_id=1, source_target_pairs={{0,1},{1,0},{2,3},{3,2},{4,5},{5,4},{6,7},{7,6},{8,9},{9,8},{10,11... | collective-permute-start | bytes 983048 | tf_op jit(solution)/shard_map/ppermute | solution.py:478
  86.6 15.4 %collective-permute-start.28 = (bf16[3,2,640,128]{3,2,1,0:T(8,128)(2,1)S(1)}, bf16[3,2,640,128]{3,2,1,0:T(8,128)(2,1)S(1)}, u32[]{:S(2)}, u32[]{:S(2)}) collective-permute-start(bf16[3,2,640,128]{3,2,1,0:T(8,128)(2,1)S(1)} %collective-permute-done.27.refs_2_), channel_id=1, source_target_pairs={{0,1},{1,0},{2,3},{3,2},{4,5},{5,4},{6,7},{7,6},{8,9},{9,8},{10,11... | collective-permute-start | bytes 2949128 | tf_op jit(solution)/shard_map/ppermute | solution.py:478
  87.1 11.5 %collective-permute-start.18 = (bf16[4,2,160,128]{3,2,1,0:T(8,128)(2,1)S(1)}, bf16[4,2,160,128]{3,2,1,0:T(8,128)(2,1)S(1)}, u32[]{:S(2)}, u32[]{:S(2)}) collective-permute-start(bf16[4,2,160,128]{3,2,1,0:T(8,128)(2,1)S(1)} %pad_maximum_fusion.own), channel_id=1, source_target_pairs={{12,0},{0,4},{4,8},{8,12},{13,1},{1,5},{5,9},{9,13},{14,2},{2,6},{... | collective-permute-start | bytes 983048 | tf_op jit(solution)/shard_map/ppermute | solution.py:483
  103.1 15.7 %collective-permute-start.25 = (bf16[4,2,160,128]{3,2,1,0:T(8,128)(2,1)}, bf16[4,2,160,128]{3,2,1,0:T(8,128)(2,1)S(1)}, u32[]{:S(2)}, u32[]{:S(2)}) collective-permute-start(bf16[4,2,160,128]{3,2,1,0:T(8,128)(2,1)} %collective-permute-done.17.plus), channel_id=1, source_target_pairs={{4,0},{8,4},{12,8},{0,12},{5,1},{9,5},{13,9},{1,13},{6,2},{10,6},{... | collective-permute-start | bytes 983048 | tf_op jit(solution)/shard_map/ppermute | solution.py:483
  104.4 12.5 %collective-permute-start.23 = (f32[8,640]{1,0:T(8,128)S(1)}, f32[8,640]{1,0:T(8,128)S(1)}, u32[]{:S(2)}, u32[]{:S(2)}) collective-permute-start(f32[8,640]{1,0:T(8,128)S(1)} %add_add_fusion.1.total), channel_id=1, source_target_pairs={{0,2},{1,3},{2,0},{3,1},{4,6},{5,7},{6,4},{7,5},{8,10},{9,11},{10,... | collective-permute-start | bytes 61448 | tf_op jit(solution)/shard_map/ppermute | solution.py:478
  105.3 11.6 %collective-permute-start.24 = (f32[8,640]{1,0:T(8,128)S(1)}, f32[8,640]{1,0:T(8,128)S(1)}, u32[]{:S(2)}, u32[]{:S(2)}) collective-permute-start(f32[8,640]{1,0:T(8,128)S(1)} %add_add_fusion.1.total), channel_id=1, source_target_pairs={{0,3},{1,2},{2,1},{3,0},{4,7},{5,6},{6,5},{7,4},{8,11},{9,10},{10,... | collective-permute-start | bytes 61448 | tf_op jit(solution)/shard_map/ppermute | solution.py:478
  105.3 11.6 %collective-permute-start.22 = (f32[8,640]{1,0:T(8,128)S(1)}, f32[8,640]{1,0:T(8,128)S(1)}, u32[]{:S(2)}, u32[]{:S(2)}) collective-permute-start(f32[8,640]{1,0:T(8,128)S(1)} %add_add_fusion.1.total), channel_id=1, source_target_pairs={{0,1},{1,0},{2,3},{3,2},{4,5},{5,4},{6,7},{7,6},{8,9},{9,8},{10,11... | collective-permute-start | bytes 61448 | tf_op jit(solution)/shard_map/ppermute | solution.py:478
  (22 other events, 112.8 us)

commit v4 on v3

--- a/solution.py
+++ b/solution.py
@@ -250,7 +250,7 @@
         base[row] = plane(lat, row, channels) + table[:, 4:5] - plane(tea, row, channels)
 
 
-def frame_kernel(place, mine, above, below, framed, packed):
+def frame_kernel(place, mine, above, below, framed):
     strip = place[0]
     edge = jnp.zeros_like(mine[0])
     before = jnp.where(strip > 0, below[1], edge)
@@ -258,9 +258,6 @@
     for row, source in enumerate((before, mine[0], mine[1], after)):
         for kx, moved in enumerate(shifts(source)):
             framed[kx, row] = moved
-    packed[0] = mine[...]
-    packed[1] = above[...]
-    packed[2] = below[...]
 
 
 def panel_rows(me, k, panel):
@@ -308,9 +305,10 @@
 
         lax.fori_loop(0, far.shape[0], step, 0)
 
-    run(2 * half, far0, diag0)
-    run(2 - 2 * half, far1, diag1)
-    run(4, far2, diag2)
+    taps = far0.shape[0]
+    run(taps * half, far0, diag0)
+    run(taps - taps * half, far1, diag1)
+    run(2 * taps, far2, diag2)
     for k in range(4):
         rows = panel_rows(me, k, panel)
         for row in range(2):
@@ -337,7 +335,9 @@
         return carry
 
     lax.fori_loop(0, 9, local, 0)
-    for first, far, diag in ((2 * half, far0, diag0), (2 - 2 * half, far1, diag1), (4, far2, diag2)):
+    taps = far0.shape[0]
+    parts = ((taps * half, far0, diag0), (taps - taps * half, far1, diag1), (2 * taps, far2, diag2))
+    for first, far, diag in parts:
         def remote(i, carry, first=first, far=far, diag=diag):
             full[first + i, far_taps, :] = far[i]
             full[first + i, diag_taps, :] = diag[i]
@@ -397,7 +397,7 @@
 
 
 def weight_pair(strip, pair, aligned, one, two, first, spread, lefts, emit):
-    panel, channels = aligned.shape[2], spread.shape[2]
+    panel, channels = aligned.shape[2], spread[0].shape[1]
     for m in range(2):
         for k in range(4):
             for row in range(2):
@@ -411,7 +411,7 @@
         product = None
         for m in range(2):
             right = jnp.concatenate(
-                [spread[k, 4 * pair + 2 * m + ky + row] for k in range(4) for row in range(2)], axis=1
+                [spread[k][4 * pair + 2 * m + ky + row] for k in range(4) for row in range(2)], axis=1
             )
             part = dot_nt(lefts[m], right)
             product = part if product is None else product + part
@@ -421,34 +421,32 @@
     lax.fori_loop(0, 3, step, 0)
 
 
-def spread_kernel(place, *refs):
-    threes, ones, spread = refs[:4], refs[4:8], refs[8]
+def spread_kernel(place, mine, above, beyond, below, spread):
     strip = place[0]
-    channels = spread.shape[2]
-    for k in range(4):
-        spread[k, 0] = jnp.zeros((channels, LANES), BF16)
-        spread[k, 9] = jnp.zeros((channels, LANES), BF16)
-        for m, source in ((0, threes[k].at[0]), (1, threes[k].at[1]), (3, threes[k].at[2]), (2, ones[k])):
-            for row in range(2):
-                spread[k, 1 + 2 * ((strip + m) & 3) + row] = source[row]
-
-
-def near_weight_kernel(place, own, plus, minus, spread, out, lefts):
+    channels = spread.shape[1]
+    spread[0] = jnp.zeros((channels, LANES), BF16)
+    spread[9] = jnp.zeros((channels, LANES), BF16)
+    for m, source in enumerate((mine, above, beyond, below)):
+        for row in range(2):
+            spread[1 + 2 * ((strip + m) & 3) + row] = source[row]
+
+
+def near_weight_kernel(place, own, plus, minus, h0, h1, h2, h3, out, lefts):
     strip = place[0]
 
     def emit(taps, product):
         out[taps] = product
 
-    weight_pair(strip, strip // 2, own, plus, minus, (strip & 1) == 0, spread, lefts, emit)
-
-
-def far_weight_kernel(cells, place, plus, minus, far, spread, near, out, lefts):
+    weight_pair(strip, strip // 2, own, plus, minus, (strip & 1) == 0, (h0, h1, h2, h3), lefts, emit)
+
+
+def far_weight_kernel(cells, place, plus, minus, far, h0, h1, h2, h3, near, out, lefts):
     strip = place[0]
 
     def emit(taps, product):
         out[taps] = (near[taps] + product) / cells
 
-    weight_pair(strip, 1 - strip // 2, far, minus, plus, (strip & 1) == 0, spread, lefts, emit)
+    weight_pair(strip, 1 - strip // 2, far, minus, plus, (strip & 1) == 0, (h0, h1, h2, h3), lefts, emit)
 
 
 VM = pl.BlockSpec(memory_space=pltpu.VMEM)
@@ -506,7 +504,7 @@
     place = jnp.stack([strip, here, part])
 
     near = jnp.transpose(conv_weight, (1, 0, 2))
-    far0 = swap(lax.dynamic_slice_in_dim(near, part * 2, 2, axis=0), "wt", 2)
+    far0 = swap(lax.dynamic_slice_in_dim(near, part * 3, 3, axis=0), "wt", 2)
 
     stats = call(stats_kernel, shape((8, channels), F32), [VM], (lat,))
     hidden, table = call(
@@ -514,23 +512,27 @@
         (shape((strip_rows, channels, width), BF16), shape((channels, LANES), F32)),
         [VM] * 6,
         (lat, after_all(stats, far0), *(swap(stats, "rows", m) for m in (1, 2, 3)), given),
+        us=0.05,
     )
     above, below = ring(hidden, "rows", 1), ring(hidden, "rows", 3)
     side = swap(after_all(near, hidden), "wt", 1)
-    far2 = swap(after_all(near, hidden)[4:9], "wt", 2)
+    far2 = swap(after_all(near, hidden)[6:9], "wt", 2)
     far1 = swap(after_all(far0, hidden), "grp", 1)
     base = call(
         base_kernel, shape((strip_rows, channels, width), F32), [VM] * 3, (lat, tea, table), us=5
     )
-    framed, packed = call(
+    framed = call(
         frame_kernel,
-        (shape((3, 4, channels, width), BF16), shape((3, strip_rows, channels, width), BF16)),
+        shape((3, 4, channels, width), BF16),
         [SM] + [VM] * 3,
         (place, after_all(hidden, base), above, below),
         us=5,
     )
     beyond = ring(above, "rows", 1)
-    threes = [packed, None, swap(packed, "wt", 2), None]
+    across = [swap(after_all(hidden, framed), "wt", 2), swap(after_all(above, framed), "wt", 2)]
+    rows_of = functools.partial(
+        call, spread_kernel, shape((10, channels, width), BF16), [SM] + [VM] * 4, us=3
+    )
     part0, block0, block1 = call(
         near_conv_kernel,
         (
@@ -554,7 +556,7 @@
             shape((2, strip_rows, panel, width), BF16),
         ),
         [SM] + [VM] * 9,
-        (place, *weights[2:], framed, base, part0),
+        (place, *weights[2:], framed, base, after_all(part0, across[0])),
         [pltpu.VMEM((2 * panel, 2 * LANES), F32)],
         us=0.05,
     )
@@ -570,26 +572,28 @@
         (after_all(place, low), *weights),
         us=5,
     )
-    stacked = jnp.stack([block0, block1, block23[0], swap(block23[1], "wt", 1)])
+    stacked = after_all(jnp.stack([block0, block1, block23[0], swap(block23[1], "wt", 1)]), across[1])
     plus, minus = ring(stacked, "rows", 1), ring(stacked, "rows", 3)
     far = ring(plus, "rows", 1)
 
-    ones = [beyond, None, swap(beyond, "wt", 2), None]
-    for k in (0, 2):
-        threes[k + 1], ones[k + 1] = swap(threes[k], "wt", 1), swap(ones[k], "wt", 1)
+    across += [swap(after_all(beyond, stacked), "wt", 2), swap(after_all(below, block23), "wt", 2)]
+    own_rows = rows_of((place, after_all(hidden, stacked), above, beyond, below))
+    other_rows = swap(own_rows, "wt", 1)
 
     grad, sums = call(
         back_kernel,
         (shape((strip_rows, channels, width), F32), shape((8, channels), F32)),
         [VM] * 7,
-        (full, low_before, low, low_after, res, lat, table),
+        (full, low_before, after_all(low, across[3]), low_after, res, lat, table),
         [
             pltpu.VMEM((3, 4, LANES, channels), BF16),
             pltpu.VMEM((2 * LANES, channels), F32),
         ],
         mib=12, us=30,
     )
-    sums = after_all(sums, plus, minus)
+    sums = after_all(sums, plus, minus, across[2])
+    across_rows = rows_of((after_all(place, sums), *across))
+    diag_rows = swap(across_rows, "wt", 1)
     one, two, three = (swap(sums, "rows", m) for m in (1, 2, 3))
     sums = (sums + one) + (two + three)
     grad_latents = call(
@@ -599,20 +603,14 @@
         (sums, given, res, grad, lat, table),
         us=0.05,
     )
-    spread = call(
-        spread_kernel,
-        shape((4, 10, channels, width), BF16),
-        [SM] + [VM] * 8,
-        (place, *threes, *ones),
-        us=5,
-    )
+    images = (own_rows, other_rows, across_rows, diag_rows)
     near_weight = call(
         near_weight_kernel,
         shape((9, panel, channels), F32),
-        [SM] + [VM] * 4,
-        (after_all(place, grad_latents), stacked, plus, minus, spread),
+        [SM] + [VM] * 7,
+        (after_all(place, grad_latents), stacked, plus, minus, *images),
         [pltpu.VMEM((2, 3 * panel, 8 * LANES), BF16)],
-        mib=12, us=30,
+        mib=14, us=30,
     )
     one, two, three = (swap(sums, "wt", m) for m in (1, 2, 3))
     sums = (sums + one) + (two + three)
@@ -622,10 +620,10 @@
     grad_weight = call(
         functools.partial(far_weight_kernel, total_cells),
         shape((9, panel, channels), F32),
-        [SM] + [VM] * 5,
-        (place, plus, minus, far, spread, near_weight),
+        [SM] + [VM] * 8,
+        (place, plus, minus, far, *images, near_weight),
         [pltpu.VMEM((2, 3 * panel, 8 * LANES), BF16)],
-        mib=14, us=0.05,
+        mib=16, us=0.05,
     )
     return (
         mean_loss,

time: 134 us -> 126 us (0.940)
  waiting for transfers between devices: 45.5 us -> 35.2 us
  local copies, waits for them, and re-layouts: 10.8 us -> 5.12 us
  Pallas kernels: 36.8 us -> 41.1 us
  starting transfers between devices: 36.1 us -> 40.2 us
    ppermute x25, waiting for transfers between devices: 31.1 us -> 21.4 us  [swap(): return lax.ppermute(x, axis, [(i, i ^ mask) for i in range(size)])]
    unnamed x26 -> x22, local copies, waits for them, and re-layouts: 9.66 us -> 3.89 us
    ppermute x25, starting transfers between devices: 19.5 us -> 24.2 us  [swap(): return lax.ppermute(x, axis, [(i, i ^ mask) for i in range(size)])]
    pallas_call x12 -> x13, Pallas kernels: 36.8 us -> 41.1 us  [call(): pl.pallas_call(kernel, out_shape=outs, in_specs=specs, out_specs=jax.tree...]
  transfers between devices with their start and end apart: 33 -> 33, of which waited for: 8 -> 10; matrix products, arithmetic and copies ran while one was open for 1% -> 1% of each run, Pallas kernels for 20% -> 24%
where the time goes in v4:
time: 126 us
  Pallas kernels  41.1 us (33%)
  starting transfers between devices  40.2 us (32%)
  waiting for transfers between devices  35.2 us (28%)
  local copies, waits for them, and re-layouts  5.12 us (4%)
  between operations  2.68 us (2%)
  other arithmetic  1.37 us (1%)
    pallas_call x13, Pallas kernels, call(): pl.pallas_call(kernel, out_shape=outs, in_specs=specs, out_specs=jax.tree...  41.1 us
    ppermute x25, starting transfers between devices, swap(): return lax.ppermute(x, axis, [(i, i ^ mask) for i in range(size)])  24.2 us
    ppermute x25, waiting for transfers between devices, swap(): return lax.ppermute(x, axis, [(i, i ^ mask) for i in range(size)])  21.4 us
    ppermute x6, waiting for transfers between devices, ring(): return lax.ppermute(x, axis, [((i + step) % size, i) for i in range(size)])  13.8 us
    ppermute x6, starting transfers between devices, ring(): return lax.ppermute(x, axis, [((i + step) % size, i) for i in range(size)])  12.6 us
    unnamed x22, local copies, waits for them, and re-layouts  3.89 us
  transfers between devices with their start and end apart: 33, of which 10 were waited for; matrix products, arithmetic and copies ran while one was open for 1% of the time, Pallas kernels for 24%

profile of v4, /device:TPU:0, one launch (start us, length us, event | category | flops | bytes accessed | tf_op | source)
XLA Modules:
  0.0 125.7 jit_solution(2810558992271562812)
XLA Ops:
  1.8 3.0 %collective-permute-start = (bf16[3,160,640]{2,1,0:T(8,128)(2,1)S(1)}, bf16[3,160,640]{2,1,0:T(8,128)(2,1)S(1)}, u32[]{:S(2)}, u32[]{:S(2)}) collective-permute-start(bf16[3,160,640]{2,1,0:T(8,128)(2,1)S(1)} %dynamic-slice_bitcast_fusion), channel_id=1, source_target_pairs={{0,2},{1,3},{2,0},{3,1},{4,6},{5,7},{6,4},{7,5},{8,10},{9,11},{10,... | collective-permute-start | bytes 1843208 | tf_op jit(solution)/shard_map/ppermute | solution.py:476
  7.8 2.6 %collective-permute-start.2 = (f32[8,640]{1,0:T(8,128)S(1)}, f32[8,640]{1,0:T(8,128)S(1)}, u32[]{:S(2)}, u32[]{:S(2)}) collective-permute-start(f32[8,640]{1,0:T(8,128)S(1)} %shard_map.93.s0), channel_id=1, source_target_pairs={{0,8},{4,12},{8,0},{12,4},{1,9},{5,13},{9,1},{13,5},{2,10},{6,14},... | collective-permute-start | bytes 61448 | tf_op jit(solution)/shard_map/ppermute | solution.py:476
  10.7 7.9 %collective-permute-done.far0 = bf16[3,160,640]{2,1,0:T(8,128)(2,1)S(1)} collective-permute-done((bf16[3,160,640]{2,1,0:T(8,128)(2,1)S(1)}, bf16[3,160,640]{2,1,0:T(8,128)(2,1)S(1)}, u32[]{:S(2)}, u32[]{:S(2)}) %collective-permute-start) | collective-permute-done | bytes 614432 | tf_op jit(solution)/shard_map/ppermute | solution.py:476
  20.6 3.9 %collective-permute-start.6 = (bf16[2,640,128]{2,1,0:T(8,128)(2,1)}, bf16[2,640,128]{2,1,0:T(8,128)(2,1)S(1)}, u32[]{:S(2)}, u32[]{:S(2)}) collective-permute-start(bf16[2,640,128]{2,1,0:T(8,128)(2,1)} %copy-done.6), channel_id=1, source_target_pairs={{4,0},{8,4},{12,8},{0,12},{5,1},{9,5},{13,9},{1,13},{6,2},{10,6},{... | collective-permute-start | bytes 983048 | tf_op jit(solution)/shard_map/ppermute | solution.py:481
  28.9 3.9 %collective-permute-done.6.above = bf16[2,640,128]{2,1,0:T(8,128)(2,1)S(1)} collective-permute-done((bf16[2,640,128]{2,1,0:T(8,128)(2,1)}, bf16[2,640,128]{2,1,0:T(8,128)(2,1)S(1)}, u32[]{:S(2)}, u32[]{:S(2)}) %collective-permute-start.6) | collective-permute-done | bytes 327712 | tf_op jit(solution)/shard_map/ppermute | solution.py:481
  32.8 7.4 %collective-permute-done.7.below = bf16[2,640,128]{2,1,0:T(8,128)(2,1)S(1)} collective-permute-done((bf16[2,640,128]{2,1,0:T(8,128)(2,1)}, bf16[2,640,128]{2,1,0:T(8,128)(2,1)S(1)}, u32[]{:S(2)}, u32[]{:S(2)}) %collective-permute-start.7) | collective-permute-done | bytes 327712 | tf_op jit(solution)/shard_map/ppermute | solution.py:481
  43.9 4.3 %shard_map.97 = (f32[2,2,160,128]{3,2,1,0:T(8,128)S(1)}, bf16[2,160,128]{2,1,0:T(8,128)(2,1)S(1)}, bf16[2,160,128]{2,1,0:T(8,128)(2,1)S(1)}) custom-call(s32[3]{0:T(128)S(1)} %pad_add_fusion.place, bf16[9,160,640]{2,1,0:T(8,128)(2,1)S(1)} %bitcast.23, bf16[9,160,640]{2,1,0:T(8,128)(2,1)} %collective-permute-done.11.side, ...), custom_call_target="tpu_custom_call" | custom-call | flops 20000000000 | bytes 60000000 | tf_op jit(solution)/shard_map/pallas_call | solution.py:457
  48.2 3.6 %collective-permute-done.12.mine = bf16[2,640,128]{2,1,0:T(8,128)(2,1)S(1)} collective-permute-done((bf16[2,640,128]{2,1,0:T(8,128)(2,1)S(1)}, bf16[2,640,128]{2,1,0:T(8,128)(2,1)S(1)}, u32[]{:S(2)}, u32[]{:S(2)}) %collective-permute-start.12) | collective-permute-done | bytes 327712 | tf_op jit(solution)/shard_map/ppermute | solution.py:476
  51.9 1.8 %collective-permute-start.22 = (bf16[2,640,128]{2,1,0:T(8,128)(2,1)S(1)}, bf16[2,640,128]{2,1,0:T(8,128)(2,1)S(1)}, u32[]{:S(2)}, u32[]{:S(2)}) collective-permute-start(bf16[2,640,128]{2,1,0:T(8,128)(2,1)S(1)} %collective-permute-done.6.above), channel_id=1, source_target_pairs={{4,0},{8,4},{12,8},{0,12},{5,1},{9,5},{13,9},{1,13},{6,2},{10,6},{... | collective-permute-start | bytes 983048 | tf_op jit(solution)/shard_map/ppermute | solution.py:481
  53.7 3.4 %shard_map.98 = (f32[2,640,128]{2,1,0:T(8,128)S(1)}, bf16[2,640,128]{2,1,0:T(8,128)(2,1)S(1)}, bf16[2,2,160,128]{3,2,1,0:T(8,128)(2,1)S(1)}) custom-call(s32[3]{0:T(128)S(1)} %pad_add_fusion.place, bf16[3,160,640]{2,1,0:T(8,128)(2,1)S(1)} %collective-permute-done.far0, bf16[3,160,640]{2,1,0:T(8,128)(2,1)S(1)} %collective-permute-done.4.far1, ...), custom_call_target="tpu_custom_call" | custom-call | flops 50000000 | bytes 150000 | tf_op jit(solution)/shard_map/pallas_call | solution.py:457
  58.7 2.2 %collective-permute-start.13 = (bf16[1,640,128]{2,1,0:T(8,128)(2,1)S(1)}, bf16[1,640,128]{2,1,0:T(8,128)(2,1)S(1)}, u32[]{:S(2)}, u32[]{:S(2)}) collective-permute-start(bf16[1,640,128]{2,1,0:T(8,128)(2,1)S(1)} %get-tuple-element.63), channel_id=1, source_target_pairs={{0,4},{4,8},{8,12},{1,5},{5,9},{9,13},{2,6},{6,10},{10,14},{3,7},{... | collective-permute-start | bytes 491528 | tf_op jit(solution)/shard_map/ppermute | solution.py:564
  62.6 2.2 %shard_map.99.full = bf16[9,640,640]{2,1,0:T(8,128)(2,1)S(1)} custom-call(s32[3]{0:T(128)S(1)} %pad_add_fusion.place, bf16[9,160,640]{2,1,0:T(8,128)(2,1)S(1)} %bitcast.24, bf16[9,160,640]{2,1,0:T(8,128)(2,1)} %collective-permute-done.11.side, bf16[3,160,640]{2,1,0:T(8,128)(2,1)S(1)} %collective-permute-done.far0, ...), custom_call_target="tpu_custom_call" | custom-call | flops 5000000000 | bytes 15000000 | tf_op jit(solution)/shard_map/pallas_call | solution.py:457
  67.7 3.4 %collective-permute-start.20 = (bf16[4,2,160,128]{3,2,1,0:T(8,128)(2,1)S(1)}, bf16[4,2,160,128]{3,2,1,0:T(8,128)(2,1)S(1)}, u32[]{:S(2)}, u32[]{:S(2)}) collective-permute-start(bf16[4,2,160,128]{3,2,1,0:T(8,128)(2,1)S(1)} %pad_maximum_fusion.own), channel_id=1, source_target_pairs={{4,0},{8,4},{12,8},{0,12},{5,1},{9,5},{13,9},{1,13},{6,2},{10,6},{... | collective-permute-start | bytes 983048 | tf_op jit(solution)/shard_map/ppermute | solution.py:481
  71.8 4.4 %collective-permute-done.15.below = bf16[2,640,128]{2,1,0:T(8,128)(2,1)S(1)} collective-permute-done((bf16[2,640,128]{2,1,0:T(8,128)(2,1)S(1)}, bf16[2,640,128]{2,1,0:T(8,128)(2,1)S(1)}, u32[]{:S(2)}, u32[]{:S(2)}) %collective-permute-start.15) | collective-permute-done | bytes 327712 | tf_op jit(solution)/shard_map/ppermute | solution.py:476
  77.7 6.2 %shard_map.100 = (f32[2,640,128]{2,1,0:T(8,128)S(1)}, f32[8,640]{1,0:T(8,128)S(1)}) custom-call(bf16[9,640,640]{2,1,0:T(8,128)(2,1)S(1)} %shard_map.99.full, bf16[1,640,128]{2,1,0:T(8,128)(2,1)S(1)} %collective-permute-done.13.before, bf16[2,640,128]{2,1,0:T(8,128)(2,1)S(1)} %get-tuple-element.49.low, ...), custom_call_target="tpu_custom_call" | custom-call | flops 30000001024 | bytes 90000000 | tf_op jit(solution)/shard_map/pallas_call | solution.py:457
  83.9 1.6 %collective-permute-done.23.beyond = bf16[2,640,128]{2,1,0:T(8,128)(2,1)S(1)} collective-permute-done((bf16[2,640,128]{2,1,0:T(8,128)(2,1)S(1)}, bf16[2,640,128]{2,1,0:T(8,128)(2,1)S(1)}, u32[]{:S(2)}, u32[]{:S(2)}) %collective-permute-start.23) | collective-permute-done | bytes 327712 | tf_op jit(solution)/shard_map/ppermute | solution.py:476
  85.6 2.5 %collective-permute-done.21.minus = bf16[4,2,160,128]{3,2,1,0:T(8,128)(2,1)S(1)} collective-permute-done((bf16[4,2,160,128]{3,2,1,0:T(8,128)(2,1)S(1)}, bf16[4,2,160,128]{3,2,1,0:T(8,128)(2,1)S(1)}, u32[]{:S(2)}, u32[]{:S(2)}) %collective-permute-start.21) | collective-permute-done | bytes 327712 | tf_op jit(solution)/shard_map/ppermute | solution.py:481
  88.0 1.8 %shard_map.103.h2 = bf16[10,640,128]{2,1,0:T(8,128)(2,1)} custom-call(s32[3]{0:T(128)S(1)} %pad_add_fusion.place, bf16[2,640,128]{2,1,0:T(8,128)(2,1)S(1)} %collective-permute-done.12.mine, bf16[2,640,128]{2,1,0:T(8,128)(2,1)S(1)} %collective-permute-done.19.above, bf16[2,640,128]{2,1,0:T(8,128)(2,1)S(1)} %collective-permute-done.23.beyond, ...), custom_call_target="tpu_custom_call" | custom-call | flops 3000000000 | bytes 9000000 | tf_op jit(solution)/shard_map/pallas_call | solution.py:457
  90.8 3.5 %collective-permute-start.26 = (f32[8,640]{1,0:T(8,128)S(1)}, f32[8,640]{1,0:T(8,128)S(1)}, u32[]{:S(2)}, u32[]{:S(2)}) collective-permute-start(f32[8,640]{1,0:T(8,128)S(1)} %get-tuple-element.57), channel_id=1, source_target_pairs={{0,12},{4,8},{8,4},{12,0},{1,13},{5,9},{9,5},{13,1},{2,14},{6,10},... | collective-permute-start | bytes 61448 | tf_op jit(solution)/shard_map/ppermute | solution.py:476
  94.6 1.7 %collective-permute-done.26 = f32[8,640]{1,0:T(8,128)S(1)} collective-permute-done((f32[8,640]{1,0:T(8,128)S(1)}, f32[8,640]{1,0:T(8,128)S(1)}, u32[]{:S(2)}, u32[]{:S(2)}) %collective-permute-start.26) | collective-permute-done | bytes 20512 | tf_op jit(solution)/shard_map/ppermute | solution.py:476
  98.3 1.8 %shard_map.101 = f32[1280,128]{1,0:T(8,128)} custom-call(f32[8,640]{1,0:T(8,128)S(1)} %add_add_fusion.1.total, f32[3,640]{1,0:T(4,128)S(1)} %pad_maximum_fusion.1.given, f32[2,640,128]{2,1,0:T(8,128)S(1)} %get-tuple-element.50.res, f32[2,640,128]{2,1,0:T(8,128)S(1)} %get-tuple-element.58.grad, f32[1280,128]{1,0:T(8,128)S(1)} %bitcast.20, ...), custom_call_target="tpu_custom_call" | custom-call | flops 50000000 | bytes 150000 | tf_op jit(solution)/shard_map/pallas_call | solution.py:457
  100.1 3.5 %collective-permute-start.30 = (bf16[4,2,160,128]{3,2,1,0:T(8,128)(2,1)S(1)}, bf16[4,2,160,128]{3,2,1,0:T(8,128)(2,1)S(1)}, u32[]{:S(2)}, u32[]{:S(2)}) collective-permute-start(bf16[4,2,160,128]{3,2,1,0:T(8,128)(2,1)S(1)} %collective-permute-done.20.plus), channel_id=1, source_target_pairs={{4,0},{8,4},{12,8},{0,12},{5,1},{9,5},{13,9},{1,13},{6,2},{10,6},{... | collective-permute-start | bytes 983048 | tf_op jit(solution)/shard_map/ppermute | solution.py:481
  106.4 8.1 %shard_map.104.near = f32[9,160,640]{2,1,0:T(8,128)S(1)} custom-call(s32[3]{0:T(128)S(1)} %pad_add_fusion.place, bf16[4,2,160,128]{3,2,1,0:T(8,128)(2,1)S(1)} %pad_maximum_fusion.own, bf16[4,2,160,128]{3,2,1,0:T(8,128)(2,1)S(1)} %collective-permute-done.20.plus, bf16[4,2,160,128]{3,2,1,0:T(8,128)(2,1)S(1)} %copy-done.4, ...), custom_call_target="tpu_custom_call" | custom-call | flops 30000001024 | bytes 90000000 | tf_op jit(solution)/shard_map/pallas_call | solution.py:457
  114.5 10.0 %shard_map.105 = f32[9,160,640]{2,1,0:T(8,128)} custom-call(s32[3]{0:T(128)S(1)} %pad_add_fusion.place, bf16[4,2,160,128]{3,2,1,0:T(8,128)(2,1)S(1)} %collective-permute-done.20.plus, bf16[4,2,160,128]{3,2,1,0:T(8,128)(2,1)S(1)} %copy-done.4, bf16[4,2,160,128]{3,2,1,0:T(8,128)(2,1)S(1)} %collective-permute-done.30.far, ...), custom_call_target="tpu_custom_call" | custom-call | flops 50000000 | bytes 150000 | tf_op jit(solution)/shard_map/pallas_call | solution.py:457
  (91 shorter events, 28.2 us)
Async XLA Ops:
  1.8 16.9 %collective-permute-start = (bf16[3,160,640]{2,1,0:T(8,128)(2,1)S(1)}, bf16[3,160,640]{2,1,0:T(8,128)(2,1)S(1)}, u32[]{:S(2)}, u32[]{:S(2)}) collective-permute-start(bf16[3,160,640]{2,1,0:T(8,128)(2,1)S(1)} %dynamic-slice_bitcast_fusion), channel_id=1, source_target_pairs={{0,2},{1,3},{2,0},{3,1},{4,6},{5,7},{6,4},{7,5},{8,10},{9,11},{10,... | collective-permute-start | bytes 1843208 | tf_op jit(solution)/shard_map/ppermute | solution.py:476
  6.2 12.4 %collective-permute-start.1 = (f32[8,640]{1,0:T(8,128)S(1)}, f32[8,640]{1,0:T(8,128)S(1)}, u32[]{:S(2)}, u32[]{:S(2)}) collective-permute-start(f32[8,640]{1,0:T(8,128)S(1)} %shard_map.93.s0), channel_id=1, source_target_pairs={{0,4},{4,0},{8,12},{12,8},{1,5},{5,1},{9,13},{13,9},{2,6},{6,2},{1... | collective-permute-start | bytes 61448 | tf_op jit(solution)/shard_map/ppermute | solution.py:476
  7.8 10.8 %collective-permute-start.2 = (f32[8,640]{1,0:T(8,128)S(1)}, f32[8,640]{1,0:T(8,128)S(1)}, u32[]{:S(2)}, u32[]{:S(2)}) collective-permute-start(f32[8,640]{1,0:T(8,128)S(1)} %shard_map.93.s0), channel_id=1, source_target_pairs={{0,8},{4,12},{8,0},{12,4},{1,9},{5,13},{9,1},{13,5},{2,10},{6,14},... | collective-permute-start | bytes 61448 | tf_op jit(solution)/shard_map/ppermute | solution.py:476
  10.4 8.2 %collective-permute-start.3 = (f32[8,640]{1,0:T(8,128)S(1)}, f32[8,640]{1,0:T(8,128)S(1)}, u32[]{:S(2)}, u32[]{:S(2)}) collective-permute-start(f32[8,640]{1,0:T(8,128)S(1)} %shard_map.93.s0), channel_id=1, source_target_pairs={{0,12},{4,8},{8,4},{12,0},{1,13},{5,9},{9,5},{13,1},{2,14},{6,10},... | collective-permute-start | bytes 61448 | tf_op jit(solution)/shard_map/ppermute | solution.py:476
  20.5 23.3 %collective-permute-start.11 = (bf16[9,160,640]{2,1,0:T(8,128)(2,1)S(1)}, bf16[9,160,640]{2,1,0:T(8,128)(2,1)}, u32[]{:S(2)}, u32[]{:S(2)}) collective-permute-start(bf16[9,160,640]{2,1,0:T(8,128)(2,1)S(1)} %bitcast.21), channel_id=1, source_target_pairs={{0,1},{1,0},{2,3},{3,2},{4,5},{5,4},{6,7},{7,6},{8,9},{9,8},{10,11... | collective-permute-start | bytes 5529608 | tf_op jit(solution)/shard_map/ppermute | solution.py:476
  20.6 12.2 %collective-permute-start.6 = (bf16[2,640,128]{2,1,0:T(8,128)(2,1)}, bf16[2,640,128]{2,1,0:T(8,128)(2,1)S(1)}, u32[]{:S(2)}, u32[]{:S(2)}) collective-permute-start(bf16[2,640,128]{2,1,0:T(8,128)(2,1)} %copy-done.6), channel_id=1, source_target_pairs={{4,0},{8,4},{12,8},{0,12},{5,1},{9,5},{13,9},{1,13},{6,2},{10,6},{... | collective-permute-start | bytes 983048 | tf_op jit(solution)/shard_map/ppermute | solution.py:481
  24.4 15.8 %collective-permute-start.7 = (bf16[2,640,128]{2,1,0:T(8,128)(2,1)}, bf16[2,640,128]{2,1,0:T(8,128)(2,1)S(1)}, u32[]{:S(2)}, u32[]{:S(2)}) collective-permute-start(bf16[2,640,128]{2,1,0:T(8,128)(2,1)} %copy-done.6), channel_id=1, source_target_pairs={{12,0},{0,4},{4,8},{8,12},{13,1},{1,5},{5,9},{9,13},{14,2},{2,6},{... | collective-permute-start | bytes 983048 | tf_op jit(solution)/shard_map/ppermute | solution.py:481
  24.5 18.8 %collective-permute-start.4 = (bf16[3,160,640]{2,1,0:T(8,128)(2,1)S(1)}, bf16[3,160,640]{2,1,0:T(8,128)(2,1)S(1)}, u32[]{:S(2)}, u32[]{:S(2)}) collective-permute-start(bf16[3,160,640]{2,1,0:T(8,128)(2,1)S(1)} %collective-permute-done.far0), channel_id=1, source_target_pairs={{0,16},{16,0},{1,17},{17,1},{2,18},{18,2},{3,19},{19,3},{4,20},{20... | collective-permute-start | bytes 1843208 | tf_op jit(solution)/shard_map/ppermute | solution.py:476
  26.1 17.2 %collective-permute-start.5 = (bf16[3,160,640]{2,1,0:T(8,128)(2,1)S(1)}, bf16[3,160,640]{2,1,0:T(8,128)(2,1)S(1)}, u32[]{:S(2)}, u32[]{:S(2)}) collective-permute-start(bf16[3,160,640]{2,1,0:T(8,128)(2,1)S(1)} %slice.27), channel_id=1, source_target_pairs={{0,2},{1,3},{2,0},{3,1},{4,6},{5,7},{6,4},{7,5},{8,10},{9,11},{10,... | collective-permute-start | bytes 1843208 | tf_op jit(solution)/shard_map/ppermute | solution.py:476
  41.2 10.7 %collective-permute-start.12 = (bf16[2,640,128]{2,1,0:T(8,128)(2,1)S(1)}, bf16[2,640,128]{2,1,0:T(8,128)(2,1)S(1)}, u32[]{:S(2)}, u32[]{:S(2)}) collective-permute-start(bf16[2,640,128]{2,1,0:T(8,128)(2,1)S(1)} %copy-done.7), channel_id=1, source_target_pairs={{0,2},{1,3},{2,0},{3,1},{4,6},{5,7},{6,4},{7,5},{8,10},{9,11},{10,... | collective-permute-start | bytes 983048 | tf_op jit(solution)/shard_map/ppermute | solution.py:476
  42.8 24.9 %collective-permute-start.19 = (bf16[2,640,128]{2,1,0:T(8,128)(2,1)S(1)}, bf16[2,640,128]{2,1,0:T(8,128)(2,1)S(1)}, u32[]{:S(2)}, u32[]{:S(2)}) collective-permute-start(bf16[2,640,128]{2,1,0:T(8,128)(2,1)S(1)} %collective-permute-done.6.above), channel_id=1, source_target_pairs={{0,2},{1,3},{2,0},{3,1},{4,6},{5,7},{6,4},{7,5},{8,10},{9,11},{10,... | collective-permute-start | bytes 983048 | tf_op jit(solution)/shard_map/ppermute | solution.py:476
  43.3 10.4 %collective-permute-start.10 = (bf16[3,160,640]{2,1,0:T(8,128)(2,1)S(1)}, bf16[3,160,640]{2,1,0:T(8,128)(2,1)S(1)}, u32[]{:S(2)}, u32[]{:S(2)}) collective-permute-start(bf16[3,160,640]{2,1,0:T(8,128)(2,1)S(1)} %collective-permute-done.5.far2), channel_id=1, source_target_pairs={{0,1},{1,0},{2,3},{3,2},{4,5},{5,4},{6,7},{7,6},{8,9},{9,8},{10,11... | collective-permute-start | bytes 1843208 | tf_op jit(solution)/shard_map/ppermute | solution.py:476
  43.3 10.4 %collective-permute-start.8 = (bf16[3,160,640]{2,1,0:T(8,128)(2,1)S(1)}, bf16[3,160,640]{2,1,0:T(8,128)(2,1)S(1)}, u32[]{:S(2)}, u32[]{:S(2)}) collective-permute-start(bf16[3,160,640]{2,1,0:T(8,128)(2,1)S(1)} %collective-permute-done.far0), channel_id=1, source_target_pairs={{0,1},{1,0},{2,3},{3,2},{4,5},{5,4},{6,7},{7,6},{8,9},{9,8},{10,11... | collective-permute-start | bytes 1843208 | tf_op jit(solution)/shard_map/ppermute | solution.py:476
  43.8 9.9 %collective-permute-start.9 = (bf16[3,160,640]{2,1,0:T(8,128)(2,1)S(1)}, bf16[3,160,640]{2,1,0:T(8,128)(2,1)S(1)}, u32[]{:S(2)}, u32[]{:S(2)}) collective-permute-start(bf16[3,160,640]{2,1,0:T(8,128)(2,1)S(1)} %collective-permute-done.4.far1), channel_id=1, source_target_pairs={{0,1},{1,0},{2,3},{3,2},{4,5},{5,4},{6,7},{7,6},{8,9},{9,8},{10,11... | collective-permute-start | bytes 1843208 | tf_op jit(solution)/shard_map/ppermute | solution.py:476
  51.9 19.2 %collective-permute-start.22 = (bf16[2,640,128]{2,1,0:T(8,128)(2,1)S(1)}, bf16[2,640,128]{2,1,0:T(8,128)(2,1)S(1)}, u32[]{:S(2)}, u32[]{:S(2)}) collective-permute-start(bf16[2,640,128]{2,1,0:T(8,128)(2,1)S(1)} %collective-permute-done.6.above), channel_id=1, source_target_pairs={{4,0},{8,4},{12,8},{0,12},{5,1},{9,5},{13,9},{1,13},{6,2},{10,6},{... | collective-permute-start | bytes 983048 | tf_op jit(solution)/shard_map/ppermute | solution.py:481
  58.7 19.0 %collective-permute-start.13 = (bf16[1,640,128]{2,1,0:T(8,128)(2,1)S(1)}, bf16[1,640,128]{2,1,0:T(8,128)(2,1)S(1)}, u32[]{:S(2)}, u32[]{:S(2)}) collective-permute-start(bf16[1,640,128]{2,1,0:T(8,128)(2,1)S(1)} %get-tuple-element.63), channel_id=1, source_target_pairs={{0,4},{4,8},{8,12},{1,5},{5,9},{9,13},{2,6},{6,10},{10,14},{3,7},{... | collective-permute-start | bytes 491528 | tf_op jit(solution)/shard_map/ppermute | solution.py:564
  64.7 13.0 %collective-permute-start.16 = (bf16[1,640,128]{2,1,0:T(8,128)(2,1)S(1)}, bf16[1,640,128]{2,1,0:T(8,128)(2,1)S(1)}, u32[]{:S(2)}, u32[]{:S(2)}) collective-permute-start(bf16[1,640,128]{2,1,0:T(8,128)(2,1)S(1)} %get-tuple-element.62), channel_id=1, source_target_pairs={{4,0},{8,4},{12,8},{5,1},{9,5},{13,9},{6,2},{10,6},{14,10},{7,3},{... | collective-permute-start | bytes 491528 | tf_op jit(solution)/shard_map/ppermute | solution.py:565
  66.1 10.2 %collective-permute-start.15 = (bf16[2,640,128]{2,1,0:T(8,128)(2,1)S(1)}, bf16[2,640,128]{2,1,0:T(8,128)(2,1)S(1)}, u32[]{:S(2)}, u32[]{:S(2)}) collective-permute-start(bf16[2,640,128]{2,1,0:T(8,128)(2,1)S(1)} %collective-permute-done.7.below), channel_id=1, source_target_pairs={{0,2},{1,3},{2,0},{3,1},{4,6},{5,7},{6,4},{7,5},{8,10},{9,11},{10,... | collective-permute-start | bytes 983048 | tf_op jit(solution)/shard_map/ppermute | solution.py:476
  67.7 17.9 %collective-permute-start.20 = (bf16[4,2,160,128]{3,2,1,0:T(8,128)(2,1)S(1)}, bf16[4,2,160,128]{3,2,1,0:T(8,128)(2,1)S(1)}, u32[]{:S(2)}, u32[]{:S(2)}) collective-permute-start(bf16[4,2,160,128]{3,2,1,0:T(8,128)(2,1)S(1)} %pad_maximum_fusion.own), channel_id=1, source_target_pairs={{4,0},{8,4},{12,8},{0,12},{5,1},{9,5},{13,9},{1,13},{6,2},{10,6},{... | collective-permute-start | bytes 983048 | tf_op jit(solution)/shard_map/ppermute | solution.py:481
  71.1 16.9 %collective-permute-start.21 = (bf16[4,2,160,128]{3,2,1,0:T(8,128)(2,1)S(1)}, bf16[4,2,160,128]{3,2,1,0:T(8,128)(2,1)S(1)}, u32[]{:S(2)}, u32[]{:S(2)}) collective-permute-start(bf16[4,2,160,128]{3,2,1,0:T(8,128)(2,1)S(1)} %pad_maximum_fusion.own), channel_id=1, source_target_pairs={{12,0},{0,4},{4,8},{8,12},{13,1},{1,5},{5,9},{9,13},{14,2},{2,6},{... | collective-permute-start | bytes 983048 | tf_op jit(solution)/shard_map/ppermute | solution.py:481
  76.2 9.3 %collective-permute-start.23 = (bf16[2,640,128]{2,1,0:T(8,128)(2,1)S(1)}, bf16[2,640,128]{2,1,0:T(8,128)(2,1)S(1)}, u32[]{:S(2)}, u32[]{:S(2)}) collective-permute-start(bf16[2,640,128]{2,1,0:T(8,128)(2,1)S(1)} %collective-permute-done.22.beyond), channel_id=1, source_target_pairs={{0,2},{1,3},{2,0},{3,1},{4,6},{5,7},{6,4},{7,5},{8,10},{9,11},{10,... | collective-permute-start | bytes 983048 | tf_op jit(solution)/shard_map/ppermute | solution.py:476
  77.7 27.7 %collective-permute-start.31 = (bf16[10,640,128]{2,1,0:T(8,128)(2,1)S(1)}, bf16[10,640,128]{2,1,0:T(8,128)(2,1)}, u32[]{:S(2)}, u32[]{:S(2)}) collective-permute-start(bf16[10,640,128]{2,1,0:T(8,128)(2,1)S(1)} %shard_map.102.h0), channel_id=1, source_target_pairs={{0,1},{1,0},{2,3},{3,2},{4,5},{5,4},{6,7},{7,6},{8,9},{9,8},{10,11... | collective-permute-start | bytes 4915208 | tf_op jit(solution)/shard_map/ppermute | solution.py:476
  89.9 15.6 %collective-permute-start.32 = (bf16[10,640,128]{2,1,0:T(8,128)(2,1)}, bf16[10,640,128]{2,1,0:T(8,128)(2,1)}, u32[]{:S(2)}, u32[]{:S(2)}) collective-permute-start(bf16[10,640,128]{2,1,0:T(8,128)(2,1)} %shard_map.103.h2), channel_id=1, source_target_pairs={{0,1},{1,0},{2,3},{3,2},{4,5},{5,4},{6,7},{7,6},{8,9},{9,8},{10,11... | collective-permute-start | bytes 4915208 | tf_op jit(solution)/shard_map/ppermute | solution.py:476
  100.1 14.5 %collective-permute-start.30 = (bf16[4,2,160,128]{3,2,1,0:T(8,128)(2,1)S(1)}, bf16[4,2,160,128]{3,2,1,0:T(8,128)(2,1)S(1)}, u32[]{:S(2)}, u32[]{:S(2)}) collective-permute-start(bf16[4,2,160,128]{3,2,1,0:T(8,128)(2,1)S(1)} %collective-permute-done.20.plus), channel_id=1, source_target_pairs={{4,0},{8,4},{12,8},{0,12},{5,1},{9,5},{13,9},{1,13},{6,2},{10,6},{... | collective-permute-start | bytes 983048 | tf_op jit(solution)/shard_map/ppermute | solution.py:481
  (20 other events, 105.2 us)

commit v5 on v4

--- a/solution.py
+++ b/solution.py
@@ -381,11 +381,12 @@
     sums[...] = as_rows([add(first), add(second), add(bottom), add(loss)], channels)
 
 
-def latents_kernel(cells, total, given, res, grad, lat, table, out):
+def latents_kernel(cells, s0, s1, s2, s3, given, res, grad, lat, table, out, total):
     channels = total.shape[1]
     member = membership(channels)
-    rows = total[...] * given[0:1]
-    means = group_sums(rows, member) / cells
+    sums = (s0[...] + s1[...]) + (s2[...] + s3[...])
+    total[...] = sums
+    means = group_sums(sums * given[0:1], member) / cells
     rows = to_channels(means, member)
     columns = as_columns([rows[0:1], rows[1:2]], channels)
     constants = table[...]
@@ -419,6 +420,14 @@
         return carry
 
     lax.fori_loop(0, 3, step, 0)
+
+
+def totals_kernel(cells, s0, s1, s2, s3, loss, grads):
+    sums = (s0[...] + s1[...]) + (s2[...] + s3[...])
+    square = jnp.sum(sums[3:4], axis=1, keepdims=True) / (cells * sums.shape[1])
+    loss[...] = jnp.broadcast_to(square, loss.shape)
+    for row, source in enumerate((2, 1, 0)):
+        grads[row : row + 1] = sums[source : source + 1] / cells
 
 
 def spread_kernel(place, mine, above, beyond, below, spread):
@@ -504,7 +513,7 @@
     place = jnp.stack([strip, here, part])
 
     near = jnp.transpose(conv_weight, (1, 0, 2))
-    far0 = swap(lax.dynamic_slice_in_dim(near, part * 3, 3, axis=0), "wt", 2)
+    far0 = swap(lax.dynamic_slice_in_dim(near, part * 2, 2, axis=0), "wt", 2)
 
     stats = call(stats_kernel, shape((8, channels), F32), [VM], (lat,))
     hidden, table = call(
@@ -516,7 +525,7 @@
     )
     above, below = ring(hidden, "rows", 1), ring(hidden, "rows", 3)
     side = swap(after_all(near, hidden), "wt", 1)
-    far2 = swap(after_all(near, hidden)[6:9], "wt", 2)
+    far2 = swap(after_all(near, far0)[4:9], "wt", 2)
     far1 = swap(after_all(far0, hidden), "grp", 1)
     base = call(
         base_kernel, shape((strip_rows, channels, width), F32), [VM] * 3, (lat, tea, table), us=5
@@ -556,7 +565,7 @@
             shape((2, strip_rows, panel, width), BF16),
         ),
         [SM] + [VM] * 9,
-        (place, *weights[2:], framed, base, after_all(part0, across[0])),
+        (place, *weights[2:], framed, base, part0),
         [pltpu.VMEM((2 * panel, 2 * LANES), F32)],
         us=0.05,
     )
@@ -564,17 +573,18 @@
     low_before = lax.ppermute(low[1:2], "rows", up)
     low_after = lax.ppermute(low[0:1], "rows", down)
     block1 = swap(block1, "wt", 1)
-    block23 = swap(block23, "wt", 2)
+    block23 = swap(after_all(block23, across[0]), "wt", 2)
+    stacked = after_all(jnp.stack([block0, block1, block23[0], swap(block23[1], "wt", 1)]), across[1])
+    plus = ring(stacked, "rows", 1)
+    minus = ring(after_all(stacked, plus), "rows", 3)
+    far = ring(plus, "rows", 1)
     full = call(
         assemble_kernel,
         shape((9, channels, channels), BF16),
         [SM] + [VM] * 8,
-        (after_all(place, low), *weights),
+        (after_all(place, stacked), *weights),
         us=5,
     )
-    stacked = after_all(jnp.stack([block0, block1, block23[0], swap(block23[1], "wt", 1)]), across[1])
-    plus, minus = ring(stacked, "rows", 1), ring(stacked, "rows", 3)
-    far = ring(plus, "rows", 1)
 
     across += [swap(after_all(beyond, stacked), "wt", 2), swap(after_all(below, block23), "wt", 2)]
     own_rows = rows_of((place, after_all(hidden, stacked), above, beyond, below))
@@ -584,23 +594,24 @@
         back_kernel,
         (shape((strip_rows, channels, width), F32), shape((8, channels), F32)),
         [VM] * 7,
-        (full, low_before, after_all(low, across[3]), low_after, res, lat, table),
+        (full, low_before, after_all(low, plus), low_after, res, lat, table),
         [
             pltpu.VMEM((3, 4, LANES, channels), BF16),
             pltpu.VMEM((2 * LANES, channels), F32),
         ],
         mib=12, us=30,
     )
-    sums = after_all(sums, plus, minus, across[2])
+    sums = after_all(sums, minus)
     across_rows = rows_of((after_all(place, sums), *across))
     diag_rows = swap(across_rows, "wt", 1)
-    one, two, three = (swap(sums, "rows", m) for m in (1, 2, 3))
-    sums = (sums + one) + (two + three)
-    grad_latents = call(
+    grad_latents, sums = call(
         functools.partial(latents_kernel, group_cells),
-        shape((channels * strip_rows, width), F32),
-        [VM] * 6,
-        (sums, given, res, grad, lat, table),
+        (shape((channels * strip_rows, width), F32), shape((8, channels), F32)),
+        [VM] * 9,
+        (
+            sums, *(swap(sums, "rows", m) for m in (1, 2, 3)),
+            given, res, grad, lat, table,
+        ),
         us=0.05,
     )
     images = (own_rows, other_rows, across_rows, diag_rows)
@@ -612,10 +623,13 @@
         [pltpu.VMEM((2, 3 * panel, 8 * LANES), BF16)],
         mib=14, us=30,
     )
-    one, two, three = (swap(sums, "wt", m) for m in (1, 2, 3))
-    sums = (sums + one) + (two + three)
-    mean_loss = (jnp.sum(sums[3]) / (total_cells * channels)).reshape(1)
-    param_grads = jnp.stack([sums[2], sums[1], sums[0]]) / total_cells
+    loss, param_grads = call(
+        functools.partial(totals_kernel, total_cells),
+        (shape((1, LANES), F32), shape((3, channels), F32)),
+        [VM] * 4,
+        (sums, *(swap(sums, "wt", m) for m in (1, 2, 3))),
+        us=0.05,
+    )
 
     grad_weight = call(
         functools.partial(far_weight_kernel, total_cells),
@@ -626,7 +640,7 @@
         mib=16, us=0.05,
     )
     return (
-        mean_loss,
+        loss[0, :1],
         grad_latents.reshape(latents.shape),
         jnp.transpose(grad_weight, (1, 0, 2)),
         param_grads,

time: 126 us -> 119 us (0.944)
  Pallas kernels: 41.1 us -> 36.9 us
  waiting for transfers between devices: 35.2 us -> 38.1 us
  local copies, waits for them, and re-layouts: 5.12 us -> 3.2 us
  between operations: 2.68 us -> 0.91 us
    ppermute x6, waiting for transfers between devices: 13.8 us -> 21.5 us  [ring(): return lax.ppermute(x, axis, [((i + step) % size, i) for i in range(size)])]
    ppermute x25, waiting for transfers between devices: 21.4 us -> 16.6 us  [swap(): return lax.ppermute(x, axis, [(i, i ^ mask) for i in range(size)])]
    pallas_call x13 -> x14, Pallas kernels: 41.1 us -> 36.9 us  [call(): pl.pallas_call(kernel, out_shape=outs, in_specs=specs, out_specs=jax.tree...]
    unnamed x22 -> x18, local copies, waits for them, and re-layouts: 3.89 us -> 2.02 us
    ppermute x25, starting transfers between devices: 24.2 us -> 22.8 us  [swap(): return lax.ppermute(x, axis, [(i, i ^ mask) for i in range(size)])]
  transfers between devices with their start and end apart: 33 -> 33, of which waited for: 10 -> 12; matrix products, arithmetic and copies ran while one was open for 1% -> 0% of each run, Pallas kernels for 24% -> 23%
where the time goes in v5:
time: 119 us; the launch traced here: 118 us
  starting transfers between devices  39 us (33%)
  waiting for transfers between devices  38.1 us (32%)
  Pallas kernels  36.9 us (31%)
  local copies, waits for them, and re-layouts  3.2 us (3%)
    pallas_call x14, Pallas kernels, call(): pl.pallas_call(kernel, out_shape=outs, in_specs=specs, out_specs=jax.tree...  36.9 us
    ppermute x25, starting transfers between devices, swap(): return lax.ppermute(x, axis, [(i, i ^ mask) for i in range(size)])  22.8 us
    ppermute x6, waiting for transfers between devices, ring(): return lax.ppermute(x, axis, [((i + step) % size, i) for i in range(size)])  21.5 us
    ppermute x25, waiting for transfers between devices, swap(): return lax.ppermute(x, axis, [(i, i ^ mask) for i in range(size)])  16.6 us
    ppermute x6, starting transfers between devices, ring(): return lax.ppermute(x, axis, [((i + step) % size, i) for i in range(size)])  12.9 us
  transfers between devices with their start and end apart: 33, of which 12 were waited for; matrix products, arithmetic and copies ran while one was open for 0% of the time, Pallas kernels for 23%

profile of v5, /device:TPU:0, one launch (start us, length us, event | category | flops | bytes accessed | tf_op | source)
XLA Modules:
  0.0 118.2 jit_solution(13947941988700290176)
XLA Ops:
  1.7 3.0 %collective-permute-start = (bf16[2,160,640]{2,1,0:T(8,128)(2,1)S(1)}, bf16[2,160,640]{2,1,0:T(8,128)(2,1)S(1)}, u32[]{:S(2)}, u32[]{:S(2)}) collective-permute-start(bf16[2,160,640]{2,1,0:T(8,128)(2,1)S(1)} %dynamic-slice_bitcast_fusion), channel_id=1, source_target_pairs={{0,2},{1,3},{2,0},{3,1},{4,6},{5,7},{6,4},{7,5},{8,10},{9,11},{10,... | collective-permute-start | bytes 1228808 | tf_op jit(solution)/shard_map/ppermute | solution.py:485
  7.7 2.6 %collective-permute-start.2 = (f32[8,640]{1,0:T(8,128)S(1)}, f32[8,640]{1,0:T(8,128)S(1)}, u32[]{:S(2)}, u32[]{:S(2)}) collective-permute-start(f32[8,640]{1,0:T(8,128)S(1)} %shard_map.93.s0), channel_id=1, source_target_pairs={{0,8},{4,12},{8,0},{12,4},{1,9},{5,13},{9,1},{13,5},{2,10},{6,14},... | collective-permute-start | bytes 61448 | tf_op jit(solution)/shard_map/ppermute | solution.py:485
  10.6 3.6 %collective-permute-done.far0 = bf16[2,160,640]{2,1,0:T(8,128)(2,1)S(1)} collective-permute-done((bf16[2,160,640]{2,1,0:T(8,128)(2,1)S(1)}, bf16[2,160,640]{2,1,0:T(8,128)(2,1)S(1)}, u32[]{:S(2)}, u32[]{:S(2)}) %collective-permute-start) | collective-permute-done | bytes 409632 | tf_op jit(solution)/shard_map/ppermute | solution.py:485
  18.7 2.9 %collective-permute-start.5 = (bf16[2,640,128]{2,1,0:T(8,128)(2,1)S(1)}, bf16[2,640,128]{2,1,0:T(8,128)(2,1)S(1)}, u32[]{:S(2)}, u32[]{:S(2)}) collective-permute-start(bf16[2,640,128]{2,1,0:T(8,128)(2,1)S(1)} %copy-done.5), channel_id=1, source_target_pairs={{4,0},{8,4},{12,8},{0,12},{5,1},{9,5},{13,9},{1,13},{6,2},{10,6},{... | collective-permute-start | bytes 983048 | tf_op jit(solution)/shard_map/ppermute | solution.py:490
  23.4 6.3 %collective-permute-done.5.above = bf16[2,640,128]{2,1,0:T(8,128)(2,1)S(1)} collective-permute-done((bf16[2,640,128]{2,1,0:T(8,128)(2,1)S(1)}, bf16[2,640,128]{2,1,0:T(8,128)(2,1)S(1)}, u32[]{:S(2)}, u32[]{:S(2)}) %collective-permute-start.5) | collective-permute-done | bytes 327712 | tf_op jit(solution)/shard_map/ppermute | solution.py:490
  29.7 7.2 %collective-permute-done.6.below = bf16[2,640,128]{2,1,0:T(8,128)(2,1)S(1)} collective-permute-done((bf16[2,640,128]{2,1,0:T(8,128)(2,1)S(1)}, bf16[2,640,128]{2,1,0:T(8,128)(2,1)S(1)}, u32[]{:S(2)}, u32[]{:S(2)}) %collective-permute-start.6) | collective-permute-done | bytes 327712 | tf_op jit(solution)/shard_map/ppermute | solution.py:490
  39.0 4.4 %collective-permute-done.9.far2 = bf16[5,160,640]{2,1,0:T(8,128)(2,1)S(1)} collective-permute-done((bf16[5,160,640]{2,1,0:T(8,128)(2,1)S(1)}, bf16[5,160,640]{2,1,0:T(8,128)(2,1)S(1)}, u32[]{:S(2)}, u32[]{:S(2)}) %collective-permute-start.9) | collective-permute-done | bytes 1024032 | tf_op jit(solution)/shard_map/ppermute | solution.py:485
  43.9 4.3 %shard_map.97 = (f32[2,2,160,128]{3,2,1,0:T(8,128)S(1)}, bf16[2,160,128]{2,1,0:T(8,128)(2,1)S(1)}, bf16[2,160,128]{2,1,0:T(8,128)(2,1)S(1)}) custom-call(s32[3]{0:T(128)S(1)} %pad_add_fusion.place, bf16[9,160,640]{2,1,0:T(8,128)(2,1)S(1)} %bitcast.24, bf16[9,160,640]{2,1,0:T(8,128)(2,1)} %collective-permute-done.4.side, ...), custom_call_target="tpu_custom_call" | custom-call | flops 20000000000 | bytes 60000000 | tf_op jit(solution)/shard_map/pallas_call | solution.py:466
  48.3 3.4 %shard_map.98 = (f32[2,640,128]{2,1,0:T(8,128)S(1)}, bf16[2,640,128]{2,1,0:T(8,128)(2,1)S(1)}, bf16[2,2,160,128]{3,2,1,0:T(8,128)(2,1)S(1)}) custom-call(s32[3]{0:T(128)S(1)} %pad_add_fusion.place, bf16[2,160,640]{2,1,0:T(8,128)(2,1)S(1)} %collective-permute-done.far0, bf16[2,160,640]{2,1,0:T(8,128)(2,1)S(1)} %collective-permute-done.8.far1, ...), custom_call_target="tpu_custom_call" | custom-call | flops 50000000 | bytes 150000 | tf_op jit(solution)/shard_map/pallas_call | solution.py:466
  53.8 2.1 %collective-permute-start.28 = (bf16[2,640,128]{2,1,0:T(8,128)(2,1)S(1)}, bf16[2,640,128]{2,1,0:T(8,128)(2,1)S(1)}, u32[]{:S(2)}, u32[]{:S(2)}) collective-permute-start(bf16[2,640,128]{2,1,0:T(8,128)(2,1)S(1)} %collective-permute-done.5.above), channel_id=1, source_target_pairs={{4,0},{8,4},{12,8},{0,12},{5,1},{9,5},{13,9},{1,13},{6,2},{10,6},{... | collective-permute-start | bytes 983048 | tf_op jit(solution)/shard_map/ppermute | solution.py:490
  55.9 2.8 %collective-permute-done.14 = bf16[2,2,160,128]{3,2,1,0:T(8,128)(2,1)S(1)} collective-permute-done((bf16[2,2,160,128]{3,2,1,0:T(8,128)(2,1)S(1)}, bf16[2,2,160,128]{3,2,1,0:T(8,128)(2,1)S(1)}, u32[]{:S(2)}, u32[]{:S(2)}) %collective-permute-start.14) | collective-permute-done | bytes 163872 | tf_op jit(solution)/shard_map/ppermute | solution.py:485
  58.9 2.0 %collective-permute-start.17 = (bf16[1,640,128]{2,1,0:T(8,128)(2,1)S(1)}, bf16[1,640,128]{2,1,0:T(8,128)(2,1)S(1)}, u32[]{:S(2)}, u32[]{:S(2)}) collective-permute-start(bf16[1,640,128]{2,1,0:T(8,128)(2,1)S(1)} %get-tuple-element.75), channel_id=1, source_target_pairs={{0,4},{4,8},{8,12},{1,5},{5,9},{9,13},{2,6},{6,10},{10,14},{3,7},{... | collective-permute-start | bytes 491528 | tf_op jit(solution)/shard_map/ppermute | solution.py:573
  63.8 1.8 %collective-permute-done.16.above = bf16[2,640,128]{2,1,0:T(8,128)(2,1)S(1)} collective-permute-done((bf16[2,640,128]{2,1,0:T(8,128)(2,1)S(1)}, bf16[2,640,128]{2,1,0:T(8,128)(2,1)S(1)}, u32[]{:S(2)}, u32[]{:S(2)}) %collective-permute-start.16) | collective-permute-done | bytes 327712 | tf_op jit(solution)/shard_map/ppermute | solution.py:485
  65.6 2.9 %collective-permute-start.18 = (bf16[4,2,160,128]{3,2,1,0:T(8,128)(2,1)S(1)}, bf16[4,2,160,128]{3,2,1,0:T(8,128)(2,1)S(1)}, u32[]{:S(2)}, u32[]{:S(2)}) collective-permute-start(bf16[4,2,160,128]{3,2,1,0:T(8,128)(2,1)S(1)} %pad_maximum_fusion.own), channel_id=1, source_target_pairs={{4,0},{8,4},{12,8},{0,12},{5,1},{9,5},{13,9},{1,13},{6,2},{10,6},{... | collective-permute-start | bytes 983048 | tf_op jit(solution)/shard_map/ppermute | solution.py:490
  69.3 2.2 %shard_map.99.full = bf16[9,640,640]{2,1,0:T(8,128)(2,1)S(1)} custom-call(s32[3]{0:T(128)S(1)} %pad_add_fusion.place, bf16[9,160,640]{2,1,0:T(8,128)(2,1)S(1)} %bitcast.25, bf16[9,160,640]{2,1,0:T(8,128)(2,1)} %collective-permute-done.4.side, bf16[2,160,640]{2,1,0:T(8,128)(2,1)S(1)} %collective-permute-done.far0, ...), custom_call_target="tpu_custom_call" | custom-call | flops 5000000000 | bytes 15000000 | tf_op jit(solution)/shard_map/pallas_call | solution.py:466
  71.5 4.7 %collective-permute-done.18.plus = bf16[4,2,160,128]{3,2,1,0:T(8,128)(2,1)S(1)} collective-permute-done((bf16[4,2,160,128]{3,2,1,0:T(8,128)(2,1)S(1)}, bf16[4,2,160,128]{3,2,1,0:T(8,128)(2,1)S(1)}, u32[]{:S(2)}, u32[]{:S(2)}) %collective-permute-start.18) | collective-permute-done | bytes 327712 | tf_op jit(solution)/shard_map/ppermute | solution.py:490
  79.2 6.2 %shard_map.100 = (f32[2,640,128]{2,1,0:T(8,128)S(1)}, f32[8,640]{1,0:T(8,128)S(1)}) custom-call(bf16[9,640,640]{2,1,0:T(8,128)(2,1)S(1)} %shard_map.99.full, bf16[1,640,128]{2,1,0:T(8,128)(2,1)S(1)} %collective-permute-done.17.before, bf16[2,640,128]{2,1,0:T(8,128)(2,1)S(1)} %get-tuple-element.59.low, ...), custom_call_target="tpu_custom_call" | custom-call | flops 30000001024 | bytes 90000000 | tf_op jit(solution)/shard_map/pallas_call | solution.py:466
  85.4 2.8 %collective-permute-done.20.minus = bf16[4,2,160,128]{3,2,1,0:T(8,128)(2,1)S(1)} collective-permute-done((bf16[4,2,160,128]{3,2,1,0:T(8,128)(2,1)S(1)}, bf16[4,2,160,128]{3,2,1,0:T(8,128)(2,1)S(1)}, u32[]{:S(2)}, u32[]{:S(2)}) %collective-permute-start.20) | collective-permute-done | bytes 327712 | tf_op jit(solution)/shard_map/ppermute | solution.py:490
  90.1 3.3 %collective-permute-start.23 = (f32[8,640]{1,0:T(8,128)S(1)}, f32[8,640]{1,0:T(8,128)S(1)}, u32[]{:S(2)}, u32[]{:S(2)}) collective-permute-start(f32[8,640]{1,0:T(8,128)S(1)} %get-tuple-element.63.s0), channel_id=1, source_target_pairs={{0,12},{4,8},{8,4},{12,0},{1,13},{5,9},{9,5},{13,1},{2,14},{6,10},... | collective-permute-start | bytes 61448 | tf_op jit(solution)/shard_map/ppermute | solution.py:485
  93.8 1.9 %collective-permute-done.23.s3 = f32[8,640]{1,0:T(8,128)S(1)} collective-permute-done((f32[8,640]{1,0:T(8,128)S(1)}, f32[8,640]{1,0:T(8,128)S(1)}, u32[]{:S(2)}, u32[]{:S(2)}) %collective-permute-start.23) | collective-permute-done | bytes 20512 | tf_op jit(solution)/shard_map/ppermute | solution.py:485
  95.6 1.8 %shard_map.101 = (f32[1280,128]{1,0:T(8,128)}, f32[8,640]{1,0:T(8,128)S(1)}) custom-call(f32[8,640]{1,0:T(8,128)S(1)} %get-tuple-element.63.s0, f32[8,640]{1,0:T(8,128)S(1)} %collective-permute-done.21.s1, f32[8,640]{1,0:T(8,128)S(1)} %collective-permute-done.22.s2, f32[8,640]{1,0:T(8,128)S(1)} %collective-permute-done.23.s3, ...), custom_call_target="tpu_custom_call" | custom-call | flops 50000000 | bytes 150000 | tf_op jit(solution)/shard_map/pallas_call | solution.py:466
  99.3 3.3 %collective-permute-start.27 = (bf16[4,2,160,128]{3,2,1,0:T(8,128)(2,1)S(1)}, bf16[4,2,160,128]{3,2,1,0:T(8,128)(2,1)S(1)}, u32[]{:S(2)}, u32[]{:S(2)}) collective-permute-start(bf16[4,2,160,128]{3,2,1,0:T(8,128)(2,1)S(1)} %collective-permute-done.18.plus), channel_id=1, source_target_pairs={{4,0},{8,4},{12,8},{0,12},{5,1},{9,5},{13,9},{1,13},{6,2},{10,6},{... | collective-permute-start | bytes 983048 | tf_op jit(solution)/shard_map/ppermute | solution.py:490
  103.2 6.2 %shard_map.105.near = f32[9,160,640]{2,1,0:T(8,128)S(1)} custom-call(s32[3]{0:T(128)S(1)} %pad_add_fusion.place, bf16[4,2,160,128]{3,2,1,0:T(8,128)(2,1)S(1)} %pad_maximum_fusion.own, bf16[4,2,160,128]{3,2,1,0:T(8,128)(2,1)S(1)} %collective-permute-done.18.plus, bf16[4,2,160,128]{3,2,1,0:T(8,128)(2,1)S(1)} %collective-permute-done.20.minus, ...), custom_call_target="tpu_custom_call" | custom-call | flops 30000001024 | bytes 90000000 | tf_op jit(solution)/shard_map/pallas_call | solution.py:466
  110.0 8.2 %shard_map.106 = f32[9,160,640]{2,1,0:T(8,128)} custom-call(s32[3]{0:T(128)S(1)} %pad_add_fusion.place, bf16[4,2,160,128]{3,2,1,0:T(8,128)(2,1)S(1)} %collective-permute-done.18.plus, bf16[4,2,160,128]{3,2,1,0:T(8,128)(2,1)S(1)} %collective-permute-done.20.minus, bf16[4,2,160,128]{3,2,1,0:T(8,128)(2,1)S(1)} %collective-permute-done.27.far, ...), custom_call_target="tpu_custom_call" | custom-call | flops 50000000 | bytes 150000 | tf_op jit(solution)/shard_map/pallas_call | solution.py:466
  (84 shorter events, 27.4 us)
Async XLA Ops:
  1.7 12.5 %collective-permute-start = (bf16[2,160,640]{2,1,0:T(8,128)(2,1)S(1)}, bf16[2,160,640]{2,1,0:T(8,128)(2,1)S(1)}, u32[]{:S(2)}, u32[]{:S(2)}) collective-permute-start(bf16[2,160,640]{2,1,0:T(8,128)(2,1)S(1)} %dynamic-slice_bitcast_fusion), channel_id=1, source_target_pairs={{0,2},{1,3},{2,0},{3,1},{4,6},{5,7},{6,4},{7,5},{8,10},{9,11},{10,... | collective-permute-start | bytes 1228808 | tf_op jit(solution)/shard_map/ppermute | solution.py:485
  6.1 8.1 %collective-permute-start.1 = (f32[8,640]{1,0:T(8,128)S(1)}, f32[8,640]{1,0:T(8,128)S(1)}, u32[]{:S(2)}, u32[]{:S(2)}) collective-permute-start(f32[8,640]{1,0:T(8,128)S(1)} %shard_map.93.s0), channel_id=1, source_target_pairs={{0,4},{4,0},{8,12},{12,8},{1,5},{5,1},{9,13},{13,9},{2,6},{6,2},{1... | collective-permute-start | bytes 61448 | tf_op jit(solution)/shard_map/ppermute | solution.py:485
  7.7 6.4 %collective-permute-start.2 = (f32[8,640]{1,0:T(8,128)S(1)}, f32[8,640]{1,0:T(8,128)S(1)}, u32[]{:S(2)}, u32[]{:S(2)}) collective-permute-start(f32[8,640]{1,0:T(8,128)S(1)} %shard_map.93.s0), channel_id=1, source_target_pairs={{0,8},{4,12},{8,0},{12,4},{1,9},{5,13},{9,1},{13,5},{2,10},{6,14},... | collective-permute-start | bytes 61448 | tf_op jit(solution)/shard_map/ppermute | solution.py:485
  10.3 5.6 %collective-permute-start.3 = (f32[8,640]{1,0:T(8,128)S(1)}, f32[8,640]{1,0:T(8,128)S(1)}, u32[]{:S(2)}, u32[]{:S(2)}) collective-permute-start(f32[8,640]{1,0:T(8,128)S(1)} %shard_map.93.s0), channel_id=1, source_target_pairs={{0,12},{4,8},{8,4},{12,0},{1,13},{5,9},{9,5},{13,1},{2,14},{6,10},... | collective-permute-start | bytes 61448 | tf_op jit(solution)/shard_map/ppermute | solution.py:485
  17.8 26.1 %collective-permute-start.4 = (bf16[9,160,640]{2,1,0:T(8,128)(2,1)S(1)}, bf16[9,160,640]{2,1,0:T(8,128)(2,1)}, u32[]{:S(2)}, u32[]{:S(2)}) collective-permute-start(bf16[9,160,640]{2,1,0:T(8,128)(2,1)S(1)} %bitcast.22), channel_id=1, source_target_pairs={{0,1},{1,0},{2,3},{3,2},{4,5},{5,4},{6,7},{7,6},{8,9},{9,8},{10,11... | collective-permute-start | bytes 5529608 | tf_op jit(solution)/shard_map/ppermute | solution.py:485
  17.9 25.5 %collective-permute-start.9 = (bf16[5,160,640]{2,1,0:T(8,128)(2,1)S(1)}, bf16[5,160,640]{2,1,0:T(8,128)(2,1)S(1)}, u32[]{:S(2)}, u32[]{:S(2)}) collective-permute-start(bf16[5,160,640]{2,1,0:T(8,128)(2,1)S(1)} %slice.18), channel_id=1, source_target_pairs={{0,2},{1,3},{2,0},{3,1},{4,6},{5,7},{6,4},{7,5},{8,10},{9,11},{10,... | collective-permute-start | bytes 3072008 | tf_op jit(solution)/shard_map/ppermute | solution.py:485
  18.7 11.0 %collective-permute-start.5 = (bf16[2,640,128]{2,1,0:T(8,128)(2,1)S(1)}, bf16[2,640,128]{2,1,0:T(8,128)(2,1)S(1)}, u32[]{:S(2)}, u32[]{:S(2)}) collective-permute-start(bf16[2,640,128]{2,1,0:T(8,128)(2,1)S(1)} %copy-done.5), channel_id=1, source_target_pairs={{4,0},{8,4},{12,8},{0,12},{5,1},{9,5},{13,9},{1,13},{6,2},{10,6},{... | collective-permute-start | bytes 983048 | tf_op jit(solution)/shard_map/ppermute | solution.py:490
  21.6 15.3 %collective-permute-start.6 = (bf16[2,640,128]{2,1,0:T(8,128)(2,1)S(1)}, bf16[2,640,128]{2,1,0:T(8,128)(2,1)S(1)}, u32[]{:S(2)}, u32[]{:S(2)}) collective-permute-start(bf16[2,640,128]{2,1,0:T(8,128)(2,1)S(1)} %copy-done.5), channel_id=1, source_target_pairs={{12,0},{0,4},{4,8},{8,12},{13,1},{1,5},{5,9},{9,13},{14,2},{2,6},{... | collective-permute-start | bytes 983048 | tf_op jit(solution)/shard_map/ppermute | solution.py:490
  21.6 17.3 %collective-permute-start.8 = (bf16[2,160,640]{2,1,0:T(8,128)(2,1)S(1)}, bf16[2,160,640]{2,1,0:T(8,128)(2,1)S(1)}, u32[]{:S(2)}, u32[]{:S(2)}) collective-permute-start(bf16[2,160,640]{2,1,0:T(8,128)(2,1)S(1)} %collective-permute-done.far0), channel_id=1, source_target_pairs={{0,16},{16,0},{1,17},{17,1},{2,18},{18,2},{3,19},{19,3},{4,20},{20... | collective-permute-start | bytes 1228808 | tf_op jit(solution)/shard_map/ppermute | solution.py:485
  37.9 13.8 %collective-permute-start.13 = (bf16[2,640,128]{2,1,0:T(8,128)(2,1)S(1)}, bf16[2,640,128]{2,1,0:T(8,128)(2,1)S(1)}, u32[]{:S(2)}, u32[]{:S(2)}) collective-permute-start(bf16[2,640,128]{2,1,0:T(8,128)(2,1)S(1)} %copy-done.5), channel_id=1, source_target_pairs={{0,2},{1,3},{2,0},{3,1},{4,6},{5,7},{6,4},{7,5},{8,10},{9,11},{10,... | collective-permute-start | bytes 983048 | tf_op jit(solution)/shard_map/ppermute | solution.py:485
  51.7 7.1 %collective-permute-start.14 = (bf16[2,2,160,128]{3,2,1,0:T(8,128)(2,1)S(1)}, bf16[2,2,160,128]{3,2,1,0:T(8,128)(2,1)S(1)}, u32[]{:S(2)}, u32[]{:S(2)}) collective-permute-start(bf16[2,2,160,128]{3,2,1,0:T(8,128)(2,1)S(1)} %get-tuple-element.54), channel_id=1, source_target_pairs={{0,2},{1,3},{2,0},{3,1},{4,6},{5,7},{6,4},{7,5},{8,10},{9,11},{10,... | collective-permute-start | bytes 491528 | tf_op jit(solution)/shard_map/ppermute | solution.py:485
  52.3 13.3 %collective-permute-start.16 = (bf16[2,640,128]{2,1,0:T(8,128)(2,1)S(1)}, bf16[2,640,128]{2,1,0:T(8,128)(2,1)S(1)}, u32[]{:S(2)}, u32[]{:S(2)}) collective-permute-start(bf16[2,640,128]{2,1,0:T(8,128)(2,1)S(1)} %collective-permute-done.5.above), channel_id=1, source_target_pairs={{0,2},{1,3},{2,0},{3,1},{4,6},{5,7},{6,4},{7,5},{8,10},{9,11},{10,... | collective-permute-start | bytes 983048 | tf_op jit(solution)/shard_map/ppermute | solution.py:485
  53.8 14.8 %collective-permute-start.28 = (bf16[2,640,128]{2,1,0:T(8,128)(2,1)S(1)}, bf16[2,640,128]{2,1,0:T(8,128)(2,1)S(1)}, u32[]{:S(2)}, u32[]{:S(2)}) collective-permute-start(bf16[2,640,128]{2,1,0:T(8,128)(2,1)S(1)} %collective-permute-done.5.above), channel_id=1, source_target_pairs={{4,0},{8,4},{12,8},{0,12},{5,1},{9,5},{13,9},{1,13},{6,2},{10,6},{... | collective-permute-start | bytes 983048 | tf_op jit(solution)/shard_map/ppermute | solution.py:490
  58.9 18.8 %collective-permute-start.17 = (bf16[1,640,128]{2,1,0:T(8,128)(2,1)S(1)}, bf16[1,640,128]{2,1,0:T(8,128)(2,1)S(1)}, u32[]{:S(2)}, u32[]{:S(2)}) collective-permute-start(bf16[1,640,128]{2,1,0:T(8,128)(2,1)S(1)} %get-tuple-element.75), channel_id=1, source_target_pairs={{0,4},{4,8},{8,12},{1,5},{5,9},{9,13},{2,6},{6,10},{10,14},{3,7},{... | collective-permute-start | bytes 491528 | tf_op jit(solution)/shard_map/ppermute | solution.py:573
  60.9 18.3 %collective-permute-start.19 = (bf16[1,640,128]{2,1,0:T(8,128)(2,1)S(1)}, bf16[1,640,128]{2,1,0:T(8,128)(2,1)S(1)}, u32[]{:S(2)}, u32[]{:S(2)}) collective-permute-start(bf16[1,640,128]{2,1,0:T(8,128)(2,1)S(1)} %get-tuple-element.74), channel_id=1, source_target_pairs={{4,0},{8,4},{12,8},{5,1},{9,5},{13,9},{6,2},{10,6},{14,10},{7,3},{... | collective-permute-start | bytes 491528 | tf_op jit(solution)/shard_map/ppermute | solution.py:574
  62.2 25.9 %collective-permute-start.31 = (bf16[2,640,128]{2,1,0:T(8,128)(2,1)S(1)}, bf16[2,640,128]{2,1,0:T(8,128)(2,1)S(1)}, u32[]{:S(2)}, u32[]{:S(2)}) collective-permute-start(bf16[2,640,128]{2,1,0:T(8,128)(2,1)S(1)} %collective-permute-done.6.below), channel_id=1, source_target_pairs={{0,2},{1,3},{2,0},{3,1},{4,6},{5,7},{6,4},{7,5},{8,10},{9,11},{10,... | collective-permute-start | bytes 983048 | tf_op jit(solution)/shard_map/ppermute | solution.py:485
  65.6 10.5 %collective-permute-start.18 = (bf16[4,2,160,128]{3,2,1,0:T(8,128)(2,1)S(1)}, bf16[4,2,160,128]{3,2,1,0:T(8,128)(2,1)S(1)}, u32[]{:S(2)}, u32[]{:S(2)}) collective-permute-start(bf16[4,2,160,128]{3,2,1,0:T(8,128)(2,1)S(1)} %pad_maximum_fusion.own), channel_id=1, source_target_pairs={{4,0},{8,4},{12,8},{0,12},{5,1},{9,5},{13,9},{1,13},{6,2},{10,6},{... | collective-permute-start | bytes 983048 | tf_op jit(solution)/shard_map/ppermute | solution.py:490
  69.2 34.0 %collective-permute-start.29 = (bf16[10,640,128]{2,1,0:T(8,128)(2,1)S(1)}, bf16[10,640,128]{2,1,0:T(8,128)(2,1)S(1)}, u32[]{:S(2)}, u32[]{:S(2)}) collective-permute-start(bf16[10,640,128]{2,1,0:T(8,128)(2,1)S(1)} %shard_map.103.h0), channel_id=1, source_target_pairs={{0,1},{1,0},{2,3},{3,2},{4,5},{5,4},{6,7},{7,6},{8,9},{9,8},{10,11... | collective-permute-start | bytes 4915208 | tf_op jit(solution)/shard_map/ppermute | solution.py:485
  76.1 12.0 %collective-permute-start.30 = (bf16[2,640,128]{2,1,0:T(8,128)(2,1)S(1)}, bf16[2,640,128]{2,1,0:T(8,128)(2,1)S(1)}, u32[]{:S(2)}, u32[]{:S(2)}) collective-permute-start(bf16[2,640,128]{2,1,0:T(8,128)(2,1)S(1)} %collective-permute-done.28.beyond), channel_id=1, source_target_pairs={{0,2},{1,3},{2,0},{3,1},{4,6},{5,7},{6,4},{7,5},{8,10},{9,11},{10,... | collective-permute-start | bytes 983048 | tf_op jit(solution)/shard_map/ppermute | solution.py:485
  77.6 10.5 %collective-permute-start.20 = (bf16[4,2,160,128]{3,2,1,0:T(8,128)(2,1)S(1)}, bf16[4,2,160,128]{3,2,1,0:T(8,128)(2,1)S(1)}, u32[]{:S(2)}, u32[]{:S(2)}) collective-permute-start(bf16[4,2,160,128]{3,2,1,0:T(8,128)(2,1)S(1)} %pad_maximum_fusion.own), channel_id=1, source_target_pairs={{12,0},{0,4},{4,8},{8,12},{13,1},{1,5},{5,9},{9,13},{14,2},{2,6},{... | collective-permute-start | bytes 983048 | tf_op jit(solution)/shard_map/ppermute | solution.py:490
  88.8 14.4 %collective-permute-start.32 = (bf16[10,640,128]{2,1,0:T(8,128)(2,1)S(1)}, bf16[10,640,128]{2,1,0:T(8,128)(2,1)S(1)}, u32[]{:S(2)}, u32[]{:S(2)}) collective-permute-start(bf16[10,640,128]{2,1,0:T(8,128)(2,1)S(1)} %shard_map.104.h2), channel_id=1, source_target_pairs={{0,1},{1,0},{2,3},{3,2},{4,5},{5,4},{6,7},{7,6},{8,9},{9,8},{10,11... | collective-permute-start | bytes 4915208 | tf_op jit(solution)/shard_map/ppermute | solution.py:485
  90.1 5.6 %collective-permute-start.23 = (f32[8,640]{1,0:T(8,128)S(1)}, f32[8,640]{1,0:T(8,128)S(1)}, u32[]{:S(2)}, u32[]{:S(2)}) collective-permute-start(f32[8,640]{1,0:T(8,128)S(1)} %get-tuple-element.63.s0), channel_id=1, source_target_pairs={{0,12},{4,8},{8,4},{12,0},{1,13},{5,9},{9,5},{13,1},{2,14},{6,10},... | collective-permute-start | bytes 61448 | tf_op jit(solution)/shard_map/ppermute | solution.py:485
  97.4 5.2 %collective-permute-start.25 = (f32[8,640]{1,0:T(8,128)S(1)}, f32[8,640]{1,0:T(8,128)S(1)}, u32[]{:S(2)}, u32[]{:S(2)}) collective-permute-start(f32[8,640]{1,0:T(8,128)S(1)} %get-tuple-element.65.s0), channel_id=1, source_target_pairs={{0,2},{1,3},{2,0},{3,1},{4,6},{5,7},{6,4},{7,5},{8,10},{9,11},{10,... | collective-permute-start | bytes 61448 | tf_op jit(solution)/shard_map/ppermute | solution.py:485
  99.3 10.7 %collective-permute-start.27 = (bf16[4,2,160,128]{3,2,1,0:T(8,128)(2,1)S(1)}, bf16[4,2,160,128]{3,2,1,0:T(8,128)(2,1)S(1)}, u32[]{:S(2)}, u32[]{:S(2)}) collective-permute-start(bf16[4,2,160,128]{3,2,1,0:T(8,128)(2,1)S(1)} %collective-permute-done.18.plus), channel_id=1, source_target_pairs={{4,0},{8,4},{12,8},{0,12},{5,1},{9,5},{13,9},{1,13},{6,2},{10,6},{... | collective-permute-start | bytes 983048 | tf_op jit(solution)/shard_map/ppermute | solution.py:490
  (18 other events, 82.4 us)

commit v6 on v5

--- a/solution.py
+++ b/solution.py
@@ -290,7 +290,8 @@
 
 
 def far_conv_kernel(
-    place, far0, far1, far2, diag0, diag1, diag2, framed, base, part, res, low, block23, total
+    place, far0, far1, far2, far3, far4, diag0, diag1, diag2, diag3, diag4, framed, base, part,
+    res, low, block23, total,
 ):
     me, half = place[1], place[2]
     panel = far0.shape[1]
@@ -305,10 +306,11 @@
 
         lax.fori_loop(0, far.shape[0], step, 0)
 
-    taps = far0.shape[0]
-    run(taps * half, far0, diag0)
-    run(taps - taps * half, far1, diag1)
-    run(2 * taps, far2, diag2)
+    run(2 * half, far0, diag0)
+    run(2 - 2 * half, far1, diag1)
+    run(4 + half, far2, diag2)
+    run(5 - half, far3, diag3)
+    run(6, far4, diag4)
     for k in range(4):
         rows = panel_rows(me, k, panel)
         for row in range(2):
@@ -323,7 +325,9 @@
             low[row, rows, :] = value.astype(BF16)
 
 
-def assemble_kernel(place, near, side, far0, far1, far2, diag0, diag1, diag2, full):
+def assemble_kernel(
+    place, near, side, far0, far1, far2, far3, far4, diag0, diag1, diag2, diag3, diag4, full
+):
     me, half = place[1], place[2]
     panel = near.shape[1]
     near_taps, side_taps = panel_rows(me, 0, panel), panel_rows(me, 1, panel)
@@ -335,8 +339,10 @@
         return carry
 
     lax.fori_loop(0, 9, local, 0)
-    taps = far0.shape[0]
-    parts = ((taps * half, far0, diag0), (taps - taps * half, far1, diag1), (2 * taps, far2, diag2))
+    parts = (
+        (2 * half, far0, diag0), (2 - 2 * half, far1, diag1), (4 + half, far2, diag2),
+        (5 - half, far3, diag3), (6, far4, diag4),
+    )
     for first, far, diag in parts:
         def remote(i, carry, first=first, far=far, diag=diag):
             full[first + i, far_taps, :] = far[i]
@@ -449,25 +455,34 @@
     weight_pair(strip, strip // 2, own, plus, minus, (strip & 1) == 0, (h0, h1, h2, h3), lefts, emit)
 
 
-def far_weight_kernel(cells, place, plus, minus, far, h0, h1, h2, h3, near, out, lefts):
+def far_weight_kernel(cells, place, plus, minus, far, h0, h1, h2, h3, near, out, lefts, held, sems):
     strip = place[0]
 
+    def written(taps, slot):
+        return pltpu.make_async_copy(held.at[taps], out.at[taps], sems.at[slot])
+
     def emit(taps, product):
-        out[taps] = (near[taps] + product) / cells
+        held[taps] = (near[taps] + product) / cells
+        for slot in range(3):
+            @pl.when(taps.start == 3 * slot)
+            def _(slot=slot):
+                written(pl.ds(3 * slot, 3), slot).start()
 
     weight_pair(strip, 1 - strip // 2, far, minus, plus, (strip & 1) == 0, (h0, h1, h2, h3), lefts, emit)
+    for slot in range(3):
+        written(pl.ds(3 * slot, 3), slot).wait()
 
 
 VM = pl.BlockSpec(memory_space=pltpu.VMEM)
 SM = pl.BlockSpec(memory_space=pltpu.SMEM)
 
 
-def call(kernel, outs, specs, args, scratch=(), mib=8, us=3):
+def call(kernel, outs, specs, args, scratch=(), mib=8, us=3, space=VM):
     return pl.pallas_call(
         kernel,
         out_shape=outs,
         in_specs=specs,
-        out_specs=jax.tree.map(lambda _: VM, outs),
+        out_specs=jax.tree.map(lambda _: space, outs),
         scratch_shapes=scratch,
         compiler_params=pltpu.CompilerParams(vmem_limit_bytes=mib << 20),
         cost_estimate=pl.CostEstimate(
@@ -514,19 +529,21 @@
 
     near = jnp.transpose(conv_weight, (1, 0, 2))
     far0 = swap(lax.dynamic_slice_in_dim(near, part * 2, 2, axis=0), "wt", 2)
+    side = swap(near, "wt", 1)
 
     stats = call(stats_kernel, shape((8, channels), F32), [VM], (lat,))
     hidden, table = call(
         functools.partial(hidden_kernel, group_cells),
         (shape((strip_rows, channels, width), BF16), shape((channels, LANES), F32)),
         [VM] * 6,
-        (lat, after_all(stats, far0), *(swap(stats, "rows", m) for m in (1, 2, 3)), given),
+        (lat, after_all(stats, far0, side), *(swap(stats, "rows", m) for m in (1, 2, 3)), given),
         us=0.05,
     )
     above, below = ring(hidden, "rows", 1), ring(hidden, "rows", 3)
-    side = swap(after_all(near, hidden), "wt", 1)
-    far2 = swap(after_all(near, far0)[4:9], "wt", 2)
-    far1 = swap(after_all(far0, hidden), "grp", 1)
+    later = after_all(near, hidden)
+    far2 = swap(lax.dynamic_slice_in_dim(later, 4 + part, 1, axis=0), "wt", 2)
+    far4 = swap(later[6:9], "wt", 2)
+    far1, far3 = swap(after_all(far0, hidden), "grp", 1), swap(far2, "grp", 1)
     base = call(
         base_kernel, shape((strip_rows, channels, width), F32), [VM] * 3, (lat, tea, table), us=5
     )
@@ -538,7 +555,7 @@
         us=5,
     )
     beyond = ring(above, "rows", 1)
-    across = [swap(after_all(hidden, framed), "wt", 2), swap(after_all(above, framed), "wt", 2)]
+    across = [swap(after_all(hidden, framed), "wt", 2)]
     rows_of = functools.partial(
         call, spread_kernel, shape((10, channels, width), BF16), [SM] + [VM] * 4, us=3
     )
@@ -554,9 +571,8 @@
         [pltpu.VMEM((2 * panel, 2 * LANES), F32)],
         us=20,
     )
-    far0, far1, far2, _ = lax.optimization_barrier((far0, far1, far2, framed))
-    diag0, diag1, diag2 = swap(far0, "wt", 1), swap(far1, "wt", 1), swap(far2, "wt", 1)
-    weights = (near, side, far0, far1, far2, diag0, diag1, diag2)
+    fars = lax.optimization_barrier((far0, far1, far2, far3, far4, framed))[:5]
+    weights = (near, side, *fars, *(swap(far, "wt", 1) for far in fars))
     res, low, block23 = call(
         far_conv_kernel,
         (
@@ -564,29 +580,32 @@
             shape((strip_rows, channels, width), BF16),
             shape((2, strip_rows, panel, width), BF16),
         ),
-        [SM] + [VM] * 9,
+        [SM] + [VM] * 13,
         (place, *weights[2:], framed, base, part0),
         [pltpu.VMEM((2 * panel, 2 * LANES), F32)],
         us=0.05,
     )
 
-    low_before = lax.ppermute(low[1:2], "rows", up)
-    low_after = lax.ppermute(low[0:1], "rows", down)
     block1 = swap(block1, "wt", 1)
     block23 = swap(after_all(block23, across[0]), "wt", 2)
-    stacked = after_all(jnp.stack([block0, block1, block23[0], swap(block23[1], "wt", 1)]), across[1])
+    stacked = jnp.stack([block0, block1, block23[0], swap(block23[1], "wt", 1)])
+    settled = after_all(low, stacked)
+    low_before = lax.ppermute(settled[1:2], "rows", up)
+    low_after = lax.ppermute(settled[0:1], "rows", down)
     plus = ring(stacked, "rows", 1)
     minus = ring(after_all(stacked, plus), "rows", 3)
     far = ring(plus, "rows", 1)
     full = call(
         assemble_kernel,
         shape((9, channels, channels), BF16),
-        [SM] + [VM] * 8,
+        [SM] + [VM] * 12,
         (after_all(place, stacked), *weights),
         us=5,
     )
 
-    across += [swap(after_all(beyond, stacked), "wt", 2), swap(after_all(below, block23), "wt", 2)]
+    for strip_in, last in ((above, block23), (below, None), (beyond, None)):
+        across.append(swap(after_all(strip_in, across[-1] if last is None else last), "wt", 2))
+    across[2:] = across[:1:-1]
     own_rows = rows_of((place, after_all(hidden, stacked), above, beyond, below))
     other_rows = swap(own_rows, "wt", 1)
 
@@ -594,7 +613,7 @@
         back_kernel,
         (shape((strip_rows, channels, width), F32), shape((8, channels), F32)),
         [VM] * 7,
-        (full, low_before, after_all(low, plus), low_after, res, lat, table),
+        (full, low_before, after_all(low, plus, across[1]), low_after, res, lat, table),
         [
             pltpu.VMEM((3, 4, LANES, channels), BF16),
             pltpu.VMEM((2 * LANES, channels), F32),
@@ -636,8 +655,12 @@
         shape((9, panel, channels), F32),
         [SM] + [VM] * 8,
         (place, plus, minus, far, *images, near_weight),
-        [pltpu.VMEM((2, 3 * panel, 8 * LANES), BF16)],
-        mib=16, us=0.05,
+        [
+            pltpu.VMEM((2, 3 * panel, 8 * LANES), BF16),
+            pltpu.VMEM((9, panel, channels), F32),
+            pltpu.SemaphoreType.DMA((3,)),
+        ],
+        mib=18, us=0.05, space=pl.BlockSpec(memory_space=pl.ANY),
     )
     return (
         loss[0, :1],

time: 119 us -> 122 us (1.025)
  waiting for transfers between devices: 38.1 us -> 44.1 us
    ppermute x25 -> x29, waiting for transfers between devices: 16.6 us -> 34.3 us  [swap(): return lax.ppermute(x, axis, [(i, i ^ mask) for i in range(size)])]
    ppermute x6, waiting for transfers between devices: 21.5 us -> 9.79 us  [ring(): return lax.ppermute(x, axis, [((i + step) % size, i) for i in range(size)])]
    ppermute x6, starting transfers between devices: 12.9 us -> 7 us  [ring(): return lax.ppermute(x, axis, [((i + step) % size, i) for i in range(size)])]
    ppermute x25 -> x29, starting transfers between devices: 22.8 us -> 26.5 us  [swap(): return lax.ppermute(x, axis, [(i, i ^ mask) for i in range(size)])]
    ppermute x2, starting transfers between devices: 3.31 us -> 4.94 us  [the longest x1 3.65 us: strips_of_four(): low_before = lax.ppermute(settled[1:2], 'rows', up)]
  transfers between devices with their start and end apart: 33 -> 37, of which waited for: 12 -> 17; matrix products, arithmetic and copies ran while one was open for 0% -> 1% of each run, Pallas kernels for 23% -> 22%
where the time goes in v6:
time: 122 us
  waiting for transfers between devices  44.1 us (36%)
  starting transfers between devices  38.4 us (31%)
  Pallas kernels  35.9 us (29%)
  local copies, waits for them, and re-layouts  2.27 us (2%)
    pallas_call x14, Pallas kernels, call(): pl.pallas_call(kernel, out_shape=outs, in_specs=specs, out_specs=jax.tree...  35.9 us
    ppermute x29, waiting for transfers between devices, swap(): return lax.ppermute(x, axis, [(i, i ^ mask) for i in range(size)])  34.3 us
    ppermute x29, starting transfers between devices, swap(): return lax.ppermute(x, axis, [(i, i ^ mask) for i in range(size)])  26.5 us
    ppermute x6, waiting for transfers between devices, ring(): return lax.ppermute(x, axis, [((i + step) % size, i) for i in range(size)])  9.79 us
    ppermute x6, starting transfers between devices, ring(): return lax.ppermute(x, axis, [((i + step) % size, i) for i in range(size)])  7 us
    ppermute x1, starting transfers between devices, strips_of_four(): low_before = lax.ppermute(settled[1:2], 'rows', up)  3.65 us
  transfers between devices with their start and end apart: 37, of which 17 were waited for; matrix products, arithmetic and copies ran while one was open for 1% of the time, Pallas kernels for 22%

profile of v6, /device:TPU:0, one launch (start us, length us, event | category | flops | bytes accessed | tf_op | source)
XLA Modules:
  0.0 121.9 jit_solution(12682517050945113069)
XLA Ops:
  2.2 2.6 %collective-permute-start.1 = (bf16[2,160,640]{2,1,0:T(8,128)(2,1)S(1)}, bf16[2,160,640]{2,1,0:T(8,128)(2,1)S(1)}, u32[]{:S(2)}, u32[]{:S(2)}) collective-permute-start(bf16[2,160,640]{2,1,0:T(8,128)(2,1)S(1)} %dynamic-slice_bitcast_fusion), channel_id=1, source_target_pairs={{0,2},{1,3},{2,0},{3,1},{4,6},{5,7},{6,4},{7,5},{8,10},{9,11},{10,... | collective-permute-start | bytes 1228808 | tf_op jit(solution)/shard_map/ppermute | solution.py:500
  7.8 2.6 %collective-permute-start.3 = (f32[8,640]{1,0:T(8,128)S(1)}, f32[8,640]{1,0:T(8,128)S(1)}, u32[]{:S(2)}, u32[]{:S(2)}) collective-permute-start(f32[8,640]{1,0:T(8,128)S(1)} %shard_map.93.s0), channel_id=1, source_target_pairs={{0,8},{4,12},{8,0},{12,4},{1,9},{5,13},{9,1},{13,5},{2,10},{6,14},... | collective-permute-start | bytes 61448 | tf_op jit(solution)/shard_map/ppermute | solution.py:500
  10.8 4.1 %collective-permute-done.1.far0 = bf16[2,160,640]{2,1,0:T(8,128)(2,1)S(1)} collective-permute-done((bf16[2,160,640]{2,1,0:T(8,128)(2,1)S(1)}, bf16[2,160,640]{2,1,0:T(8,128)(2,1)S(1)}, u32[]{:S(2)}, u32[]{:S(2)}) %collective-permute-start.1) | collective-permute-done | bytes 409632 | tf_op jit(solution)/shard_map/ppermute | solution.py:500
  17.1 2.8 %collective-permute-start.5 = (bf16[2,640,128]{2,1,0:T(8,128)(2,1)S(1)}, bf16[2,640,128]{2,1,0:T(8,128)(2,1)S(1)}, u32[]{:S(2)}, u32[]{:S(2)}) collective-permute-start(bf16[2,640,128]{2,1,0:T(8,128)(2,1)S(1)} %get-tuple-element.70.mine), channel_id=1, source_target_pairs={{4,0},{8,4},{12,8},{0,12},{5,1},{9,5},{13,9},{1,13},{6,2},{10,6},{... | collective-permute-start | bytes 983048 | tf_op jit(solution)/shard_map/ppermute | solution.py:505
  23.9 5.7 %collective-permute-done.9.far2 = bf16[1,160,640]{2,1,0:T(8,128)(2,1)S(1)} collective-permute-done((bf16[1,160,640]{2,1,0:T(8,128)(2,1)S(1)}, bf16[1,160,640]{2,1,0:T(8,128)(2,1)S(1)}, u32[]{:S(2)}, u32[]{:S(2)}) %collective-permute-start.9) | collective-permute-done | bytes 204832 | tf_op jit(solution)/shard_map/ppermute | solution.py:500
  30.2 4.6 %collective-permute-done.6.below = bf16[2,640,128]{2,1,0:T(8,128)(2,1)S(1)} collective-permute-done((bf16[2,640,128]{2,1,0:T(8,128)(2,1)S(1)}, bf16[2,640,128]{2,1,0:T(8,128)(2,1)S(1)}, u32[]{:S(2)}, u32[]{:S(2)}) %collective-permute-start.6) | collective-permute-done | bytes 327712 | tf_op jit(solution)/shard_map/ppermute | solution.py:505
  35.7 5.2 %collective-permute-done.11.far4 = bf16[3,160,640]{2,1,0:T(8,128)(2,1)S(1)} collective-permute-done((bf16[3,160,640]{2,1,0:T(8,128)(2,1)S(1)}, bf16[3,160,640]{2,1,0:T(8,128)(2,1)S(1)}, u32[]{:S(2)}, u32[]{:S(2)}) %collective-permute-start.11) | collective-permute-done | bytes 614432 | tf_op jit(solution)/shard_map/ppermute | solution.py:500
  43.5 4.3 %shard_map.97 = (f32[2,2,160,128]{3,2,1,0:T(8,128)S(1)}, bf16[2,160,128]{2,1,0:T(8,128)(2,1)S(1)}, bf16[2,160,128]{2,1,0:T(8,128)(2,1)S(1)}) custom-call(s32[3]{0:T(128)S(1)} %pad_add_fusion.place, bf16[9,160,640]{2,1,0:T(8,128)(2,1)S(1)} %bitcast.25, bf16[9,160,640]{2,1,0:T(8,128)(2,1)} %collective-permute-done.side, ...), custom_call_target="tpu_custom_call" | custom-call | flops 20000000000 | bytes 60000000 | tf_op jit(solution)/shard_map/pallas_call | solution.py:481
  47.8 3.2 %shard_map.98 = (f32[2,640,128]{2,1,0:T(8,128)S(1)}, bf16[2,640,128]{2,1,0:T(8,128)(2,1)S(1)}, bf16[2,2,160,128]{3,2,1,0:T(8,128)(2,1)S(1)}) custom-call(s32[3]{0:T(128)S(1)} %pad_add_fusion.place, bf16[2,160,640]{2,1,0:T(8,128)(2,1)S(1)} %collective-permute-done.1.far0, bf16[2,160,640]{2,1,0:T(8,128)(2,1)S(1)} %collective-permute-done.8.far1, ...), custom_call_target="tpu_custom_call" | custom-call | flops 50000000 | bytes 150000 | tf_op jit(solution)/shard_map/pallas_call | solution.py:481
  52.6 4.9 %collective-permute-done.18 = bf16[2,2,160,128]{3,2,1,0:T(8,128)(2,1)S(1)} collective-permute-done((bf16[2,2,160,128]{3,2,1,0:T(8,128)(2,1)S(1)}, bf16[2,2,160,128]{3,2,1,0:T(8,128)(2,1)S(1)}, u32[]{:S(2)}, u32[]{:S(2)}) %collective-permute-start.18) | collective-permute-done | bytes 163872 | tf_op jit(solution)/shard_map/ppermute | solution.py:500
  57.6 3.6 %collective-permute-start.32 = (bf16[2,640,128]{2,1,0:T(8,128)(2,1)S(1)}, bf16[2,640,128]{2,1,0:T(8,128)(2,1)S(1)}, u32[]{:S(2)}, u32[]{:S(2)}) collective-permute-start(bf16[2,640,128]{2,1,0:T(8,128)(2,1)S(1)} %collective-permute-done.5.above), channel_id=1, source_target_pairs={{4,0},{8,4},{12,8},{0,12},{5,1},{9,5},{13,9},{1,13},{6,2},{10,6},{... | collective-permute-start | bytes 983048 | tf_op jit(solution)/shard_map/ppermute | solution.py:505
  62.5 3.6 %collective-permute-start.20 = (bf16[1,640,128]{2,1,0:T(8,128)(2,1)S(1)}, bf16[1,640,128]{2,1,0:T(8,128)(2,1)S(1)}, u32[]{:S(2)}, u32[]{:S(2)}) collective-permute-start(bf16[1,640,128]{2,1,0:T(8,128)(2,1)S(1)} %get-tuple-element.77), channel_id=1, source_target_pairs={{0,4},{4,8},{8,12},{1,5},{5,9},{9,13},{2,6},{6,10},{10,14},{3,7},{... | collective-permute-start | bytes 491528 | tf_op jit(solution)/shard_map/ppermute | solution.py:593
  67.5 1.8 %collective-permute-done.32.beyond = bf16[2,640,128]{2,1,0:T(8,128)(2,1)S(1)} collective-permute-done((bf16[2,640,128]{2,1,0:T(8,128)(2,1)S(1)}, bf16[2,640,128]{2,1,0:T(8,128)(2,1)S(1)}, u32[]{:S(2)}, u32[]{:S(2)}) %collective-permute-start.32) | collective-permute-done | bytes 327712 | tf_op jit(solution)/shard_map/ppermute | solution.py:505
  71.8 2.1 %shard_map.99.full = bf16[9,640,640]{2,1,0:T(8,128)(2,1)S(1)} custom-call(s32[3]{0:T(128)S(1)} %pad_add_fusion.place, bf16[9,160,640]{2,1,0:T(8,128)(2,1)S(1)} %bitcast.26, bf16[9,160,640]{2,1,0:T(8,128)(2,1)} %collective-permute-done.side, bf16[2,160,640]{2,1,0:T(8,128)(2,1)S(1)} %collective-permute-done.1.far0, ...), custom_call_target="tpu_custom_call" | custom-call | flops 5000000000 | bytes 15000000 | tf_op jit(solution)/shard_map/pallas_call | solution.py:481
  74.0 2.3 %collective-permute-done.21.plus = bf16[4,2,160,128]{3,2,1,0:T(8,128)(2,1)S(1)} collective-permute-done((bf16[4,2,160,128]{3,2,1,0:T(8,128)(2,1)S(1)}, bf16[4,2,160,128]{3,2,1,0:T(8,128)(2,1)S(1)}, u32[]{:S(2)}, u32[]{:S(2)}) %collective-permute-start.21) | collective-permute-done | bytes 327712 | tf_op jit(solution)/shard_map/ppermute | solution.py:505
  76.3 3.8 %collective-permute-done.34.below = bf16[2,640,128]{2,1,0:T(8,128)(2,1)S(1)} collective-permute-done((bf16[2,640,128]{2,1,0:T(8,128)(2,1)S(1)}, bf16[2,640,128]{2,1,0:T(8,128)(2,1)S(1)}, u32[]{:S(2)}, u32[]{:S(2)}) %collective-permute-start.34) | collective-permute-done | bytes 327712 | tf_op jit(solution)/shard_map/ppermute | solution.py:500
  81.1 6.2 %shard_map.100 = (f32[2,640,128]{2,1,0:T(8,128)S(1)}, f32[8,640]{1,0:T(8,128)S(1)}) custom-call(bf16[9,640,640]{2,1,0:T(8,128)(2,1)S(1)} %shard_map.99.full, bf16[1,640,128]{2,1,0:T(8,128)(2,1)S(1)} %collective-permute-done.20.before, bf16[2,640,128]{2,1,0:T(8,128)(2,1)S(1)} %get-tuple-element.61.low, ...), custom_call_target="tpu_custom_call" | custom-call | flops 30000001024 | bytes 90000000 | tf_op jit(solution)/shard_map/pallas_call | solution.py:481
  89.2 1.9 %collective-permute-start.25 = (f32[8,640]{1,0:T(8,128)S(1)}, f32[8,640]{1,0:T(8,128)S(1)}, u32[]{:S(2)}, u32[]{:S(2)}) collective-permute-start(f32[8,640]{1,0:T(8,128)S(1)} %get-tuple-element.65.s0), channel_id=1, source_target_pairs={{0,4},{4,0},{8,12},{12,8},{1,5},{5,1},{9,13},{13,9},{2,6},{6,2},{1... | collective-permute-start | bytes 61448 | tf_op jit(solution)/shard_map/ppermute | solution.py:500
  91.1 4.1 %collective-permute-start.26 = (f32[8,640]{1,0:T(8,128)S(1)}, f32[8,640]{1,0:T(8,128)S(1)}, u32[]{:S(2)}, u32[]{:S(2)}) collective-permute-start(f32[8,640]{1,0:T(8,128)S(1)} %get-tuple-element.65.s0), channel_id=1, source_target_pairs={{0,8},{4,12},{8,0},{12,4},{1,9},{5,13},{9,1},{13,5},{2,10},{6,14},... | collective-permute-start | bytes 61448 | tf_op jit(solution)/shard_map/ppermute | solution.py:500
  95.2 1.8 %collective-permute-done.26.s2 = f32[8,640]{1,0:T(8,128)S(1)} collective-permute-done((f32[8,640]{1,0:T(8,128)S(1)}, f32[8,640]{1,0:T(8,128)S(1)}, u32[]{:S(2)}, u32[]{:S(2)}) %collective-permute-start.26) | collective-permute-done | bytes 20512 | tf_op jit(solution)/shard_map/ppermute | solution.py:500
  97.0 3.7 %collective-permute-done.27.s3 = f32[8,640]{1,0:T(8,128)S(1)} collective-permute-done((f32[8,640]{1,0:T(8,128)S(1)}, f32[8,640]{1,0:T(8,128)S(1)}, u32[]{:S(2)}, u32[]{:S(2)}) %collective-permute-start.27) | collective-permute-done | bytes 20512 | tf_op jit(solution)/shard_map/ppermute | solution.py:500
  100.8 1.8 %shard_map.101 = (f32[1280,128]{1,0:T(8,128)}, f32[8,640]{1,0:T(8,128)S(1)}) custom-call(f32[8,640]{1,0:T(8,128)S(1)} %get-tuple-element.65.s0, f32[8,640]{1,0:T(8,128)S(1)} %collective-permute-done.25.s1, f32[8,640]{1,0:T(8,128)S(1)} %collective-permute-done.26.s2, f32[8,640]{1,0:T(8,128)S(1)} %collective-permute-done.27.s3, ...), custom_call_target="tpu_custom_call" | custom-call | flops 50000000 | bytes 150000 | tf_op jit(solution)/shard_map/pallas_call | solution.py:481
  107.3 6.2 %shard_map.105.near = f32[9,160,640]{2,1,0:T(8,128)S(1)} custom-call(s32[3]{0:T(128)S(1)} %pad_add_fusion.place, bf16[4,2,160,128]{3,2,1,0:T(8,128)(2,1)S(1)} %pad_maximum_fusion.own, bf16[4,2,160,128]{3,2,1,0:T(8,128)(2,1)S(1)} %collective-permute-done.21.plus, bf16[4,2,160,128]{3,2,1,0:T(8,128)(2,1)S(1)} %collective-permute-done.24.minus, ...), custom_call_target="tpu_custom_call" | custom-call | flops 30000001024 | bytes 90000000 | tf_op jit(solution)/shard_map/pallas_call | solution.py:481
  114.3 7.4 %shard_map.106 = f32[9,160,640]{2,1,0:T(8,128)} custom-call(s32[3]{0:T(128)S(1)} %pad_add_fusion.place, bf16[4,2,160,128]{3,2,1,0:T(8,128)(2,1)S(1)} %collective-permute-done.21.plus, bf16[4,2,160,128]{3,2,1,0:T(8,128)(2,1)S(1)} %collective-permute-done.24.minus, bf16[4,2,160,128]{3,2,1,0:T(8,128)(2,1)S(1)} %collective-permute-done.31.far, ...), custom_call_target="tpu_custom_call" | custom-call | flops 50000000 | bytes 150000 | tf_op jit(solution)/shard_map/pallas_call | solution.py:481
  (89 shorter events, 30.2 us)
Async XLA Ops:
  0.6 14.3 %collective-permute-start = (bf16[9,160,640]{2,1,0:T(8,128)(2,1)}, bf16[9,160,640]{2,1,0:T(8,128)(2,1)}, u32[]{:S(2)}, u32[]{:S(2)}) collective-permute-start(bf16[9,160,640]{2,1,0:T(8,128)(2,1)} %bitcast.22), channel_id=1, source_target_pairs={{0,1},{1,0},{2,3},{3,2},{4,5},{5,4},{6,7},{7,6},{8,9},{9,8},{10,11... | collective-permute-start | bytes 5529608 | tf_op jit(solution)/shard_map/ppermute | solution.py:500
  2.2 12.7 %collective-permute-start.1 = (bf16[2,160,640]{2,1,0:T(8,128)(2,1)S(1)}, bf16[2,160,640]{2,1,0:T(8,128)(2,1)S(1)}, u32[]{:S(2)}, u32[]{:S(2)}) collective-permute-start(bf16[2,160,640]{2,1,0:T(8,128)(2,1)S(1)} %dynamic-slice_bitcast_fusion), channel_id=1, source_target_pairs={{0,2},{1,3},{2,0},{3,1},{4,6},{5,7},{6,4},{7,5},{8,10},{9,11},{10,... | collective-permute-start | bytes 1228808 | tf_op jit(solution)/shard_map/ppermute | solution.py:500
  6.2 8.7 %collective-permute-start.2 = (f32[8,640]{1,0:T(8,128)S(1)}, f32[8,640]{1,0:T(8,128)S(1)}, u32[]{:S(2)}, u32[]{:S(2)}) collective-permute-start(f32[8,640]{1,0:T(8,128)S(1)} %shard_map.93.s0), channel_id=1, source_target_pairs={{0,4},{4,0},{8,12},{12,8},{1,5},{5,1},{9,13},{13,9},{2,6},{6,2},{1... | collective-permute-start | bytes 61448 | tf_op jit(solution)/shard_map/ppermute | solution.py:500
  7.8 7.1 %collective-permute-start.3 = (f32[8,640]{1,0:T(8,128)S(1)}, f32[8,640]{1,0:T(8,128)S(1)}, u32[]{:S(2)}, u32[]{:S(2)}) collective-permute-start(f32[8,640]{1,0:T(8,128)S(1)} %shard_map.93.s0), channel_id=1, source_target_pairs={{0,8},{4,12},{8,0},{12,4},{1,9},{5,13},{9,1},{13,5},{2,10},{6,14},... | collective-permute-start | bytes 61448 | tf_op jit(solution)/shard_map/ppermute | solution.py:500
  17.1 13.1 %collective-permute-start.5 = (bf16[2,640,128]{2,1,0:T(8,128)(2,1)S(1)}, bf16[2,640,128]{2,1,0:T(8,128)(2,1)S(1)}, u32[]{:S(2)}, u32[]{:S(2)}) collective-permute-start(bf16[2,640,128]{2,1,0:T(8,128)(2,1)S(1)} %get-tuple-element.70.mine), channel_id=1, source_target_pairs={{4,0},{8,4},{12,8},{0,12},{5,1},{9,5},{13,9},{1,13},{6,2},{10,6},{... | collective-permute-start | bytes 983048 | tf_op jit(solution)/shard_map/ppermute | solution.py:505
  20.0 14.8 %collective-permute-start.6 = (bf16[2,640,128]{2,1,0:T(8,128)(2,1)S(1)}, bf16[2,640,128]{2,1,0:T(8,128)(2,1)S(1)}, u32[]{:S(2)}, u32[]{:S(2)}) collective-permute-start(bf16[2,640,128]{2,1,0:T(8,128)(2,1)S(1)} %get-tuple-element.70.mine), channel_id=1, source_target_pairs={{12,0},{0,4},{4,8},{8,12},{13,1},{1,5},{5,9},{9,13},{14,2},{2,6},{... | collective-permute-start | bytes 983048 | tf_op jit(solution)/shard_map/ppermute | solution.py:505
  20.0 15.7 %collective-permute-start.8 = (bf16[2,160,640]{2,1,0:T(8,128)(2,1)S(1)}, bf16[2,160,640]{2,1,0:T(8,128)(2,1)S(1)}, u32[]{:S(2)}, u32[]{:S(2)}) collective-permute-start(bf16[2,160,640]{2,1,0:T(8,128)(2,1)S(1)} %collective-permute-done.1.far0), channel_id=1, source_target_pairs={{0,16},{16,0},{1,17},{17,1},{2,18},{18,2},{3,19},{19,3},{4,20},{20... | collective-permute-start | bytes 1228808 | tf_op jit(solution)/shard_map/ppermute | solution.py:500
  21.6 8.1 %collective-permute-start.9 = (bf16[1,160,640]{2,1,0:T(8,128)(2,1)S(1)}, bf16[1,160,640]{2,1,0:T(8,128)(2,1)S(1)}, u32[]{:S(2)}, u32[]{:S(2)}) collective-permute-start(bf16[1,160,640]{2,1,0:T(8,128)(2,1)S(1)} %constant_dynamic-slice_fusion), channel_id=1, source_target_pairs={{0,2},{1,3},{2,0},{3,1},{4,6},{5,7},{6,4},{7,5},{8,10},{9,11},{10,... | collective-permute-start | bytes 614408 | tf_op jit(solution)/shard_map/ppermute | solution.py:500
  23.1 17.8 %collective-permute-start.11 = (bf16[3,160,640]{2,1,0:T(8,128)(2,1)S(1)}, bf16[3,160,640]{2,1,0:T(8,128)(2,1)S(1)}, u32[]{:S(2)}, u32[]{:S(2)}) collective-permute-start(bf16[3,160,640]{2,1,0:T(8,128)(2,1)S(1)} %slice.18), channel_id=1, source_target_pairs={{0,2},{1,3},{2,0},{3,1},{4,6},{5,7},{6,4},{7,5},{8,10},{9,11},{10,... | collective-permute-start | bytes 1843208 | tf_op jit(solution)/shard_map/ppermute | solution.py:500
  29.7 6.1 %collective-permute-start.10 = (bf16[1,160,640]{2,1,0:T(8,128)(2,1)S(1)}, bf16[1,160,640]{2,1,0:T(8,128)(2,1)S(1)}, u32[]{:S(2)}, u32[]{:S(2)}) collective-permute-start(bf16[1,160,640]{2,1,0:T(8,128)(2,1)S(1)} %collective-permute-done.9.far2), channel_id=1, source_target_pairs={{0,16},{16,0},{1,17},{17,1},{2,18},{18,2},{3,19},{19,3},{4,20},{20... | collective-permute-start | bytes 614408 | tf_op jit(solution)/shard_map/ppermute | solution.py:500
  40.9 10.1 %collective-permute-start.17 = (bf16[2,640,128]{2,1,0:T(8,128)(2,1)S(1)}, bf16[2,640,128]{2,1,0:T(8,128)(2,1)S(1)}, u32[]{:S(2)}, u32[]{:S(2)}) collective-permute-start(bf16[2,640,128]{2,1,0:T(8,128)(2,1)S(1)} %get-tuple-element.70.mine), channel_id=1, source_target_pairs={{0,2},{1,3},{2,0},{3,1},{4,6},{5,7},{6,4},{7,5},{8,10},{9,11},{10,... | collective-permute-start | bytes 983048 | tf_op jit(solution)/shard_map/ppermute | solution.py:500
  51.1 6.4 %collective-permute-start.18 = (bf16[2,2,160,128]{3,2,1,0:T(8,128)(2,1)S(1)}, bf16[2,2,160,128]{3,2,1,0:T(8,128)(2,1)S(1)}, u32[]{:S(2)}, u32[]{:S(2)}) collective-permute-start(bf16[2,2,160,128]{3,2,1,0:T(8,128)(2,1)S(1)} %get-tuple-element.56), channel_id=1, source_target_pairs={{0,2},{1,3},{2,0},{3,1},{4,6},{5,7},{6,4},{7,5},{8,10},{9,11},{10,... | collective-permute-start | bytes 491528 | tf_op jit(solution)/shard_map/ppermute | solution.py:500
  52.6 9.5 %collective-permute-start.7 = (bf16[2,160,128]{2,1,0:T(8,128)(2,1)S(1)}, bf16[2,160,128]{2,1,0:T(8,128)(2,1)S(1)}, u32[]{:S(2)}, u32[]{:S(2)}) collective-permute-start(bf16[2,160,128]{2,1,0:T(8,128)(2,1)S(1)} %get-tuple-element.45), channel_id=1, source_target_pairs={{0,1},{1,0},{2,3},{3,2},{4,5},{5,4},{6,7},{7,6},{8,9},{9,8},{10,11... | collective-permute-start | bytes 245768 | tf_op jit(solution)/shard_map/ppermute | solution.py:500
  57.6 11.7 %collective-permute-start.32 = (bf16[2,640,128]{2,1,0:T(8,128)(2,1)S(1)}, bf16[2,640,128]{2,1,0:T(8,128)(2,1)S(1)}, u32[]{:S(2)}, u32[]{:S(2)}) collective-permute-start(bf16[2,640,128]{2,1,0:T(8,128)(2,1)S(1)} %collective-permute-done.5.above), channel_id=1, source_target_pairs={{4,0},{8,4},{12,8},{0,12},{5,1},{9,5},{13,9},{1,13},{6,2},{10,6},{... | collective-permute-start | bytes 983048 | tf_op jit(solution)/shard_map/ppermute | solution.py:505
  61.2 9.8 %collective-permute-start.22 = (bf16[2,640,128]{2,1,0:T(8,128)(2,1)S(1)}, bf16[2,640,128]{2,1,0:T(8,128)(2,1)S(1)}, u32[]{:S(2)}, u32[]{:S(2)}) collective-permute-start(bf16[2,640,128]{2,1,0:T(8,128)(2,1)S(1)} %collective-permute-done.5.above), channel_id=1, source_target_pairs={{0,2},{1,3},{2,0},{3,1},{4,6},{5,7},{6,4},{7,5},{8,10},{9,11},{10,... | collective-permute-start | bytes 983048 | tf_op jit(solution)/shard_map/ppermute | solution.py:500
  62.1 14.2 %collective-permute-start.21 = (bf16[4,2,160,128]{3,2,1,0:T(8,128)(2,1)S(1)}, bf16[4,2,160,128]{3,2,1,0:T(8,128)(2,1)S(1)}, u32[]{:S(2)}, u32[]{:S(2)}) collective-permute-start(bf16[4,2,160,128]{3,2,1,0:T(8,128)(2,1)S(1)} %pad_maximum_fusion.own), channel_id=1, source_target_pairs={{4,0},{8,4},{12,8},{0,12},{5,1},{9,5},{13,9},{1,13},{6,2},{10,6},{... | collective-permute-start | bytes 983048 | tf_op jit(solution)/shard_map/ppermute | solution.py:505
  62.5 18.6 %collective-permute-start.20 = (bf16[1,640,128]{2,1,0:T(8,128)(2,1)S(1)}, bf16[1,640,128]{2,1,0:T(8,128)(2,1)S(1)}, u32[]{:S(2)}, u32[]{:S(2)}) collective-permute-start(bf16[1,640,128]{2,1,0:T(8,128)(2,1)S(1)} %get-tuple-element.77), channel_id=1, source_target_pairs={{0,4},{4,8},{8,12},{1,5},{5,9},{9,13},{2,6},{6,10},{10,14},{3,7},{... | collective-permute-start | bytes 491528 | tf_op jit(solution)/shard_map/ppermute | solution.py:593
  66.2 14.9 %collective-permute-start.23 = (bf16[1,640,128]{2,1,0:T(8,128)(2,1)S(1)}, bf16[1,640,128]{2,1,0:T(8,128)(2,1)S(1)}, u32[]{:S(2)}, u32[]{:S(2)}) collective-permute-start(bf16[1,640,128]{2,1,0:T(8,128)(2,1)S(1)} %get-tuple-element.76), channel_id=1, source_target_pairs={{4,0},{8,4},{12,8},{5,1},{9,5},{13,9},{6,2},{10,6},{14,10},{7,3},{... | collective-permute-start | bytes 491528 | tf_op jit(solution)/shard_map/ppermute | solution.py:594
  69.9 37.4 %collective-permute-start.33 = (bf16[10,640,128]{2,1,0:T(8,128)(2,1)S(1)}, bf16[10,640,128]{2,1,0:T(8,128)(2,1)S(1)}, u32[]{:S(2)}, u32[]{:S(2)}) collective-permute-start(bf16[10,640,128]{2,1,0:T(8,128)(2,1)S(1)} %shard_map.103.h0), channel_id=1, source_target_pairs={{0,1},{1,0},{2,3},{3,2},{4,5},{5,4},{6,7},{7,6},{8,9},{9,8},{10,11... | collective-permute-start | bytes 4915208 | tf_op jit(solution)/shard_map/ppermute | solution.py:500
  70.9 9.2 %collective-permute-start.34 = (bf16[2,640,128]{2,1,0:T(8,128)(2,1)S(1)}, bf16[2,640,128]{2,1,0:T(8,128)(2,1)S(1)}, u32[]{:S(2)}, u32[]{:S(2)}) collective-permute-start(bf16[2,640,128]{2,1,0:T(8,128)(2,1)S(1)} %collective-permute-done.6.below), channel_id=1, source_target_pairs={{0,2},{1,3},{2,0},{3,1},{4,6},{5,7},{6,4},{7,5},{8,10},{9,11},{10,... | collective-permute-start | bytes 983048 | tf_op jit(solution)/shard_map/ppermute | solution.py:500
  76.3 11.4 %collective-permute-start.24 = (bf16[4,2,160,128]{3,2,1,0:T(8,128)(2,1)S(1)}, bf16[4,2,160,128]{3,2,1,0:T(8,128)(2,1)S(1)}, u32[]{:S(2)}, u32[]{:S(2)}) collective-permute-start(bf16[4,2,160,128]{3,2,1,0:T(8,128)(2,1)S(1)} %pad_maximum_fusion.own), channel_id=1, source_target_pairs={{12,0},{0,4},{4,8},{8,12},{13,1},{1,5},{5,9},{9,13},{14,2},{2,6},{... | collective-permute-start | bytes 983048 | tf_op jit(solution)/shard_map/ppermute | solution.py:505
  80.1 8.3 %collective-permute-start.35 = (bf16[2,640,128]{2,1,0:T(8,128)(2,1)S(1)}, bf16[2,640,128]{2,1,0:T(8,128)(2,1)S(1)}, u32[]{:S(2)}, u32[]{:S(2)}) collective-permute-start(bf16[2,640,128]{2,1,0:T(8,128)(2,1)S(1)} %collective-permute-done.32.beyond), channel_id=1, source_target_pairs={{0,2},{1,3},{2,0},{3,1},{4,6},{5,7},{6,4},{7,5},{8,10},{9,11},{10,... | collective-permute-start | bytes 983048 | tf_op jit(solution)/shard_map/ppermute | solution.py:500
  89.1 18.2 %collective-permute-start.36 = (bf16[10,640,128]{2,1,0:T(8,128)(2,1)S(1)}, bf16[10,640,128]{2,1,0:T(8,128)(2,1)S(1)}, u32[]{:S(2)}, u32[]{:S(2)}) collective-permute-start(bf16[10,640,128]{2,1,0:T(8,128)(2,1)S(1)} %shard_map.104.h2), channel_id=1, source_target_pairs={{0,1},{1,0},{2,3},{3,2},{4,5},{5,4},{6,7},{7,6},{8,9},{9,8},{10,11... | collective-permute-start | bytes 4915208 | tf_op jit(solution)/shard_map/ppermute | solution.py:500
  104.4 9.9 %collective-permute-start.31 = (bf16[4,2,160,128]{3,2,1,0:T(8,128)(2,1)S(1)}, bf16[4,2,160,128]{3,2,1,0:T(8,128)(2,1)S(1)}, u32[]{:S(2)}, u32[]{:S(2)}) collective-permute-start(bf16[4,2,160,128]{3,2,1,0:T(8,128)(2,1)S(1)} %collective-permute-done.21.plus), channel_id=1, source_target_pairs={{4,0},{8,4},{12,8},{0,12},{5,1},{9,5},{13,9},{1,13},{6,2},{10,6},{... | collective-permute-start | bytes 983048 | tf_op jit(solution)/shard_map/ppermute | solution.py:505
  (20 other events, 112.9 us)

commit v7 on v6

--- a/solution.py
+++ b/solution.py
@@ -587,7 +587,7 @@
     )
 
     block1 = swap(block1, "wt", 1)
-    block23 = swap(after_all(block23, across[0]), "wt", 2)
+    block23 = swap(after_all(block23, across[0], beyond), "wt", 2)
     stacked = jnp.stack([block0, block1, block23[0], swap(block23[1], "wt", 1)])
     settled = after_all(low, stacked)
     low_before = lax.ppermute(settled[1:2], "rows", up)
@@ -613,7 +613,7 @@
         back_kernel,
         (shape((strip_rows, channels, width), F32), shape((8, channels), F32)),
         [VM] * 7,
-        (full, low_before, after_all(low, plus, across[1]), low_after, res, lat, table),
+        (full, low_before, after_all(low, plus, across[1], other_rows), low_after, res, lat, table),
         [
             pltpu.VMEM((3, 4, LANES, channels), BF16),
             pltpu.VMEM((2 * LANES, channels), F32),
@@ -622,7 +622,6 @@
     )
     sums = after_all(sums, minus)
     across_rows = rows_of((after_all(place, sums), *across))
-    diag_rows = swap(across_rows, "wt", 1)
     grad_latents, sums = call(
         functools.partial(latents_kernel, group_cells),
         (shape((channels * strip_rows, width), F32), shape((8, channels), F32)),
@@ -633,6 +632,7 @@
         ),
         us=0.05,
     )
+    diag_rows = swap(after_all(across_rows, grad_latents), "wt", 1)
     images = (own_rows, other_rows, across_rows, diag_rows)
     near_weight = call(
         near_weight_kernel,
@@ -646,7 +646,7 @@
         functools.partial(totals_kernel, total_cells),
         (shape((1, LANES), F32), shape((3, channels), F32)),
         [VM] * 4,
-        (sums, *(swap(sums, "wt", m) for m in (1, 2, 3))),
+        (after_all(sums, near_weight), *(swap(sums, "wt", m) for m in (1, 2, 3))),
         us=0.05,
     )
 
@@ -654,7 +654,7 @@
         functools.partial(far_weight_kernel, total_cells),
         shape((9, panel, channels), F32),
         [SM] + [VM] * 8,
-        (place, plus, minus, far, *images, near_weight),
+        (place, plus, minus, far, *images, after_all(near_weight, param_grads)),
         [
             pltpu.VMEM((2, 3 * panel, 8 * LANES), BF16),
             pltpu.VMEM((9, panel, channels), F32),

time: 122 us -> 118 us (0.967)
  waiting for transfers between devices: 44.1 us -> 41.1 us
  starting transfers between devices: 38.4 us -> 37.1 us
    ppermute x6, waiting for transfers between devices: 9.79 us -> 4.57 us  [ring(): return lax.ppermute(x, axis, [((i + step) % size, i) for i in range(size)])]
    ppermute x29, starting transfers between devices: 26.5 us -> 23.2 us  [swap(): return lax.ppermute(x, axis, [(i, i ^ mask) for i in range(size)])]
    ppermute x6, starting transfers between devices: 7 us -> 10.3 us  [ring(): return lax.ppermute(x, axis, [((i + step) % size, i) for i in range(size)])]
    ppermute x29, waiting for transfers between devices: 34.3 us -> 36.6 us  [swap(): return lax.ppermute(x, axis, [(i, i ^ mask) for i in range(size)])]
    ppermute x1, starting transfers between devices: 3.65 us -> 2.3 us  [strips_of_four(): low_before = lax.ppermute(settled[1:2], 'rows', up)]
  transfers between devices with their start and end apart: 37 -> 37, of which waited for: 17 -> 10; matrix products, arithmetic and copies ran while one was open for 1% -> 1% of each run, Pallas kernels for 22% -> 21%
where the time goes in v7:
time: 118 us
  waiting for transfers between devices  41.1 us (35%)
  starting transfers between devices  37.1 us (31%)
  Pallas kernels  35.9 us (30%)
  local copies, waits for them, and re-layouts  2.27 us (2%)
    ppermute x29, waiting for transfers between devices, swap(): return lax.ppermute(x, axis, [(i, i ^ mask) for i in range(size)])  36.6 us
    pallas_call x14, Pallas kernels, call(): pl.pallas_call(kernel, out_shape=outs, in_specs=specs, out_specs=jax.tree...  35.9 us
    ppermute x29, starting transfers between devices, swap(): return lax.ppermute(x, axis, [(i, i ^ mask) for i in range(size)])  23.2 us
    ppermute x6, starting transfers between devices, ring(): return lax.ppermute(x, axis, [((i + step) % size, i) for i in range(size)])  10.3 us
    ppermute x6, waiting for transfers between devices, ring(): return lax.ppermute(x, axis, [((i + step) % size, i) for i in range(size)])  4.57 us
  transfers between devices with their start and end apart: 37, of which 10 were waited for; matrix products, arithmetic and copies ran while one was open for 1% of the time, Pallas kernels for 21%

profile of v7, /device:TPU:0, one launch (start us, length us, event | category | flops | bytes accessed | tf_op | source)
XLA Modules:
  0.0 117.6 jit_solution(13323421445761141660)
XLA Ops:
  2.2 2.6 %collective-permute-start.1 = (bf16[2,160,640]{2,1,0:T(8,128)(2,1)S(1)}, bf16[2,160,640]{2,1,0:T(8,128)(2,1)S(1)}, u32[]{:S(2)}, u32[]{:S(2)}) collective-permute-start(bf16[2,160,640]{2,1,0:T(8,128)(2,1)S(1)} %dynamic-slice_bitcast_fusion), channel_id=1, source_target_pairs={{0,2},{1,3},{2,0},{3,1},{4,6},{5,7},{6,4},{7,5},{8,10},{9,11},{10,... | collective-permute-start | bytes 1228808 | tf_op jit(solution)/shard_map/ppermute | solution.py:500
  7.8 2.6 %collective-permute-start.3 = (f32[8,640]{1,0:T(8,128)S(1)}, f32[8,640]{1,0:T(8,128)S(1)}, u32[]{:S(2)}, u32[]{:S(2)}) collective-permute-start(f32[8,640]{1,0:T(8,128)S(1)} %shard_map.93.s0), channel_id=1, source_target_pairs={{0,8},{4,12},{8,0},{12,4},{1,9},{5,13},{9,1},{13,5},{2,10},{6,14},... | collective-permute-start | bytes 61448 | tf_op jit(solution)/shard_map/ppermute | solution.py:500
  10.8 4.1 %collective-permute-done.1.far0 = bf16[2,160,640]{2,1,0:T(8,128)(2,1)S(1)} collective-permute-done((bf16[2,160,640]{2,1,0:T(8,128)(2,1)S(1)}, bf16[2,160,640]{2,1,0:T(8,128)(2,1)S(1)}, u32[]{:S(2)}, u32[]{:S(2)}) %collective-permute-start.1) | collective-permute-done | bytes 409632 | tf_op jit(solution)/shard_map/ppermute | solution.py:500
  17.1 2.8 %collective-permute-start.5 = (bf16[2,640,128]{2,1,0:T(8,128)(2,1)S(1)}, bf16[2,640,128]{2,1,0:T(8,128)(2,1)S(1)}, u32[]{:S(2)}, u32[]{:S(2)}) collective-permute-start(bf16[2,640,128]{2,1,0:T(8,128)(2,1)S(1)} %get-tuple-element.64.mine), channel_id=1, source_target_pairs={{4,0},{8,4},{12,8},{0,12},{5,1},{9,5},{13,9},{1,13},{6,2},{10,6},{... | collective-permute-start | bytes 983048 | tf_op jit(solution)/shard_map/ppermute | solution.py:505
  23.9 5.7 %collective-permute-done.9.far2 = bf16[1,160,640]{2,1,0:T(8,128)(2,1)S(1)} collective-permute-done((bf16[1,160,640]{2,1,0:T(8,128)(2,1)S(1)}, bf16[1,160,640]{2,1,0:T(8,128)(2,1)S(1)}, u32[]{:S(2)}, u32[]{:S(2)}) %collective-permute-start.9) | collective-permute-done | bytes 204832 | tf_op jit(solution)/shard_map/ppermute | solution.py:500
  30.2 4.6 %collective-permute-done.6.below = bf16[2,640,128]{2,1,0:T(8,128)(2,1)S(1)} collective-permute-done((bf16[2,640,128]{2,1,0:T(8,128)(2,1)S(1)}, bf16[2,640,128]{2,1,0:T(8,128)(2,1)S(1)}, u32[]{:S(2)}, u32[]{:S(2)}) %collective-permute-start.6) | collective-permute-done | bytes 327712 | tf_op jit(solution)/shard_map/ppermute | solution.py:505
  35.7 5.2 %collective-permute-done.11.far4 = bf16[3,160,640]{2,1,0:T(8,128)(2,1)S(1)} collective-permute-done((bf16[3,160,640]{2,1,0:T(8,128)(2,1)S(1)}, bf16[3,160,640]{2,1,0:T(8,128)(2,1)S(1)}, u32[]{:S(2)}, u32[]{:S(2)}) %collective-permute-start.11) | collective-permute-done | bytes 614432 | tf_op jit(solution)/shard_map/ppermute | solution.py:500
  42.9 3.5 %collective-permute-start.18 = (bf16[2,640,128]{2,1,0:T(8,128)(2,1)S(1)}, bf16[2,640,128]{2,1,0:T(8,128)(2,1)S(1)}, u32[]{:S(2)}, u32[]{:S(2)}) collective-permute-start(bf16[2,640,128]{2,1,0:T(8,128)(2,1)S(1)} %collective-permute-done.5.above), channel_id=1, source_target_pairs={{4,0},{8,4},{12,8},{0,12},{5,1},{9,5},{13,9},{1,13},{6,2},{10,6},{... | collective-permute-start | bytes 983048 | tf_op jit(solution)/shard_map/ppermute | solution.py:505
  47.1 4.3 %shard_map.97 = (f32[2,2,160,128]{3,2,1,0:T(8,128)S(1)}, bf16[2,160,128]{2,1,0:T(8,128)(2,1)S(1)}, bf16[2,160,128]{2,1,0:T(8,128)(2,1)S(1)}) custom-call(s32[3]{0:T(128)S(1)} %pad_add_fusion.place, bf16[9,160,640]{2,1,0:T(8,128)(2,1)S(1)} %bitcast.25, bf16[9,160,640]{2,1,0:T(8,128)(2,1)} %collective-permute-done.side, ...), custom_call_target="tpu_custom_call" | custom-call | flops 20000000000 | bytes 60000000 | tf_op jit(solution)/shard_map/pallas_call | solution.py:481
  51.4 3.2 %shard_map.98 = (f32[2,640,128]{2,1,0:T(8,128)S(1)}, bf16[2,640,128]{2,1,0:T(8,128)(2,1)S(1)}, bf16[2,2,160,128]{3,2,1,0:T(8,128)(2,1)S(1)}) custom-call(s32[3]{0:T(128)S(1)} %pad_add_fusion.place, bf16[2,160,640]{2,1,0:T(8,128)(2,1)S(1)} %collective-permute-done.1.far0, bf16[2,160,640]{2,1,0:T(8,128)(2,1)S(1)} %collective-permute-done.8.far1, ...), custom_call_target="tpu_custom_call" | custom-call | flops 50000000 | bytes 150000 | tf_op jit(solution)/shard_map/pallas_call | solution.py:481
  55.4 5.8 %collective-permute-done.19 = bf16[2,2,160,128]{3,2,1,0:T(8,128)(2,1)S(1)} collective-permute-done((bf16[2,2,160,128]{3,2,1,0:T(8,128)(2,1)S(1)}, bf16[2,2,160,128]{3,2,1,0:T(8,128)(2,1)S(1)}, u32[]{:S(2)}, u32[]{:S(2)}) %collective-permute-start.19) | collective-permute-done | bytes 163872 | tf_op jit(solution)/shard_map/ppermute | solution.py:500
  64.1 1.6 %collective-permute-start.22 = (bf16[4,2,160,128]{3,2,1,0:T(8,128)(2,1)S(1)}, bf16[4,2,160,128]{3,2,1,0:T(8,128)(2,1)S(1)}, u32[]{:S(2)}, u32[]{:S(2)}) collective-permute-start(bf16[4,2,160,128]{3,2,1,0:T(8,128)(2,1)S(1)} %pad_maximum_fusion.own), channel_id=1, source_target_pairs={{4,0},{8,4},{12,8},{0,12},{5,1},{9,5},{13,9},{1,13},{6,2},{10,6},{... | collective-permute-start | bytes 983048 | tf_op jit(solution)/shard_map/ppermute | solution.py:505
  65.8 2.3 %collective-permute-start.21 = (bf16[1,640,128]{2,1,0:T(8,128)(2,1)S(1)}, bf16[1,640,128]{2,1,0:T(8,128)(2,1)S(1)}, u32[]{:S(2)}, u32[]{:S(2)}) collective-permute-start(bf16[1,640,128]{2,1,0:T(8,128)(2,1)S(1)} %get-tuple-element.83), channel_id=1, source_target_pairs={{0,4},{4,8},{8,12},{1,5},{5,9},{9,13},{2,6},{6,10},{10,14},{3,7},{... | collective-permute-start | bytes 491528 | tf_op jit(solution)/shard_map/ppermute | solution.py:593
  69.4 4.2 %collective-permute-done.23.above = bf16[2,640,128]{2,1,0:T(8,128)(2,1)S(1)} collective-permute-done((bf16[2,640,128]{2,1,0:T(8,128)(2,1)S(1)}, bf16[2,640,128]{2,1,0:T(8,128)(2,1)S(1)}, u32[]{:S(2)}, u32[]{:S(2)}) %collective-permute-start.23) | collective-permute-done | bytes 327712 | tf_op jit(solution)/shard_map/ppermute | solution.py:500
  74.1 2.1 %shard_map.99.full = bf16[9,640,640]{2,1,0:T(8,128)(2,1)S(1)} custom-call(s32[3]{0:T(128)S(1)} %pad_add_fusion.place, bf16[9,160,640]{2,1,0:T(8,128)(2,1)S(1)} %bitcast.26, bf16[9,160,640]{2,1,0:T(8,128)(2,1)} %collective-permute-done.side, bf16[2,160,640]{2,1,0:T(8,128)(2,1)S(1)} %collective-permute-done.1.far0, ...), custom_call_target="tpu_custom_call" | custom-call | flops 5000000000 | bytes 15000000 | tf_op jit(solution)/shard_map/pallas_call | solution.py:481
  76.3 6.4 %collective-permute-done.30.below = bf16[2,640,128]{2,1,0:T(8,128)(2,1)S(1)} collective-permute-done((bf16[2,640,128]{2,1,0:T(8,128)(2,1)S(1)}, bf16[2,640,128]{2,1,0:T(8,128)(2,1)S(1)}, u32[]{:S(2)}, u32[]{:S(2)}) %collective-permute-start.30) | collective-permute-done | bytes 327712 | tf_op jit(solution)/shard_map/ppermute | solution.py:500
  83.3 6.2 %shard_map.101 = (f32[2,640,128]{2,1,0:T(8,128)S(1)}, f32[8,640]{1,0:T(8,128)S(1)}) custom-call(bf16[9,640,640]{2,1,0:T(8,128)(2,1)S(1)} %shard_map.99.full, bf16[1,640,128]{2,1,0:T(8,128)(2,1)S(1)} %collective-permute-done.21.before, bf16[2,640,128]{2,1,0:T(8,128)(2,1)S(1)} %get-tuple-element.65.low, ...), custom_call_target="tpu_custom_call" | custom-call | flops 30000001024 | bytes 90000000 | tf_op jit(solution)/shard_map/pallas_call | solution.py:481
  89.6 2.2 %collective-permute-start.28 = (f32[8,640]{1,0:T(8,128)S(1)}, f32[8,640]{1,0:T(8,128)S(1)}, u32[]{:S(2)}, u32[]{:S(2)}) collective-permute-start(f32[8,640]{1,0:T(8,128)S(1)} %get-tuple-element.69.s0), channel_id=1, source_target_pairs={{0,8},{4,12},{8,0},{12,4},{1,9},{5,13},{9,1},{13,5},{2,10},{6,14},... | collective-permute-start | bytes 61448 | tf_op jit(solution)/shard_map/ppermute | solution.py:500
  91.8 2.2 %collective-permute-start.29 = (f32[8,640]{1,0:T(8,128)S(1)}, f32[8,640]{1,0:T(8,128)S(1)}, u32[]{:S(2)}, u32[]{:S(2)}) collective-permute-start(f32[8,640]{1,0:T(8,128)S(1)} %get-tuple-element.69.s0), channel_id=1, source_target_pairs={{0,12},{4,8},{8,4},{12,0},{1,13},{5,9},{9,5},{13,1},{2,14},{6,10},... | collective-permute-start | bytes 61448 | tf_op jit(solution)/shard_map/ppermute | solution.py:500
  94.6 2.7 %collective-permute-done.29.s3 = f32[8,640]{1,0:T(8,128)S(1)} collective-permute-done((f32[8,640]{1,0:T(8,128)S(1)}, f32[8,640]{1,0:T(8,128)S(1)}, u32[]{:S(2)}, u32[]{:S(2)}) %collective-permute-start.29) | collective-permute-done | bytes 20512 | tf_op jit(solution)/shard_map/ppermute | solution.py:500
  97.3 1.8 %shard_map.102 = (f32[1280,128]{1,0:T(8,128)}, f32[8,640]{1,0:T(8,128)S(1)}) custom-call(f32[8,640]{1,0:T(8,128)S(1)} %get-tuple-element.69.s0, f32[8,640]{1,0:T(8,128)S(1)} %collective-permute-done.27.s1, f32[8,640]{1,0:T(8,128)S(1)} %collective-permute-done.28.s2, f32[8,640]{1,0:T(8,128)S(1)} %collective-permute-done.29.s3, ...), custom_call_target="tpu_custom_call" | custom-call | flops 50000000 | bytes 150000 | tf_op jit(solution)/shard_map/pallas_call | solution.py:481
  99.1 2.2 %collective-permute-start.36 = (bf16[4,2,160,128]{3,2,1,0:T(8,128)(2,1)S(1)}, bf16[4,2,160,128]{3,2,1,0:T(8,128)(2,1)S(1)}, u32[]{:S(2)}, u32[]{:S(2)}) collective-permute-start(bf16[4,2,160,128]{3,2,1,0:T(8,128)(2,1)S(1)} %collective-permute-done.22.plus), channel_id=1, source_target_pairs={{4,0},{8,4},{12,8},{0,12},{5,1},{9,5},{13,9},{1,13},{6,2},{10,6},{... | collective-permute-start | bytes 983048 | tf_op jit(solution)/shard_map/ppermute | solution.py:505
  103.2 6.2 %shard_map.104.near = f32[9,160,640]{2,1,0:T(8,128)S(1)} custom-call(s32[3]{0:T(128)S(1)} %pad_add_fusion.place, bf16[4,2,160,128]{3,2,1,0:T(8,128)(2,1)S(1)} %pad_maximum_fusion.own, bf16[4,2,160,128]{3,2,1,0:T(8,128)(2,1)S(1)} %collective-permute-done.22.plus, bf16[4,2,160,128]{3,2,1,0:T(8,128)(2,1)S(1)} %collective-permute-done.26.minus, ...), custom_call_target="tpu_custom_call" | custom-call | flops 30000001024 | bytes 90000000 | tf_op jit(solution)/shard_map/pallas_call | solution.py:481
  110.1 7.4 %shard_map.106 = f32[9,160,640]{2,1,0:T(8,128)} custom-call(s32[3]{0:T(128)S(1)} %pad_add_fusion.place, bf16[4,2,160,128]{3,2,1,0:T(8,128)(2,1)S(1)} %collective-permute-done.22.plus, bf16[4,2,160,128]{3,2,1,0:T(8,128)(2,1)S(1)} %collective-permute-done.26.minus, bf16[4,2,160,128]{3,2,1,0:T(8,128)(2,1)S(1)} %collective-permute-done.36.far, ...), custom_call_target="tpu_custom_call" | custom-call | flops 50000000 | bytes 150000 | tf_op jit(solution)/shard_map/pallas_call | solution.py:481
  (89 shorter events, 24.4 us)
Async XLA Ops:
  0.6 14.3 %collective-permute-start = (bf16[9,160,640]{2,1,0:T(8,128)(2,1)}, bf16[9,160,640]{2,1,0:T(8,128)(2,1)}, u32[]{:S(2)}, u32[]{:S(2)}) collective-permute-start(bf16[9,160,640]{2,1,0:T(8,128)(2,1)} %bitcast.22), channel_id=1, source_target_pairs={{0,1},{1,0},{2,3},{3,2},{4,5},{5,4},{6,7},{7,6},{8,9},{9,8},{10,11... | collective-permute-start | bytes 5529608 | tf_op jit(solution)/shard_map/ppermute | solution.py:500
  2.2 12.7 %collective-permute-start.1 = (bf16[2,160,640]{2,1,0:T(8,128)(2,1)S(1)}, bf16[2,160,640]{2,1,0:T(8,128)(2,1)S(1)}, u32[]{:S(2)}, u32[]{:S(2)}) collective-permute-start(bf16[2,160,640]{2,1,0:T(8,128)(2,1)S(1)} %dynamic-slice_bitcast_fusion), channel_id=1, source_target_pairs={{0,2},{1,3},{2,0},{3,1},{4,6},{5,7},{6,4},{7,5},{8,10},{9,11},{10,... | collective-permute-start | bytes 1228808 | tf_op jit(solution)/shard_map/ppermute | solution.py:500
  6.2 8.7 %collective-permute-start.2 = (f32[8,640]{1,0:T(8,128)S(1)}, f32[8,640]{1,0:T(8,128)S(1)}, u32[]{:S(2)}, u32[]{:S(2)}) collective-permute-start(f32[8,640]{1,0:T(8,128)S(1)} %shard_map.93.s0), channel_id=1, source_target_pairs={{0,4},{4,0},{8,12},{12,8},{1,5},{5,1},{9,13},{13,9},{2,6},{6,2},{1... | collective-permute-start | bytes 61448 | tf_op jit(solution)/shard_map/ppermute | solution.py:500
  7.8 7.1 %collective-permute-start.3 = (f32[8,640]{1,0:T(8,128)S(1)}, f32[8,640]{1,0:T(8,128)S(1)}, u32[]{:S(2)}, u32[]{:S(2)}) collective-permute-start(f32[8,640]{1,0:T(8,128)S(1)} %shard_map.93.s0), channel_id=1, source_target_pairs={{0,8},{4,12},{8,0},{12,4},{1,9},{5,13},{9,1},{13,5},{2,10},{6,14},... | collective-permute-start | bytes 61448 | tf_op jit(solution)/shard_map/ppermute | solution.py:500
  17.1 13.1 %collective-permute-start.5 = (bf16[2,640,128]{2,1,0:T(8,128)(2,1)S(1)}, bf16[2,640,128]{2,1,0:T(8,128)(2,1)S(1)}, u32[]{:S(2)}, u32[]{:S(2)}) collective-permute-start(bf16[2,640,128]{2,1,0:T(8,128)(2,1)S(1)} %get-tuple-element.64.mine), channel_id=1, source_target_pairs={{4,0},{8,4},{12,8},{0,12},{5,1},{9,5},{13,9},{1,13},{6,2},{10,6},{... | collective-permute-start | bytes 983048 | tf_op jit(solution)/shard_map/ppermute | solution.py:505
  20.0 14.8 %collective-permute-start.6 = (bf16[2,640,128]{2,1,0:T(8,128)(2,1)S(1)}, bf16[2,640,128]{2,1,0:T(8,128)(2,1)S(1)}, u32[]{:S(2)}, u32[]{:S(2)}) collective-permute-start(bf16[2,640,128]{2,1,0:T(8,128)(2,1)S(1)} %get-tuple-element.64.mine), channel_id=1, source_target_pairs={{12,0},{0,4},{4,8},{8,12},{13,1},{1,5},{5,9},{9,13},{14,2},{2,6},{... | collective-permute-start | bytes 983048 | tf_op jit(solution)/shard_map/ppermute | solution.py:505
  20.0 15.7 %collective-permute-start.8 = (bf16[2,160,640]{2,1,0:T(8,128)(2,1)S(1)}, bf16[2,160,640]{2,1,0:T(8,128)(2,1)S(1)}, u32[]{:S(2)}, u32[]{:S(2)}) collective-permute-start(bf16[2,160,640]{2,1,0:T(8,128)(2,1)S(1)} %collective-permute-done.1.far0), channel_id=1, source_target_pairs={{0,16},{16,0},{1,17},{17,1},{2,18},{18,2},{3,19},{19,3},{4,20},{20... | collective-permute-start | bytes 1228808 | tf_op jit(solution)/shard_map/ppermute | solution.py:500
  21.6 8.1 %collective-permute-start.9 = (bf16[1,160,640]{2,1,0:T(8,128)(2,1)S(1)}, bf16[1,160,640]{2,1,0:T(8,128)(2,1)S(1)}, u32[]{:S(2)}, u32[]{:S(2)}) collective-permute-start(bf16[1,160,640]{2,1,0:T(8,128)(2,1)S(1)} %constant_dynamic-slice_fusion), channel_id=1, source_target_pairs={{0,2},{1,3},{2,0},{3,1},{4,6},{5,7},{6,4},{7,5},{8,10},{9,11},{10,... | collective-permute-start | bytes 614408 | tf_op jit(solution)/shard_map/ppermute | solution.py:500
  23.1 17.8 %collective-permute-start.11 = (bf16[3,160,640]{2,1,0:T(8,128)(2,1)S(1)}, bf16[3,160,640]{2,1,0:T(8,128)(2,1)S(1)}, u32[]{:S(2)}, u32[]{:S(2)}) collective-permute-start(bf16[3,160,640]{2,1,0:T(8,128)(2,1)S(1)} %slice.18), channel_id=1, source_target_pairs={{0,2},{1,3},{2,0},{3,1},{4,6},{5,7},{6,4},{7,5},{8,10},{9,11},{10,... | collective-permute-start | bytes 1843208 | tf_op jit(solution)/shard_map/ppermute | solution.py:500
  41.4 13.2 %collective-permute-start.17 = (bf16[2,640,128]{2,1,0:T(8,128)(2,1)S(1)}, bf16[2,640,128]{2,1,0:T(8,128)(2,1)S(1)}, u32[]{:S(2)}, u32[]{:S(2)}) collective-permute-start(bf16[2,640,128]{2,1,0:T(8,128)(2,1)S(1)} %get-tuple-element.64.mine), channel_id=1, source_target_pairs={{0,2},{1,3},{2,0},{3,1},{4,6},{5,7},{6,4},{7,5},{8,10},{9,11},{10,... | collective-permute-start | bytes 983048 | tf_op jit(solution)/shard_map/ppermute | solution.py:500
  42.9 11.7 %collective-permute-start.18 = (bf16[2,640,128]{2,1,0:T(8,128)(2,1)S(1)}, bf16[2,640,128]{2,1,0:T(8,128)(2,1)S(1)}, u32[]{:S(2)}, u32[]{:S(2)}) collective-permute-start(bf16[2,640,128]{2,1,0:T(8,128)(2,1)S(1)} %collective-permute-done.5.above), channel_id=1, source_target_pairs={{4,0},{8,4},{12,8},{0,12},{5,1},{9,5},{13,9},{1,13},{6,2},{10,6},{... | collective-permute-start | bytes 983048 | tf_op jit(solution)/shard_map/ppermute | solution.py:505
  54.7 6.6 %collective-permute-start.19 = (bf16[2,2,160,128]{3,2,1,0:T(8,128)(2,1)S(1)}, bf16[2,2,160,128]{3,2,1,0:T(8,128)(2,1)S(1)}, u32[]{:S(2)}, u32[]{:S(2)}) collective-permute-start(bf16[2,2,160,128]{3,2,1,0:T(8,128)(2,1)S(1)} %get-tuple-element.59), channel_id=1, source_target_pairs={{0,2},{1,3},{2,0},{3,1},{4,6},{5,7},{6,4},{7,5},{8,10},{9,11},{10,... | collective-permute-start | bytes 491528 | tf_op jit(solution)/shard_map/ppermute | solution.py:500
  63.4 19.9 %collective-permute-start.24 = (bf16[10,640,128]{2,1,0:T(8,128)(2,1)S(1)}, bf16[10,640,128]{2,1,0:T(8,128)(2,1)S(1)}, u32[]{:S(2)}, u32[]{:S(2)}) collective-permute-start(bf16[10,640,128]{2,1,0:T(8,128)(2,1)S(1)} %shard_map.100.h0), channel_id=1, source_target_pairs={{0,1},{1,0},{2,3},{3,2},{4,5},{5,4},{6,7},{7,6},{8,9},{9,8},{10,11... | collective-permute-start | bytes 4915208 | tf_op jit(solution)/shard_map/ppermute | solution.py:500
  63.6 10.0 %collective-permute-start.23 = (bf16[2,640,128]{2,1,0:T(8,128)(2,1)S(1)}, bf16[2,640,128]{2,1,0:T(8,128)(2,1)S(1)}, u32[]{:S(2)}, u32[]{:S(2)}) collective-permute-start(bf16[2,640,128]{2,1,0:T(8,128)(2,1)S(1)} %collective-permute-done.5.above), channel_id=1, source_target_pairs={{0,2},{1,3},{2,0},{3,1},{4,6},{5,7},{6,4},{7,5},{8,10},{9,11},{10,... | collective-permute-start | bytes 983048 | tf_op jit(solution)/shard_map/ppermute | solution.py:500
  64.1 12.1 %collective-permute-start.22 = (bf16[4,2,160,128]{3,2,1,0:T(8,128)(2,1)S(1)}, bf16[4,2,160,128]{3,2,1,0:T(8,128)(2,1)S(1)}, u32[]{:S(2)}, u32[]{:S(2)}) collective-permute-start(bf16[4,2,160,128]{3,2,1,0:T(8,128)(2,1)S(1)} %pad_maximum_fusion.own), channel_id=1, source_target_pairs={{4,0},{8,4},{12,8},{0,12},{5,1},{9,5},{13,9},{1,13},{6,2},{10,6},{... | collective-permute-start | bytes 983048 | tf_op jit(solution)/shard_map/ppermute | solution.py:505
  65.8 17.5 %collective-permute-start.21 = (bf16[1,640,128]{2,1,0:T(8,128)(2,1)S(1)}, bf16[1,640,128]{2,1,0:T(8,128)(2,1)S(1)}, u32[]{:S(2)}, u32[]{:S(2)}) collective-permute-start(bf16[1,640,128]{2,1,0:T(8,128)(2,1)S(1)} %get-tuple-element.83), channel_id=1, source_target_pairs={{0,4},{4,8},{8,12},{1,5},{5,9},{9,13},{2,6},{6,10},{10,14},{3,7},{... | collective-permute-start | bytes 491528 | tf_op jit(solution)/shard_map/ppermute | solution.py:593
  68.1 15.2 %collective-permute-start.25 = (bf16[1,640,128]{2,1,0:T(8,128)(2,1)S(1)}, bf16[1,640,128]{2,1,0:T(8,128)(2,1)S(1)}, u32[]{:S(2)}, u32[]{:S(2)}) collective-permute-start(bf16[1,640,128]{2,1,0:T(8,128)(2,1)S(1)} %get-tuple-element.82), channel_id=1, source_target_pairs={{4,0},{8,4},{12,8},{5,1},{9,5},{13,9},{6,2},{10,6},{14,10},{7,3},{... | collective-permute-start | bytes 491528 | tf_op jit(solution)/shard_map/ppermute | solution.py:594
  73.6 9.2 %collective-permute-start.30 = (bf16[2,640,128]{2,1,0:T(8,128)(2,1)S(1)}, bf16[2,640,128]{2,1,0:T(8,128)(2,1)S(1)}, u32[]{:S(2)}, u32[]{:S(2)}) collective-permute-start(bf16[2,640,128]{2,1,0:T(8,128)(2,1)S(1)} %collective-permute-done.6.below), channel_id=1, source_target_pairs={{0,2},{1,3},{2,0},{3,1},{4,6},{5,7},{6,4},{7,5},{8,10},{9,11},{10,... | collective-permute-start | bytes 983048 | tf_op jit(solution)/shard_map/ppermute | solution.py:500
  76.3 13.2 %collective-permute-start.26 = (bf16[4,2,160,128]{3,2,1,0:T(8,128)(2,1)S(1)}, bf16[4,2,160,128]{3,2,1,0:T(8,128)(2,1)S(1)}, u32[]{:S(2)}, u32[]{:S(2)}) collective-permute-start(bf16[4,2,160,128]{3,2,1,0:T(8,128)(2,1)S(1)} %pad_maximum_fusion.own), channel_id=1, source_target_pairs={{12,0},{0,4},{4,8},{8,12},{13,1},{1,5},{5,9},{9,13},{14,2},{2,6},{... | collective-permute-start | bytes 983048 | tf_op jit(solution)/shard_map/ppermute | solution.py:505
  82.7 11.2 %collective-permute-start.31 = (bf16[2,640,128]{2,1,0:T(8,128)(2,1)S(1)}, bf16[2,640,128]{2,1,0:T(8,128)(2,1)S(1)}, u32[]{:S(2)}, u32[]{:S(2)}) collective-permute-start(bf16[2,640,128]{2,1,0:T(8,128)(2,1)S(1)} %collective-permute-done.18.beyond), channel_id=1, source_target_pairs={{0,2},{1,3},{2,0},{3,1},{4,6},{5,7},{6,4},{7,5},{8,10},{9,11},{10,... | collective-permute-start | bytes 983048 | tf_op jit(solution)/shard_map/ppermute | solution.py:500
  99.1 10.9 %collective-permute-start.36 = (bf16[4,2,160,128]{3,2,1,0:T(8,128)(2,1)S(1)}, bf16[4,2,160,128]{3,2,1,0:T(8,128)(2,1)S(1)}, u32[]{:S(2)}, u32[]{:S(2)}) collective-permute-start(bf16[4,2,160,128]{3,2,1,0:T(8,128)(2,1)S(1)} %collective-permute-done.22.plus), channel_id=1, source_target_pairs={{4,0},{8,4},{12,8},{0,12},{5,1},{9,5},{13,9},{1,13},{6,2},{10,6},{... | collective-permute-start | bytes 983048 | tf_op jit(solution)/shard_map/ppermute | solution.py:505
  101.3 8.1 %collective-permute-start.33 = (f32[8,640]{1,0:T(8,128)S(1)}, f32[8,640]{1,0:T(8,128)S(1)}, u32[]{:S(2)}, u32[]{:S(2)}) collective-permute-start(f32[8,640]{1,0:T(8,128)S(1)} %get-tuple-element.78.s0), channel_id=1, source_target_pairs={{0,1},{1,0},{2,3},{3,2},{4,5},{5,4},{6,7},{7,6},{8,9},{9,8},{10,11... | collective-permute-start | bytes 61448 | tf_op jit(solution)/shard_map/ppermute | solution.py:500
  101.5 7.9 %collective-permute-start.34 = (f32[8,640]{1,0:T(8,128)S(1)}, f32[8,640]{1,0:T(8,128)S(1)}, u32[]{:S(2)}, u32[]{:S(2)}) collective-permute-start(f32[8,640]{1,0:T(8,128)S(1)} %get-tuple-element.78.s0), channel_id=1, source_target_pairs={{0,2},{1,3},{2,0},{3,1},{4,6},{5,7},{6,4},{7,5},{8,10},{9,11},{10,... | collective-permute-start | bytes 61448 | tf_op jit(solution)/shard_map/ppermute | solution.py:500
  103.0 6.4 %collective-permute-start.35 = (f32[8,640]{1,0:T(8,128)S(1)}, f32[8,640]{1,0:T(8,128)S(1)}, u32[]{:S(2)}, u32[]{:S(2)}) collective-permute-start(f32[8,640]{1,0:T(8,128)S(1)} %get-tuple-element.78.s0), channel_id=1, source_target_pairs={{0,3},{1,2},{2,1},{3,0},{4,7},{5,6},{6,5},{7,4},{8,11},{9,10},{10,... | collective-permute-start | bytes 61448 | tf_op jit(solution)/shard_map/ppermute | solution.py:500
  (20 other events, 118.9 us)

commit v8 on v7

--- a/solution.py
+++ b/solution.py
@@ -555,7 +555,6 @@
         us=5,
     )
     beyond = ring(above, "rows", 1)
-    across = [swap(after_all(hidden, framed), "wt", 2)]
     rows_of = functools.partial(
         call, spread_kernel, shape((10, channels, width), BF16), [SM] + [VM] * 4, us=3
     )
@@ -571,7 +570,7 @@
         [pltpu.VMEM((2 * panel, 2 * LANES), F32)],
         us=20,
     )
-    fars = lax.optimization_barrier((far0, far1, far2, far3, far4, framed))[:5]
+    fars = lax.optimization_barrier((far0, far1, far2, far3, far4, part0, beyond))[:5]
     weights = (near, side, *fars, *(swap(far, "wt", 1) for far in fars))
     res, low, block23 = call(
         far_conv_kernel,
@@ -587,7 +586,7 @@
     )
 
     block1 = swap(block1, "wt", 1)
-    block23 = swap(after_all(block23, across[0], beyond), "wt", 2)
+    block23 = swap(block23, "wt", 2)
     stacked = jnp.stack([block0, block1, block23[0], swap(block23[1], "wt", 1)])
     settled = after_all(low, stacked)
     low_before = lax.ppermute(settled[1:2], "rows", up)
@@ -603,9 +602,9 @@
         us=5,
     )
 
-    for strip_in, last in ((above, block23), (below, None), (beyond, None)):
-        across.append(swap(after_all(strip_in, across[-1] if last is None else last), "wt", 2))
-    across[2:] = across[:1:-1]
+    across = [swap(after_all(hidden, block23), "wt", 2)]
+    across.append(swap(after_all(above, across[0]), "wt", 2))
+    below_across = swap(after_all(below, across[1]), "wt", 2)
     own_rows = rows_of((place, after_all(hidden, stacked), above, beyond, below))
     other_rows = swap(own_rows, "wt", 1)
 
@@ -621,6 +620,7 @@
         mib=12, us=30,
     )
     sums = after_all(sums, minus)
+    across += [swap(after_all(beyond, grad), "wt", 2), below_across]
     across_rows = rows_of((after_all(place, sums), *across))
     grad_latents, sums = call(
         functools.partial(latents_kernel, group_cells),

time: 118 us -> 115 us (0.975)
  waiting for transfers between devices: 41.1 us -> 34.8 us
  starting transfers between devices: 37.1 us -> 40.6 us
    ppermute x29, waiting for transfers between devices: 36.6 us -> 32.5 us  [swap(): return lax.ppermute(x, axis, [(i, i ^ mask) for i in range(size)])]
    ppermute x29, starting transfers between devices: 23.2 us -> 25.9 us  [swap(): return lax.ppermute(x, axis, [(i, i ^ mask) for i in range(size)])]
    ppermute x6, waiting for transfers between devices: 4.57 us -> 2.31 us  [ring(): return lax.ppermute(x, axis, [((i + step) % size, i) for i in range(size)])]
    ppermute x6, starting transfers between devices: 10.3 us -> 12.2 us  [ring(): return lax.ppermute(x, axis, [((i + step) % size, i) for i in range(size)])]
  transfers between devices with their start and end apart: 37 -> 37, of which waited for: 10 -> 14; matrix products, arithmetic and copies ran while one was open for 1% -> 1% of each run, Pallas kernels for 21% -> 20%
where the time goes in v8:
time: 115 us
  starting transfers between devices  40.6 us (35%)
  Pallas kernels  35.9 us (31%)
  waiting for transfers between devices  34.8 us (30%)
  local copies, waits for them, and re-layouts  2.27 us (2%)
    pallas_call x14, Pallas kernels, call(): pl.pallas_call(kernel, out_shape=outs, in_specs=specs, out_specs=jax.tree...  35.9 us
    ppermute x29, waiting for transfers between devices, swap(): return lax.ppermute(x, axis, [(i, i ^ mask) for i in range(size)])  32.5 us
    ppermute x29, starting transfers between devices, swap(): return lax.ppermute(x, axis, [(i, i ^ mask) for i in range(size)])  25.9 us
    ppermute x6, starting transfers between devices, ring(): return lax.ppermute(x, axis, [((i + step) % size, i) for i in range(size)])  12.2 us
    ppermute x6, waiting for transfers between devices, ring(): return lax.ppermute(x, axis, [((i + step) % size, i) for i in range(size)])  2.31 us
  transfers between devices with their start and end apart: 37, of which 14 were waited for; matrix products, arithmetic and copies ran while one was open for 1% of the time, Pallas kernels for 20%

profile of v8, /device:TPU:0, one launch (start us, length us, event | category | flops | bytes accessed | tf_op | source)
XLA Modules:
  0.0 114.9 jit_solution(3547110393124694639)
XLA Ops:
  2.2 2.6 %collective-permute-start.1 = (bf16[2,160,640]{2,1,0:T(8,128)(2,1)S(1)}, bf16[2,160,640]{2,1,0:T(8,128)(2,1)S(1)}, u32[]{:S(2)}, u32[]{:S(2)}) collective-permute-start(bf16[2,160,640]{2,1,0:T(8,128)(2,1)S(1)} %dynamic-slice_bitcast_fusion), channel_id=1, source_target_pairs={{0,2},{1,3},{2,0},{3,1},{4,6},{5,7},{6,4},{7,5},{8,10},{9,11},{10,... | collective-permute-start | bytes 1228808 | tf_op jit(solution)/shard_map/ppermute | solution.py:500
  6.2 1.6 %collective-permute-start.2 = (f32[8,640]{1,0:T(8,128)S(1)}, f32[8,640]{1,0:T(8,128)S(1)}, u32[]{:S(2)}, u32[]{:S(2)}) collective-permute-start(f32[8,640]{1,0:T(8,128)S(1)} %shard_map.93.s0), channel_id=1, source_target_pairs={{0,4},{4,0},{8,12},{12,8},{1,5},{5,1},{9,13},{13,9},{2,6},{6,2},{1... | collective-permute-start | bytes 61448 | tf_op jit(solution)/shard_map/ppermute | solution.py:500
  7.8 2.6 %collective-permute-start.3 = (f32[8,640]{1,0:T(8,128)S(1)}, f32[8,640]{1,0:T(8,128)S(1)}, u32[]{:S(2)}, u32[]{:S(2)}) collective-permute-start(f32[8,640]{1,0:T(8,128)S(1)} %shard_map.93.s0), channel_id=1, source_target_pairs={{0,8},{4,12},{8,0},{12,4},{1,9},{5,13},{9,1},{13,5},{2,10},{6,14},... | collective-permute-start | bytes 61448 | tf_op jit(solution)/shard_map/ppermute | solution.py:500
  10.8 4.1 %collective-permute-done.1.far0 = bf16[2,160,640]{2,1,0:T(8,128)(2,1)S(1)} collective-permute-done((bf16[2,160,640]{2,1,0:T(8,128)(2,1)S(1)}, bf16[2,160,640]{2,1,0:T(8,128)(2,1)S(1)}, u32[]{:S(2)}, u32[]{:S(2)}) %collective-permute-start.1) | collective-permute-done | bytes 409632 | tf_op jit(solution)/shard_map/ppermute | solution.py:500
  17.1 2.8 %collective-permute-start.5 = (bf16[2,640,128]{2,1,0:T(8,128)(2,1)S(1)}, bf16[2,640,128]{2,1,0:T(8,128)(2,1)S(1)}, u32[]{:S(2)}, u32[]{:S(2)}) collective-permute-start(bf16[2,640,128]{2,1,0:T(8,128)(2,1)S(1)} %get-tuple-element.62.mine), channel_id=1, source_target_pairs={{4,0},{8,4},{12,8},{0,12},{5,1},{9,5},{13,9},{1,13},{6,2},{10,6},{... | collective-permute-start | bytes 983048 | tf_op jit(solution)/shard_map/ppermute | solution.py:505
  21.6 1.6 %collective-permute-start.9 = (bf16[1,160,640]{2,1,0:T(8,128)(2,1)S(1)}, bf16[1,160,640]{2,1,0:T(8,128)(2,1)S(1)}, u32[]{:S(2)}, u32[]{:S(2)}) collective-permute-start(bf16[1,160,640]{2,1,0:T(8,128)(2,1)S(1)} %constant_dynamic-slice_fusion), channel_id=1, source_target_pairs={{0,2},{1,3},{2,0},{3,1},{4,6},{5,7},{6,4},{7,5},{8,10},{9,11},{10,... | collective-permute-start | bytes 614408 | tf_op jit(solution)/shard_map/ppermute | solution.py:500
  23.9 5.7 %collective-permute-done.9.far2 = bf16[1,160,640]{2,1,0:T(8,128)(2,1)S(1)} collective-permute-done((bf16[1,160,640]{2,1,0:T(8,128)(2,1)S(1)}, bf16[1,160,640]{2,1,0:T(8,128)(2,1)S(1)}, u32[]{:S(2)}, u32[]{:S(2)}) %collective-permute-start.9) | collective-permute-done | bytes 204832 | tf_op jit(solution)/shard_map/ppermute | solution.py:500
  30.2 3.8 %collective-permute-start.12 = (bf16[2,640,128]{2,1,0:T(8,128)(2,1)S(1)}, bf16[2,640,128]{2,1,0:T(8,128)(2,1)S(1)}, u32[]{:S(2)}, u32[]{:S(2)}) collective-permute-start(bf16[2,640,128]{2,1,0:T(8,128)(2,1)S(1)} %collective-permute-done.5.above), channel_id=1, source_target_pairs={{4,0},{8,4},{12,8},{0,12},{5,1},{9,5},{13,9},{1,13},{6,2},{10,6},{... | collective-permute-start | bytes 983048 | tf_op jit(solution)/shard_map/ppermute | solution.py:505
  34.0 2.1 %collective-permute-done.6.below = bf16[2,640,128]{2,1,0:T(8,128)(2,1)S(1)} collective-permute-done((bf16[2,640,128]{2,1,0:T(8,128)(2,1)S(1)}, bf16[2,640,128]{2,1,0:T(8,128)(2,1)S(1)}, u32[]{:S(2)}, u32[]{:S(2)}) %collective-permute-start.6) | collective-permute-done | bytes 327712 | tf_op jit(solution)/shard_map/ppermute | solution.py:505
  37.0 4.4 %shard_map.97 = (f32[2,2,160,128]{3,2,1,0:T(8,128)S(1)}, bf16[2,160,128]{2,1,0:T(8,128)(2,1)S(1)}, bf16[2,160,128]{2,1,0:T(8,128)(2,1)S(1)}) custom-call(s32[3]{0:T(128)S(1)} %pad_add_fusion.place, bf16[9,160,640]{2,1,0:T(8,128)(2,1)S(1)} %bitcast.25, bf16[9,160,640]{2,1,0:T(8,128)(2,1)} %collective-permute-done.side, ...), custom_call_target="tpu_custom_call" | custom-call | flops 20000000000 | bytes 60000000 | tf_op jit(solution)/shard_map/pallas_call | solution.py:481
  42.7 2.5 %collective-permute-done.15.diag2 = bf16[1,160,640]{2,1,0:T(8,128)(2,1)S(1)} collective-permute-done((bf16[1,160,640]{2,1,0:T(8,128)(2,1)S(1)}, bf16[1,160,640]{2,1,0:T(8,128)(2,1)S(1)}, u32[]{:S(2)}, u32[]{:S(2)}) %collective-permute-start.15) | collective-permute-done | bytes 204832 | tf_op jit(solution)/shard_map/ppermute | solution.py:500
  45.5 3.2 %shard_map.98 = (f32[2,640,128]{2,1,0:T(8,128)S(1)}, bf16[2,640,128]{2,1,0:T(8,128)(2,1)S(1)}, bf16[2,2,160,128]{3,2,1,0:T(8,128)(2,1)S(1)}) custom-call(s32[3]{0:T(128)S(1)} %pad_add_fusion.place, bf16[2,160,640]{2,1,0:T(8,128)(2,1)S(1)} %collective-permute-done.1.far0, bf16[2,160,640]{2,1,0:T(8,128)(2,1)S(1)} %collective-permute-done.8.far1, ...), custom_call_target="tpu_custom_call" | custom-call | flops 50000000 | bytes 150000 | tf_op jit(solution)/shard_map/pallas_call | solution.py:481
  50.2 4.7 %collective-permute-done.18 = bf16[2,2,160,128]{3,2,1,0:T(8,128)(2,1)S(1)} collective-permute-done((bf16[2,2,160,128]{3,2,1,0:T(8,128)(2,1)S(1)}, bf16[2,2,160,128]{3,2,1,0:T(8,128)(2,1)S(1)}, u32[]{:S(2)}, u32[]{:S(2)}) %collective-permute-start.18) | collective-permute-done | bytes 163872 | tf_op jit(solution)/shard_map/ppermute | solution.py:500
  58.8 3.5 %collective-permute-start.21 = (bf16[4,2,160,128]{3,2,1,0:T(8,128)(2,1)S(1)}, bf16[4,2,160,128]{3,2,1,0:T(8,128)(2,1)S(1)}, u32[]{:S(2)}, u32[]{:S(2)}) collective-permute-start(bf16[4,2,160,128]{3,2,1,0:T(8,128)(2,1)S(1)} %pad_maximum_fusion.own), channel_id=1, source_target_pairs={{4,0},{8,4},{12,8},{0,12},{5,1},{9,5},{13,9},{1,13},{6,2},{10,6},{... | collective-permute-start | bytes 983048 | tf_op jit(solution)/shard_map/ppermute | solution.py:505
  64.9 2.3 %collective-permute-done.22.mine = bf16[2,640,128]{2,1,0:T(8,128)(2,1)S(1)} collective-permute-done((bf16[2,640,128]{2,1,0:T(8,128)(2,1)S(1)}, bf16[2,640,128]{2,1,0:T(8,128)(2,1)S(1)}, u32[]{:S(2)}, u32[]{:S(2)}) %collective-permute-start.22) | collective-permute-done | bytes 327712 | tf_op jit(solution)/shard_map/ppermute | solution.py:500
  68.7 2.1 %shard_map.99.full = bf16[9,640,640]{2,1,0:T(8,128)(2,1)S(1)} custom-call(s32[3]{0:T(128)S(1)} %pad_add_fusion.place, bf16[9,160,640]{2,1,0:T(8,128)(2,1)S(1)} %bitcast.26, bf16[9,160,640]{2,1,0:T(8,128)(2,1)} %collective-permute-done.side, bf16[2,160,640]{2,1,0:T(8,128)(2,1)S(1)} %collective-permute-done.1.far0, ...), custom_call_target="tpu_custom_call" | custom-call | flops 5000000000 | bytes 15000000 | tf_op jit(solution)/shard_map/pallas_call | solution.py:481
  72.3 4.1 %collective-permute-done.23.above = bf16[2,640,128]{2,1,0:T(8,128)(2,1)S(1)} collective-permute-done((bf16[2,640,128]{2,1,0:T(8,128)(2,1)S(1)}, bf16[2,640,128]{2,1,0:T(8,128)(2,1)S(1)}, u32[]{:S(2)}, u32[]{:S(2)}) %collective-permute-start.23) | collective-permute-done | bytes 327712 | tf_op jit(solution)/shard_map/ppermute | solution.py:500
  77.9 6.2 %shard_map.101 = (f32[2,640,128]{2,1,0:T(8,128)S(1)}, f32[8,640]{1,0:T(8,128)S(1)}) custom-call(bf16[9,640,640]{2,1,0:T(8,128)(2,1)S(1)} %shard_map.99.full, bf16[1,640,128]{2,1,0:T(8,128)(2,1)S(1)} %collective-permute-done.20.before, bf16[2,640,128]{2,1,0:T(8,128)(2,1)S(1)} %get-tuple-element.63.low, ...), custom_call_target="tpu_custom_call" | custom-call | flops 30000001024 | bytes 90000000 | tf_op jit(solution)/shard_map/pallas_call | solution.py:481
  86.1 2.7 %collective-permute-start.28 = (f32[8,640]{1,0:T(8,128)S(1)}, f32[8,640]{1,0:T(8,128)S(1)}, u32[]{:S(2)}, u32[]{:S(2)}) collective-permute-start(f32[8,640]{1,0:T(8,128)S(1)} %get-tuple-element.67.s0), channel_id=1, source_target_pairs={{0,8},{4,12},{8,0},{12,4},{1,9},{5,13},{9,1},{13,5},{2,10},{6,14},... | collective-permute-start | bytes 61448 | tf_op jit(solution)/shard_map/ppermute | solution.py:500
  89.1 2.1 %collective-permute-done.28.s2 = f32[8,640]{1,0:T(8,128)S(1)} collective-permute-done((f32[8,640]{1,0:T(8,128)S(1)}, f32[8,640]{1,0:T(8,128)S(1)}, u32[]{:S(2)}, u32[]{:S(2)}) %collective-permute-start.28) | collective-permute-done | bytes 20512 | tf_op jit(solution)/shard_map/ppermute | solution.py:500
  91.2 3.2 %collective-permute-done.29.s3 = f32[8,640]{1,0:T(8,128)S(1)} collective-permute-done((f32[8,640]{1,0:T(8,128)S(1)}, f32[8,640]{1,0:T(8,128)S(1)}, u32[]{:S(2)}, u32[]{:S(2)}) %collective-permute-start.29) | collective-permute-done | bytes 20512 | tf_op jit(solution)/shard_map/ppermute | solution.py:500
  94.4 1.8 %shard_map.102 = (f32[1280,128]{1,0:T(8,128)}, f32[8,640]{1,0:T(8,128)S(1)}) custom-call(f32[8,640]{1,0:T(8,128)S(1)} %get-tuple-element.67.s0, f32[8,640]{1,0:T(8,128)S(1)} %collective-permute-done.27.s1, f32[8,640]{1,0:T(8,128)S(1)} %collective-permute-done.28.s2, f32[8,640]{1,0:T(8,128)S(1)} %collective-permute-done.29.s3, ...), custom_call_target="tpu_custom_call" | custom-call | flops 50000000 | bytes 150000 | tf_op jit(solution)/shard_map/pallas_call | solution.py:481
  100.4 6.2 %shard_map.104.near = f32[9,160,640]{2,1,0:T(8,128)S(1)} custom-call(s32[3]{0:T(128)S(1)} %pad_add_fusion.place, bf16[4,2,160,128]{3,2,1,0:T(8,128)(2,1)S(1)} %pad_maximum_fusion.own, bf16[4,2,160,128]{3,2,1,0:T(8,128)(2,1)S(1)} %collective-permute-done.21.plus, bf16[4,2,160,128]{3,2,1,0:T(8,128)(2,1)S(1)} %collective-permute-done.26.minus, ...), custom_call_target="tpu_custom_call" | custom-call | flops 30000001024 | bytes 90000000 | tf_op jit(solution)/shard_map/pallas_call | solution.py:481
  107.3 7.4 %shard_map.106 = f32[9,160,640]{2,1,0:T(8,128)} custom-call(s32[3]{0:T(128)S(1)} %pad_add_fusion.place, bf16[4,2,160,128]{3,2,1,0:T(8,128)(2,1)S(1)} %collective-permute-done.21.plus, bf16[4,2,160,128]{3,2,1,0:T(8,128)(2,1)S(1)} %collective-permute-done.26.minus, bf16[4,2,160,128]{3,2,1,0:T(8,128)(2,1)S(1)} %collective-permute-done.36.far, ...), custom_call_target="tpu_custom_call" | custom-call | flops 50000000 | bytes 150000 | tf_op jit(solution)/shard_map/pallas_call | solution.py:481
  (89 shorter events, 30.4 us)
Async XLA Ops:
  0.6 14.3 %collective-permute-start = (bf16[9,160,640]{2,1,0:T(8,128)(2,1)}, bf16[9,160,640]{2,1,0:T(8,128)(2,1)}, u32[]{:S(2)}, u32[]{:S(2)}) collective-permute-start(bf16[9,160,640]{2,1,0:T(8,128)(2,1)} %bitcast.22), channel_id=1, source_target_pairs={{0,1},{1,0},{2,3},{3,2},{4,5},{5,4},{6,7},{7,6},{8,9},{9,8},{10,11... | collective-permute-start | bytes 5529608 | tf_op jit(solution)/shard_map/ppermute | solution.py:500
  2.2 12.7 %collective-permute-start.1 = (bf16[2,160,640]{2,1,0:T(8,128)(2,1)S(1)}, bf16[2,160,640]{2,1,0:T(8,128)(2,1)S(1)}, u32[]{:S(2)}, u32[]{:S(2)}) collective-permute-start(bf16[2,160,640]{2,1,0:T(8,128)(2,1)S(1)} %dynamic-slice_bitcast_fusion), channel_id=1, source_target_pairs={{0,2},{1,3},{2,0},{3,1},{4,6},{5,7},{6,4},{7,5},{8,10},{9,11},{10,... | collective-permute-start | bytes 1228808 | tf_op jit(solution)/shard_map/ppermute | solution.py:500
  6.2 8.7 %collective-permute-start.2 = (f32[8,640]{1,0:T(8,128)S(1)}, f32[8,640]{1,0:T(8,128)S(1)}, u32[]{:S(2)}, u32[]{:S(2)}) collective-permute-start(f32[8,640]{1,0:T(8,128)S(1)} %shard_map.93.s0), channel_id=1, source_target_pairs={{0,4},{4,0},{8,12},{12,8},{1,5},{5,1},{9,13},{13,9},{2,6},{6,2},{1... | collective-permute-start | bytes 61448 | tf_op jit(solution)/shard_map/ppermute | solution.py:500
  7.8 7.1 %collective-permute-start.3 = (f32[8,640]{1,0:T(8,128)S(1)}, f32[8,640]{1,0:T(8,128)S(1)}, u32[]{:S(2)}, u32[]{:S(2)}) collective-permute-start(f32[8,640]{1,0:T(8,128)S(1)} %shard_map.93.s0), channel_id=1, source_target_pairs={{0,8},{4,12},{8,0},{12,4},{1,9},{5,13},{9,1},{13,5},{2,10},{6,14},... | collective-permute-start | bytes 61448 | tf_op jit(solution)/shard_map/ppermute | solution.py:500
  17.1 13.1 %collective-permute-start.5 = (bf16[2,640,128]{2,1,0:T(8,128)(2,1)S(1)}, bf16[2,640,128]{2,1,0:T(8,128)(2,1)S(1)}, u32[]{:S(2)}, u32[]{:S(2)}) collective-permute-start(bf16[2,640,128]{2,1,0:T(8,128)(2,1)S(1)} %get-tuple-element.62.mine), channel_id=1, source_target_pairs={{4,0},{8,4},{12,8},{0,12},{5,1},{9,5},{13,9},{1,13},{6,2},{10,6},{... | collective-permute-start | bytes 983048 | tf_op jit(solution)/shard_map/ppermute | solution.py:505
  20.0 16.1 %collective-permute-start.6 = (bf16[2,640,128]{2,1,0:T(8,128)(2,1)S(1)}, bf16[2,640,128]{2,1,0:T(8,128)(2,1)S(1)}, u32[]{:S(2)}, u32[]{:S(2)}) collective-permute-start(bf16[2,640,128]{2,1,0:T(8,128)(2,1)S(1)} %get-tuple-element.62.mine), channel_id=1, source_target_pairs={{12,0},{0,4},{4,8},{8,12},{13,1},{1,5},{5,9},{9,13},{14,2},{2,6},{... | collective-permute-start | bytes 983048 | tf_op jit(solution)/shard_map/ppermute | solution.py:505
  20.0 21.4 %collective-permute-start.8 = (bf16[2,160,640]{2,1,0:T(8,128)(2,1)S(1)}, bf16[2,160,640]{2,1,0:T(8,128)(2,1)S(1)}, u32[]{:S(2)}, u32[]{:S(2)}) collective-permute-start(bf16[2,160,640]{2,1,0:T(8,128)(2,1)S(1)} %collective-permute-done.1.far0), channel_id=1, source_target_pairs={{0,16},{16,0},{1,17},{17,1},{2,18},{18,2},{3,19},{19,3},{4,20},{20... | collective-permute-start | bytes 1228808 | tf_op jit(solution)/shard_map/ppermute | solution.py:500
  21.6 8.1 %collective-permute-start.9 = (bf16[1,160,640]{2,1,0:T(8,128)(2,1)S(1)}, bf16[1,160,640]{2,1,0:T(8,128)(2,1)S(1)}, u32[]{:S(2)}, u32[]{:S(2)}) collective-permute-start(bf16[1,160,640]{2,1,0:T(8,128)(2,1)S(1)} %constant_dynamic-slice_fusion), channel_id=1, source_target_pairs={{0,2},{1,3},{2,0},{3,1},{4,6},{5,7},{6,4},{7,5},{8,10},{9,11},{10,... | collective-permute-start | bytes 614408 | tf_op jit(solution)/shard_map/ppermute | solution.py:500
  23.1 18.3 %collective-permute-start.11 = (bf16[3,160,640]{2,1,0:T(8,128)(2,1)S(1)}, bf16[3,160,640]{2,1,0:T(8,128)(2,1)S(1)}, u32[]{:S(2)}, u32[]{:S(2)}) collective-permute-start(bf16[3,160,640]{2,1,0:T(8,128)(2,1)S(1)} %slice.18), channel_id=1, source_target_pairs={{0,2},{1,3},{2,0},{3,1},{4,6},{5,7},{6,4},{7,5},{8,10},{9,11},{10,... | collective-permute-start | bytes 1843208 | tf_op jit(solution)/shard_map/ppermute | solution.py:500
  29.7 11.8 %collective-permute-start.10 = (bf16[1,160,640]{2,1,0:T(8,128)(2,1)S(1)}, bf16[1,160,640]{2,1,0:T(8,128)(2,1)S(1)}, u32[]{:S(2)}, u32[]{:S(2)}) collective-permute-start(bf16[1,160,640]{2,1,0:T(8,128)(2,1)S(1)} %collective-permute-done.9.far2), channel_id=1, source_target_pairs={{0,16},{16,0},{1,17},{17,1},{2,18},{18,2},{3,19},{19,3},{4,20},{20... | collective-permute-start | bytes 614408 | tf_op jit(solution)/shard_map/ppermute | solution.py:500
  30.2 11.5 %collective-permute-start.12 = (bf16[2,640,128]{2,1,0:T(8,128)(2,1)S(1)}, bf16[2,640,128]{2,1,0:T(8,128)(2,1)S(1)}, u32[]{:S(2)}, u32[]{:S(2)}) collective-permute-start(bf16[2,640,128]{2,1,0:T(8,128)(2,1)S(1)} %collective-permute-done.5.above), channel_id=1, source_target_pairs={{4,0},{8,4},{12,8},{0,12},{5,1},{9,5},{13,9},{1,13},{6,2},{10,6},{... | collective-permute-start | bytes 983048 | tf_op jit(solution)/shard_map/ppermute | solution.py:505
  57.1 20.8 %collective-permute-start.24 = (bf16[10,640,128]{2,1,0:T(8,128)(2,1)S(1)}, bf16[10,640,128]{2,1,0:T(8,128)(2,1)S(1)}, u32[]{:S(2)}, u32[]{:S(2)}) collective-permute-start(bf16[10,640,128]{2,1,0:T(8,128)(2,1)S(1)} %shard_map.100.h0), channel_id=1, source_target_pairs={{0,1},{1,0},{2,3},{3,2},{4,5},{5,4},{6,7},{7,6},{8,9},{9,8},{10,11... | collective-permute-start | bytes 4915208 | tf_op jit(solution)/shard_map/ppermute | solution.py:500
  57.3 10.0 %collective-permute-start.22 = (bf16[2,640,128]{2,1,0:T(8,128)(2,1)S(1)}, bf16[2,640,128]{2,1,0:T(8,128)(2,1)S(1)}, u32[]{:S(2)}, u32[]{:S(2)}) collective-permute-start(bf16[2,640,128]{2,1,0:T(8,128)(2,1)S(1)} %get-tuple-element.62.mine), channel_id=1, source_target_pairs={{0,2},{1,3},{2,0},{3,1},{4,6},{5,7},{6,4},{7,5},{8,10},{9,11},{10,... | collective-permute-start | bytes 983048 | tf_op jit(solution)/shard_map/ppermute | solution.py:500
  58.8 12.1 %collective-permute-start.21 = (bf16[4,2,160,128]{3,2,1,0:T(8,128)(2,1)S(1)}, bf16[4,2,160,128]{3,2,1,0:T(8,128)(2,1)S(1)}, u32[]{:S(2)}, u32[]{:S(2)}) collective-permute-start(bf16[4,2,160,128]{3,2,1,0:T(8,128)(2,1)S(1)} %pad_maximum_fusion.own), channel_id=1, source_target_pairs={{4,0},{8,4},{12,8},{0,12},{5,1},{9,5},{13,9},{1,13},{6,2},{10,6},{... | collective-permute-start | bytes 983048 | tf_op jit(solution)/shard_map/ppermute | solution.py:505
  62.3 15.6 %collective-permute-start.20 = (bf16[1,640,128]{2,1,0:T(8,128)(2,1)S(1)}, bf16[1,640,128]{2,1,0:T(8,128)(2,1)S(1)}, u32[]{:S(2)}, u32[]{:S(2)}) collective-permute-start(bf16[1,640,128]{2,1,0:T(8,128)(2,1)S(1)} %get-tuple-element.81), channel_id=1, source_target_pairs={{0,4},{4,8},{8,12},{1,5},{5,9},{9,13},{2,6},{6,10},{10,14},{3,7},{... | collective-permute-start | bytes 491528 | tf_op jit(solution)/shard_map/ppermute | solution.py:592
  63.6 14.3 %collective-permute-start.25 = (bf16[1,640,128]{2,1,0:T(8,128)(2,1)S(1)}, bf16[1,640,128]{2,1,0:T(8,128)(2,1)S(1)}, u32[]{:S(2)}, u32[]{:S(2)}) collective-permute-start(bf16[1,640,128]{2,1,0:T(8,128)(2,1)S(1)} %get-tuple-element.80), channel_id=1, source_target_pairs={{4,0},{8,4},{12,8},{5,1},{9,5},{13,9},{6,2},{10,6},{14,10},{7,3},{... | collective-permute-start | bytes 491528 | tf_op jit(solution)/shard_map/ppermute | solution.py:593
  67.3 9.2 %collective-permute-start.23 = (bf16[2,640,128]{2,1,0:T(8,128)(2,1)S(1)}, bf16[2,640,128]{2,1,0:T(8,128)(2,1)S(1)}, u32[]{:S(2)}, u32[]{:S(2)}) collective-permute-start(bf16[2,640,128]{2,1,0:T(8,128)(2,1)S(1)} %collective-permute-done.5.above), channel_id=1, source_target_pairs={{0,2},{1,3},{2,0},{3,1},{4,6},{5,7},{6,4},{7,5},{8,10},{9,11},{10,... | collective-permute-start | bytes 983048 | tf_op jit(solution)/shard_map/ppermute | solution.py:500
  70.9 13.8 %collective-permute-start.26 = (bf16[4,2,160,128]{3,2,1,0:T(8,128)(2,1)S(1)}, bf16[4,2,160,128]{3,2,1,0:T(8,128)(2,1)S(1)}, u32[]{:S(2)}, u32[]{:S(2)}) collective-permute-start(bf16[4,2,160,128]{3,2,1,0:T(8,128)(2,1)S(1)} %pad_maximum_fusion.own), channel_id=1, source_target_pairs={{12,0},{0,4},{4,8},{8,12},{13,1},{1,5},{5,9},{9,13},{14,2},{2,6},{... | collective-permute-start | bytes 983048 | tf_op jit(solution)/shard_map/ppermute | solution.py:505
  76.4 19.7 %collective-permute-start.31 = (bf16[2,640,128]{2,1,0:T(8,128)(2,1)S(1)}, bf16[2,640,128]{2,1,0:T(8,128)(2,1)S(1)}, u32[]{:S(2)}, u32[]{:S(2)}) collective-permute-start(bf16[2,640,128]{2,1,0:T(8,128)(2,1)S(1)} %collective-permute-done.6.below), channel_id=1, source_target_pairs={{0,2},{1,3},{2,0},{3,1},{4,6},{5,7},{6,4},{7,5},{8,10},{9,11},{10,... | collective-permute-start | bytes 983048 | tf_op jit(solution)/shard_map/ppermute | solution.py:500
  84.1 12.0 %collective-permute-start.30 = (bf16[2,640,128]{2,1,0:T(8,128)(2,1)S(1)}, bf16[2,640,128]{2,1,0:T(8,128)(2,1)S(1)}, u32[]{:S(2)}, u32[]{:S(2)}) collective-permute-start(bf16[2,640,128]{2,1,0:T(8,128)(2,1)S(1)} %collective-permute-done.12.beyond), channel_id=1, source_target_pairs={{0,2},{1,3},{2,0},{3,1},{4,6},{5,7},{6,4},{7,5},{8,10},{9,11},{10,... | collective-permute-start | bytes 983048 | tf_op jit(solution)/shard_map/ppermute | solution.py:500
  96.9 10.4 %collective-permute-start.36 = (bf16[4,2,160,128]{3,2,1,0:T(8,128)(2,1)S(1)}, bf16[4,2,160,128]{3,2,1,0:T(8,128)(2,1)S(1)}, u32[]{:S(2)}, u32[]{:S(2)}) collective-permute-start(bf16[4,2,160,128]{3,2,1,0:T(8,128)(2,1)S(1)} %collective-permute-done.21.plus), channel_id=1, source_target_pairs={{4,0},{8,4},{12,8},{0,12},{5,1},{9,5},{13,9},{1,13},{6,2},{10,6},{... | collective-permute-start | bytes 983048 | tf_op jit(solution)/shard_map/ppermute | solution.py:505
  97.5 9.2 %collective-permute-start.33 = (f32[8,640]{1,0:T(8,128)S(1)}, f32[8,640]{1,0:T(8,128)S(1)}, u32[]{:S(2)}, u32[]{:S(2)}) collective-permute-start(f32[8,640]{1,0:T(8,128)S(1)} %get-tuple-element.76.s0), channel_id=1, source_target_pairs={{0,1},{1,0},{2,3},{3,2},{4,5},{5,4},{6,7},{7,6},{8,9},{9,8},{10,11... | collective-permute-start | bytes 61448 | tf_op jit(solution)/shard_map/ppermute | solution.py:500
  97.5 9.2 %collective-permute-start.34 = (f32[8,640]{1,0:T(8,128)S(1)}, f32[8,640]{1,0:T(8,128)S(1)}, u32[]{:S(2)}, u32[]{:S(2)}) collective-permute-start(f32[8,640]{1,0:T(8,128)S(1)} %get-tuple-element.76.s0), channel_id=1, source_target_pairs={{0,2},{1,3},{2,0},{3,1},{4,6},{5,7},{6,4},{7,5},{8,10},{9,11},{10,... | collective-permute-start | bytes 61448 | tf_op jit(solution)/shard_map/ppermute | solution.py:500
  99.0 7.7 %collective-permute-start.35 = (f32[8,640]{1,0:T(8,128)S(1)}, f32[8,640]{1,0:T(8,128)S(1)}, u32[]{:S(2)}, u32[]{:S(2)}) collective-permute-start(f32[8,640]{1,0:T(8,128)S(1)} %get-tuple-element.76.s0), channel_id=1, source_target_pairs={{0,3},{1,2},{2,1},{3,0},{4,7},{5,6},{6,5},{7,4},{8,11},{9,10},{10,... | collective-permute-start | bytes 61448 | tf_op jit(solution)/shard_map/ppermute | solution.py:500
  (20 other events, 107.4 us)

commit v9 on v8

--- a/solution.py
+++ b/solution.py
@@ -604,22 +604,22 @@
 
     across = [swap(after_all(hidden, block23), "wt", 2)]
     across.append(swap(after_all(above, across[0]), "wt", 2))
-    below_across = swap(after_all(below, across[1]), "wt", 2)
-    own_rows = rows_of((place, after_all(hidden, stacked), above, beyond, below))
+    below_across = swap(after_all(below, across[0]), "wt", 2)
+    own_rows = rows_of((after_all(place, low_before), hidden, above, beyond, below))
     other_rows = swap(own_rows, "wt", 1)
 
     grad, sums = call(
         back_kernel,
         (shape((strip_rows, channels, width), F32), shape((8, channels), F32)),
         [VM] * 7,
-        (full, low_before, after_all(low, plus, across[1], other_rows), low_after, res, lat, table),
+        (full, low_before, after_all(low, plus), low_after, res, lat, table),
         [
             pltpu.VMEM((3, 4, LANES, channels), BF16),
             pltpu.VMEM((2 * LANES, channels), F32),
         ],
         mib=12, us=30,
     )
-    sums = after_all(sums, minus)
+    sums = after_all(sums, minus, across[1], below_across, other_rows)
     across += [swap(after_all(beyond, grad), "wt", 2), below_across]
     across_rows = rows_of((after_all(place, sums), *across))
     grad_latents, sums = call(

time: 115 us -> 120 us (1.043)
  waiting for transfers between devices: 34.8 us -> 37.8 us
  starting transfers between devices: 40.6 us -> 42.4 us
    ppermute x1, waiting for transfers between devices: 0.01 us -> 6.07 us  [strips_of_four(): low_before = lax.ppermute(settled[1:2], 'rows', up)]
    ppermute x29, waiting for transfers between devices: 32.5 us -> 29.4 us  [swap(): return lax.ppermute(x, axis, [(i, i ^ mask) for i in range(size)])]
    ppermute x6, starting transfers between devices: 12.2 us -> 13.8 us  [ring(): return lax.ppermute(x, axis, [((i + step) % size, i) for i in range(size)])]
  transfers between devices with their start and end apart: 37 -> 37, of which waited for: 14 -> 13; matrix products, arithmetic and copies ran while one was open for 1% -> 1% of each run, Pallas kernels for 20% -> 19%
where the time goes in v9:
time: 120 us
  starting transfers between devices  42.4 us (35%)
  waiting for transfers between devices  37.8 us (31%)
  Pallas kernels  35.9 us (30%)
  local copies, waits for them, and re-layouts  2.27 us (2%)
    pallas_call x14, Pallas kernels, call(): pl.pallas_call(kernel, out_shape=outs, in_specs=specs, out_specs=jax.tree...  35.9 us
    ppermute x29, waiting for transfers between devices, swap(): return lax.ppermute(x, axis, [(i, i ^ mask) for i in range(size)])  29.4 us
    ppermute x29, starting transfers between devices, swap(): return lax.ppermute(x, axis, [(i, i ^ mask) for i in range(size)])  26 us
    ppermute x6, starting transfers between devices, ring(): return lax.ppermute(x, axis, [((i + step) % size, i) for i in range(size)])  13.8 us
    ppermute x1, waiting for transfers between devices, strips_of_four(): low_before = lax.ppermute(settled[1:2], 'rows', up)  6.07 us
  transfers between devices with their start and end apart: 37, of which 13 were waited for; matrix products, arithmetic and copies ran while one was open for 1% of the time, Pallas kernels for 19%

profile of v9, /device:TPU:0, one launch (start us, length us, event | category | flops | bytes accessed | tf_op | source)
XLA Modules:
  0.0 119.6 jit_solution(17912499031748951261)
XLA Ops:
  2.2 2.6 %collective-permute-start.1 = (bf16[2,160,640]{2,1,0:T(8,128)(2,1)S(1)}, bf16[2,160,640]{2,1,0:T(8,128)(2,1)S(1)}, u32[]{:S(2)}, u32[]{:S(2)}) collective-permute-start(bf16[2,160,640]{2,1,0:T(8,128)(2,1)S(1)} %dynamic-slice_bitcast_fusion), channel_id=1, source_target_pairs={{0,2},{1,3},{2,0},{3,1},{4,6},{5,7},{6,4},{7,5},{8,10},{9,11},{10,... | collective-permute-start | bytes 1228808 | tf_op jit(solution)/shard_map/ppermute | solution.py:500
  7.8 2.6 %collective-permute-start.3 = (f32[8,640]{1,0:T(8,128)S(1)}, f32[8,640]{1,0:T(8,128)S(1)}, u32[]{:S(2)}, u32[]{:S(2)}) collective-permute-start(f32[8,640]{1,0:T(8,128)S(1)} %shard_map.93.s0), channel_id=1, source_target_pairs={{0,8},{4,12},{8,0},{12,4},{1,9},{5,13},{9,1},{13,5},{2,10},{6,14},... | collective-permute-start | bytes 61448 | tf_op jit(solution)/shard_map/ppermute | solution.py:500
  10.8 4.1 %collective-permute-done.1.far0 = bf16[2,160,640]{2,1,0:T(8,128)(2,1)S(1)} collective-permute-done((bf16[2,160,640]{2,1,0:T(8,128)(2,1)S(1)}, bf16[2,160,640]{2,1,0:T(8,128)(2,1)S(1)}, u32[]{:S(2)}, u32[]{:S(2)}) %collective-permute-start.1) | collective-permute-done | bytes 409632 | tf_op jit(solution)/shard_map/ppermute | solution.py:500
  17.1 2.8 %collective-permute-start.5 = (bf16[2,640,128]{2,1,0:T(8,128)(2,1)S(1)}, bf16[2,640,128]{2,1,0:T(8,128)(2,1)S(1)}, u32[]{:S(2)}, u32[]{:S(2)}) collective-permute-start(bf16[2,640,128]{2,1,0:T(8,128)(2,1)S(1)} %get-tuple-element.64.mine), channel_id=1, source_target_pairs={{4,0},{8,4},{12,8},{0,12},{5,1},{9,5},{13,9},{1,13},{6,2},{10,6},{... | collective-permute-start | bytes 983048 | tf_op jit(solution)/shard_map/ppermute | solution.py:505
  23.9 5.7 %collective-permute-done.9.far2 = bf16[1,160,640]{2,1,0:T(8,128)(2,1)S(1)} collective-permute-done((bf16[1,160,640]{2,1,0:T(8,128)(2,1)S(1)}, bf16[1,160,640]{2,1,0:T(8,128)(2,1)S(1)}, u32[]{:S(2)}, u32[]{:S(2)}) %collective-permute-start.9) | collective-permute-done | bytes 204832 | tf_op jit(solution)/shard_map/ppermute | solution.py:500
  30.2 3.8 %collective-permute-start.12 = (bf16[2,640,128]{2,1,0:T(8,128)(2,1)S(1)}, bf16[2,640,128]{2,1,0:T(8,128)(2,1)S(1)}, u32[]{:S(2)}, u32[]{:S(2)}) collective-permute-start(bf16[2,640,128]{2,1,0:T(8,128)(2,1)S(1)} %collective-permute-done.5.above), channel_id=1, source_target_pairs={{4,0},{8,4},{12,8},{0,12},{5,1},{9,5},{13,9},{1,13},{6,2},{10,6},{... | collective-permute-start | bytes 983048 | tf_op jit(solution)/shard_map/ppermute | solution.py:505
  34.0 2.1 %collective-permute-done.6.below = bf16[2,640,128]{2,1,0:T(8,128)(2,1)S(1)} collective-permute-done((bf16[2,640,128]{2,1,0:T(8,128)(2,1)S(1)}, bf16[2,640,128]{2,1,0:T(8,128)(2,1)S(1)}, u32[]{:S(2)}, u32[]{:S(2)}) %collective-permute-start.6) | collective-permute-done | bytes 327712 | tf_op jit(solution)/shard_map/ppermute | solution.py:505
  37.0 4.4 %shard_map.97 = (f32[2,2,160,128]{3,2,1,0:T(8,128)S(1)}, bf16[2,160,128]{2,1,0:T(8,128)(2,1)S(1)}, bf16[2,160,128]{2,1,0:T(8,128)(2,1)S(1)}) custom-call(s32[3]{0:T(128)S(1)} %pad_add_fusion.place, bf16[9,160,640]{2,1,0:T(8,128)(2,1)S(1)} %bitcast.25, bf16[9,160,640]{2,1,0:T(8,128)(2,1)} %collective-permute-done.side, ...), custom_call_target="tpu_custom_call" | custom-call | flops 20000000000 | bytes 60000000 | tf_op jit(solution)/shard_map/pallas_call | solution.py:481
  42.7 2.5 %collective-permute-done.15.diag2 = bf16[1,160,640]{2,1,0:T(8,128)(2,1)S(1)} collective-permute-done((bf16[1,160,640]{2,1,0:T(8,128)(2,1)S(1)}, bf16[1,160,640]{2,1,0:T(8,128)(2,1)S(1)}, u32[]{:S(2)}, u32[]{:S(2)}) %collective-permute-start.15) | collective-permute-done | bytes 204832 | tf_op jit(solution)/shard_map/ppermute | solution.py:500
  45.5 3.2 %shard_map.98 = (f32[2,640,128]{2,1,0:T(8,128)S(1)}, bf16[2,640,128]{2,1,0:T(8,128)(2,1)S(1)}, bf16[2,2,160,128]{3,2,1,0:T(8,128)(2,1)S(1)}) custom-call(s32[3]{0:T(128)S(1)} %pad_add_fusion.place, bf16[2,160,640]{2,1,0:T(8,128)(2,1)S(1)} %collective-permute-done.1.far0, bf16[2,160,640]{2,1,0:T(8,128)(2,1)S(1)} %collective-permute-done.8.far1, ...), custom_call_target="tpu_custom_call" | custom-call | flops 50000000 | bytes 150000 | tf_op jit(solution)/shard_map/pallas_call | solution.py:481
  50.2 4.7 %collective-permute-done.18 = bf16[2,2,160,128]{3,2,1,0:T(8,128)(2,1)S(1)} collective-permute-done((bf16[2,2,160,128]{3,2,1,0:T(8,128)(2,1)S(1)}, bf16[2,2,160,128]{3,2,1,0:T(8,128)(2,1)S(1)}, u32[]{:S(2)}, u32[]{:S(2)}) %collective-permute-start.18) | collective-permute-done | bytes 163872 | tf_op jit(solution)/shard_map/ppermute | solution.py:500
  56.7 3.6 %collective-permute-start.21 = (bf16[4,2,160,128]{3,2,1,0:T(8,128)(2,1)S(1)}, bf16[4,2,160,128]{3,2,1,0:T(8,128)(2,1)S(1)}, u32[]{:S(2)}, u32[]{:S(2)}) collective-permute-start(bf16[4,2,160,128]{3,2,1,0:T(8,128)(2,1)S(1)} %pad_maximum_fusion.own), channel_id=1, source_target_pairs={{4,0},{8,4},{12,8},{0,12},{5,1},{9,5},{13,9},{1,13},{6,2},{10,6},{... | collective-permute-start | bytes 983048 | tf_op jit(solution)/shard_map/ppermute | solution.py:505
  62.9 2.1 %shard_map.99.full = bf16[9,640,640]{2,1,0:T(8,128)(2,1)S(1)} custom-call(s32[3]{0:T(128)S(1)} %pad_add_fusion.place, bf16[9,160,640]{2,1,0:T(8,128)(2,1)S(1)} %bitcast.26, bf16[9,160,640]{2,1,0:T(8,128)(2,1)} %collective-permute-done.side, bf16[2,160,640]{2,1,0:T(8,128)(2,1)S(1)} %collective-permute-done.1.far0, ...), custom_call_target="tpu_custom_call" | custom-call | flops 5000000000 | bytes 15000000 | tf_op jit(solution)/shard_map/pallas_call | solution.py:481
  65.0 6.1 %collective-permute-done.20.before = bf16[1,640,128]{2,1,0:T(8,128)(2,1)S(1)} collective-permute-done((bf16[1,640,128]{2,1,0:T(8,128)(2,1)S(1)}, bf16[1,640,128]{2,1,0:T(8,128)(2,1)S(1)}, u32[]{:S(2)}, u32[]{:S(2)}) %collective-permute-start.20) | collective-permute-done | bytes 163872 | tf_op jit(solution)/shard_map/ppermute | solution.py:592
  74.0 2.5 %collective-permute-start.23 = (bf16[4,2,160,128]{3,2,1,0:T(8,128)(2,1)S(1)}, bf16[4,2,160,128]{3,2,1,0:T(8,128)(2,1)S(1)}, u32[]{:S(2)}, u32[]{:S(2)}) collective-permute-start(bf16[4,2,160,128]{3,2,1,0:T(8,128)(2,1)S(1)} %pad_maximum_fusion.own), channel_id=1, source_target_pairs={{12,0},{0,4},{4,8},{8,12},{13,1},{1,5},{5,9},{9,13},{14,2},{2,6},{... | collective-permute-start | bytes 983048 | tf_op jit(solution)/shard_map/ppermute | solution.py:505
  76.5 6.2 %shard_map.100 = (f32[2,640,128]{2,1,0:T(8,128)S(1)}, f32[8,640]{1,0:T(8,128)S(1)}) custom-call(bf16[9,640,640]{2,1,0:T(8,128)(2,1)S(1)} %shard_map.99.full, bf16[1,640,128]{2,1,0:T(8,128)(2,1)S(1)} %collective-permute-done.20.before, bf16[2,640,128]{2,1,0:T(8,128)(2,1)S(1)} %get-tuple-element.60.low, ...), custom_call_target="tpu_custom_call" | custom-call | flops 30000001024 | bytes 90000000 | tf_op jit(solution)/shard_map/pallas_call | solution.py:481
  83.9 5.6 %collective-permute-done.26.below = bf16[2,640,128]{2,1,0:T(8,128)(2,1)S(1)} collective-permute-done((bf16[2,640,128]{2,1,0:T(8,128)(2,1)S(1)}, bf16[2,640,128]{2,1,0:T(8,128)(2,1)S(1)}, u32[]{:S(2)}, u32[]{:S(2)}) %collective-permute-start.26) | collective-permute-done | bytes 327712 | tf_op jit(solution)/shard_map/ppermute | solution.py:500
  89.5 2.5 %collective-permute-start.28 = (f32[8,640]{1,0:T(8,128)S(1)}, f32[8,640]{1,0:T(8,128)S(1)}, u32[]{:S(2)}, u32[]{:S(2)}) collective-permute-start(f32[8,640]{1,0:T(8,128)S(1)} %get-tuple-element.68.s0), channel_id=1, source_target_pairs={{0,4},{4,0},{8,12},{12,8},{1,5},{5,1},{9,13},{13,9},{2,6},{6,2},{1... | collective-permute-start | bytes 61448 | tf_op jit(solution)/shard_map/ppermute | solution.py:500
  92.0 2.3 %collective-permute-start.29 = (f32[8,640]{1,0:T(8,128)S(1)}, f32[8,640]{1,0:T(8,128)S(1)}, u32[]{:S(2)}, u32[]{:S(2)}) collective-permute-start(f32[8,640]{1,0:T(8,128)S(1)} %get-tuple-element.68.s0), channel_id=1, source_target_pairs={{0,8},{4,12},{8,0},{12,4},{1,9},{5,13},{9,1},{13,5},{2,10},{6,14},... | collective-permute-start | bytes 61448 | tf_op jit(solution)/shard_map/ppermute | solution.py:500
  94.4 1.6 %collective-permute-done.31.beyond = bf16[2,640,128]{2,1,0:T(8,128)(2,1)S(1)} collective-permute-done((bf16[2,640,128]{2,1,0:T(8,128)(2,1)S(1)}, bf16[2,640,128]{2,1,0:T(8,128)(2,1)S(1)}, u32[]{:S(2)}, u32[]{:S(2)}) %collective-permute-start.31) | collective-permute-done | bytes 327712 | tf_op jit(solution)/shard_map/ppermute | solution.py:500
  96.7 3.1 %collective-permute-done.30.s3 = f32[8,640]{1,0:T(8,128)S(1)} collective-permute-done((f32[8,640]{1,0:T(8,128)S(1)}, f32[8,640]{1,0:T(8,128)S(1)}, u32[]{:S(2)}, u32[]{:S(2)}) %collective-permute-start.30) | collective-permute-done | bytes 20512 | tf_op jit(solution)/shard_map/ppermute | solution.py:500
  99.9 1.8 %shard_map.102 = (f32[1280,128]{1,0:T(8,128)}, f32[8,640]{1,0:T(8,128)S(1)}) custom-call(f32[8,640]{1,0:T(8,128)S(1)} %get-tuple-element.68.s0, f32[8,640]{1,0:T(8,128)S(1)} %collective-permute-done.28.s1, f32[8,640]{1,0:T(8,128)S(1)} %collective-permute-done.29.s2, f32[8,640]{1,0:T(8,128)S(1)} %collective-permute-done.30.s3, ...), custom_call_target="tpu_custom_call" | custom-call | flops 50000000 | bytes 150000 | tf_op jit(solution)/shard_map/pallas_call | solution.py:481
  105.2 6.2 %shard_map.104.near = f32[9,160,640]{2,1,0:T(8,128)S(1)} custom-call(s32[3]{0:T(128)S(1)} %pad_add_fusion.place, bf16[4,2,160,128]{3,2,1,0:T(8,128)(2,1)S(1)} %pad_maximum_fusion.own, bf16[4,2,160,128]{3,2,1,0:T(8,128)(2,1)S(1)} %collective-permute-done.21.plus, bf16[4,2,160,128]{3,2,1,0:T(8,128)(2,1)S(1)} %collective-permute-done.23.minus, ...), custom_call_target="tpu_custom_call" | custom-call | flops 30000001024 | bytes 90000000 | tf_op jit(solution)/shard_map/pallas_call | solution.py:481
  112.0 7.4 %shard_map.106 = f32[9,160,640]{2,1,0:T(8,128)} custom-call(s32[3]{0:T(128)S(1)} %pad_add_fusion.place, bf16[4,2,160,128]{3,2,1,0:T(8,128)(2,1)S(1)} %collective-permute-done.21.plus, bf16[4,2,160,128]{3,2,1,0:T(8,128)(2,1)S(1)} %collective-permute-done.23.minus, bf16[4,2,160,128]{3,2,1,0:T(8,128)(2,1)S(1)} %collective-permute-done.36.far, ...), custom_call_target="tpu_custom_call" | custom-call | flops 50000000 | bytes 150000 | tf_op jit(solution)/shard_map/pallas_call | solution.py:481
  (89 shorter events, 28.9 us)
Async XLA Ops:
  0.6 14.3 %collective-permute-start = (bf16[9,160,640]{2,1,0:T(8,128)(2,1)}, bf16[9,160,640]{2,1,0:T(8,128)(2,1)}, u32[]{:S(2)}, u32[]{:S(2)}) collective-permute-start(bf16[9,160,640]{2,1,0:T(8,128)(2,1)} %bitcast.22), channel_id=1, source_target_pairs={{0,1},{1,0},{2,3},{3,2},{4,5},{5,4},{6,7},{7,6},{8,9},{9,8},{10,11... | collective-permute-start | bytes 5529608 | tf_op jit(solution)/shard_map/ppermute | solution.py:500
  2.2 12.7 %collective-permute-start.1 = (bf16[2,160,640]{2,1,0:T(8,128)(2,1)S(1)}, bf16[2,160,640]{2,1,0:T(8,128)(2,1)S(1)}, u32[]{:S(2)}, u32[]{:S(2)}) collective-permute-start(bf16[2,160,640]{2,1,0:T(8,128)(2,1)S(1)} %dynamic-slice_bitcast_fusion), channel_id=1, source_target_pairs={{0,2},{1,3},{2,0},{3,1},{4,6},{5,7},{6,4},{7,5},{8,10},{9,11},{10,... | collective-permute-start | bytes 1228808 | tf_op jit(solution)/shard_map/ppermute | solution.py:500
  6.2 8.7 %collective-permute-start.2 = (f32[8,640]{1,0:T(8,128)S(1)}, f32[8,640]{1,0:T(8,128)S(1)}, u32[]{:S(2)}, u32[]{:S(2)}) collective-permute-start(f32[8,640]{1,0:T(8,128)S(1)} %shard_map.93.s0), channel_id=1, source_target_pairs={{0,4},{4,0},{8,12},{12,8},{1,5},{5,1},{9,13},{13,9},{2,6},{6,2},{1... | collective-permute-start | bytes 61448 | tf_op jit(solution)/shard_map/ppermute | solution.py:500
  17.1 13.1 %collective-permute-start.5 = (bf16[2,640,128]{2,1,0:T(8,128)(2,1)S(1)}, bf16[2,640,128]{2,1,0:T(8,128)(2,1)S(1)}, u32[]{:S(2)}, u32[]{:S(2)}) collective-permute-start(bf16[2,640,128]{2,1,0:T(8,128)(2,1)S(1)} %get-tuple-element.64.mine), channel_id=1, source_target_pairs={{4,0},{8,4},{12,8},{0,12},{5,1},{9,5},{13,9},{1,13},{6,2},{10,6},{... | collective-permute-start | bytes 983048 | tf_op jit(solution)/shard_map/ppermute | solution.py:505
  20.0 16.1 %collective-permute-start.6 = (bf16[2,640,128]{2,1,0:T(8,128)(2,1)S(1)}, bf16[2,640,128]{2,1,0:T(8,128)(2,1)S(1)}, u32[]{:S(2)}, u32[]{:S(2)}) collective-permute-start(bf16[2,640,128]{2,1,0:T(8,128)(2,1)S(1)} %get-tuple-element.64.mine), channel_id=1, source_target_pairs={{12,0},{0,4},{4,8},{8,12},{13,1},{1,5},{5,9},{9,13},{14,2},{2,6},{... | collective-permute-start | bytes 983048 | tf_op jit(solution)/shard_map/ppermute | solution.py:505
  20.0 21.4 %collective-permute-start.8 = (bf16[2,160,640]{2,1,0:T(8,128)(2,1)S(1)}, bf16[2,160,640]{2,1,0:T(8,128)(2,1)S(1)}, u32[]{:S(2)}, u32[]{:S(2)}) collective-permute-start(bf16[2,160,640]{2,1,0:T(8,128)(2,1)S(1)} %collective-permute-done.1.far0), channel_id=1, source_target_pairs={{0,16},{16,0},{1,17},{17,1},{2,18},{18,2},{3,19},{19,3},{4,20},{20... | collective-permute-start | bytes 1228808 | tf_op jit(solution)/shard_map/ppermute | solution.py:500
  21.6 8.1 %collective-permute-start.9 = (bf16[1,160,640]{2,1,0:T(8,128)(2,1)S(1)}, bf16[1,160,640]{2,1,0:T(8,128)(2,1)S(1)}, u32[]{:S(2)}, u32[]{:S(2)}) collective-permute-start(bf16[1,160,640]{2,1,0:T(8,128)(2,1)S(1)} %constant_dynamic-slice_fusion), channel_id=1, source_target_pairs={{0,2},{1,3},{2,0},{3,1},{4,6},{5,7},{6,4},{7,5},{8,10},{9,11},{10,... | collective-permute-start | bytes 614408 | tf_op jit(solution)/shard_map/ppermute | solution.py:500
  23.1 18.3 %collective-permute-start.11 = (bf16[3,160,640]{2,1,0:T(8,128)(2,1)S(1)}, bf16[3,160,640]{2,1,0:T(8,128)(2,1)S(1)}, u32[]{:S(2)}, u32[]{:S(2)}) collective-permute-start(bf16[3,160,640]{2,1,0:T(8,128)(2,1)S(1)} %slice.18), channel_id=1, source_target_pairs={{0,2},{1,3},{2,0},{3,1},{4,6},{5,7},{6,4},{7,5},{8,10},{9,11},{10,... | collective-permute-start | bytes 1843208 | tf_op jit(solution)/shard_map/ppermute | solution.py:500
  29.7 11.8 %collective-permute-start.10 = (bf16[1,160,640]{2,1,0:T(8,128)(2,1)S(1)}, bf16[1,160,640]{2,1,0:T(8,128)(2,1)S(1)}, u32[]{:S(2)}, u32[]{:S(2)}) collective-permute-start(bf16[1,160,640]{2,1,0:T(8,128)(2,1)S(1)} %collective-permute-done.9.far2), channel_id=1, source_target_pairs={{0,16},{16,0},{1,17},{17,1},{2,18},{18,2},{3,19},{19,3},{4,20},{20... | collective-permute-start | bytes 614408 | tf_op jit(solution)/shard_map/ppermute | solution.py:500
  30.2 11.5 %collective-permute-start.12 = (bf16[2,640,128]{2,1,0:T(8,128)(2,1)S(1)}, bf16[2,640,128]{2,1,0:T(8,128)(2,1)S(1)}, u32[]{:S(2)}, u32[]{:S(2)}) collective-permute-start(bf16[2,640,128]{2,1,0:T(8,128)(2,1)S(1)} %collective-permute-done.5.above), channel_id=1, source_target_pairs={{4,0},{8,4},{12,8},{0,12},{5,1},{9,5},{13,9},{1,13},{6,2},{10,6},{... | collective-permute-start | bytes 983048 | tf_op jit(solution)/shard_map/ppermute | solution.py:505
  55.1 16.8 %collective-permute-start.24 = (bf16[2,640,128]{2,1,0:T(8,128)(2,1)S(1)}, bf16[2,640,128]{2,1,0:T(8,128)(2,1)S(1)}, u32[]{:S(2)}, u32[]{:S(2)}) collective-permute-start(bf16[2,640,128]{2,1,0:T(8,128)(2,1)S(1)} %get-tuple-element.64.mine), channel_id=1, source_target_pairs={{0,2},{1,3},{2,0},{3,1},{4,6},{5,7},{6,4},{7,5},{8,10},{9,11},{10,... | collective-permute-start | bytes 983048 | tf_op jit(solution)/shard_map/ppermute | solution.py:500
  56.7 17.3 %collective-permute-start.21 = (bf16[4,2,160,128]{3,2,1,0:T(8,128)(2,1)S(1)}, bf16[4,2,160,128]{3,2,1,0:T(8,128)(2,1)S(1)}, u32[]{:S(2)}, u32[]{:S(2)}) collective-permute-start(bf16[4,2,160,128]{3,2,1,0:T(8,128)(2,1)S(1)} %pad_maximum_fusion.own), channel_id=1, source_target_pairs={{4,0},{8,4},{12,8},{0,12},{5,1},{9,5},{13,9},{1,13},{6,2},{10,6},{... | collective-permute-start | bytes 983048 | tf_op jit(solution)/shard_map/ppermute | solution.py:505
  60.3 10.8 %collective-permute-start.20 = (bf16[1,640,128]{2,1,0:T(8,128)(2,1)S(1)}, bf16[1,640,128]{2,1,0:T(8,128)(2,1)S(1)}, u32[]{:S(2)}, u32[]{:S(2)}) collective-permute-start(bf16[1,640,128]{2,1,0:T(8,128)(2,1)S(1)} %get-tuple-element.81), channel_id=1, source_target_pairs={{0,4},{4,8},{8,12},{1,5},{5,9},{9,13},{2,6},{6,10},{10,14},{3,7},{... | collective-permute-start | bytes 491528 | tf_op jit(solution)/shard_map/ppermute | solution.py:592
  61.6 14.9 %collective-permute-start.22 = (bf16[1,640,128]{2,1,0:T(8,128)(2,1)S(1)}, bf16[1,640,128]{2,1,0:T(8,128)(2,1)S(1)}, u32[]{:S(2)}, u32[]{:S(2)}) collective-permute-start(bf16[1,640,128]{2,1,0:T(8,128)(2,1)S(1)} %get-tuple-element.80), channel_id=1, source_target_pairs={{4,0},{8,4},{12,8},{5,1},{9,5},{13,9},{6,2},{10,6},{14,10},{7,3},{... | collective-permute-start | bytes 491528 | tf_op jit(solution)/shard_map/ppermute | solution.py:593
  71.8 17.7 %collective-permute-start.27 = (bf16[10,640,128]{2,1,0:T(8,128)(2,1)S(1)}, bf16[10,640,128]{2,1,0:T(8,128)(2,1)S(1)}, u32[]{:S(2)}, u32[]{:S(2)}) collective-permute-start(bf16[10,640,128]{2,1,0:T(8,128)(2,1)S(1)} %shard_map.101.h0), channel_id=1, source_target_pairs={{0,1},{1,0},{2,3},{3,2},{4,5},{5,4},{6,7},{7,6},{8,9},{9,8},{10,11... | collective-permute-start | bytes 4915208 | tf_op jit(solution)/shard_map/ppermute | solution.py:500
  71.9 12.0 %collective-permute-start.25 = (bf16[2,640,128]{2,1,0:T(8,128)(2,1)S(1)}, bf16[2,640,128]{2,1,0:T(8,128)(2,1)S(1)}, u32[]{:S(2)}, u32[]{:S(2)}) collective-permute-start(bf16[2,640,128]{2,1,0:T(8,128)(2,1)S(1)} %collective-permute-done.5.above), channel_id=1, source_target_pairs={{0,2},{1,3},{2,0},{3,1},{4,6},{5,7},{6,4},{7,5},{8,10},{9,11},{10,... | collective-permute-start | bytes 983048 | tf_op jit(solution)/shard_map/ppermute | solution.py:500
  73.1 16.4 %collective-permute-start.26 = (bf16[2,640,128]{2,1,0:T(8,128)(2,1)S(1)}, bf16[2,640,128]{2,1,0:T(8,128)(2,1)S(1)}, u32[]{:S(2)}, u32[]{:S(2)}) collective-permute-start(bf16[2,640,128]{2,1,0:T(8,128)(2,1)S(1)} %collective-permute-done.6.below), channel_id=1, source_target_pairs={{0,2},{1,3},{2,0},{3,1},{4,6},{5,7},{6,4},{7,5},{8,10},{9,11},{10,... | collective-permute-start | bytes 983048 | tf_op jit(solution)/shard_map/ppermute | solution.py:500
  74.0 15.5 %collective-permute-start.23 = (bf16[4,2,160,128]{3,2,1,0:T(8,128)(2,1)S(1)}, bf16[4,2,160,128]{3,2,1,0:T(8,128)(2,1)S(1)}, u32[]{:S(2)}, u32[]{:S(2)}) collective-permute-start(bf16[4,2,160,128]{3,2,1,0:T(8,128)(2,1)S(1)} %pad_maximum_fusion.own), channel_id=1, source_target_pairs={{12,0},{0,4},{4,8},{8,12},{13,1},{1,5},{5,9},{9,13},{14,2},{2,6},{... | collective-permute-start | bytes 983048 | tf_op jit(solution)/shard_map/ppermute | solution.py:505
  82.7 13.4 %collective-permute-start.31 = (bf16[2,640,128]{2,1,0:T(8,128)(2,1)S(1)}, bf16[2,640,128]{2,1,0:T(8,128)(2,1)S(1)}, u32[]{:S(2)}, u32[]{:S(2)}) collective-permute-start(bf16[2,640,128]{2,1,0:T(8,128)(2,1)S(1)} %collective-permute-done.12.beyond), channel_id=1, source_target_pairs={{0,2},{1,3},{2,0},{3,1},{4,6},{5,7},{6,4},{7,5},{8,10},{9,11},{10,... | collective-permute-start | bytes 983048 | tf_op jit(solution)/shard_map/ppermute | solution.py:500
  89.5 7.2 %collective-permute-start.28 = (f32[8,640]{1,0:T(8,128)S(1)}, f32[8,640]{1,0:T(8,128)S(1)}, u32[]{:S(2)}, u32[]{:S(2)}) collective-permute-start(f32[8,640]{1,0:T(8,128)S(1)} %get-tuple-element.68.s0), channel_id=1, source_target_pairs={{0,4},{4,0},{8,12},{12,8},{1,5},{5,1},{9,13},{13,9},{2,6},{6,2},{1... | collective-permute-start | bytes 61448 | tf_op jit(solution)/shard_map/ppermute | solution.py:500
  101.7 10.4 %collective-permute-start.36 = (bf16[4,2,160,128]{3,2,1,0:T(8,128)(2,1)S(1)}, bf16[4,2,160,128]{3,2,1,0:T(8,128)(2,1)S(1)}, u32[]{:S(2)}, u32[]{:S(2)}) collective-permute-start(bf16[4,2,160,128]{3,2,1,0:T(8,128)(2,1)S(1)} %collective-permute-done.21.plus), channel_id=1, source_target_pairs={{4,0},{8,4},{12,8},{0,12},{5,1},{9,5},{13,9},{1,13},{6,2},{10,6},{... | collective-permute-start | bytes 983048 | tf_op jit(solution)/shard_map/ppermute | solution.py:505
  102.8 8.6 %collective-permute-start.33 = (f32[8,640]{1,0:T(8,128)S(1)}, f32[8,640]{1,0:T(8,128)S(1)}, u32[]{:S(2)}, u32[]{:S(2)}) collective-permute-start(f32[8,640]{1,0:T(8,128)S(1)} %get-tuple-element.76.s0), channel_id=1, source_target_pairs={{0,1},{1,0},{2,3},{3,2},{4,5},{5,4},{6,7},{7,6},{8,9},{9,8},{10,11... | collective-permute-start | bytes 61448 | tf_op jit(solution)/shard_map/ppermute | solution.py:500
  103.0 8.4 %collective-permute-start.34 = (f32[8,640]{1,0:T(8,128)S(1)}, f32[8,640]{1,0:T(8,128)S(1)}, u32[]{:S(2)}, u32[]{:S(2)}) collective-permute-start(f32[8,640]{1,0:T(8,128)S(1)} %get-tuple-element.76.s0), channel_id=1, source_target_pairs={{0,2},{1,3},{2,0},{3,1},{4,6},{5,7},{6,4},{7,5},{8,10},{9,11},{10,... | collective-permute-start | bytes 61448 | tf_op jit(solution)/shard_map/ppermute | solution.py:500
  104.2 7.2 %collective-permute-start.35 = (f32[8,640]{1,0:T(8,128)S(1)}, f32[8,640]{1,0:T(8,128)S(1)}, u32[]{:S(2)}, u32[]{:S(2)}) collective-permute-start(f32[8,640]{1,0:T(8,128)S(1)} %get-tuple-element.76.s0), channel_id=1, source_target_pairs={{0,3},{1,2},{2,1},{3,0},{4,7},{5,6},{6,5},{7,4},{8,11},{9,10},{10,... | collective-permute-start | bytes 61448 | tf_op jit(solution)/shard_map/ppermute | solution.py:500
  (20 other events, 111.6 us)

commit v10 on v8

--- a/solution.py
+++ b/solution.py
@@ -403,13 +403,15 @@
         out[pl.ds(row, channels, stride=2), :] = res[row] + inverse * change
 
 
-def weight_pair(strip, pair, aligned, one, two, first, spread, lefts, emit):
-    panel, channels = aligned.shape[2], spread[0].shape[1]
+def weight_pair(strip, pair, aligned, one, two, first, images, base, lefts, emit):
+    panel, channels = aligned.shape[2], images[0].shape[1]
     for m in range(2):
-        for k in range(4):
+        for k in range(2):
             for row in range(2):
                 lane = pl.ds((2 * k + row) * LANES, LANES)
-                source = aligned[k, row] if m == 0 else jnp.where(first, one[k, row], two[k, row])
+                source = aligned[base + k, row]
+                if m == 1:
+                    source = jnp.where(first, one[base + k, row], two[base + k, row])
                 moved = shifts(source)
                 for kx in range(3):
                     lefts[(strip & 1) ^ m, kx * panel : (kx + 1) * panel, lane] = moved[2 - kx]
@@ -418,7 +420,7 @@
         product = None
         for m in range(2):
             right = jnp.concatenate(
-                [spread[k][4 * pair + 2 * m + ky + row] for k in range(4) for row in range(2)], axis=1
+                [images[k][4 * pair + 2 * m + ky + row] for k in range(2) for row in range(2)], axis=1
             )
             part = dot_nt(lefts[m], right)
             product = part if product is None else product + part
@@ -446,29 +448,43 @@
             spread[1 + 2 * ((strip + m) & 3) + row] = source[row]
 
 
-def near_weight_kernel(place, own, plus, minus, h0, h1, h2, h3, out, lefts):
+def near_weight_kernel(place, own, plus, minus, h0, h1, out, lefts):
     strip = place[0]
 
     def emit(taps, product):
         out[taps] = product
 
-    weight_pair(strip, strip // 2, own, plus, minus, (strip & 1) == 0, (h0, h1, h2, h3), lefts, emit)
+    weight_pair(strip, strip // 2, own, plus, minus, (strip & 1) == 0, (h0, h1), 0, lefts, emit)
+
+
+def next_weight_kernel(place, own, plus, minus, h2, h3, near, out, lefts):
+    strip = place[0]
+
+    def emit(taps, product):
+        out[taps] = near[taps] + product
+
+    weight_pair(strip, strip // 2, own, plus, minus, (strip & 1) == 0, (h2, h3), 2, lefts, emit)
 
 
 def far_weight_kernel(cells, place, plus, minus, far, h0, h1, h2, h3, near, out, lefts, held, sems):
     strip = place[0]
+    pair, even = 1 - strip // 2, (strip & 1) == 0
 
     def written(taps, slot):
         return pltpu.make_async_copy(held.at[taps], out.at[taps], sems.at[slot])
 
+    def keep(taps, product):
+        held[taps] = product
+
     def emit(taps, product):
-        held[taps] = (near[taps] + product) / cells
+        held[taps] = (near[taps] + (held[taps] + product)) / cells
         for slot in range(3):
             @pl.when(taps.start == 3 * slot)
             def _(slot=slot):
                 written(pl.ds(3 * slot, 3), slot).start()
 
-    weight_pair(strip, 1 - strip // 2, far, minus, plus, (strip & 1) == 0, (h0, h1, h2, h3), lefts, emit)
+    weight_pair(strip, pair, far, minus, plus, even, (h0, h1), 0, lefts, keep)
+    weight_pair(strip, pair, far, minus, plus, even, (h2, h3), 2, lefts, emit)
     for slot in range(3):
         written(pl.ds(3 * slot, 3), slot).wait()
 
@@ -605,48 +621,56 @@
     across = [swap(after_all(hidden, block23), "wt", 2)]
     across.append(swap(after_all(above, across[0]), "wt", 2))
     below_across = swap(after_all(below, across[1]), "wt", 2)
-    own_rows = rows_of((place, after_all(hidden, stacked), above, beyond, below))
+    own_rows = rows_of((after_all(place, full), hidden, above, beyond, below))
     other_rows = swap(own_rows, "wt", 1)
 
     grad, sums = call(
         back_kernel,
         (shape((strip_rows, channels, width), F32), shape((8, channels), F32)),
         [VM] * 7,
-        (full, low_before, after_all(low, plus, across[1], other_rows), low_after, res, lat, table),
+        (full, low_before, after_all(low, plus, across[1]), low_after, res, lat, table),
         [
             pltpu.VMEM((3, 4, LANES, channels), BF16),
             pltpu.VMEM((2 * LANES, channels), F32),
         ],
         mib=12, us=30,
     )
-    sums = after_all(sums, minus)
+    sums = after_all(sums, minus, other_rows, below_across)
     across += [swap(after_all(beyond, grad), "wt", 2), below_across]
     across_rows = rows_of((after_all(place, sums), *across))
+    near_weight = call(
+        near_weight_kernel,
+        shape((9, panel, channels), F32),
+        [SM] + [VM] * 5,
+        (after_all(place, sums), stacked, plus, minus, own_rows, other_rows),
+        [pltpu.VMEM((2, 3 * panel, 4 * LANES), BF16)],
+        mib=14, us=30,
+    )
     grad_latents, sums = call(
         functools.partial(latents_kernel, group_cells),
         (shape((channels * strip_rows, width), F32), shape((8, channels), F32)),
         [VM] * 9,
         (
-            sums, *(swap(sums, "rows", m) for m in (1, 2, 3)),
+            after_all(sums, near_weight), *(swap(sums, "rows", m) for m in (1, 2, 3)),
             given, res, grad, lat, table,
         ),
         us=0.05,
     )
     diag_rows = swap(after_all(across_rows, grad_latents), "wt", 1)
     images = (own_rows, other_rows, across_rows, diag_rows)
-    near_weight = call(
-        near_weight_kernel,
+    next_weight = call(
+        next_weight_kernel,
         shape((9, panel, channels), F32),
-        [SM] + [VM] * 7,
-        (after_all(place, grad_latents), stacked, plus, minus, *images),
-        [pltpu.VMEM((2, 3 * panel, 8 * LANES), BF16)],
-        mib=14, us=30,
+        [SM] + [VM] * 6,
+        (after_all(place, grad_latents), stacked, plus, minus, across_rows, diag_rows, near_weight),
+        [pltpu.VMEM((2, 3 * panel, 4 * LANES), BF16)],
+        mib=16, us=30,
     )
     loss, param_grads = call(
         functools.partial(totals_kernel, total_cells),
         (shape((1, LANES), F32), shape((3, channels), F32)),
         [VM] * 4,
-        (after_all(sums, near_weight), *(swap(sums, "wt", m) for m in (1, 2, 3))),
+        (after_all(sums, next_weight), *(swap(sums, "wt", m) for m in (1, 2, 3))),
         us=0.05,
     )
 
@@ -654,9 +678,9 @@
         functools.partial(far_weight_kernel, total_cells),
         shape((9, panel, channels), F32),
         [SM] + [VM] * 8,
-        (place, plus, minus, far, *images, after_all(near_weight, param_grads)),
+        (place, plus, minus, far, *images, after_all(next_weight, param_grads)),
         [
-            pltpu.VMEM((2, 3 * panel, 8 * LANES), BF16),
+            pltpu.VMEM((2, 3 * panel, 4 * LANES), BF16),
             pltpu.VMEM((9, panel, channels), F32),
             pltpu.SemaphoreType.DMA((3,)),
         ],

time: 115 us -> 113 us (0.983)
  waiting for transfers between devices: 34.8 us -> 28.5 us
  starting transfers between devices: 40.6 us -> 42.9 us
  Pallas kernels: 35.9 us -> 37.9 us
    ppermute x29, waiting for transfers between devices: 32.5 us -> 25.2 us  [swap(): return lax.ppermute(x, axis, [(i, i ^ mask) for i in range(size)])]
    ppermute x6, starting transfers between devices: 12.2 us -> 14.3 us  [ring(): return lax.ppermute(x, axis, [((i + step) % size, i) for i in range(size)])]
    pallas_call x14 -> x15, Pallas kernels: 35.9 us -> 37.9 us  [call(): pl.pallas_call(kernel, out_shape=outs, in_specs=specs, out_specs=jax.tree...]
  transfers between devices with their start and end apart: 37 -> 37, of which waited for: 14 -> 13; matrix products, arithmetic and copies ran while one was open for 1% -> 1% of each run, Pallas kernels for 20% -> 21%
where the time goes in v10:
time: 113 us
  starting transfers between devices  42.9 us (38%)
  Pallas kernels  37.9 us (34%)
  waiting for transfers between devices  28.5 us (25%)
  local copies, waits for them, and re-layouts  2.27 us (2%)
    pallas_call x15, Pallas kernels, call(): pl.pallas_call(kernel, out_shape=outs, in_specs=specs, out_specs=jax.tree...  37.9 us
    ppermute x29, starting transfers between devices, swap(): return lax.ppermute(x, axis, [(i, i ^ mask) for i in range(size)])  26 us
    ppermute x29, waiting for transfers between devices, swap(): return lax.ppermute(x, axis, [(i, i ^ mask) for i in range(size)])  25.2 us
    ppermute x6, starting transfers between devices, ring(): return lax.ppermute(x, axis, [((i + step) % size, i) for i in range(size)])  14.3 us
    ppermute x6, waiting for transfers between devices, ring(): return lax.ppermute(x, axis, [((i + step) % size, i) for i in range(size)])  3.34 us
  transfers between devices with their start and end apart: 37, of which 13 were waited for; matrix products, arithmetic and copies ran while one was open for 1% of the time, Pallas kernels for 21%

profile of v10, /device:TPU:0, one launch (start us, length us, event | category | flops | bytes accessed | tf_op | source)
XLA Modules:
  0.0 112.8 jit_solution(6746119580814091336)
XLA Ops:
  2.2 2.6 %collective-permute-start.1 = (bf16[2,160,640]{2,1,0:T(8,128)(2,1)S(1)}, bf16[2,160,640]{2,1,0:T(8,128)(2,1)S(1)}, u32[]{:S(2)}, u32[]{:S(2)}) collective-permute-start(bf16[2,160,640]{2,1,0:T(8,128)(2,1)S(1)} %dynamic-slice_bitcast_fusion), channel_id=1, source_target_pairs={{0,2},{1,3},{2,0},{3,1},{4,6},{5,7},{6,4},{7,5},{8,10},{9,11},{10,... | collective-permute-start | bytes 1228808 | tf_op jit(solution)/shard_map/ppermute | solution.py:516
  6.2 1.6 %collective-permute-start.2 = (f32[8,640]{1,0:T(8,128)S(1)}, f32[8,640]{1,0:T(8,128)S(1)}, u32[]{:S(2)}, u32[]{:S(2)}) collective-permute-start(f32[8,640]{1,0:T(8,128)S(1)} %shard_map.93.s0), channel_id=1, source_target_pairs={{0,4},{4,0},{8,12},{12,8},{1,5},{5,1},{9,13},{13,9},{2,6},{6,2},{1... | collective-permute-start | bytes 61448 | tf_op jit(solution)/shard_map/ppermute | solution.py:516
  7.8 2.6 %collective-permute-start.3 = (f32[8,640]{1,0:T(8,128)S(1)}, f32[8,640]{1,0:T(8,128)S(1)}, u32[]{:S(2)}, u32[]{:S(2)}) collective-permute-start(f32[8,640]{1,0:T(8,128)S(1)} %shard_map.93.s0), channel_id=1, source_target_pairs={{0,8},{4,12},{8,0},{12,4},{1,9},{5,13},{9,1},{13,5},{2,10},{6,14},... | collective-permute-start | bytes 61448 | tf_op jit(solution)/shard_map/ppermute | solution.py:516
  10.8 4.1 %collective-permute-done.1.far0 = bf16[2,160,640]{2,1,0:T(8,128)(2,1)S(1)} collective-permute-done((bf16[2,160,640]{2,1,0:T(8,128)(2,1)S(1)}, bf16[2,160,640]{2,1,0:T(8,128)(2,1)S(1)}, u32[]{:S(2)}, u32[]{:S(2)}) %collective-permute-start.1) | collective-permute-done | bytes 409632 | tf_op jit(solution)/shard_map/ppermute | solution.py:516
  17.1 2.8 %collective-permute-start.5 = (bf16[2,640,128]{2,1,0:T(8,128)(2,1)S(1)}, bf16[2,640,128]{2,1,0:T(8,128)(2,1)S(1)}, u32[]{:S(2)}, u32[]{:S(2)}) collective-permute-start(bf16[2,640,128]{2,1,0:T(8,128)(2,1)S(1)} %get-tuple-element.61.mine), channel_id=1, source_target_pairs={{4,0},{8,4},{12,8},{0,12},{5,1},{9,5},{13,9},{1,13},{6,2},{10,6},{... | collective-permute-start | bytes 983048 | tf_op jit(solution)/shard_map/ppermute | solution.py:521
  23.9 5.7 %collective-permute-done.9.far2 = bf16[1,160,640]{2,1,0:T(8,128)(2,1)S(1)} collective-permute-done((bf16[1,160,640]{2,1,0:T(8,128)(2,1)S(1)}, bf16[1,160,640]{2,1,0:T(8,128)(2,1)S(1)}, u32[]{:S(2)}, u32[]{:S(2)}) %collective-permute-start.9) | collective-permute-done | bytes 204832 | tf_op jit(solution)/shard_map/ppermute | solution.py:516
  30.2 3.8 %collective-permute-start.12 = (bf16[2,640,128]{2,1,0:T(8,128)(2,1)S(1)}, bf16[2,640,128]{2,1,0:T(8,128)(2,1)S(1)}, u32[]{:S(2)}, u32[]{:S(2)}) collective-permute-start(bf16[2,640,128]{2,1,0:T(8,128)(2,1)S(1)} %collective-permute-done.5.above), channel_id=1, source_target_pairs={{4,0},{8,4},{12,8},{0,12},{5,1},{9,5},{13,9},{1,13},{6,2},{10,6},{... | collective-permute-start | bytes 983048 | tf_op jit(solution)/shard_map/ppermute | solution.py:521
  34.0 2.1 %collective-permute-done.6.below = bf16[2,640,128]{2,1,0:T(8,128)(2,1)S(1)} collective-permute-done((bf16[2,640,128]{2,1,0:T(8,128)(2,1)S(1)}, bf16[2,640,128]{2,1,0:T(8,128)(2,1)S(1)}, u32[]{:S(2)}, u32[]{:S(2)}) %collective-permute-start.6) | collective-permute-done | bytes 327712 | tf_op jit(solution)/shard_map/ppermute | solution.py:521
  37.0 4.4 %shard_map.97 = (f32[2,2,160,128]{3,2,1,0:T(8,128)S(1)}, bf16[2,160,128]{2,1,0:T(8,128)(2,1)S(1)}, bf16[2,160,128]{2,1,0:T(8,128)(2,1)S(1)}) custom-call(s32[3]{0:T(128)S(1)} %pad_add_fusion.place, bf16[9,160,640]{2,1,0:T(8,128)(2,1)S(1)} %bitcast.25, bf16[9,160,640]{2,1,0:T(8,128)(2,1)} %collective-permute-done.side, ...), custom_call_target="tpu_custom_call" | custom-call | flops 20000000000 | bytes 60000000 | tf_op jit(solution)/shard_map/pallas_call | solution.py:497
  42.7 2.5 %collective-permute-done.15.diag2 = bf16[1,160,640]{2,1,0:T(8,128)(2,1)S(1)} collective-permute-done((bf16[1,160,640]{2,1,0:T(8,128)(2,1)S(1)}, bf16[1,160,640]{2,1,0:T(8,128)(2,1)S(1)}, u32[]{:S(2)}, u32[]{:S(2)}) %collective-permute-start.15) | collective-permute-done | bytes 204832 | tf_op jit(solution)/shard_map/ppermute | solution.py:516
  45.5 3.2 %shard_map.98 = (f32[2,640,128]{2,1,0:T(8,128)S(1)}, bf16[2,640,128]{2,1,0:T(8,128)(2,1)S(1)}, bf16[2,2,160,128]{3,2,1,0:T(8,128)(2,1)S(1)}) custom-call(s32[3]{0:T(128)S(1)} %pad_add_fusion.place, bf16[2,160,640]{2,1,0:T(8,128)(2,1)S(1)} %collective-permute-done.1.far0, bf16[2,160,640]{2,1,0:T(8,128)(2,1)S(1)} %collective-permute-done.8.far1, ...), custom_call_target="tpu_custom_call" | custom-call | flops 50000000 | bytes 150000 | tf_op jit(solution)/shard_map/pallas_call | solution.py:497
  50.2 4.7 %collective-permute-done.18 = bf16[2,2,160,128]{3,2,1,0:T(8,128)(2,1)S(1)} collective-permute-done((bf16[2,2,160,128]{3,2,1,0:T(8,128)(2,1)S(1)}, bf16[2,2,160,128]{3,2,1,0:T(8,128)(2,1)S(1)}, u32[]{:S(2)}, u32[]{:S(2)}) %collective-permute-start.18) | collective-permute-done | bytes 163872 | tf_op jit(solution)/shard_map/ppermute | solution.py:516
  56.7 3.6 %collective-permute-start.21 = (bf16[4,2,160,128]{3,2,1,0:T(8,128)(2,1)S(1)}, bf16[4,2,160,128]{3,2,1,0:T(8,128)(2,1)S(1)}, u32[]{:S(2)}, u32[]{:S(2)}) collective-permute-start(bf16[4,2,160,128]{3,2,1,0:T(8,128)(2,1)S(1)} %pad_maximum_fusion.own), channel_id=1, source_target_pairs={{4,0},{8,4},{12,8},{0,12},{5,1},{9,5},{13,9},{1,13},{6,2},{10,6},{... | collective-permute-start | bytes 983048 | tf_op jit(solution)/shard_map/ppermute | solution.py:521
  62.9 2.3 %collective-permute-done.22.mine = bf16[2,640,128]{2,1,0:T(8,128)(2,1)S(1)} collective-permute-done((bf16[2,640,128]{2,1,0:T(8,128)(2,1)S(1)}, bf16[2,640,128]{2,1,0:T(8,128)(2,1)S(1)}, u32[]{:S(2)}, u32[]{:S(2)}) %collective-permute-start.22) | collective-permute-done | bytes 327712 | tf_op jit(solution)/shard_map/ppermute | solution.py:516
  66.7 2.1 %shard_map.99.full = bf16[9,640,640]{2,1,0:T(8,128)(2,1)S(1)} custom-call(s32[3]{0:T(128)S(1)} %pad_add_fusion.place, bf16[9,160,640]{2,1,0:T(8,128)(2,1)S(1)} %bitcast.26, bf16[9,160,640]{2,1,0:T(8,128)(2,1)} %collective-permute-done.side, bf16[2,160,640]{2,1,0:T(8,128)(2,1)S(1)} %collective-permute-done.1.far0, ...), custom_call_target="tpu_custom_call" | custom-call | flops 5000000000 | bytes 15000000 | tf_op jit(solution)/shard_map/pallas_call | solution.py:497
  71.0 3.4 %collective-permute-done.23.above = bf16[2,640,128]{2,1,0:T(8,128)(2,1)S(1)} collective-permute-done((bf16[2,640,128]{2,1,0:T(8,128)(2,1)S(1)}, bf16[2,640,128]{2,1,0:T(8,128)(2,1)S(1)}, u32[]{:S(2)}, u32[]{:S(2)}) %collective-permute-start.23) | collective-permute-done | bytes 327712 | tf_op jit(solution)/shard_map/ppermute | solution.py:516
  76.0 6.2 %shard_map.100 = (f32[2,640,128]{2,1,0:T(8,128)S(1)}, f32[8,640]{1,0:T(8,128)S(1)}) custom-call(bf16[9,640,640]{2,1,0:T(8,128)(2,1)S(1)} %shard_map.99.full, bf16[1,640,128]{2,1,0:T(8,128)(2,1)S(1)} %collective-permute-done.20.before, bf16[2,640,128]{2,1,0:T(8,128)(2,1)S(1)} %get-tuple-element.63.low, ...), custom_call_target="tpu_custom_call" | custom-call | flops 30000001024 | bytes 90000000 | tf_op jit(solution)/shard_map/pallas_call | solution.py:497
  84.3 2.7 %collective-permute-start.29 = (f32[8,640]{1,0:T(8,128)S(1)}, f32[8,640]{1,0:T(8,128)S(1)}, u32[]{:S(2)}, u32[]{:S(2)}) collective-permute-start(f32[8,640]{1,0:T(8,128)S(1)} %get-tuple-element.71.s0), channel_id=1, source_target_pairs={{0,8},{4,12},{8,0},{12,4},{1,9},{5,13},{9,1},{13,5},{2,10},{6,14},... | collective-permute-start | bytes 61448 | tf_op jit(solution)/shard_map/ppermute | solution.py:516
  87.3 3.7 %shard_map.102.near = f32[9,160,640]{2,1,0:T(8,128)S(1)} custom-call(s32[3]{0:T(128)S(1)} %pad_add_fusion.place, bf16[4,2,160,128]{3,2,1,0:T(8,128)(2,1)S(1)} %pad_maximum_fusion.own, bf16[4,2,160,128]{3,2,1,0:T(8,128)(2,1)S(1)} %collective-permute-done.21.plus, bf16[4,2,160,128]{3,2,1,0:T(8,128)(2,1)S(1)} %collective-permute-done.25.minus, ...), custom_call_target="tpu_custom_call" | custom-call | flops 30000001024 | bytes 90000000 | tf_op jit(solution)/shard_map/pallas_call | solution.py:497
  92.5 1.8 %shard_map.103 = (f32[1280,128]{1,0:T(8,128)}, f32[8,640]{1,0:T(8,128)S(1)}) custom-call(f32[8,640]{1,0:T(8,128)S(1)} %get-tuple-element.71.s0, f32[8,640]{1,0:T(8,128)S(1)} %collective-permute-done.28.s1, f32[8,640]{1,0:T(8,128)S(1)} %collective-permute-done.29.s2, f32[8,640]{1,0:T(8,128)S(1)} %collective-permute-done.30.s3, ...), custom_call_target="tpu_custom_call" | custom-call | flops 50000000 | bytes 150000 | tf_op jit(solution)/shard_map/pallas_call | solution.py:497
  94.3 2.7 %collective-permute-start.36 = (bf16[4,2,160,128]{3,2,1,0:T(8,128)(2,1)S(1)}, bf16[4,2,160,128]{3,2,1,0:T(8,128)(2,1)S(1)}, u32[]{:S(2)}, u32[]{:S(2)}) collective-permute-start(bf16[4,2,160,128]{3,2,1,0:T(8,128)(2,1)S(1)} %collective-permute-done.21.plus), channel_id=1, source_target_pairs={{4,0},{8,4},{12,8},{0,12},{5,1},{9,5},{13,9},{1,13},{6,2},{10,6},{... | collective-permute-start | bytes 983048 | tf_op jit(solution)/shard_map/ppermute | solution.py:521
  97.2 1.9 %collective-permute-start.34 = (f32[8,640]{1,0:T(8,128)S(1)}, f32[8,640]{1,0:T(8,128)S(1)}, u32[]{:S(2)}, u32[]{:S(2)}) collective-permute-start(f32[8,640]{1,0:T(8,128)S(1)} %get-tuple-element.78.s0), channel_id=1, source_target_pairs={{0,2},{1,3},{2,0},{3,1},{4,6},{5,7},{6,4},{7,5},{8,10},{9,11},{10,... | collective-permute-start | bytes 61448 | tf_op jit(solution)/shard_map/ppermute | solution.py:516
  99.1 3.8 %shard_map.105.near = f32[9,160,640]{2,1,0:T(8,128)S(1)} custom-call(s32[3]{0:T(128)S(1)} %pad_add_fusion.place, bf16[4,2,160,128]{3,2,1,0:T(8,128)(2,1)S(1)} %pad_maximum_fusion.own, bf16[4,2,160,128]{3,2,1,0:T(8,128)(2,1)S(1)} %collective-permute-done.21.plus, bf16[4,2,160,128]{3,2,1,0:T(8,128)(2,1)S(1)} %collective-permute-done.25.minus, ...), custom_call_target="tpu_custom_call" | custom-call | flops 30000001024 | bytes 90000000 | tf_op jit(solution)/shard_map/pallas_call | solution.py:497
  104.6 8.1 %shard_map.107 = f32[9,160,640]{2,1,0:T(8,128)} custom-call(s32[3]{0:T(128)S(1)} %pad_add_fusion.place, bf16[4,2,160,128]{3,2,1,0:T(8,128)(2,1)S(1)} %collective-permute-done.21.plus, bf16[4,2,160,128]{3,2,1,0:T(8,128)(2,1)S(1)} %collective-permute-done.25.minus, bf16[4,2,160,128]{3,2,1,0:T(8,128)(2,1)S(1)} %collective-permute-done.36.far, ...), custom_call_target="tpu_custom_call" | custom-call | flops 50000000 | bytes 150000 | tf_op jit(solution)/shard_map/pallas_call | solution.py:497
  (90 shorter events, 29.3 us)
Async XLA Ops:
  0.6 14.3 %collective-permute-start = (bf16[9,160,640]{2,1,0:T(8,128)(2,1)}, bf16[9,160,640]{2,1,0:T(8,128)(2,1)}, u32[]{:S(2)}, u32[]{:S(2)}) collective-permute-start(bf16[9,160,640]{2,1,0:T(8,128)(2,1)} %bitcast.22), channel_id=1, source_target_pairs={{0,1},{1,0},{2,3},{3,2},{4,5},{5,4},{6,7},{7,6},{8,9},{9,8},{10,11... | collective-permute-start | bytes 5529608 | tf_op jit(solution)/shard_map/ppermute | solution.py:516
  2.2 12.7 %collective-permute-start.1 = (bf16[2,160,640]{2,1,0:T(8,128)(2,1)S(1)}, bf16[2,160,640]{2,1,0:T(8,128)(2,1)S(1)}, u32[]{:S(2)}, u32[]{:S(2)}) collective-permute-start(bf16[2,160,640]{2,1,0:T(8,128)(2,1)S(1)} %dynamic-slice_bitcast_fusion), channel_id=1, source_target_pairs={{0,2},{1,3},{2,0},{3,1},{4,6},{5,7},{6,4},{7,5},{8,10},{9,11},{10,... | collective-permute-start | bytes 1228808 | tf_op jit(solution)/shard_map/ppermute | solution.py:516
  6.2 8.7 %collective-permute-start.2 = (f32[8,640]{1,0:T(8,128)S(1)}, f32[8,640]{1,0:T(8,128)S(1)}, u32[]{:S(2)}, u32[]{:S(2)}) collective-permute-start(f32[8,640]{1,0:T(8,128)S(1)} %shard_map.93.s0), channel_id=1, source_target_pairs={{0,4},{4,0},{8,12},{12,8},{1,5},{5,1},{9,13},{13,9},{2,6},{6,2},{1... | collective-permute-start | bytes 61448 | tf_op jit(solution)/shard_map/ppermute | solution.py:516
  7.8 7.1 %collective-permute-start.3 = (f32[8,640]{1,0:T(8,128)S(1)}, f32[8,640]{1,0:T(8,128)S(1)}, u32[]{:S(2)}, u32[]{:S(2)}) collective-permute-start(f32[8,640]{1,0:T(8,128)S(1)} %shard_map.93.s0), channel_id=1, source_target_pairs={{0,8},{4,12},{8,0},{12,4},{1,9},{5,13},{9,1},{13,5},{2,10},{6,14},... | collective-permute-start | bytes 61448 | tf_op jit(solution)/shard_map/ppermute | solution.py:516
  17.1 13.1 %collective-permute-start.5 = (bf16[2,640,128]{2,1,0:T(8,128)(2,1)S(1)}, bf16[2,640,128]{2,1,0:T(8,128)(2,1)S(1)}, u32[]{:S(2)}, u32[]{:S(2)}) collective-permute-start(bf16[2,640,128]{2,1,0:T(8,128)(2,1)S(1)} %get-tuple-element.61.mine), channel_id=1, source_target_pairs={{4,0},{8,4},{12,8},{0,12},{5,1},{9,5},{13,9},{1,13},{6,2},{10,6},{... | collective-permute-start | bytes 983048 | tf_op jit(solution)/shard_map/ppermute | solution.py:521
  20.0 16.1 %collective-permute-start.6 = (bf16[2,640,128]{2,1,0:T(8,128)(2,1)S(1)}, bf16[2,640,128]{2,1,0:T(8,128)(2,1)S(1)}, u32[]{:S(2)}, u32[]{:S(2)}) collective-permute-start(bf16[2,640,128]{2,1,0:T(8,128)(2,1)S(1)} %get-tuple-element.61.mine), channel_id=1, source_target_pairs={{12,0},{0,4},{4,8},{8,12},{13,1},{1,5},{5,9},{9,13},{14,2},{2,6},{... | collective-permute-start | bytes 983048 | tf_op jit(solution)/shard_map/ppermute | solution.py:521
  20.0 21.4 %collective-permute-start.8 = (bf16[2,160,640]{2,1,0:T(8,128)(2,1)S(1)}, bf16[2,160,640]{2,1,0:T(8,128)(2,1)S(1)}, u32[]{:S(2)}, u32[]{:S(2)}) collective-permute-start(bf16[2,160,640]{2,1,0:T(8,128)(2,1)S(1)} %collective-permute-done.1.far0), channel_id=1, source_target_pairs={{0,16},{16,0},{1,17},{17,1},{2,18},{18,2},{3,19},{19,3},{4,20},{20... | collective-permute-start | bytes 1228808 | tf_op jit(solution)/shard_map/ppermute | solution.py:516
  21.6 8.1 %collective-permute-start.9 = (bf16[1,160,640]{2,1,0:T(8,128)(2,1)S(1)}, bf16[1,160,640]{2,1,0:T(8,128)(2,1)S(1)}, u32[]{:S(2)}, u32[]{:S(2)}) collective-permute-start(bf16[1,160,640]{2,1,0:T(8,128)(2,1)S(1)} %constant_dynamic-slice_fusion), channel_id=1, source_target_pairs={{0,2},{1,3},{2,0},{3,1},{4,6},{5,7},{6,4},{7,5},{8,10},{9,11},{10,... | collective-permute-start | bytes 614408 | tf_op jit(solution)/shard_map/ppermute | solution.py:516
  23.1 18.3 %collective-permute-start.11 = (bf16[3,160,640]{2,1,0:T(8,128)(2,1)S(1)}, bf16[3,160,640]{2,1,0:T(8,128)(2,1)S(1)}, u32[]{:S(2)}, u32[]{:S(2)}) collective-permute-start(bf16[3,160,640]{2,1,0:T(8,128)(2,1)S(1)} %slice.18), channel_id=1, source_target_pairs={{0,2},{1,3},{2,0},{3,1},{4,6},{5,7},{6,4},{7,5},{8,10},{9,11},{10,... | collective-permute-start | bytes 1843208 | tf_op jit(solution)/shard_map/ppermute | solution.py:516
  29.7 11.8 %collective-permute-start.10 = (bf16[1,160,640]{2,1,0:T(8,128)(2,1)S(1)}, bf16[1,160,640]{2,1,0:T(8,128)(2,1)S(1)}, u32[]{:S(2)}, u32[]{:S(2)}) collective-permute-start(bf16[1,160,640]{2,1,0:T(8,128)(2,1)S(1)} %collective-permute-done.9.far2), channel_id=1, source_target_pairs={{0,16},{16,0},{1,17},{17,1},{2,18},{18,2},{3,19},{19,3},{4,20},{20... | collective-permute-start | bytes 614408 | tf_op jit(solution)/shard_map/ppermute | solution.py:516
  30.2 11.5 %collective-permute-start.12 = (bf16[2,640,128]{2,1,0:T(8,128)(2,1)S(1)}, bf16[2,640,128]{2,1,0:T(8,128)(2,1)S(1)}, u32[]{:S(2)}, u32[]{:S(2)}) collective-permute-start(bf16[2,640,128]{2,1,0:T(8,128)(2,1)S(1)} %collective-permute-done.5.above), channel_id=1, source_target_pairs={{4,0},{8,4},{12,8},{0,12},{5,1},{9,5},{13,9},{1,13},{6,2},{10,6},{... | collective-permute-start | bytes 983048 | tf_op jit(solution)/shard_map/ppermute | solution.py:521
  50.2 6.4 %collective-permute-start.7 = (bf16[2,160,128]{2,1,0:T(8,128)(2,1)S(1)}, bf16[2,160,128]{2,1,0:T(8,128)(2,1)S(1)}, u32[]{:S(2)}, u32[]{:S(2)}) collective-permute-start(bf16[2,160,128]{2,1,0:T(8,128)(2,1)S(1)} %get-tuple-element.48), channel_id=1, source_target_pairs={{0,1},{1,0},{2,3},{3,2},{4,5},{5,4},{6,7},{7,6},{8,9},{9,8},{10,11... | collective-permute-start | bytes 245768 | tf_op jit(solution)/shard_map/ppermute | solution.py:516
  55.1 10.1 %collective-permute-start.22 = (bf16[2,640,128]{2,1,0:T(8,128)(2,1)S(1)}, bf16[2,640,128]{2,1,0:T(8,128)(2,1)S(1)}, u32[]{:S(2)}, u32[]{:S(2)}) collective-permute-start(bf16[2,640,128]{2,1,0:T(8,128)(2,1)S(1)} %get-tuple-element.61.mine), channel_id=1, source_target_pairs={{0,2},{1,3},{2,0},{3,1},{4,6},{5,7},{6,4},{7,5},{8,10},{9,11},{10,... | collective-permute-start | bytes 983048 | tf_op jit(solution)/shard_map/ppermute | solution.py:516
  56.7 12.9 %collective-permute-start.21 = (bf16[4,2,160,128]{3,2,1,0:T(8,128)(2,1)S(1)}, bf16[4,2,160,128]{3,2,1,0:T(8,128)(2,1)S(1)}, u32[]{:S(2)}, u32[]{:S(2)}) collective-permute-start(bf16[4,2,160,128]{3,2,1,0:T(8,128)(2,1)S(1)} %pad_maximum_fusion.own), channel_id=1, source_target_pairs={{4,0},{8,4},{12,8},{0,12},{5,1},{9,5},{13,9},{1,13},{6,2},{10,6},{... | collective-permute-start | bytes 983048 | tf_op jit(solution)/shard_map/ppermute | solution.py:521
  60.3 15.7 %collective-permute-start.20 = (bf16[1,640,128]{2,1,0:T(8,128)(2,1)S(1)}, bf16[1,640,128]{2,1,0:T(8,128)(2,1)S(1)}, u32[]{:S(2)}, u32[]{:S(2)}) collective-permute-start(bf16[1,640,128]{2,1,0:T(8,128)(2,1)S(1)} %get-tuple-element.83), channel_id=1, source_target_pairs={{0,4},{4,8},{8,12},{1,5},{5,9},{9,13},{2,6},{6,10},{10,14},{3,7},{... | collective-permute-start | bytes 491528 | tf_op jit(solution)/shard_map/ppermute | solution.py:608
  61.6 14.4 %collective-permute-start.24 = (bf16[1,640,128]{2,1,0:T(8,128)(2,1)S(1)}, bf16[1,640,128]{2,1,0:T(8,128)(2,1)S(1)}, u32[]{:S(2)}, u32[]{:S(2)}) collective-permute-start(bf16[1,640,128]{2,1,0:T(8,128)(2,1)S(1)} %get-tuple-element.82), channel_id=1, source_target_pairs={{4,0},{8,4},{12,8},{5,1},{9,5},{13,9},{6,2},{10,6},{14,10},{7,3},{... | collective-permute-start | bytes 491528 | tf_op jit(solution)/shard_map/ppermute | solution.py:609
  65.2 9.3 %collective-permute-start.23 = (bf16[2,640,128]{2,1,0:T(8,128)(2,1)S(1)}, bf16[2,640,128]{2,1,0:T(8,128)(2,1)S(1)}, u32[]{:S(2)}, u32[]{:S(2)}) collective-permute-start(bf16[2,640,128]{2,1,0:T(8,128)(2,1)S(1)} %collective-permute-done.5.above), channel_id=1, source_target_pairs={{0,2},{1,3},{2,0},{3,1},{4,6},{5,7},{6,4},{7,5},{8,10},{9,11},{10,... | collective-permute-start | bytes 983048 | tf_op jit(solution)/shard_map/ppermute | solution.py:516
  69.5 13.3 %collective-permute-start.26 = (bf16[10,640,128]{2,1,0:T(8,128)(2,1)S(1)}, bf16[10,640,128]{2,1,0:T(8,128)(2,1)S(1)}, u32[]{:S(2)}, u32[]{:S(2)}) collective-permute-start(bf16[10,640,128]{2,1,0:T(8,128)(2,1)S(1)} %shard_map.101.h0), channel_id=1, source_target_pairs={{0,1},{1,0},{2,3},{3,2},{4,5},{5,4},{6,7},{7,6},{8,9},{9,8},{10,11... | collective-permute-start | bytes 4915208 | tf_op jit(solution)/shard_map/ppermute | solution.py:516
  69.6 13.2 %collective-permute-start.25 = (bf16[4,2,160,128]{3,2,1,0:T(8,128)(2,1)S(1)}, bf16[4,2,160,128]{3,2,1,0:T(8,128)(2,1)S(1)}, u32[]{:S(2)}, u32[]{:S(2)}) collective-permute-start(bf16[4,2,160,128]{3,2,1,0:T(8,128)(2,1)S(1)} %pad_maximum_fusion.own), channel_id=1, source_target_pairs={{12,0},{0,4},{4,8},{8,12},{13,1},{1,5},{5,9},{9,13},{14,2},{2,6},{... | collective-permute-start | bytes 983048 | tf_op jit(solution)/shard_map/ppermute | solution.py:521
  74.5 8.4 %collective-permute-start.27 = (bf16[2,640,128]{2,1,0:T(8,128)(2,1)S(1)}, bf16[2,640,128]{2,1,0:T(8,128)(2,1)S(1)}, u32[]{:S(2)}, u32[]{:S(2)}) collective-permute-start(bf16[2,640,128]{2,1,0:T(8,128)(2,1)S(1)} %collective-permute-done.6.below), channel_id=1, source_target_pairs={{0,2},{1,3},{2,0},{3,1},{4,6},{5,7},{6,4},{7,5},{8,10},{9,11},{10,... | collective-permute-start | bytes 983048 | tf_op jit(solution)/shard_map/ppermute | solution.py:516
  82.2 8.7 %collective-permute-start.31 = (bf16[2,640,128]{2,1,0:T(8,128)(2,1)S(1)}, bf16[2,640,128]{2,1,0:T(8,128)(2,1)S(1)}, u32[]{:S(2)}, u32[]{:S(2)}) collective-permute-start(bf16[2,640,128]{2,1,0:T(8,128)(2,1)S(1)} %collective-permute-done.12.beyond), channel_id=1, source_target_pairs={{0,2},{1,3},{2,0},{3,1},{4,6},{5,7},{6,4},{7,5},{8,10},{9,11},{10,... | collective-permute-start | bytes 983048 | tf_op jit(solution)/shard_map/ppermute | solution.py:516
  82.9 8.8 %collective-permute-start.28 = (f32[8,640]{1,0:T(8,128)S(1)}, f32[8,640]{1,0:T(8,128)S(1)}, u32[]{:S(2)}, u32[]{:S(2)}) collective-permute-start(f32[8,640]{1,0:T(8,128)S(1)} %get-tuple-element.71.s0), channel_id=1, source_target_pairs={{0,4},{4,0},{8,12},{12,8},{1,5},{5,1},{9,13},{13,9},{2,6},{6,2},{1... | collective-permute-start | bytes 61448 | tf_op jit(solution)/shard_map/ppermute | solution.py:516
  84.3 7.4 %collective-permute-start.29 = (f32[8,640]{1,0:T(8,128)S(1)}, f32[8,640]{1,0:T(8,128)S(1)}, u32[]{:S(2)}, u32[]{:S(2)}) collective-permute-start(f32[8,640]{1,0:T(8,128)S(1)} %get-tuple-element.71.s0), channel_id=1, source_target_pairs={{0,8},{4,12},{8,0},{12,4},{1,9},{5,13},{9,1},{13,5},{2,10},{6,14},... | collective-permute-start | bytes 61448 | tf_op jit(solution)/shard_map/ppermute | solution.py:516
  94.3 10.3 %collective-permute-start.36 = (bf16[4,2,160,128]{3,2,1,0:T(8,128)(2,1)S(1)}, bf16[4,2,160,128]{3,2,1,0:T(8,128)(2,1)S(1)}, u32[]{:S(2)}, u32[]{:S(2)}) collective-permute-start(bf16[4,2,160,128]{3,2,1,0:T(8,128)(2,1)S(1)} %collective-permute-done.21.plus), channel_id=1, source_target_pairs={{4,0},{8,4},{12,8},{0,12},{5,1},{9,5},{13,9},{1,13},{6,2},{10,6},{... | collective-permute-start | bytes 983048 | tf_op jit(solution)/shard_map/ppermute | solution.py:521
  (20 other events, 110.2 us)

commit v11 on v10

--- a/solution.py
+++ b/solution.py
@@ -620,7 +620,7 @@
 
     across = [swap(after_all(hidden, block23), "wt", 2)]
     across.append(swap(after_all(above, across[0]), "wt", 2))
-    below_across = swap(after_all(below, across[1]), "wt", 2)
+    below_across = swap(after_all(below, across[0]), "wt", 2)
     own_rows = rows_of((after_all(place, full), hidden, above, beyond, below))
     other_rows = swap(own_rows, "wt", 1)
 
@@ -628,14 +628,14 @@
         back_kernel,
         (shape((strip_rows, channels, width), F32), shape((8, channels), F32)),
         [VM] * 7,
-        (full, low_before, after_all(low, plus, across[1]), low_after, res, lat, table),
+        (full, low_before, after_all(low, plus), low_after, res, lat, table),
         [
             pltpu.VMEM((3, 4, LANES, channels), BF16),
             pltpu.VMEM((2 * LANES, channels), F32),
         ],
         mib=12, us=30,
     )
-    sums = after_all(sums, minus, other_rows, below_across)
+    sums = after_all(sums, minus, other_rows, across[1], below_across)
     across += [swap(after_all(beyond, grad), "wt", 2), below_across]
     across_rows = rows_of((after_all(place, sums), *across))
     near_weight = call(

time: 113 us -> 113 us (level)
  waiting for transfers between devices: 28.5 us -> 24.3 us
  starting transfers between devices: 42.9 us -> 46.3 us
    ppermute x29, waiting for transfers between devices: 25.2 us -> 16.9 us  [swap(): return lax.ppermute(x, axis, [(i, i ^ mask) for i in range(size)])]
    ppermute x29, starting transfers between devices: 26 us -> 28.6 us  [swap(): return lax.ppermute(x, axis, [(i, i ^ mask) for i in range(size)])]
    ppermute x6, waiting for transfers between devices: 3.34 us -> 5.89 us  [ring(): return lax.ppermute(x, axis, [((i + step) % size, i) for i in range(size)])]
    ppermute x1, waiting for transfers between devices: 0.01 us -> 1.54 us  [strips_of_four(): low_before = lax.ppermute(settled[1:2], 'rows', up)]
  transfers between devices with their start and end apart: 37 -> 37, of which waited for: 13 -> 12; matrix products, arithmetic and copies ran while one was open for 1% -> 1% of each run, Pallas kernels for 21% -> 21%
where the time goes in v11:
time: 113 us
  starting transfers between devices  46.3 us (41%)
  Pallas kernels  37.9 us (34%)
  waiting for transfers between devices  24.3 us (22%)
  local copies, waits for them, and re-layouts  3.35 us (3%)
    pallas_call x15, Pallas kernels, call(): pl.pallas_call(kernel, out_shape=outs, in_specs=specs, out_specs=jax.tree...  37.9 us
    ppermute x29, starting transfers between devices, swap(): return lax.ppermute(x, axis, [(i, i ^ mask) for i in range(size)])  28.6 us
    ppermute x29, waiting for transfers between devices, swap(): return lax.ppermute(x, axis, [(i, i ^ mask) for i in range(size)])  16.9 us
    ppermute x6, starting transfers between devices, ring(): return lax.ppermute(x, axis, [((i + step) % size, i) for i in range(size)])  15.1 us
    ppermute x6, waiting for transfers between devices, ring(): return lax.ppermute(x, axis, [((i + step) % size, i) for i in range(size)])  5.89 us
  transfers between devices with their start and end apart: 37, of which 12 were waited for; matrix products, arithmetic and copies ran while one was open for 1% of the time, Pallas kernels for 21%

profile of v11, /device:TPU:0, one launch (start us, length us, event | category | flops | bytes accessed | tf_op | source)
XLA Modules:
  0.0 113.2 jit_solution(6349669095848183556)
XLA Ops:
  2.2 2.6 %collective-permute-start.1 = (bf16[2,160,640]{2,1,0:T(8,128)(2,1)S(1)}, bf16[2,160,640]{2,1,0:T(8,128)(2,1)S(1)}, u32[]{:S(2)}, u32[]{:S(2)}) collective-permute-start(bf16[2,160,640]{2,1,0:T(8,128)(2,1)S(1)} %dynamic-slice_bitcast_fusion), channel_id=1, source_target_pairs={{0,2},{1,3},{2,0},{3,1},{4,6},{5,7},{6,4},{7,5},{8,10},{9,11},{10,... | collective-permute-start | bytes 1228808 | tf_op jit(solution)/shard_map/ppermute | solution.py:516
  6.2 1.6 %collective-permute-start.2 = (f32[8,640]{1,0:T(8,128)S(1)}, f32[8,640]{1,0:T(8,128)S(1)}, u32[]{:S(2)}, u32[]{:S(2)}) collective-permute-start(f32[8,640]{1,0:T(8,128)S(1)} %shard_map.93.s0), channel_id=1, source_target_pairs={{0,4},{4,0},{8,12},{12,8},{1,5},{5,1},{9,13},{13,9},{2,6},{6,2},{1... | collective-permute-start | bytes 61448 | tf_op jit(solution)/shard_map/ppermute | solution.py:516
  7.8 2.6 %collective-permute-start.3 = (f32[8,640]{1,0:T(8,128)S(1)}, f32[8,640]{1,0:T(8,128)S(1)}, u32[]{:S(2)}, u32[]{:S(2)}) collective-permute-start(f32[8,640]{1,0:T(8,128)S(1)} %shard_map.93.s0), channel_id=1, source_target_pairs={{0,8},{4,12},{8,0},{12,4},{1,9},{5,13},{9,1},{13,5},{2,10},{6,14},... | collective-permute-start | bytes 61448 | tf_op jit(solution)/shard_map/ppermute | solution.py:516
  10.8 4.1 %collective-permute-done.1.far0 = bf16[2,160,640]{2,1,0:T(8,128)(2,1)S(1)} collective-permute-done((bf16[2,160,640]{2,1,0:T(8,128)(2,1)S(1)}, bf16[2,160,640]{2,1,0:T(8,128)(2,1)S(1)}, u32[]{:S(2)}, u32[]{:S(2)}) %collective-permute-start.1) | collective-permute-done | bytes 409632 | tf_op jit(solution)/shard_map/ppermute | solution.py:516
  17.1 2.8 %collective-permute-start.5 = (bf16[2,640,128]{2,1,0:T(8,128)(2,1)S(1)}, bf16[2,640,128]{2,1,0:T(8,128)(2,1)S(1)}, u32[]{:S(2)}, u32[]{:S(2)}) collective-permute-start(bf16[2,640,128]{2,1,0:T(8,128)(2,1)S(1)} %get-tuple-element.66.mine), channel_id=1, source_target_pairs={{4,0},{8,4},{12,8},{0,12},{5,1},{9,5},{13,9},{1,13},{6,2},{10,6},{... | collective-permute-start | bytes 983048 | tf_op jit(solution)/shard_map/ppermute | solution.py:521
  25.1 1.8 %collective-permute-done.9.far2 = bf16[1,160,640]{2,1,0:T(8,128)(2,1)S(1)} collective-permute-done((bf16[1,160,640]{2,1,0:T(8,128)(2,1)S(1)}, bf16[1,160,640]{2,1,0:T(8,128)(2,1)S(1)}, u32[]{:S(2)}, u32[]{:S(2)}) %collective-permute-start.9) | collective-permute-done | bytes 204832 | tf_op jit(solution)/shard_map/ppermute | solution.py:516
  26.9 2.6 %collective-permute-start.10 = (bf16[1,160,640]{2,1,0:T(8,128)(2,1)S(1)}, bf16[1,160,640]{2,1,0:T(8,128)(2,1)S(1)}, u32[]{:S(2)}, u32[]{:S(2)}) collective-permute-start(bf16[1,160,640]{2,1,0:T(8,128)(2,1)S(1)} %collective-permute-done.9.far2), channel_id=1, source_target_pairs={{0,16},{16,0},{1,17},{17,1},{2,18},{18,2},{3,19},{19,3},{4,20},{20... | collective-permute-start | bytes 614408 | tf_op jit(solution)/shard_map/ppermute | solution.py:516
  29.4 3.6 %collective-permute-start.12 = (bf16[2,640,128]{2,1,0:T(8,128)(2,1)S(1)}, bf16[2,640,128]{2,1,0:T(8,128)(2,1)S(1)}, u32[]{:S(2)}, u32[]{:S(2)}) collective-permute-start(bf16[2,640,128]{2,1,0:T(8,128)(2,1)S(1)} %collective-permute-done.5.above), channel_id=1, source_target_pairs={{4,0},{8,4},{12,8},{0,12},{5,1},{9,5},{13,9},{1,13},{6,2},{10,6},{... | collective-permute-start | bytes 983048 | tf_op jit(solution)/shard_map/ppermute | solution.py:521
  33.0 3.1 %collective-permute-done.6.below = bf16[2,640,128]{2,1,0:T(8,128)(2,1)S(1)} collective-permute-done((bf16[2,640,128]{2,1,0:T(8,128)(2,1)S(1)}, bf16[2,640,128]{2,1,0:T(8,128)(2,1)S(1)}, u32[]{:S(2)}, u32[]{:S(2)}) %collective-permute-start.6) | collective-permute-done | bytes 327712 | tf_op jit(solution)/shard_map/ppermute | solution.py:521
  37.0 4.4 %shard_map.97 = (f32[2,2,160,128]{3,2,1,0:T(8,128)S(1)}, bf16[2,160,128]{2,1,0:T(8,128)(2,1)S(1)}, bf16[2,160,128]{2,1,0:T(8,128)(2,1)S(1)}) custom-call(s32[3]{0:T(128)S(1)} %pad_add_fusion.place, bf16[9,160,640]{2,1,0:T(8,128)(2,1)S(1)} %bitcast.25, bf16[9,160,640]{2,1,0:T(8,128)(2,1)} %collective-permute-done.side, ...), custom_call_target="tpu_custom_call" | custom-call | flops 20000000000 | bytes 60000000 | tf_op jit(solution)/shard_map/pallas_call | solution.py:497
  42.7 2.5 %collective-permute-done.15.diag2 = bf16[1,160,640]{2,1,0:T(8,128)(2,1)S(1)} collective-permute-done((bf16[1,160,640]{2,1,0:T(8,128)(2,1)S(1)}, bf16[1,160,640]{2,1,0:T(8,128)(2,1)S(1)}, u32[]{:S(2)}, u32[]{:S(2)}) %collective-permute-start.15) | collective-permute-done | bytes 204832 | tf_op jit(solution)/shard_map/ppermute | solution.py:516
  45.5 3.2 %shard_map.98 = (f32[2,640,128]{2,1,0:T(8,128)S(1)}, bf16[2,640,128]{2,1,0:T(8,128)(2,1)S(1)}, bf16[2,2,160,128]{3,2,1,0:T(8,128)(2,1)S(1)}) custom-call(s32[3]{0:T(128)S(1)} %pad_add_fusion.place, bf16[2,160,640]{2,1,0:T(8,128)(2,1)S(1)} %collective-permute-done.1.far0, bf16[2,160,640]{2,1,0:T(8,128)(2,1)S(1)} %collective-permute-done.8.far1, ...), custom_call_target="tpu_custom_call" | custom-call | flops 50000000 | bytes 150000 | tf_op jit(solution)/shard_map/pallas_call | solution.py:497
  50.2 4.7 %collective-permute-done.18 = bf16[2,2,160,128]{3,2,1,0:T(8,128)(2,1)S(1)} collective-permute-done((bf16[2,2,160,128]{3,2,1,0:T(8,128)(2,1)S(1)}, bf16[2,2,160,128]{3,2,1,0:T(8,128)(2,1)S(1)}, u32[]{:S(2)}, u32[]{:S(2)}) %collective-permute-start.18) | collective-permute-done | bytes 163872 | tf_op jit(solution)/shard_map/ppermute | solution.py:516
  56.7 3.6 %collective-permute-start.21 = (bf16[4,2,160,128]{3,2,1,0:T(8,128)(2,1)S(1)}, bf16[4,2,160,128]{3,2,1,0:T(8,128)(2,1)S(1)}, u32[]{:S(2)}, u32[]{:S(2)}) collective-permute-start(bf16[4,2,160,128]{3,2,1,0:T(8,128)(2,1)S(1)} %pad_maximum_fusion.own), channel_id=1, source_target_pairs={{4,0},{8,4},{12,8},{0,12},{5,1},{9,5},{13,9},{1,13},{6,2},{10,6},{... | collective-permute-start | bytes 983048 | tf_op jit(solution)/shard_map/ppermute | solution.py:521
  60.3 2.1 %shard_map.99.full = bf16[9,640,640]{2,1,0:T(8,128)(2,1)S(1)} custom-call(s32[3]{0:T(128)S(1)} %pad_add_fusion.place, bf16[9,160,640]{2,1,0:T(8,128)(2,1)S(1)} %bitcast.26, bf16[9,160,640]{2,1,0:T(8,128)(2,1)} %collective-permute-done.side, bf16[2,160,640]{2,1,0:T(8,128)(2,1)S(1)} %collective-permute-done.1.far0, ...), custom_call_target="tpu_custom_call" | custom-call | flops 5000000000 | bytes 15000000 | tf_op jit(solution)/shard_map/pallas_call | solution.py:497
  71.1 2.5 %collective-permute-start.23 = (bf16[4,2,160,128]{3,2,1,0:T(8,128)(2,1)S(1)}, bf16[4,2,160,128]{3,2,1,0:T(8,128)(2,1)S(1)}, u32[]{:S(2)}, u32[]{:S(2)}) collective-permute-start(bf16[4,2,160,128]{3,2,1,0:T(8,128)(2,1)S(1)} %pad_maximum_fusion.own), channel_id=1, source_target_pairs={{12,0},{0,4},{4,8},{8,12},{13,1},{1,5},{5,9},{9,13},{14,2},{2,6},{... | collective-permute-start | bytes 983048 | tf_op jit(solution)/shard_map/ppermute | solution.py:521
  73.6 6.2 %shard_map.100 = (f32[2,640,128]{2,1,0:T(8,128)S(1)}, f32[8,640]{1,0:T(8,128)S(1)}) custom-call(bf16[9,640,640]{2,1,0:T(8,128)(2,1)S(1)} %shard_map.99.full, bf16[1,640,128]{2,1,0:T(8,128)(2,1)S(1)} %collective-permute-done.20.before, bf16[2,640,128]{2,1,0:T(8,128)(2,1)S(1)} %get-tuple-element.61.low, ...), custom_call_target="tpu_custom_call" | custom-call | flops 30000001024 | bytes 90000000 | tf_op jit(solution)/shard_map/pallas_call | solution.py:497
  81.1 2.4 %collective-permute-done.27.below = bf16[2,640,128]{2,1,0:T(8,128)(2,1)S(1)} collective-permute-done((bf16[2,640,128]{2,1,0:T(8,128)(2,1)S(1)}, bf16[2,640,128]{2,1,0:T(8,128)(2,1)S(1)}, u32[]{:S(2)}, u32[]{:S(2)}) %collective-permute-start.27) | collective-permute-done | bytes 327712 | tf_op jit(solution)/shard_map/ppermute | solution.py:516
  83.4 2.6 %collective-permute-start.28 = (f32[8,640]{1,0:T(8,128)S(1)}, f32[8,640]{1,0:T(8,128)S(1)}, u32[]{:S(2)}, u32[]{:S(2)}) collective-permute-start(f32[8,640]{1,0:T(8,128)S(1)} %get-tuple-element.71.s0), channel_id=1, source_target_pairs={{0,4},{4,0},{8,12},{12,8},{1,5},{5,1},{9,13},{13,9},{2,6},{6,2},{1... | collective-permute-start | bytes 61448 | tf_op jit(solution)/shard_map/ppermute | solution.py:516
  88.5 3.7 %shard_map.102.near = f32[9,160,640]{2,1,0:T(8,128)S(1)} custom-call(s32[3]{0:T(128)S(1)} %pad_add_fusion.place, bf16[4,2,160,128]{3,2,1,0:T(8,128)(2,1)S(1)} %pad_maximum_fusion.own, bf16[4,2,160,128]{3,2,1,0:T(8,128)(2,1)S(1)} %collective-permute-done.21.plus, bf16[4,2,160,128]{3,2,1,0:T(8,128)(2,1)S(1)} %collective-permute-done.23.minus, ...), custom_call_target="tpu_custom_call" | custom-call | flops 30000001024 | bytes 90000000 | tf_op jit(solution)/shard_map/pallas_call | solution.py:497
  92.9 1.8 %shard_map.103 = (f32[1280,128]{1,0:T(8,128)}, f32[8,640]{1,0:T(8,128)S(1)}) custom-call(f32[8,640]{1,0:T(8,128)S(1)} %get-tuple-element.71.s0, f32[8,640]{1,0:T(8,128)S(1)} %collective-permute-done.28.s1, f32[8,640]{1,0:T(8,128)S(1)} %collective-permute-done.29.s2, f32[8,640]{1,0:T(8,128)S(1)} %collective-permute-done.30.s3, ...), custom_call_target="tpu_custom_call" | custom-call | flops 50000000 | bytes 150000 | tf_op jit(solution)/shard_map/pallas_call | solution.py:497
  94.7 2.6 %collective-permute-start.36 = (bf16[4,2,160,128]{3,2,1,0:T(8,128)(2,1)S(1)}, bf16[4,2,160,128]{3,2,1,0:T(8,128)(2,1)S(1)}, u32[]{:S(2)}, u32[]{:S(2)}) collective-permute-start(bf16[4,2,160,128]{3,2,1,0:T(8,128)(2,1)S(1)} %collective-permute-done.21.plus), channel_id=1, source_target_pairs={{4,0},{8,4},{12,8},{0,12},{5,1},{9,5},{13,9},{1,13},{6,2},{10,6},{... | collective-permute-start | bytes 983048 | tf_op jit(solution)/shard_map/ppermute | solution.py:521
  99.1 3.8 %shard_map.105.near = f32[9,160,640]{2,1,0:T(8,128)S(1)} custom-call(s32[3]{0:T(128)S(1)} %pad_add_fusion.place, bf16[4,2,160,128]{3,2,1,0:T(8,128)(2,1)S(1)} %pad_maximum_fusion.own, bf16[4,2,160,128]{3,2,1,0:T(8,128)(2,1)S(1)} %collective-permute-done.21.plus, bf16[4,2,160,128]{3,2,1,0:T(8,128)(2,1)S(1)} %collective-permute-done.23.minus, ...), custom_call_target="tpu_custom_call" | custom-call | flops 30000001024 | bytes 90000000 | tf_op jit(solution)/shard_map/pallas_call | solution.py:497
  104.9 8.1 %shard_map.107 = f32[9,160,640]{2,1,0:T(8,128)} custom-call(s32[3]{0:T(128)S(1)} %pad_add_fusion.place, bf16[4,2,160,128]{3,2,1,0:T(8,128)(2,1)S(1)} %collective-permute-done.21.plus, bf16[4,2,160,128]{3,2,1,0:T(8,128)(2,1)S(1)} %collective-permute-done.23.minus, bf16[4,2,160,128]{3,2,1,0:T(8,128)(2,1)S(1)} %collective-permute-done.36.far, ...), custom_call_target="tpu_custom_call" | custom-call | flops 50000000 | bytes 150000 | tf_op jit(solution)/shard_map/pallas_call | solution.py:497
  (90 shorter events, 33.1 us)
Async XLA Ops:
  0.6 14.3 %collective-permute-start = (bf16[9,160,640]{2,1,0:T(8,128)(2,1)}, bf16[9,160,640]{2,1,0:T(8,128)(2,1)}, u32[]{:S(2)}, u32[]{:S(2)}) collective-permute-start(bf16[9,160,640]{2,1,0:T(8,128)(2,1)} %bitcast.22), channel_id=1, source_target_pairs={{0,1},{1,0},{2,3},{3,2},{4,5},{5,4},{6,7},{7,6},{8,9},{9,8},{10,11... | collective-permute-start | bytes 5529608 | tf_op jit(solution)/shard_map/ppermute | solution.py:516
  2.2 12.7 %collective-permute-start.1 = (bf16[2,160,640]{2,1,0:T(8,128)(2,1)S(1)}, bf16[2,160,640]{2,1,0:T(8,128)(2,1)S(1)}, u32[]{:S(2)}, u32[]{:S(2)}) collective-permute-start(bf16[2,160,640]{2,1,0:T(8,128)(2,1)S(1)} %dynamic-slice_bitcast_fusion), channel_id=1, source_target_pairs={{0,2},{1,3},{2,0},{3,1},{4,6},{5,7},{6,4},{7,5},{8,10},{9,11},{10,... | collective-permute-start | bytes 1228808 | tf_op jit(solution)/shard_map/ppermute | solution.py:516
  6.2 8.7 %collective-permute-start.2 = (f32[8,640]{1,0:T(8,128)S(1)}, f32[8,640]{1,0:T(8,128)S(1)}, u32[]{:S(2)}, u32[]{:S(2)}) collective-permute-start(f32[8,640]{1,0:T(8,128)S(1)} %shard_map.93.s0), channel_id=1, source_target_pairs={{0,4},{4,0},{8,12},{12,8},{1,5},{5,1},{9,13},{13,9},{2,6},{6,2},{1... | collective-permute-start | bytes 61448 | tf_op jit(solution)/shard_map/ppermute | solution.py:516
  7.8 7.1 %collective-permute-start.3 = (f32[8,640]{1,0:T(8,128)S(1)}, f32[8,640]{1,0:T(8,128)S(1)}, u32[]{:S(2)}, u32[]{:S(2)}) collective-permute-start(f32[8,640]{1,0:T(8,128)S(1)} %shard_map.93.s0), channel_id=1, source_target_pairs={{0,8},{4,12},{8,0},{12,4},{1,9},{5,13},{9,1},{13,5},{2,10},{6,14},... | collective-permute-start | bytes 61448 | tf_op jit(solution)/shard_map/ppermute | solution.py:516
  17.1 12.3 %collective-permute-start.5 = (bf16[2,640,128]{2,1,0:T(8,128)(2,1)S(1)}, bf16[2,640,128]{2,1,0:T(8,128)(2,1)S(1)}, u32[]{:S(2)}, u32[]{:S(2)}) collective-permute-start(bf16[2,640,128]{2,1,0:T(8,128)(2,1)S(1)} %get-tuple-element.66.mine), channel_id=1, source_target_pairs={{4,0},{8,4},{12,8},{0,12},{5,1},{9,5},{13,9},{1,13},{6,2},{10,6},{... | collective-permute-start | bytes 983048 | tf_op jit(solution)/shard_map/ppermute | solution.py:521
  20.0 16.1 %collective-permute-start.6 = (bf16[2,640,128]{2,1,0:T(8,128)(2,1)S(1)}, bf16[2,640,128]{2,1,0:T(8,128)(2,1)S(1)}, u32[]{:S(2)}, u32[]{:S(2)}) collective-permute-start(bf16[2,640,128]{2,1,0:T(8,128)(2,1)S(1)} %get-tuple-element.66.mine), channel_id=1, source_target_pairs={{12,0},{0,4},{4,8},{8,12},{13,1},{1,5},{5,9},{9,13},{14,2},{2,6},{... | collective-permute-start | bytes 983048 | tf_op jit(solution)/shard_map/ppermute | solution.py:521
  20.0 6.9 %collective-permute-start.9 = (bf16[1,160,640]{2,1,0:T(8,128)(2,1)S(1)}, bf16[1,160,640]{2,1,0:T(8,128)(2,1)S(1)}, u32[]{:S(2)}, u32[]{:S(2)}) collective-permute-start(bf16[1,160,640]{2,1,0:T(8,128)(2,1)S(1)} %constant_dynamic-slice_fusion), channel_id=1, source_target_pairs={{0,2},{1,3},{2,0},{3,1},{4,6},{5,7},{6,4},{7,5},{8,10},{9,11},{10,... | collective-permute-start | bytes 614408 | tf_op jit(solution)/shard_map/ppermute | solution.py:516
  22.9 18.4 %collective-permute-start.8 = (bf16[2,160,640]{2,1,0:T(8,128)(2,1)S(1)}, bf16[2,160,640]{2,1,0:T(8,128)(2,1)S(1)}, u32[]{:S(2)}, u32[]{:S(2)}) collective-permute-start(bf16[2,160,640]{2,1,0:T(8,128)(2,1)S(1)} %collective-permute-done.1.far0), channel_id=1, source_target_pairs={{0,16},{16,0},{1,17},{17,1},{2,18},{18,2},{3,19},{19,3},{4,20},{20... | collective-permute-start | bytes 1228808 | tf_op jit(solution)/shard_map/ppermute | solution.py:516
  24.5 16.9 %collective-permute-start.11 = (bf16[3,160,640]{2,1,0:T(8,128)(2,1)S(1)}, bf16[3,160,640]{2,1,0:T(8,128)(2,1)S(1)}, u32[]{:S(2)}, u32[]{:S(2)}) collective-permute-start(bf16[3,160,640]{2,1,0:T(8,128)(2,1)S(1)} %slice.18), channel_id=1, source_target_pairs={{0,2},{1,3},{2,0},{3,1},{4,6},{5,7},{6,4},{7,5},{8,10},{9,11},{10,... | collective-permute-start | bytes 1843208 | tf_op jit(solution)/shard_map/ppermute | solution.py:516
  26.9 14.6 %collective-permute-start.10 = (bf16[1,160,640]{2,1,0:T(8,128)(2,1)S(1)}, bf16[1,160,640]{2,1,0:T(8,128)(2,1)S(1)}, u32[]{:S(2)}, u32[]{:S(2)}) collective-permute-start(bf16[1,160,640]{2,1,0:T(8,128)(2,1)S(1)} %collective-permute-done.9.far2), channel_id=1, source_target_pairs={{0,16},{16,0},{1,17},{17,1},{2,18},{18,2},{3,19},{19,3},{4,20},{20... | collective-permute-start | bytes 614408 | tf_op jit(solution)/shard_map/ppermute | solution.py:516
  29.4 12.2 %collective-permute-start.12 = (bf16[2,640,128]{2,1,0:T(8,128)(2,1)S(1)}, bf16[2,640,128]{2,1,0:T(8,128)(2,1)S(1)}, u32[]{:S(2)}, u32[]{:S(2)}) collective-permute-start(bf16[2,640,128]{2,1,0:T(8,128)(2,1)S(1)} %collective-permute-done.5.above), channel_id=1, source_target_pairs={{4,0},{8,4},{12,8},{0,12},{5,1},{9,5},{13,9},{1,13},{6,2},{10,6},{... | collective-permute-start | bytes 983048 | tf_op jit(solution)/shard_map/ppermute | solution.py:521
  50.2 6.4 %collective-permute-start.7 = (bf16[2,160,128]{2,1,0:T(8,128)(2,1)S(1)}, bf16[2,160,128]{2,1,0:T(8,128)(2,1)S(1)}, u32[]{:S(2)}, u32[]{:S(2)}) collective-permute-start(bf16[2,160,128]{2,1,0:T(8,128)(2,1)S(1)} %get-tuple-element.48), channel_id=1, source_target_pairs={{0,1},{1,0},{2,3},{3,2},{4,5},{5,4},{6,7},{7,6},{8,9},{9,8},{10,11... | collective-permute-start | bytes 245768 | tf_op jit(solution)/shard_map/ppermute | solution.py:516
  55.1 10.7 %collective-permute-start.25 = (bf16[2,640,128]{2,1,0:T(8,128)(2,1)S(1)}, bf16[2,640,128]{2,1,0:T(8,128)(2,1)S(1)}, u32[]{:S(2)}, u32[]{:S(2)}) collective-permute-start(bf16[2,640,128]{2,1,0:T(8,128)(2,1)S(1)} %get-tuple-element.66.mine), channel_id=1, source_target_pairs={{0,2},{1,3},{2,0},{3,1},{4,6},{5,7},{6,4},{7,5},{8,10},{9,11},{10,... | collective-permute-start | bytes 983048 | tf_op jit(solution)/shard_map/ppermute | solution.py:516
  56.7 11.7 %collective-permute-start.21 = (bf16[4,2,160,128]{3,2,1,0:T(8,128)(2,1)S(1)}, bf16[4,2,160,128]{3,2,1,0:T(8,128)(2,1)S(1)}, u32[]{:S(2)}, u32[]{:S(2)}) collective-permute-start(bf16[4,2,160,128]{3,2,1,0:T(8,128)(2,1)S(1)} %pad_maximum_fusion.own), channel_id=1, source_target_pairs={{4,0},{8,4},{12,8},{0,12},{5,1},{9,5},{13,9},{1,13},{6,2},{10,6},{... | collective-permute-start | bytes 983048 | tf_op jit(solution)/shard_map/ppermute | solution.py:521
  62.4 8.7 %collective-permute-start.20 = (bf16[1,640,128]{2,1,0:T(8,128)(2,1)S(1)}, bf16[1,640,128]{2,1,0:T(8,128)(2,1)S(1)}, u32[]{:S(2)}, u32[]{:S(2)}) collective-permute-start(bf16[1,640,128]{2,1,0:T(8,128)(2,1)S(1)} %get-tuple-element.83), channel_id=1, source_target_pairs={{0,4},{4,8},{8,12},{1,5},{5,9},{9,13},{2,6},{6,10},{10,14},{3,7},{... | collective-permute-start | bytes 491528 | tf_op jit(solution)/shard_map/ppermute | solution.py:608
  63.7 9.8 %collective-permute-start.22 = (bf16[1,640,128]{2,1,0:T(8,128)(2,1)S(1)}, bf16[1,640,128]{2,1,0:T(8,128)(2,1)S(1)}, u32[]{:S(2)}, u32[]{:S(2)}) collective-permute-start(bf16[1,640,128]{2,1,0:T(8,128)(2,1)S(1)} %get-tuple-element.82), channel_id=1, source_target_pairs={{4,0},{8,4},{12,8},{5,1},{9,5},{13,9},{6,2},{10,6},{14,10},{7,3},{... | collective-permute-start | bytes 491528 | tf_op jit(solution)/shard_map/ppermute | solution.py:609
  65.7 17.7 %collective-permute-start.24 = (bf16[10,640,128]{2,1,0:T(8,128)(2,1)S(1)}, bf16[10,640,128]{2,1,0:T(8,128)(2,1)S(1)}, u32[]{:S(2)}, u32[]{:S(2)}) collective-permute-start(bf16[10,640,128]{2,1,0:T(8,128)(2,1)S(1)} %shard_map.101.h0), channel_id=1, source_target_pairs={{0,1},{1,0},{2,3},{3,2},{4,5},{5,4},{6,7},{7,6},{8,9},{9,8},{10,11... | collective-permute-start | bytes 4915208 | tf_op jit(solution)/shard_map/ppermute | solution.py:516
  65.8 15.2 %collective-permute-start.26 = (bf16[2,640,128]{2,1,0:T(8,128)(2,1)S(1)}, bf16[2,640,128]{2,1,0:T(8,128)(2,1)S(1)}, u32[]{:S(2)}, u32[]{:S(2)}) collective-permute-start(bf16[2,640,128]{2,1,0:T(8,128)(2,1)S(1)} %collective-permute-done.5.above), channel_id=1, source_target_pairs={{0,2},{1,3},{2,0},{3,1},{4,6},{5,7},{6,4},{7,5},{8,10},{9,11},{10,... | collective-permute-start | bytes 983048 | tf_op jit(solution)/shard_map/ppermute | solution.py:516
  68.4 15.0 %collective-permute-start.27 = (bf16[2,640,128]{2,1,0:T(8,128)(2,1)S(1)}, bf16[2,640,128]{2,1,0:T(8,128)(2,1)S(1)}, u32[]{:S(2)}, u32[]{:S(2)}) collective-permute-start(bf16[2,640,128]{2,1,0:T(8,128)(2,1)S(1)} %collective-permute-done.6.below), channel_id=1, source_target_pairs={{0,2},{1,3},{2,0},{3,1},{4,6},{5,7},{6,4},{7,5},{8,10},{9,11},{10,... | collective-permute-start | bytes 983048 | tf_op jit(solution)/shard_map/ppermute | solution.py:516
  71.1 12.3 %collective-permute-start.23 = (bf16[4,2,160,128]{3,2,1,0:T(8,128)(2,1)S(1)}, bf16[4,2,160,128]{3,2,1,0:T(8,128)(2,1)S(1)}, u32[]{:S(2)}, u32[]{:S(2)}) collective-permute-start(bf16[4,2,160,128]{3,2,1,0:T(8,128)(2,1)S(1)} %pad_maximum_fusion.own), channel_id=1, source_target_pairs={{12,0},{0,4},{4,8},{8,12},{13,1},{1,5},{5,9},{9,13},{14,2},{2,6},{... | collective-permute-start | bytes 983048 | tf_op jit(solution)/shard_map/ppermute | solution.py:521
  79.8 12.4 %collective-permute-start.31 = (bf16[2,640,128]{2,1,0:T(8,128)(2,1)S(1)}, bf16[2,640,128]{2,1,0:T(8,128)(2,1)S(1)}, u32[]{:S(2)}, u32[]{:S(2)}) collective-permute-start(bf16[2,640,128]{2,1,0:T(8,128)(2,1)S(1)} %collective-permute-done.12.beyond), channel_id=1, source_target_pairs={{0,2},{1,3},{2,0},{3,1},{4,6},{5,7},{6,4},{7,5},{8,10},{9,11},{10,... | collective-permute-start | bytes 983048 | tf_op jit(solution)/shard_map/ppermute | solution.py:516
  83.4 9.5 %collective-permute-start.28 = (f32[8,640]{1,0:T(8,128)S(1)}, f32[8,640]{1,0:T(8,128)S(1)}, u32[]{:S(2)}, u32[]{:S(2)}) collective-permute-start(f32[8,640]{1,0:T(8,128)S(1)} %get-tuple-element.71.s0), channel_id=1, source_target_pairs={{0,4},{4,0},{8,12},{12,8},{1,5},{5,1},{9,13},{13,9},{2,6},{6,2},{1... | collective-permute-start | bytes 61448 | tf_op jit(solution)/shard_map/ppermute | solution.py:516
  86.1 6.8 %collective-permute-start.29 = (f32[8,640]{1,0:T(8,128)S(1)}, f32[8,640]{1,0:T(8,128)S(1)}, u32[]{:S(2)}, u32[]{:S(2)}) collective-permute-start(f32[8,640]{1,0:T(8,128)S(1)} %get-tuple-element.71.s0), channel_id=1, source_target_pairs={{0,8},{4,12},{8,0},{12,4},{1,9},{5,13},{9,1},{13,5},{2,10},{6,14},... | collective-permute-start | bytes 61448 | tf_op jit(solution)/shard_map/ppermute | solution.py:516
  94.7 10.2 %collective-permute-start.36 = (bf16[4,2,160,128]{3,2,1,0:T(8,128)(2,1)S(1)}, bf16[4,2,160,128]{3,2,1,0:T(8,128)(2,1)S(1)}, u32[]{:S(2)}, u32[]{:S(2)}) collective-permute-start(bf16[4,2,160,128]{3,2,1,0:T(8,128)(2,1)S(1)} %collective-permute-done.21.plus), channel_id=1, source_target_pairs={{4,0},{8,4},{12,8},{0,12},{5,1},{9,5},{13,9},{1,13},{6,2},{10,6},{... | collective-permute-start | bytes 983048 | tf_op jit(solution)/shard_map/ppermute | solution.py:521
  (20 other events, 96.5 us)

commit v12 on v11

--- a/solution.py
+++ b/solution.py
@@ -635,17 +635,17 @@
         ],
         mib=12, us=30,
     )
-    sums = after_all(sums, minus, other_rows, across[1], below_across)
     across += [swap(after_all(beyond, grad), "wt", 2), below_across]
-    across_rows = rows_of((after_all(place, sums), *across))
+    sums = after_all(sums, minus)
     near_weight = call(
         near_weight_kernel,
         shape((9, panel, channels), F32),
         [SM] + [VM] * 5,
-        (after_all(place, sums), stacked, plus, minus, own_rows, other_rows),
+        (after_all(place, sums, across[1], below_across), stacked, plus, minus, own_rows, other_rows),
         [pltpu.VMEM((2, 3 * panel, 4 * LANES), BF16)],
         mib=14, us=30,
     )
+    across_rows = rows_of((after_all(place, near_weight), *across))
     grad_latents, sums = call(
         functools.partial(latents_kernel, group_cells),
         (shape((channels * strip_rows, width), F32), shape((8, channels), F32)),

time: 113 us -> 113 us (level)
  starting transfers between devices: 46.3 us -> 44.9 us
    ppermute x6, waiting for transfers between devices: 5.89 us -> 8.69 us  [ring(): return lax.ppermute(x, axis, [((i + step) % size, i) for i in range(size)])]
    ppermute x29, waiting for transfers between devices: 16.9 us -> 14.6 us  [swap(): return lax.ppermute(x, axis, [(i, i ^ mask) for i in range(size)])]
where the time goes in v12:
time: 113 us; the launch traced here: 112 us
  starting transfers between devices  44.9 us (40%)
  Pallas kernels  37.9 us (34%)
  waiting for transfers between devices  24.8 us (22%)
  local copies, waits for them, and re-layouts  3.35 us (3%)
    pallas_call x15, Pallas kernels, call(): pl.pallas_call(kernel, out_shape=outs, in_specs=specs, out_specs=jax.tree...  37.9 us
    ppermute x29, starting transfers between devices, swap(): return lax.ppermute(x, axis, [(i, i ^ mask) for i in range(size)])  28 us
    ppermute x29, waiting for transfers between devices, swap(): return lax.ppermute(x, axis, [(i, i ^ mask) for i in range(size)])  14.6 us
    ppermute x6, starting transfers between devices, ring(): return lax.ppermute(x, axis, [((i + step) % size, i) for i in range(size)])  14.4 us
    ppermute x6, waiting for transfers between devices, ring(): return lax.ppermute(x, axis, [((i + step) % size, i) for i in range(size)])  8.69 us
  transfers between devices with their start and end apart: 37, of which 12 were waited for; matrix products, arithmetic and copies ran while one was open for 1% of the time, Pallas kernels for 21%

profile of v12, /device:TPU:0, one launch (start us, length us, event | category | flops | bytes accessed | tf_op | source)
XLA Modules:
  0.0 112.2 jit_solution(12478845320954599761)
XLA Ops:
  2.2 2.6 %collective-permute-start.1 = (bf16[2,160,640]{2,1,0:T(8,128)(2,1)S(1)}, bf16[2,160,640]{2,1,0:T(8,128)(2,1)S(1)}, u32[]{:S(2)}, u32[]{:S(2)}) collective-permute-start(bf16[2,160,640]{2,1,0:T(8,128)(2,1)S(1)} %dynamic-slice_bitcast_fusion), channel_id=1, source_target_pairs={{0,2},{1,3},{2,0},{3,1},{4,6},{5,7},{6,4},{7,5},{8,10},{9,11},{10,... | collective-permute-start | bytes 1228808 | tf_op jit(solution)/shard_map/ppermute | solution.py:516
  7.8 2.6 %collective-permute-start.3 = (f32[8,640]{1,0:T(8,128)S(1)}, f32[8,640]{1,0:T(8,128)S(1)}, u32[]{:S(2)}, u32[]{:S(2)}) collective-permute-start(f32[8,640]{1,0:T(8,128)S(1)} %shard_map.93.s0), channel_id=1, source_target_pairs={{0,8},{4,12},{8,0},{12,4},{1,9},{5,13},{9,1},{13,5},{2,10},{6,14},... | collective-permute-start | bytes 61448 | tf_op jit(solution)/shard_map/ppermute | solution.py:516
  10.8 4.1 %collective-permute-done.1.far0 = bf16[2,160,640]{2,1,0:T(8,128)(2,1)S(1)} collective-permute-done((bf16[2,160,640]{2,1,0:T(8,128)(2,1)S(1)}, bf16[2,160,640]{2,1,0:T(8,128)(2,1)S(1)}, u32[]{:S(2)}, u32[]{:S(2)}) %collective-permute-start.1) | collective-permute-done | bytes 409632 | tf_op jit(solution)/shard_map/ppermute | solution.py:516
  17.1 2.8 %collective-permute-start.5 = (bf16[2,640,128]{2,1,0:T(8,128)(2,1)S(1)}, bf16[2,640,128]{2,1,0:T(8,128)(2,1)S(1)}, u32[]{:S(2)}, u32[]{:S(2)}) collective-permute-start(bf16[2,640,128]{2,1,0:T(8,128)(2,1)S(1)} %get-tuple-element.67.mine), channel_id=1, source_target_pairs={{4,0},{8,4},{12,8},{0,12},{5,1},{9,5},{13,9},{1,13},{6,2},{10,6},{... | collective-permute-start | bytes 983048 | tf_op jit(solution)/shard_map/ppermute | solution.py:521
  25.1 1.8 %collective-permute-done.9.far2 = bf16[1,160,640]{2,1,0:T(8,128)(2,1)S(1)} collective-permute-done((bf16[1,160,640]{2,1,0:T(8,128)(2,1)S(1)}, bf16[1,160,640]{2,1,0:T(8,128)(2,1)S(1)}, u32[]{:S(2)}, u32[]{:S(2)}) %collective-permute-start.9) | collective-permute-done | bytes 204832 | tf_op jit(solution)/shard_map/ppermute | solution.py:516
  26.9 2.6 %collective-permute-start.10 = (bf16[1,160,640]{2,1,0:T(8,128)(2,1)S(1)}, bf16[1,160,640]{2,1,0:T(8,128)(2,1)S(1)}, u32[]{:S(2)}, u32[]{:S(2)}) collective-permute-start(bf16[1,160,640]{2,1,0:T(8,128)(2,1)S(1)} %collective-permute-done.9.far2), channel_id=1, source_target_pairs={{0,16},{16,0},{1,17},{17,1},{2,18},{18,2},{3,19},{19,3},{4,20},{20... | collective-permute-start | bytes 614408 | tf_op jit(solution)/shard_map/ppermute | solution.py:516
  29.4 3.6 %collective-permute-start.12 = (bf16[2,640,128]{2,1,0:T(8,128)(2,1)S(1)}, bf16[2,640,128]{2,1,0:T(8,128)(2,1)S(1)}, u32[]{:S(2)}, u32[]{:S(2)}) collective-permute-start(bf16[2,640,128]{2,1,0:T(8,128)(2,1)S(1)} %collective-permute-done.5.above), channel_id=1, source_target_pairs={{4,0},{8,4},{12,8},{0,12},{5,1},{9,5},{13,9},{1,13},{6,2},{10,6},{... | collective-permute-start | bytes 983048 | tf_op jit(solution)/shard_map/ppermute | solution.py:521
  33.0 3.1 %collective-permute-done.6.below = bf16[2,640,128]{2,1,0:T(8,128)(2,1)S(1)} collective-permute-done((bf16[2,640,128]{2,1,0:T(8,128)(2,1)S(1)}, bf16[2,640,128]{2,1,0:T(8,128)(2,1)S(1)}, u32[]{:S(2)}, u32[]{:S(2)}) %collective-permute-start.6) | collective-permute-done | bytes 327712 | tf_op jit(solution)/shard_map/ppermute | solution.py:521
  37.0 4.4 %shard_map.97 = (f32[2,2,160,128]{3,2,1,0:T(8,128)S(1)}, bf16[2,160,128]{2,1,0:T(8,128)(2,1)S(1)}, bf16[2,160,128]{2,1,0:T(8,128)(2,1)S(1)}) custom-call(s32[3]{0:T(128)S(1)} %pad_add_fusion.place, bf16[9,160,640]{2,1,0:T(8,128)(2,1)S(1)} %bitcast.25, bf16[9,160,640]{2,1,0:T(8,128)(2,1)} %collective-permute-done.side, ...), custom_call_target="tpu_custom_call" | custom-call | flops 20000000000 | bytes 60000000 | tf_op jit(solution)/shard_map/pallas_call | solution.py:497
  42.7 2.5 %collective-permute-done.15.diag2 = bf16[1,160,640]{2,1,0:T(8,128)(2,1)S(1)} collective-permute-done((bf16[1,160,640]{2,1,0:T(8,128)(2,1)S(1)}, bf16[1,160,640]{2,1,0:T(8,128)(2,1)S(1)}, u32[]{:S(2)}, u32[]{:S(2)}) %collective-permute-start.15) | collective-permute-done | bytes 204832 | tf_op jit(solution)/shard_map/ppermute | solution.py:516
  45.5 3.2 %shard_map.98 = (f32[2,640,128]{2,1,0:T(8,128)S(1)}, bf16[2,640,128]{2,1,0:T(8,128)(2,1)S(1)}, bf16[2,2,160,128]{3,2,1,0:T(8,128)(2,1)S(1)}) custom-call(s32[3]{0:T(128)S(1)} %pad_add_fusion.place, bf16[2,160,640]{2,1,0:T(8,128)(2,1)S(1)} %collective-permute-done.1.far0, bf16[2,160,640]{2,1,0:T(8,128)(2,1)S(1)} %collective-permute-done.8.far1, ...), custom_call_target="tpu_custom_call" | custom-call | flops 50000000 | bytes 150000 | tf_op jit(solution)/shard_map/pallas_call | solution.py:497
  50.2 4.7 %collective-permute-done.18 = bf16[2,2,160,128]{3,2,1,0:T(8,128)(2,1)S(1)} collective-permute-done((bf16[2,2,160,128]{3,2,1,0:T(8,128)(2,1)S(1)}, bf16[2,2,160,128]{3,2,1,0:T(8,128)(2,1)S(1)}, u32[]{:S(2)}, u32[]{:S(2)}) %collective-permute-start.18) | collective-permute-done | bytes 163872 | tf_op jit(solution)/shard_map/ppermute | solution.py:516
  56.7 3.6 %collective-permute-start.21 = (bf16[4,2,160,128]{3,2,1,0:T(8,128)(2,1)S(1)}, bf16[4,2,160,128]{3,2,1,0:T(8,128)(2,1)S(1)}, u32[]{:S(2)}, u32[]{:S(2)}) collective-permute-start(bf16[4,2,160,128]{3,2,1,0:T(8,128)(2,1)S(1)} %pad_maximum_fusion.own), channel_id=1, source_target_pairs={{4,0},{8,4},{12,8},{0,12},{5,1},{9,5},{13,9},{1,13},{6,2},{10,6},{... | collective-permute-start | bytes 983048 | tf_op jit(solution)/shard_map/ppermute | solution.py:521
  60.3 2.1 %shard_map.99.full = bf16[9,640,640]{2,1,0:T(8,128)(2,1)S(1)} custom-call(s32[3]{0:T(128)S(1)} %pad_add_fusion.place, bf16[9,160,640]{2,1,0:T(8,128)(2,1)S(1)} %bitcast.26, bf16[9,160,640]{2,1,0:T(8,128)(2,1)} %collective-permute-done.side, bf16[2,160,640]{2,1,0:T(8,128)(2,1)S(1)} %collective-permute-done.1.far0, ...), custom_call_target="tpu_custom_call" | custom-call | flops 5000000000 | bytes 15000000 | tf_op jit(solution)/shard_map/pallas_call | solution.py:497
  71.1 2.5 %collective-permute-start.23 = (bf16[4,2,160,128]{3,2,1,0:T(8,128)(2,1)S(1)}, bf16[4,2,160,128]{3,2,1,0:T(8,128)(2,1)S(1)}, u32[]{:S(2)}, u32[]{:S(2)}) collective-permute-start(bf16[4,2,160,128]{3,2,1,0:T(8,128)(2,1)S(1)} %pad_maximum_fusion.own), channel_id=1, source_target_pairs={{12,0},{0,4},{4,8},{8,12},{13,1},{1,5},{5,9},{9,13},{14,2},{2,6},{... | collective-permute-start | bytes 983048 | tf_op jit(solution)/shard_map/ppermute | solution.py:521
  73.6 6.2 %shard_map.100 = (f32[2,640,128]{2,1,0:T(8,128)S(1)}, f32[8,640]{1,0:T(8,128)S(1)}) custom-call(bf16[9,640,640]{2,1,0:T(8,128)(2,1)S(1)} %shard_map.99.full, bf16[1,640,128]{2,1,0:T(8,128)(2,1)S(1)} %collective-permute-done.20.before, bf16[2,640,128]{2,1,0:T(8,128)(2,1)S(1)} %get-tuple-element.62.low, ...), custom_call_target="tpu_custom_call" | custom-call | flops 30000001024 | bytes 90000000 | tf_op jit(solution)/shard_map/pallas_call | solution.py:497
  81.0 2.2 %collective-permute-done.23.minus = bf16[4,2,160,128]{3,2,1,0:T(8,128)(2,1)S(1)} collective-permute-done((bf16[4,2,160,128]{3,2,1,0:T(8,128)(2,1)S(1)}, bf16[4,2,160,128]{3,2,1,0:T(8,128)(2,1)S(1)}, u32[]{:S(2)}, u32[]{:S(2)}) %collective-permute-start.23) | collective-permute-done | bytes 327712 | tf_op jit(solution)/shard_map/ppermute | solution.py:521
  83.3 2.3 %collective-permute-start.29 = (f32[8,640]{1,0:T(8,128)S(1)}, f32[8,640]{1,0:T(8,128)S(1)}, u32[]{:S(2)}, u32[]{:S(2)}) collective-permute-start(f32[8,640]{1,0:T(8,128)S(1)} %get-tuple-element.72.s0), channel_id=1, source_target_pairs={{0,8},{4,12},{8,0},{12,4},{1,9},{5,13},{9,1},{13,5},{2,10},{6,14},... | collective-permute-start | bytes 61448 | tf_op jit(solution)/shard_map/ppermute | solution.py:516
  85.6 2.1 %collective-permute-start.30 = (f32[8,640]{1,0:T(8,128)S(1)}, f32[8,640]{1,0:T(8,128)S(1)}, u32[]{:S(2)}, u32[]{:S(2)}) collective-permute-start(f32[8,640]{1,0:T(8,128)S(1)} %get-tuple-element.72.s0), channel_id=1, source_target_pairs={{0,12},{4,8},{8,4},{12,0},{1,13},{5,9},{9,5},{13,1},{2,14},{6,10},... | collective-permute-start | bytes 61448 | tf_op jit(solution)/shard_map/ppermute | solution.py:516
  87.7 3.7 %shard_map.102.near = f32[9,160,640]{2,1,0:T(8,128)S(1)} custom-call(s32[3]{0:T(128)S(1)} %pad_add_fusion.place, bf16[4,2,160,128]{3,2,1,0:T(8,128)(2,1)S(1)} %pad_maximum_fusion.own, bf16[4,2,160,128]{3,2,1,0:T(8,128)(2,1)S(1)} %collective-permute-done.21.plus, bf16[4,2,160,128]{3,2,1,0:T(8,128)(2,1)S(1)} %collective-permute-done.23.minus, ...), custom_call_target="tpu_custom_call" | custom-call | flops 30000001024 | bytes 90000000 | tf_op jit(solution)/shard_map/pallas_call | solution.py:497
  93.9 1.9 %collective-permute-start.36 = (bf16[4,2,160,128]{3,2,1,0:T(8,128)(2,1)S(1)}, bf16[4,2,160,128]{3,2,1,0:T(8,128)(2,1)S(1)}, u32[]{:S(2)}, u32[]{:S(2)}) collective-permute-start(bf16[4,2,160,128]{3,2,1,0:T(8,128)(2,1)S(1)} %collective-permute-done.21.plus), channel_id=1, source_target_pairs={{4,0},{8,4},{12,8},{0,12},{5,1},{9,5},{13,9},{1,13},{6,2},{10,6},{... | collective-permute-start | bytes 983048 | tf_op jit(solution)/shard_map/ppermute | solution.py:521
  97.6 3.8 %shard_map.105.near = f32[9,160,640]{2,1,0:T(8,128)S(1)} custom-call(s32[3]{0:T(128)S(1)} %pad_add_fusion.place, bf16[4,2,160,128]{3,2,1,0:T(8,128)(2,1)S(1)} %pad_maximum_fusion.own, bf16[4,2,160,128]{3,2,1,0:T(8,128)(2,1)S(1)} %collective-permute-done.21.plus, bf16[4,2,160,128]{3,2,1,0:T(8,128)(2,1)S(1)} %collective-permute-done.23.minus, ...), custom_call_target="tpu_custom_call" | custom-call | flops 30000001024 | bytes 90000000 | tf_op jit(solution)/shard_map/pallas_call | solution.py:497
  102.1 1.9 %collective-permute-done.36.far = bf16[4,2,160,128]{3,2,1,0:T(8,128)(2,1)S(1)} collective-permute-done((bf16[4,2,160,128]{3,2,1,0:T(8,128)(2,1)S(1)}, bf16[4,2,160,128]{3,2,1,0:T(8,128)(2,1)S(1)}, u32[]{:S(2)}, u32[]{:S(2)}) %collective-permute-start.36) | collective-permute-done | bytes 327712 | tf_op jit(solution)/shard_map/ppermute | solution.py:521
  104.0 8.1 %shard_map.107 = f32[9,160,640]{2,1,0:T(8,128)} custom-call(s32[3]{0:T(128)S(1)} %pad_add_fusion.place, bf16[4,2,160,128]{3,2,1,0:T(8,128)(2,1)S(1)} %collective-permute-done.21.plus, bf16[4,2,160,128]{3,2,1,0:T(8,128)(2,1)S(1)} %collective-permute-done.23.minus, bf16[4,2,160,128]{3,2,1,0:T(8,128)(2,1)S(1)} %collective-permute-done.36.far, ...), custom_call_target="tpu_custom_call" | custom-call | flops 50000000 | bytes 150000 | tf_op jit(solution)/shard_map/pallas_call | solution.py:497
  (90 shorter events, 32.8 us)
Async XLA Ops:
  0.6 14.3 %collective-permute-start = (bf16[9,160,640]{2,1,0:T(8,128)(2,1)}, bf16[9,160,640]{2,1,0:T(8,128)(2,1)}, u32[]{:S(2)}, u32[]{:S(2)}) collective-permute-start(bf16[9,160,640]{2,1,0:T(8,128)(2,1)} %bitcast.22), channel_id=1, source_target_pairs={{0,1},{1,0},{2,3},{3,2},{4,5},{5,4},{6,7},{7,6},{8,9},{9,8},{10,11... | collective-permute-start | bytes 5529608 | tf_op jit(solution)/shard_map/ppermute | solution.py:516
  2.2 12.7 %collective-permute-start.1 = (bf16[2,160,640]{2,1,0:T(8,128)(2,1)S(1)}, bf16[2,160,640]{2,1,0:T(8,128)(2,1)S(1)}, u32[]{:S(2)}, u32[]{:S(2)}) collective-permute-start(bf16[2,160,640]{2,1,0:T(8,128)(2,1)S(1)} %dynamic-slice_bitcast_fusion), channel_id=1, source_target_pairs={{0,2},{1,3},{2,0},{3,1},{4,6},{5,7},{6,4},{7,5},{8,10},{9,11},{10,... | collective-permute-start | bytes 1228808 | tf_op jit(solution)/shard_map/ppermute | solution.py:516
  6.2 8.7 %collective-permute-start.2 = (f32[8,640]{1,0:T(8,128)S(1)}, f32[8,640]{1,0:T(8,128)S(1)}, u32[]{:S(2)}, u32[]{:S(2)}) collective-permute-start(f32[8,640]{1,0:T(8,128)S(1)} %shard_map.93.s0), channel_id=1, source_target_pairs={{0,4},{4,0},{8,12},{12,8},{1,5},{5,1},{9,13},{13,9},{2,6},{6,2},{1... | collective-permute-start | bytes 61448 | tf_op jit(solution)/shard_map/ppermute | solution.py:516
  7.8 7.1 %collective-permute-start.3 = (f32[8,640]{1,0:T(8,128)S(1)}, f32[8,640]{1,0:T(8,128)S(1)}, u32[]{:S(2)}, u32[]{:S(2)}) collective-permute-start(f32[8,640]{1,0:T(8,128)S(1)} %shard_map.93.s0), channel_id=1, source_target_pairs={{0,8},{4,12},{8,0},{12,4},{1,9},{5,13},{9,1},{13,5},{2,10},{6,14},... | collective-permute-start | bytes 61448 | tf_op jit(solution)/shard_map/ppermute | solution.py:516
  17.1 12.3 %collective-permute-start.5 = (bf16[2,640,128]{2,1,0:T(8,128)(2,1)S(1)}, bf16[2,640,128]{2,1,0:T(8,128)(2,1)S(1)}, u32[]{:S(2)}, u32[]{:S(2)}) collective-permute-start(bf16[2,640,128]{2,1,0:T(8,128)(2,1)S(1)} %get-tuple-element.67.mine), channel_id=1, source_target_pairs={{4,0},{8,4},{12,8},{0,12},{5,1},{9,5},{13,9},{1,13},{6,2},{10,6},{... | collective-permute-start | bytes 983048 | tf_op jit(solution)/shard_map/ppermute | solution.py:521
  20.0 16.1 %collective-permute-start.6 = (bf16[2,640,128]{2,1,0:T(8,128)(2,1)S(1)}, bf16[2,640,128]{2,1,0:T(8,128)(2,1)S(1)}, u32[]{:S(2)}, u32[]{:S(2)}) collective-permute-start(bf16[2,640,128]{2,1,0:T(8,128)(2,1)S(1)} %get-tuple-element.67.mine), channel_id=1, source_target_pairs={{12,0},{0,4},{4,8},{8,12},{13,1},{1,5},{5,9},{9,13},{14,2},{2,6},{... | collective-permute-start | bytes 983048 | tf_op jit(solution)/shard_map/ppermute | solution.py:521
  20.0 6.9 %collective-permute-start.9 = (bf16[1,160,640]{2,1,0:T(8,128)(2,1)S(1)}, bf16[1,160,640]{2,1,0:T(8,128)(2,1)S(1)}, u32[]{:S(2)}, u32[]{:S(2)}) collective-permute-start(bf16[1,160,640]{2,1,0:T(8,128)(2,1)S(1)} %constant_dynamic-slice_fusion), channel_id=1, source_target_pairs={{0,2},{1,3},{2,0},{3,1},{4,6},{5,7},{6,4},{7,5},{8,10},{9,11},{10,... | collective-permute-start | bytes 614408 | tf_op jit(solution)/shard_map/ppermute | solution.py:516
  22.9 18.4 %collective-permute-start.8 = (bf16[2,160,640]{2,1,0:T(8,128)(2,1)S(1)}, bf16[2,160,640]{2,1,0:T(8,128)(2,1)S(1)}, u32[]{:S(2)}, u32[]{:S(2)}) collective-permute-start(bf16[2,160,640]{2,1,0:T(8,128)(2,1)S(1)} %collective-permute-done.1.far0), channel_id=1, source_target_pairs={{0,16},{16,0},{1,17},{17,1},{2,18},{18,2},{3,19},{19,3},{4,20},{20... | collective-permute-start | bytes 1228808 | tf_op jit(solution)/shard_map/ppermute | solution.py:516
  24.5 16.9 %collective-permute-start.11 = (bf16[3,160,640]{2,1,0:T(8,128)(2,1)S(1)}, bf16[3,160,640]{2,1,0:T(8,128)(2,1)S(1)}, u32[]{:S(2)}, u32[]{:S(2)}) collective-permute-start(bf16[3,160,640]{2,1,0:T(8,128)(2,1)S(1)} %slice.18), channel_id=1, source_target_pairs={{0,2},{1,3},{2,0},{3,1},{4,6},{5,7},{6,4},{7,5},{8,10},{9,11},{10,... | collective-permute-start | bytes 1843208 | tf_op jit(solution)/shard_map/ppermute | solution.py:516
  26.9 14.6 %collective-permute-start.10 = (bf16[1,160,640]{2,1,0:T(8,128)(2,1)S(1)}, bf16[1,160,640]{2,1,0:T(8,128)(2,1)S(1)}, u32[]{:S(2)}, u32[]{:S(2)}) collective-permute-start(bf16[1,160,640]{2,1,0:T(8,128)(2,1)S(1)} %collective-permute-done.9.far2), channel_id=1, source_target_pairs={{0,16},{16,0},{1,17},{17,1},{2,18},{18,2},{3,19},{19,3},{4,20},{20... | collective-permute-start | bytes 614408 | tf_op jit(solution)/shard_map/ppermute | solution.py:516
  29.4 12.2 %collective-permute-start.12 = (bf16[2,640,128]{2,1,0:T(8,128)(2,1)S(1)}, bf16[2,640,128]{2,1,0:T(8,128)(2,1)S(1)}, u32[]{:S(2)}, u32[]{:S(2)}) collective-permute-start(bf16[2,640,128]{2,1,0:T(8,128)(2,1)S(1)} %collective-permute-done.5.above), channel_id=1, source_target_pairs={{4,0},{8,4},{12,8},{0,12},{5,1},{9,5},{13,9},{1,13},{6,2},{10,6},{... | collective-permute-start | bytes 983048 | tf_op jit(solution)/shard_map/ppermute | solution.py:521
  55.1 10.7 %collective-permute-start.24 = (bf16[2,640,128]{2,1,0:T(8,128)(2,1)S(1)}, bf16[2,640,128]{2,1,0:T(8,128)(2,1)S(1)}, u32[]{:S(2)}, u32[]{:S(2)}) collective-permute-start(bf16[2,640,128]{2,1,0:T(8,128)(2,1)S(1)} %get-tuple-element.67.mine), channel_id=1, source_target_pairs={{0,2},{1,3},{2,0},{3,1},{4,6},{5,7},{6,4},{7,5},{8,10},{9,11},{10,... | collective-permute-start | bytes 983048 | tf_op jit(solution)/shard_map/ppermute | solution.py:516
  56.7 11.7 %collective-permute-start.21 = (bf16[4,2,160,128]{3,2,1,0:T(8,128)(2,1)S(1)}, bf16[4,2,160,128]{3,2,1,0:T(8,128)(2,1)S(1)}, u32[]{:S(2)}, u32[]{:S(2)}) collective-permute-start(bf16[4,2,160,128]{3,2,1,0:T(8,128)(2,1)S(1)} %pad_maximum_fusion.own), channel_id=1, source_target_pairs={{4,0},{8,4},{12,8},{0,12},{5,1},{9,5},{13,9},{1,13},{6,2},{10,6},{... | collective-permute-start | bytes 983048 | tf_op jit(solution)/shard_map/ppermute | solution.py:521
  62.4 8.7 %collective-permute-start.20 = (bf16[1,640,128]{2,1,0:T(8,128)(2,1)S(1)}, bf16[1,640,128]{2,1,0:T(8,128)(2,1)S(1)}, u32[]{:S(2)}, u32[]{:S(2)}) collective-permute-start(bf16[1,640,128]{2,1,0:T(8,128)(2,1)S(1)} %get-tuple-element.85), channel_id=1, source_target_pairs={{0,4},{4,8},{8,12},{1,5},{5,9},{9,13},{2,6},{6,10},{10,14},{3,7},{... | collective-permute-start | bytes 491528 | tf_op jit(solution)/shard_map/ppermute | solution.py:608
  63.7 9.8 %collective-permute-start.22 = (bf16[1,640,128]{2,1,0:T(8,128)(2,1)S(1)}, bf16[1,640,128]{2,1,0:T(8,128)(2,1)S(1)}, u32[]{:S(2)}, u32[]{:S(2)}) collective-permute-start(bf16[1,640,128]{2,1,0:T(8,128)(2,1)S(1)} %get-tuple-element.84), channel_id=1, source_target_pairs={{4,0},{8,4},{12,8},{5,1},{9,5},{13,9},{6,2},{10,6},{14,10},{7,3},{... | collective-permute-start | bytes 491528 | tf_op jit(solution)/shard_map/ppermute | solution.py:609
  65.7 21.9 %collective-permute-start.27 = (bf16[10,640,128]{2,1,0:T(8,128)(2,1)S(1)}, bf16[10,640,128]{2,1,0:T(8,128)(2,1)S(1)}, u32[]{:S(2)}, u32[]{:S(2)}) collective-permute-start(bf16[10,640,128]{2,1,0:T(8,128)(2,1)S(1)} %shard_map.101.h0), channel_id=1, source_target_pairs={{0,1},{1,0},{2,3},{3,2},{4,5},{5,4},{6,7},{7,6},{8,9},{9,8},{10,11... | collective-permute-start | bytes 4915208 | tf_op jit(solution)/shard_map/ppermute | solution.py:516
  65.8 17.5 %collective-permute-start.25 = (bf16[2,640,128]{2,1,0:T(8,128)(2,1)S(1)}, bf16[2,640,128]{2,1,0:T(8,128)(2,1)S(1)}, u32[]{:S(2)}, u32[]{:S(2)}) collective-permute-start(bf16[2,640,128]{2,1,0:T(8,128)(2,1)S(1)} %collective-permute-done.5.above), channel_id=1, source_target_pairs={{0,2},{1,3},{2,0},{3,1},{4,6},{5,7},{6,4},{7,5},{8,10},{9,11},{10,... | collective-permute-start | bytes 983048 | tf_op jit(solution)/shard_map/ppermute | solution.py:516
  68.4 17.2 %collective-permute-start.26 = (bf16[2,640,128]{2,1,0:T(8,128)(2,1)S(1)}, bf16[2,640,128]{2,1,0:T(8,128)(2,1)S(1)}, u32[]{:S(2)}, u32[]{:S(2)}) collective-permute-start(bf16[2,640,128]{2,1,0:T(8,128)(2,1)S(1)} %collective-permute-done.6.below), channel_id=1, source_target_pairs={{0,2},{1,3},{2,0},{3,1},{4,6},{5,7},{6,4},{7,5},{8,10},{9,11},{10,... | collective-permute-start | bytes 983048 | tf_op jit(solution)/shard_map/ppermute | solution.py:516
  71.1 12.2 %collective-permute-start.23 = (bf16[4,2,160,128]{3,2,1,0:T(8,128)(2,1)S(1)}, bf16[4,2,160,128]{3,2,1,0:T(8,128)(2,1)S(1)}, u32[]{:S(2)}, u32[]{:S(2)}) collective-permute-start(bf16[4,2,160,128]{3,2,1,0:T(8,128)(2,1)S(1)} %pad_maximum_fusion.own), channel_id=1, source_target_pairs={{12,0},{0,4},{4,8},{8,12},{13,1},{1,5},{5,9},{9,13},{14,2},{2,6},{... | collective-permute-start | bytes 983048 | tf_op jit(solution)/shard_map/ppermute | solution.py:521
  79.8 11.5 %collective-permute-start.31 = (bf16[2,640,128]{2,1,0:T(8,128)(2,1)S(1)}, bf16[2,640,128]{2,1,0:T(8,128)(2,1)S(1)}, u32[]{:S(2)}, u32[]{:S(2)}) collective-permute-start(bf16[2,640,128]{2,1,0:T(8,128)(2,1)S(1)} %collective-permute-done.12.beyond), channel_id=1, source_target_pairs={{0,2},{1,3},{2,0},{3,1},{4,6},{5,7},{6,4},{7,5},{8,10},{9,11},{10,... | collective-permute-start | bytes 983048 | tf_op jit(solution)/shard_map/ppermute | solution.py:516
  83.3 8.8 %collective-permute-start.28 = (f32[8,640]{1,0:T(8,128)S(1)}, f32[8,640]{1,0:T(8,128)S(1)}, u32[]{:S(2)}, u32[]{:S(2)}) collective-permute-start(f32[8,640]{1,0:T(8,128)S(1)} %get-tuple-element.72.s0), channel_id=1, source_target_pairs={{0,4},{4,0},{8,12},{12,8},{1,5},{5,1},{9,13},{13,9},{2,6},{6,2},{1... | collective-permute-start | bytes 61448 | tf_op jit(solution)/shard_map/ppermute | solution.py:516
  83.3 8.8 %collective-permute-start.29 = (f32[8,640]{1,0:T(8,128)S(1)}, f32[8,640]{1,0:T(8,128)S(1)}, u32[]{:S(2)}, u32[]{:S(2)}) collective-permute-start(f32[8,640]{1,0:T(8,128)S(1)} %get-tuple-element.72.s0), channel_id=1, source_target_pairs={{0,8},{4,12},{8,0},{12,4},{1,9},{5,13},{9,1},{13,5},{2,10},{6,14},... | collective-permute-start | bytes 61448 | tf_op jit(solution)/shard_map/ppermute | solution.py:516
  85.6 6.5 %collective-permute-start.30 = (f32[8,640]{1,0:T(8,128)S(1)}, f32[8,640]{1,0:T(8,128)S(1)}, u32[]{:S(2)}, u32[]{:S(2)}) collective-permute-start(f32[8,640]{1,0:T(8,128)S(1)} %get-tuple-element.72.s0), channel_id=1, source_target_pairs={{0,12},{4,8},{8,4},{12,0},{1,13},{5,9},{9,5},{13,1},{2,14},{6,10},... | collective-permute-start | bytes 61448 | tf_op jit(solution)/shard_map/ppermute | solution.py:516
  93.9 10.1 %collective-permute-start.36 = (bf16[4,2,160,128]{3,2,1,0:T(8,128)(2,1)S(1)}, bf16[4,2,160,128]{3,2,1,0:T(8,128)(2,1)S(1)}, u32[]{:S(2)}, u32[]{:S(2)}) collective-permute-start(bf16[4,2,160,128]{3,2,1,0:T(8,128)(2,1)S(1)} %collective-permute-done.21.plus), channel_id=1, source_target_pairs={{4,0},{8,4},{12,8},{0,12},{5,1},{9,5},{13,9},{1,13},{6,2},{10,6},{... | collective-permute-start | bytes 983048 | tf_op jit(solution)/shard_map/ppermute | solution.py:521
  (20 other events, 96.6 us)

commit v13 on v12

--- a/solution.py
+++ b/solution.py
@@ -656,7 +656,7 @@
         ),
         us=0.05,
     )
-    diag_rows = swap(after_all(across_rows, grad_latents), "wt", 1)
+    diag_rows = swap(after_all(across_rows, grad_latents, far), "wt", 1)
     images = (own_rows, other_rows, across_rows, diag_rows)
     next_weight = call(
         next_weight_kernel,

time: 113 us -> 113 us (level)
    ppermute x29, waiting for transfers between devices: 14.6 us -> 16.7 us  [swap(): return lax.ppermute(x, axis, [(i, i ^ mask) for i in range(size)])]
    ppermute x6, waiting for transfers between devices: 8.69 us -> 6.81 us  [ring(): return lax.ppermute(x, axis, [((i + step) % size, i) for i in range(size)])]
  transfers between devices with their start and end apart: 37 -> 37, of which waited for: 12 -> 14; matrix products, arithmetic and copies ran while one was open for 1% -> 1% of each run, Pallas kernels for 21% -> 22%
where the time goes in v13:
time: 113 us; the launch traced here: 112 us
  starting transfers between devices  44.9 us (40%)
  Pallas kernels  37.8 us (33%)
  waiting for transfers between devices  25.1 us (22%)
  local copies, waits for them, and re-layouts  3.35 us (3%)
    pallas_call x15, Pallas kernels, call(): pl.pallas_call(kernel, out_shape=outs, in_specs=specs, out_specs=jax.tree...  37.8 us
    ppermute x29, starting transfers between devices, swap(): return lax.ppermute(x, axis, [(i, i ^ mask) for i in range(size)])  28.1 us
    ppermute x29, waiting for transfers between devices, swap(): return lax.ppermute(x, axis, [(i, i ^ mask) for i in range(size)])  16.7 us
    ppermute x6, starting transfers between devices, ring(): return lax.ppermute(x, axis, [((i + step) % size, i) for i in range(size)])  14.2 us
    ppermute x6, waiting for transfers between devices, ring(): return lax.ppermute(x, axis, [((i + step) % size, i) for i in range(size)])  6.81 us
  transfers between devices with their start and end apart: 37, of which 14 were waited for; matrix products, arithmetic and copies ran while one was open for 1% of the time, Pallas kernels for 22%

profile of v13, /device:TPU:0, one launch (start us, length us, event | category | flops | bytes accessed | tf_op | source)
XLA Modules:
  0.0 112.3 jit_solution(1745390846987109527)
XLA Ops:
  2.2 2.6 %collective-permute-start.1 = (bf16[2,160,640]{2,1,0:T(8,128)(2,1)S(1)}, bf16[2,160,640]{2,1,0:T(8,128)(2,1)S(1)}, u32[]{:S(2)}, u32[]{:S(2)}) collective-permute-start(bf16[2,160,640]{2,1,0:T(8,128)(2,1)S(1)} %dynamic-slice_bitcast_fusion), channel_id=1, source_target_pairs={{0,2},{1,3},{2,0},{3,1},{4,6},{5,7},{6,4},{7,5},{8,10},{9,11},{10,... | collective-permute-start | bytes 1228808 | tf_op jit(solution)/shard_map/ppermute | solution.py:516
  6.2 1.6 %collective-permute-start.2 = (f32[8,640]{1,0:T(8,128)S(1)}, f32[8,640]{1,0:T(8,128)S(1)}, u32[]{:S(2)}, u32[]{:S(2)}) collective-permute-start(f32[8,640]{1,0:T(8,128)S(1)} %shard_map.93.s0), channel_id=1, source_target_pairs={{0,4},{4,0},{8,12},{12,8},{1,5},{5,1},{9,13},{13,9},{2,6},{6,2},{1... | collective-permute-start | bytes 61448 | tf_op jit(solution)/shard_map/ppermute | solution.py:516
  7.8 2.6 %collective-permute-start.3 = (f32[8,640]{1,0:T(8,128)S(1)}, f32[8,640]{1,0:T(8,128)S(1)}, u32[]{:S(2)}, u32[]{:S(2)}) collective-permute-start(f32[8,640]{1,0:T(8,128)S(1)} %shard_map.93.s0), channel_id=1, source_target_pairs={{0,8},{4,12},{8,0},{12,4},{1,9},{5,13},{9,1},{13,5},{2,10},{6,14},... | collective-permute-start | bytes 61448 | tf_op jit(solution)/shard_map/ppermute | solution.py:516
  10.8 4.1 %collective-permute-done.1.far0 = bf16[2,160,640]{2,1,0:T(8,128)(2,1)S(1)} collective-permute-done((bf16[2,160,640]{2,1,0:T(8,128)(2,1)S(1)}, bf16[2,160,640]{2,1,0:T(8,128)(2,1)S(1)}, u32[]{:S(2)}, u32[]{:S(2)}) %collective-permute-start.1) | collective-permute-done | bytes 409632 | tf_op jit(solution)/shard_map/ppermute | solution.py:516
  17.1 2.8 %collective-permute-start.5 = (bf16[2,640,128]{2,1,0:T(8,128)(2,1)S(1)}, bf16[2,640,128]{2,1,0:T(8,128)(2,1)S(1)}, u32[]{:S(2)}, u32[]{:S(2)}) collective-permute-start(bf16[2,640,128]{2,1,0:T(8,128)(2,1)S(1)} %get-tuple-element.67.mine), channel_id=1, source_target_pairs={{4,0},{8,4},{12,8},{0,12},{5,1},{9,5},{13,9},{1,13},{6,2},{10,6},{... | collective-permute-start | bytes 983048 | tf_op jit(solution)/shard_map/ppermute | solution.py:521
  25.1 1.8 %collective-permute-done.9.far2 = bf16[1,160,640]{2,1,0:T(8,128)(2,1)S(1)} collective-permute-done((bf16[1,160,640]{2,1,0:T(8,128)(2,1)S(1)}, bf16[1,160,640]{2,1,0:T(8,128)(2,1)S(1)}, u32[]{:S(2)}, u32[]{:S(2)}) %collective-permute-start.9) | collective-permute-done | bytes 204832 | tf_op jit(solution)/shard_map/ppermute | solution.py:516
  26.9 2.6 %collective-permute-start.10 = (bf16[1,160,640]{2,1,0:T(8,128)(2,1)S(1)}, bf16[1,160,640]{2,1,0:T(8,128)(2,1)S(1)}, u32[]{:S(2)}, u32[]{:S(2)}) collective-permute-start(bf16[1,160,640]{2,1,0:T(8,128)(2,1)S(1)} %collective-permute-done.9.far2), channel_id=1, source_target_pairs={{0,16},{16,0},{1,17},{17,1},{2,18},{18,2},{3,19},{19,3},{4,20},{20... | collective-permute-start | bytes 614408 | tf_op jit(solution)/shard_map/ppermute | solution.py:516
  29.4 3.6 %collective-permute-start.12 = (bf16[2,640,128]{2,1,0:T(8,128)(2,1)S(1)}, bf16[2,640,128]{2,1,0:T(8,128)(2,1)S(1)}, u32[]{:S(2)}, u32[]{:S(2)}) collective-permute-start(bf16[2,640,128]{2,1,0:T(8,128)(2,1)S(1)} %collective-permute-done.5.above), channel_id=1, source_target_pairs={{4,0},{8,4},{12,8},{0,12},{5,1},{9,5},{13,9},{1,13},{6,2},{10,6},{... | collective-permute-start | bytes 983048 | tf_op jit(solution)/shard_map/ppermute | solution.py:521
  33.0 3.1 %collective-permute-done.6.below = bf16[2,640,128]{2,1,0:T(8,128)(2,1)S(1)} collective-permute-done((bf16[2,640,128]{2,1,0:T(8,128)(2,1)S(1)}, bf16[2,640,128]{2,1,0:T(8,128)(2,1)S(1)}, u32[]{:S(2)}, u32[]{:S(2)}) %collective-permute-start.6) | collective-permute-done | bytes 327712 | tf_op jit(solution)/shard_map/ppermute | solution.py:521
  37.0 4.4 %shard_map.97 = (f32[2,2,160,128]{3,2,1,0:T(8,128)S(1)}, bf16[2,160,128]{2,1,0:T(8,128)(2,1)S(1)}, bf16[2,160,128]{2,1,0:T(8,128)(2,1)S(1)}) custom-call(s32[3]{0:T(128)S(1)} %pad_add_fusion.place, bf16[9,160,640]{2,1,0:T(8,128)(2,1)S(1)} %bitcast.25, bf16[9,160,640]{2,1,0:T(8,128)(2,1)} %collective-permute-done.side, ...), custom_call_target="tpu_custom_call" | custom-call | flops 20000000000 | bytes 60000000 | tf_op jit(solution)/shard_map/pallas_call | solution.py:497
  42.7 2.5 %collective-permute-done.15.diag2 = bf16[1,160,640]{2,1,0:T(8,128)(2,1)S(1)} collective-permute-done((bf16[1,160,640]{2,1,0:T(8,128)(2,1)S(1)}, bf16[1,160,640]{2,1,0:T(8,128)(2,1)S(1)}, u32[]{:S(2)}, u32[]{:S(2)}) %collective-permute-start.15) | collective-permute-done | bytes 204832 | tf_op jit(solution)/shard_map/ppermute | solution.py:516
  45.5 3.2 %shard_map.98 = (f32[2,640,128]{2,1,0:T(8,128)S(1)}, bf16[2,640,128]{2,1,0:T(8,128)(2,1)S(1)}, bf16[2,2,160,128]{3,2,1,0:T(8,128)(2,1)S(1)}) custom-call(s32[3]{0:T(128)S(1)} %pad_add_fusion.place, bf16[2,160,640]{2,1,0:T(8,128)(2,1)S(1)} %collective-permute-done.1.far0, bf16[2,160,640]{2,1,0:T(8,128)(2,1)S(1)} %collective-permute-done.8.far1, ...), custom_call_target="tpu_custom_call" | custom-call | flops 50000000 | bytes 150000 | tf_op jit(solution)/shard_map/pallas_call | solution.py:497
  50.2 4.7 %collective-permute-done.18 = bf16[2,2,160,128]{3,2,1,0:T(8,128)(2,1)S(1)} collective-permute-done((bf16[2,2,160,128]{3,2,1,0:T(8,128)(2,1)S(1)}, bf16[2,2,160,128]{3,2,1,0:T(8,128)(2,1)S(1)}, u32[]{:S(2)}, u32[]{:S(2)}) %collective-permute-start.18) | collective-permute-done | bytes 163872 | tf_op jit(solution)/shard_map/ppermute | solution.py:516
  56.7 3.6 %collective-permute-start.21 = (bf16[4,2,160,128]{3,2,1,0:T(8,128)(2,1)S(1)}, bf16[4,2,160,128]{3,2,1,0:T(8,128)(2,1)S(1)}, u32[]{:S(2)}, u32[]{:S(2)}) collective-permute-start(bf16[4,2,160,128]{3,2,1,0:T(8,128)(2,1)S(1)} %pad_maximum_fusion.own), channel_id=1, source_target_pairs={{4,0},{8,4},{12,8},{0,12},{5,1},{9,5},{13,9},{1,13},{6,2},{10,6},{... | collective-permute-start | bytes 983048 | tf_op jit(solution)/shard_map/ppermute | solution.py:521
  60.3 2.1 %shard_map.99.full = bf16[9,640,640]{2,1,0:T(8,128)(2,1)S(1)} custom-call(s32[3]{0:T(128)S(1)} %pad_add_fusion.place, bf16[9,160,640]{2,1,0:T(8,128)(2,1)S(1)} %bitcast.26, bf16[9,160,640]{2,1,0:T(8,128)(2,1)} %collective-permute-done.side, bf16[2,160,640]{2,1,0:T(8,128)(2,1)S(1)} %collective-permute-done.1.far0, ...), custom_call_target="tpu_custom_call" | custom-call | flops 5000000000 | bytes 15000000 | tf_op jit(solution)/shard_map/pallas_call | solution.py:497
  71.1 2.5 %collective-permute-start.23 = (bf16[4,2,160,128]{3,2,1,0:T(8,128)(2,1)S(1)}, bf16[4,2,160,128]{3,2,1,0:T(8,128)(2,1)S(1)}, u32[]{:S(2)}, u32[]{:S(2)}) collective-permute-start(bf16[4,2,160,128]{3,2,1,0:T(8,128)(2,1)S(1)} %pad_maximum_fusion.own), channel_id=1, source_target_pairs={{12,0},{0,4},{4,8},{8,12},{13,1},{1,5},{5,9},{9,13},{14,2},{2,6},{... | collective-permute-start | bytes 983048 | tf_op jit(solution)/shard_map/ppermute | solution.py:521
  73.6 6.2 %shard_map.100 = (f32[2,640,128]{2,1,0:T(8,128)S(1)}, f32[8,640]{1,0:T(8,128)S(1)}) custom-call(bf16[9,640,640]{2,1,0:T(8,128)(2,1)S(1)} %shard_map.99.full, bf16[1,640,128]{2,1,0:T(8,128)(2,1)S(1)} %collective-permute-done.20.before, bf16[2,640,128]{2,1,0:T(8,128)(2,1)S(1)} %get-tuple-element.62.low, ...), custom_call_target="tpu_custom_call" | custom-call | flops 30000001024 | bytes 90000000 | tf_op jit(solution)/shard_map/pallas_call | solution.py:497
  81.0 2.2 %collective-permute-done.23.minus = bf16[4,2,160,128]{3,2,1,0:T(8,128)(2,1)S(1)} collective-permute-done((bf16[4,2,160,128]{3,2,1,0:T(8,128)(2,1)S(1)}, bf16[4,2,160,128]{3,2,1,0:T(8,128)(2,1)S(1)}, u32[]{:S(2)}, u32[]{:S(2)}) %collective-permute-start.23) | collective-permute-done | bytes 327712 | tf_op jit(solution)/shard_map/ppermute | solution.py:521
  83.3 1.7 %collective-permute-start.32 = (bf16[4,2,160,128]{3,2,1,0:T(8,128)(2,1)S(1)}, bf16[4,2,160,128]{3,2,1,0:T(8,128)(2,1)S(1)}, u32[]{:S(2)}, u32[]{:S(2)}) collective-permute-start(bf16[4,2,160,128]{3,2,1,0:T(8,128)(2,1)S(1)} %collective-permute-done.21.plus), channel_id=1, source_target_pairs={{4,0},{8,4},{12,8},{0,12},{5,1},{9,5},{13,9},{1,13},{6,2},{10,6},{... | collective-permute-start | bytes 983048 | tf_op jit(solution)/shard_map/ppermute | solution.py:521
  86.1 3.3 %collective-permute-start.30 = (f32[8,640]{1,0:T(8,128)S(1)}, f32[8,640]{1,0:T(8,128)S(1)}, u32[]{:S(2)}, u32[]{:S(2)}) collective-permute-start(f32[8,640]{1,0:T(8,128)S(1)} %get-tuple-element.72.s0), channel_id=1, source_target_pairs={{0,12},{4,8},{8,4},{12,0},{1,13},{5,9},{9,5},{13,1},{2,14},{6,10},... | collective-permute-start | bytes 61448 | tf_op jit(solution)/shard_map/ppermute | solution.py:516
  89.4 3.7 %shard_map.102.near = f32[9,160,640]{2,1,0:T(8,128)S(1)} custom-call(s32[3]{0:T(128)S(1)} %pad_add_fusion.place, bf16[4,2,160,128]{3,2,1,0:T(8,128)(2,1)S(1)} %pad_maximum_fusion.own, bf16[4,2,160,128]{3,2,1,0:T(8,128)(2,1)S(1)} %collective-permute-done.21.plus, bf16[4,2,160,128]{3,2,1,0:T(8,128)(2,1)S(1)} %collective-permute-done.23.minus, ...), custom_call_target="tpu_custom_call" | custom-call | flops 30000001024 | bytes 90000000 | tf_op jit(solution)/shard_map/pallas_call | solution.py:497
  93.7 1.8 %shard_map.103 = (f32[1280,128]{1,0:T(8,128)}, f32[8,640]{1,0:T(8,128)S(1)}) custom-call(f32[8,640]{1,0:T(8,128)S(1)} %get-tuple-element.72.s0, f32[8,640]{1,0:T(8,128)S(1)} %collective-permute-done.28.s1, f32[8,640]{1,0:T(8,128)S(1)} %collective-permute-done.29.s2, f32[8,640]{1,0:T(8,128)S(1)} %collective-permute-done.30.s3, ...), custom_call_target="tpu_custom_call" | custom-call | flops 50000000 | bytes 150000 | tf_op jit(solution)/shard_map/pallas_call | solution.py:497
  99.7 3.7 %shard_map.105.near = f32[9,160,640]{2,1,0:T(8,128)S(1)} custom-call(s32[3]{0:T(128)S(1)} %pad_add_fusion.place, bf16[4,2,160,128]{3,2,1,0:T(8,128)(2,1)S(1)} %pad_maximum_fusion.own, bf16[4,2,160,128]{3,2,1,0:T(8,128)(2,1)S(1)} %collective-permute-done.21.plus, bf16[4,2,160,128]{3,2,1,0:T(8,128)(2,1)S(1)} %collective-permute-done.23.minus, ...), custom_call_target="tpu_custom_call" | custom-call | flops 30000001024 | bytes 90000000 | tf_op jit(solution)/shard_map/pallas_call | solution.py:497
  104.1 8.1 %shard_map.107 = f32[9,160,640]{2,1,0:T(8,128)} custom-call(s32[3]{0:T(128)S(1)} %pad_add_fusion.place, bf16[4,2,160,128]{3,2,1,0:T(8,128)(2,1)S(1)} %collective-permute-done.21.plus, bf16[4,2,160,128]{3,2,1,0:T(8,128)(2,1)S(1)} %collective-permute-done.23.minus, bf16[4,2,160,128]{3,2,1,0:T(8,128)(2,1)S(1)} %collective-permute-done.32.far, ...), custom_call_target="tpu_custom_call" | custom-call | flops 50000000 | bytes 150000 | tf_op jit(solution)/shard_map/pallas_call | solution.py:497
  (90 shorter events, 32.8 us)
Async XLA Ops:
  0.6 14.3 %collective-permute-start = (bf16[9,160,640]{2,1,0:T(8,128)(2,1)}, bf16[9,160,640]{2,1,0:T(8,128)(2,1)}, u32[]{:S(2)}, u32[]{:S(2)}) collective-permute-start(bf16[9,160,640]{2,1,0:T(8,128)(2,1)} %bitcast.22), channel_id=1, source_target_pairs={{0,1},{1,0},{2,3},{3,2},{4,5},{5,4},{6,7},{7,6},{8,9},{9,8},{10,11... | collective-permute-start | bytes 5529608 | tf_op jit(solution)/shard_map/ppermute | solution.py:516
  2.2 12.7 %collective-permute-start.1 = (bf16[2,160,640]{2,1,0:T(8,128)(2,1)S(1)}, bf16[2,160,640]{2,1,0:T(8,128)(2,1)S(1)}, u32[]{:S(2)}, u32[]{:S(2)}) collective-permute-start(bf16[2,160,640]{2,1,0:T(8,128)(2,1)S(1)} %dynamic-slice_bitcast_fusion), channel_id=1, source_target_pairs={{0,2},{1,3},{2,0},{3,1},{4,6},{5,7},{6,4},{7,5},{8,10},{9,11},{10,... | collective-permute-start | bytes 1228808 | tf_op jit(solution)/shard_map/ppermute | solution.py:516
  6.2 8.7 %collective-permute-start.2 = (f32[8,640]{1,0:T(8,128)S(1)}, f32[8,640]{1,0:T(8,128)S(1)}, u32[]{:S(2)}, u32[]{:S(2)}) collective-permute-start(f32[8,640]{1,0:T(8,128)S(1)} %shard_map.93.s0), channel_id=1, source_target_pairs={{0,4},{4,0},{8,12},{12,8},{1,5},{5,1},{9,13},{13,9},{2,6},{6,2},{1... | collective-permute-start | bytes 61448 | tf_op jit(solution)/shard_map/ppermute | solution.py:516
  7.8 7.1 %collective-permute-start.3 = (f32[8,640]{1,0:T(8,128)S(1)}, f32[8,640]{1,0:T(8,128)S(1)}, u32[]{:S(2)}, u32[]{:S(2)}) collective-permute-start(f32[8,640]{1,0:T(8,128)S(1)} %shard_map.93.s0), channel_id=1, source_target_pairs={{0,8},{4,12},{8,0},{12,4},{1,9},{5,13},{9,1},{13,5},{2,10},{6,14},... | collective-permute-start | bytes 61448 | tf_op jit(solution)/shard_map/ppermute | solution.py:516
  17.1 12.3 %collective-permute-start.5 = (bf16[2,640,128]{2,1,0:T(8,128)(2,1)S(1)}, bf16[2,640,128]{2,1,0:T(8,128)(2,1)S(1)}, u32[]{:S(2)}, u32[]{:S(2)}) collective-permute-start(bf16[2,640,128]{2,1,0:T(8,128)(2,1)S(1)} %get-tuple-element.67.mine), channel_id=1, source_target_pairs={{4,0},{8,4},{12,8},{0,12},{5,1},{9,5},{13,9},{1,13},{6,2},{10,6},{... | collective-permute-start | bytes 983048 | tf_op jit(solution)/shard_map/ppermute | solution.py:521
  20.0 16.1 %collective-permute-start.6 = (bf16[2,640,128]{2,1,0:T(8,128)(2,1)S(1)}, bf16[2,640,128]{2,1,0:T(8,128)(2,1)S(1)}, u32[]{:S(2)}, u32[]{:S(2)}) collective-permute-start(bf16[2,640,128]{2,1,0:T(8,128)(2,1)S(1)} %get-tuple-element.67.mine), channel_id=1, source_target_pairs={{12,0},{0,4},{4,8},{8,12},{13,1},{1,5},{5,9},{9,13},{14,2},{2,6},{... | collective-permute-start | bytes 983048 | tf_op jit(solution)/shard_map/ppermute | solution.py:521
  22.9 18.4 %collective-permute-start.8 = (bf16[2,160,640]{2,1,0:T(8,128)(2,1)S(1)}, bf16[2,160,640]{2,1,0:T(8,128)(2,1)S(1)}, u32[]{:S(2)}, u32[]{:S(2)}) collective-permute-start(bf16[2,160,640]{2,1,0:T(8,128)(2,1)S(1)} %collective-permute-done.1.far0), channel_id=1, source_target_pairs={{0,16},{16,0},{1,17},{17,1},{2,18},{18,2},{3,19},{19,3},{4,20},{20... | collective-permute-start | bytes 1228808 | tf_op jit(solution)/shard_map/ppermute | solution.py:516
  24.5 16.9 %collective-permute-start.11 = (bf16[3,160,640]{2,1,0:T(8,128)(2,1)S(1)}, bf16[3,160,640]{2,1,0:T(8,128)(2,1)S(1)}, u32[]{:S(2)}, u32[]{:S(2)}) collective-permute-start(bf16[3,160,640]{2,1,0:T(8,128)(2,1)S(1)} %slice.18), channel_id=1, source_target_pairs={{0,2},{1,3},{2,0},{3,1},{4,6},{5,7},{6,4},{7,5},{8,10},{9,11},{10,... | collective-permute-start | bytes 1843208 | tf_op jit(solution)/shard_map/ppermute | solution.py:516
  26.9 14.6 %collective-permute-start.10 = (bf16[1,160,640]{2,1,0:T(8,128)(2,1)S(1)}, bf16[1,160,640]{2,1,0:T(8,128)(2,1)S(1)}, u32[]{:S(2)}, u32[]{:S(2)}) collective-permute-start(bf16[1,160,640]{2,1,0:T(8,128)(2,1)S(1)} %collective-permute-done.9.far2), channel_id=1, source_target_pairs={{0,16},{16,0},{1,17},{17,1},{2,18},{18,2},{3,19},{19,3},{4,20},{20... | collective-permute-start | bytes 614408 | tf_op jit(solution)/shard_map/ppermute | solution.py:516
  29.4 12.2 %collective-permute-start.12 = (bf16[2,640,128]{2,1,0:T(8,128)(2,1)S(1)}, bf16[2,640,128]{2,1,0:T(8,128)(2,1)S(1)}, u32[]{:S(2)}, u32[]{:S(2)}) collective-permute-start(bf16[2,640,128]{2,1,0:T(8,128)(2,1)S(1)} %collective-permute-done.5.above), channel_id=1, source_target_pairs={{4,0},{8,4},{12,8},{0,12},{5,1},{9,5},{13,9},{1,13},{6,2},{10,6},{... | collective-permute-start | bytes 983048 | tf_op jit(solution)/shard_map/ppermute | solution.py:521
  55.1 10.7 %collective-permute-start.24 = (bf16[2,640,128]{2,1,0:T(8,128)(2,1)S(1)}, bf16[2,640,128]{2,1,0:T(8,128)(2,1)S(1)}, u32[]{:S(2)}, u32[]{:S(2)}) collective-permute-start(bf16[2,640,128]{2,1,0:T(8,128)(2,1)S(1)} %get-tuple-element.67.mine), channel_id=1, source_target_pairs={{0,2},{1,3},{2,0},{3,1},{4,6},{5,7},{6,4},{7,5},{8,10},{9,11},{10,... | collective-permute-start | bytes 983048 | tf_op jit(solution)/shard_map/ppermute | solution.py:516
  56.7 11.7 %collective-permute-start.21 = (bf16[4,2,160,128]{3,2,1,0:T(8,128)(2,1)S(1)}, bf16[4,2,160,128]{3,2,1,0:T(8,128)(2,1)S(1)}, u32[]{:S(2)}, u32[]{:S(2)}) collective-permute-start(bf16[4,2,160,128]{3,2,1,0:T(8,128)(2,1)S(1)} %pad_maximum_fusion.own), channel_id=1, source_target_pairs={{4,0},{8,4},{12,8},{0,12},{5,1},{9,5},{13,9},{1,13},{6,2},{10,6},{... | collective-permute-start | bytes 983048 | tf_op jit(solution)/shard_map/ppermute | solution.py:521
  62.4 8.7 %collective-permute-start.20 = (bf16[1,640,128]{2,1,0:T(8,128)(2,1)S(1)}, bf16[1,640,128]{2,1,0:T(8,128)(2,1)S(1)}, u32[]{:S(2)}, u32[]{:S(2)}) collective-permute-start(bf16[1,640,128]{2,1,0:T(8,128)(2,1)S(1)} %get-tuple-element.85), channel_id=1, source_target_pairs={{0,4},{4,8},{8,12},{1,5},{5,9},{9,13},{2,6},{6,10},{10,14},{3,7},{... | collective-permute-start | bytes 491528 | tf_op jit(solution)/shard_map/ppermute | solution.py:608
  63.7 9.8 %collective-permute-start.22 = (bf16[1,640,128]{2,1,0:T(8,128)(2,1)S(1)}, bf16[1,640,128]{2,1,0:T(8,128)(2,1)S(1)}, u32[]{:S(2)}, u32[]{:S(2)}) collective-permute-start(bf16[1,640,128]{2,1,0:T(8,128)(2,1)S(1)} %get-tuple-element.84), channel_id=1, source_target_pairs={{4,0},{8,4},{12,8},{5,1},{9,5},{13,9},{6,2},{10,6},{14,10},{7,3},{... | collective-permute-start | bytes 491528 | tf_op jit(solution)/shard_map/ppermute | solution.py:609
  65.7 20.4 %collective-permute-start.27 = (bf16[10,640,128]{2,1,0:T(8,128)(2,1)S(1)}, bf16[10,640,128]{2,1,0:T(8,128)(2,1)S(1)}, u32[]{:S(2)}, u32[]{:S(2)}) collective-permute-start(bf16[10,640,128]{2,1,0:T(8,128)(2,1)S(1)} %shard_map.101.h0), channel_id=1, source_target_pairs={{0,1},{1,0},{2,3},{3,2},{4,5},{5,4},{6,7},{7,6},{8,9},{9,8},{10,11... | collective-permute-start | bytes 4915208 | tf_op jit(solution)/shard_map/ppermute | solution.py:516
  65.8 19.2 %collective-permute-start.25 = (bf16[2,640,128]{2,1,0:T(8,128)(2,1)S(1)}, bf16[2,640,128]{2,1,0:T(8,128)(2,1)S(1)}, u32[]{:S(2)}, u32[]{:S(2)}) collective-permute-start(bf16[2,640,128]{2,1,0:T(8,128)(2,1)S(1)} %collective-permute-done.5.above), channel_id=1, source_target_pairs={{0,2},{1,3},{2,0},{3,1},{4,6},{5,7},{6,4},{7,5},{8,10},{9,11},{10,... | collective-permute-start | bytes 983048 | tf_op jit(solution)/shard_map/ppermute | solution.py:516
  68.4 16.9 %collective-permute-start.26 = (bf16[2,640,128]{2,1,0:T(8,128)(2,1)S(1)}, bf16[2,640,128]{2,1,0:T(8,128)(2,1)S(1)}, u32[]{:S(2)}, u32[]{:S(2)}) collective-permute-start(bf16[2,640,128]{2,1,0:T(8,128)(2,1)S(1)} %collective-permute-done.6.below), channel_id=1, source_target_pairs={{0,2},{1,3},{2,0},{3,1},{4,6},{5,7},{6,4},{7,5},{8,10},{9,11},{10,... | collective-permute-start | bytes 983048 | tf_op jit(solution)/shard_map/ppermute | solution.py:516
  71.1 12.2 %collective-permute-start.23 = (bf16[4,2,160,128]{3,2,1,0:T(8,128)(2,1)S(1)}, bf16[4,2,160,128]{3,2,1,0:T(8,128)(2,1)S(1)}, u32[]{:S(2)}, u32[]{:S(2)}) collective-permute-start(bf16[4,2,160,128]{3,2,1,0:T(8,128)(2,1)S(1)} %pad_maximum_fusion.own), channel_id=1, source_target_pairs={{12,0},{0,4},{4,8},{8,12},{13,1},{1,5},{5,9},{9,13},{14,2},{2,6},{... | collective-permute-start | bytes 983048 | tf_op jit(solution)/shard_map/ppermute | solution.py:521
  79.8 15.7 %collective-permute-start.31 = (bf16[2,640,128]{2,1,0:T(8,128)(2,1)S(1)}, bf16[2,640,128]{2,1,0:T(8,128)(2,1)S(1)}, u32[]{:S(2)}, u32[]{:S(2)}) collective-permute-start(bf16[2,640,128]{2,1,0:T(8,128)(2,1)S(1)} %collective-permute-done.12.beyond), channel_id=1, source_target_pairs={{0,2},{1,3},{2,0},{3,1},{4,6},{5,7},{6,4},{7,5},{8,10},{9,11},{10,... | collective-permute-start | bytes 983048 | tf_op jit(solution)/shard_map/ppermute | solution.py:516
  83.3 12.9 %collective-permute-start.32 = (bf16[4,2,160,128]{3,2,1,0:T(8,128)(2,1)S(1)}, bf16[4,2,160,128]{3,2,1,0:T(8,128)(2,1)S(1)}, u32[]{:S(2)}, u32[]{:S(2)}) collective-permute-start(bf16[4,2,160,128]{3,2,1,0:T(8,128)(2,1)S(1)} %collective-permute-done.21.plus), channel_id=1, source_target_pairs={{4,0},{8,4},{12,8},{0,12},{5,1},{9,5},{13,9},{1,13},{6,2},{10,6},{... | collective-permute-start | bytes 983048 | tf_op jit(solution)/shard_map/ppermute | solution.py:521
  85.0 8.5 %collective-permute-start.28 = (f32[8,640]{1,0:T(8,128)S(1)}, f32[8,640]{1,0:T(8,128)S(1)}, u32[]{:S(2)}, u32[]{:S(2)}) collective-permute-start(f32[8,640]{1,0:T(8,128)S(1)} %get-tuple-element.72.s0), channel_id=1, source_target_pairs={{0,4},{4,0},{8,12},{12,8},{1,5},{5,1},{9,13},{13,9},{2,6},{6,2},{1... | collective-permute-start | bytes 61448 | tf_op jit(solution)/shard_map/ppermute | solution.py:516
  85.3 8.2 %collective-permute-start.29 = (f32[8,640]{1,0:T(8,128)S(1)}, f32[8,640]{1,0:T(8,128)S(1)}, u32[]{:S(2)}, u32[]{:S(2)}) collective-permute-start(f32[8,640]{1,0:T(8,128)S(1)} %get-tuple-element.72.s0), channel_id=1, source_target_pairs={{0,8},{4,12},{8,0},{12,4},{1,9},{5,13},{9,1},{13,5},{2,10},{6,14},... | collective-permute-start | bytes 61448 | tf_op jit(solution)/shard_map/ppermute | solution.py:516
  86.1 7.6 %collective-permute-start.30 = (f32[8,640]{1,0:T(8,128)S(1)}, f32[8,640]{1,0:T(8,128)S(1)}, u32[]{:S(2)}, u32[]{:S(2)}) collective-permute-start(f32[8,640]{1,0:T(8,128)S(1)} %get-tuple-element.72.s0), channel_id=1, source_target_pairs={{0,12},{4,8},{8,4},{12,0},{1,13},{5,9},{9,5},{13,1},{2,14},{6,10},... | collective-permute-start | bytes 61448 | tf_op jit(solution)/shard_map/ppermute | solution.py:516
  96.3 7.2 %collective-permute-start.34 = (f32[8,640]{1,0:T(8,128)S(1)}, f32[8,640]{1,0:T(8,128)S(1)}, u32[]{:S(2)}, u32[]{:S(2)}) collective-permute-start(f32[8,640]{1,0:T(8,128)S(1)} %get-tuple-element.80.s0), channel_id=1, source_target_pairs={{0,1},{1,0},{2,3},{3,2},{4,5},{5,4},{6,7},{7,6},{8,9},{9,8},{10,11... | collective-permute-start | bytes 61448 | tf_op jit(solution)/shard_map/ppermute | solution.py:516
  (20 other events, 100.0 us)
